TPU v7x, 256 devices: a whole 4x4x8 slice. The times are simulated.
256 devices in a mesh: space: 32 (over z_lo, x, core), hist: 8 (over z_hi, y).
Axes of the slice: x: 4, y: 4, z: 8 (z_hi: 2, z_lo: 4; z = z_hi * 4 + z_lo), core: 2. Of those that a mesh axis runs over, the one named last changes fastest.
Arguments:
- history: bfloat16 [32, 64, 16384], P('hist', None, 'space'), may hold values from -6 to 6
- right_factor: bfloat16 [512, 80, 16384], P('hist', None, 'space'), may hold values from -0.25 to 0.25
- left_factor: bfloat16 [512, 80, 16384], P('hist', None, 'space'), may hold values from -0.125 to 0.125
- pair_rank: int32 [512, 32], P('hist', 'space'), may hold values from 20 to 80
- pair_lag: int32 [512, 32], P('hist', 'space'), may hold values from 0 to 3
- near_block: bfloat16 [3, 16384, 512], P(None, 'space'), may hold values from -0.09695897 to 0.09695897, as said below
- self_term: float32 [16384], P('space'), may hold values from 1 to 1.5
- excitation: float32 [64, 16384], P(None, 'space'), may hold values from -6 to 6
Outputs:
- new_current: float32 [64, 16384], P(None, 'space')
- next_history: bfloat16 [32, 64, 16384], P('hist', None, 'space')
Inputs may be any that keep to these rules, and one draw needn't show every extreme that they name: Entries of near_block lie within 3.8 times (1536) to the power -0.5 in magnitude.
All inputs are finite; a program needn't handle non-finite values.
Results may differ from a plain program's by a relative error of at most 0.015.
Values may be sent and summed in bfloat16 or wider, within the bound.
No kernel may reach another device: no remote copies, remote signals or barrier semaphores. Data moves between devices by JAX's collectives and lax.ppermute only.
A program may use at most 64 MiB of HBM per device.

v0:
```python
import jax
import jax.numpy as jnp
from jax import lax
from jax.sharding import PartitionSpec as P

SWEEPS = 8


def from_everyone(shard, axis):
    devices = lax.axis_size(axis)
    return lax.all_to_all(
        jnp.broadcast_to(shard[None], (devices, *shard.shape)), axis, 0, 0, tiled=True
    )


def of_everyone(shard, axis):
    everything = from_everyone(shard, axis)
    return jnp.sum(everything.astype(jnp.float32), axis=0)


def padded_2(block, sides, width):
    for axis, dim in sides:
        count = lax.axis_size(axis)
        forward = [(i, i + 1) for i in range(count - 1)]
        backward = [(target, source) for source, target in forward]
        low = lax.ppermute(
            lax.slice_in_dim(block, block.shape[dim] - width, None, axis=dim), axis, forward
        )
        high = lax.ppermute(lax.slice_in_dim(block, 0, width, axis=dim), axis, backward)
        block = jnp.concatenate([low, block, high], axis=dim)
    return block


def from_behind(value, axis, steps):
    count = lax.axis_size(axis)
    initial, last = (max(0, -steps), min(count, count - steps))
    return lax.ppermute(value, axis, [(source, source + steps) for source in range(initial, last)])


def per_device(
    history, right_factor, left_factor, pair_rank, pair_lag, near_block, self_term, excitation
):
    time_steps = history.shape[1]
    block_width = history.shape[2]
    pair_dev = right_factor.shape[0]
    rank_most = right_factor.shape[1]
    space_size = lax.axis_size("space")
    per_target = pair_dev // space_size
    chosen = jnp.take(history, pair_lag[:, 0], axis=0)
    coefficient = jnp.einsum(
        "prb,pkb->prk", right_factor, chosen, preferred_element_type=jnp.float32
    )
    levels = lax.broadcasted_iota(jnp.int32, (1, rank_most, 1), 1)
    coefficient = jnp.where(levels < pair_rank[:, 0][:, None, None], coefficient, 0.0).astype(
        jnp.bfloat16
    )
    coefficient = coefficient.reshape(space_size, per_target * rank_most, time_steps)
    left_rows = left_factor.reshape(space_size, per_target * rank_most, block_width)
    partial_value = jnp.einsum(
        "tck,tcb->tkb", coefficient, left_rows, preferred_element_type=jnp.float32
    )
    arrived = lax.all_to_all(
        partial_value.astype(jnp.bfloat16), "space", split_axis=0, concat_axis=0, tiled=True
    ).astype(partial_value.dtype)
    far_field = jnp.sum(arrived, axis=0)
    far_field = of_everyone(far_field.astype(jnp.bfloat16), "hist").astype(jnp.float32)
    right_side = excitation - far_field
    current = jnp.zeros(right_side.shape, jnp.float32)
    for sweep_index in range(SWEEPS):
        rounded = current.astype(jnp.bfloat16)
        padded = padded_2(rounded, (("space", 1),), block_width)
        product = self_term[None, :] * current
        for offset in range(3):
            beside = padded[:, offset * block_width : (offset + 1) * block_width]
            product = product + lax.dot_general(
                beside,
                near_block[offset],
                (((1,), (1,)), ((), ())),
                preferred_element_type=jnp.float32,
            )
        current = current + (right_side - product) / self_term[None, :]
    incoming = from_behind(history[-1], "hist", 1)
    newest = jnp.where(lax.axis_index("hist") == 0, current.astype(jnp.bfloat16), incoming)
    next_history = jnp.concatenate([newest[None], history[:-1]], axis=0)
    return (current, next_history)


def solution(mesh):
    in_specs = (
        P("hist", None, "space"),
        P("hist", None, "space"),
        P("hist", None, "space"),
        P("hist", "space"),
        P("hist", "space"),
        P(None, "space", None),
        P("space"),
        P(None, "space"),
    )
    out_specs = (P(None, "space"), P("hist", None, "space"))
    return jax.shard_map(
        per_device, mesh=mesh, in_specs=in_specs, out_specs=out_specs, check_vma=False
    )
```

profile of v0, /device:TPU:39, one launch (start us, length us, event | category | flops | bytes accessed | tf_op | source)
XLA Modules:
  0.0 178.7 jit_solution(10707911468935272907)
XLA Ops:
  0.6 0.7 fusion.100
  1.3 0.7 and_bitcast_fusion
  2.0 0.7 iota_compare_fusion
  2.7 3.7 %gather_fusion = bf16[64,64,512]{2,1,0:T(8,128)(2,1)} fusion(bf16[4,64,512]{2,1,0:T(8,128)(2,1)} %param.8, s32[1024]{0:T(1024)S(1)} %pad_clamp_fusion), kind=kCustom, calls=%fused_computation | custom fusion | bytes 8388864 | tf_op jit(solution)/shard_map/jit(_take)/gather | solution.py:49
  6.4 5.3 %fusion.6 = bf16[64,80,64]{1,2,0:T(8,128)(2,1)S(1)} fusion(bf16[64,80,512]{2,1,0:T(8,128)(2,1)} %param.9, bf16[64,64,512]{2,1,0:T(8,128)(2,1)} %gather_fusion, pred[64]{0:T(512)(128)(4,1)S(1)} %and_bitcast_fusion, pred[64,80]{1,0:T(8,128)(4,1)S(1)} %iota_compare_fusion), kind=kOutput, calls=%fused_computation.7 | convolution fusion | flops 338296832 | bytes 10097728 | tf_op jit(solution)/shard_map/prb,pkb->prk/dot_general | solution.py:50
  11.8 0.7 copy.12
  12.4 0.7 reshape.43
  13.1 5.0 %convolution_convert_fusion = bf16[32,64,512]{2,1,0:T(8,128)(2,1)} fusion(bf16[32,160,512]{2,1,0:T(8,128)(2,1)} %bitcast.104, bf16[32,160,64]{1,0,2:T(8,128)(2,1)S(1)} %reshape.43), kind=kOutput, calls=%fused_computation.6 | convolution fusion | flops 336592896 | bytes 7995392 | tf_op jit(solution)/shard_map/tck,tcb->tkb/dot_general | solution.py:59
  18.1 8.9 %all-to-all-start = ((bf16[32,64,512]{2,1,0:T(8,128)(2,1)}), bf16[32,64,512]{2,1,0:T(8,128)(2,1)}, u32[]{:S(2)}, u32[]{:S(2)}) async-start(bf16[32,64,512]{2,1,0:T(8,128)(2,1)} %convolution_convert_fusion), calls=%async_computation | async-start | bytes 4194304 | tf_op jit(solution)/shard_map/all_to_all | solution.py:62
  27.0 3.5 %collective-permute-start = (bf16[64,512]{1,0:T(8,128)(2,1)S(1)}, bf16[64,512]{1,0:T(8,128)(2,1)S(1)}, u32[]{:S(2)}, u32[]{:S(2)}) collective-permute-start(bf16[64,512]{1,0:T(8,128)(2,1)S(1)} %convert_element_type.45), channel_id=1, source_target_pairs={{0,8},{8,16},{16,24},{24,32},{32,40},{40,48},{48,56},{56,64},{64,7... | collective-permute-start | bytes 196616 | tf_op jit(solution)/shard_map/ppermute | solution.py:26
  30.6 1.9 %collective-permute-start.1 = (bf16[64,512]{1,0:T(8,128)(2,1)S(1)}, bf16[64,512]{1,0:T(8,128)(2,1)S(1)}, u32[]{:S(2)}, u32[]{:S(2)}) collective-permute-start(bf16[64,512]{1,0:T(8,128)(2,1)S(1)} %convert_element_type.45), channel_id=1, source_target_pairs={{8,0},{16,8},{24,16},{32,24},{40,32},{48,40},{56,48},{64,56},{72,6... | collective-permute-start | bytes 196616 | tf_op jit(solution)/shard_map/ppermute | solution.py:29
  32.5 40.1 %all-to-all-done = bf16[32,64,512]{2,1,0:T(8,128)(2,1)} async-done(((bf16[32,64,512]{2,1,0:T(8,128)(2,1)}), bf16[32,64,512]{2,1,0:T(8,128)(2,1)}, u32[]{:S(2)}, u32[]{:S(2)}) %all-to-all-start) | async-done | bytes 2097184 | tf_op jit(solution)/shard_map/all_to_all | solution.py:62
  72.6 1.9 %reduce_sum.21 = bf16[64,512]{1,0:T(8,128)(2,1)S(1)} reduce(bf16[32,64,512]{2,1,0:T(8,128)(2,1)} %all-to-all-done, bf16[]{:T(256)} %constant.25.clone.1), dimensions={0}, to_apply=%region_0.1 | reduce | flops 1015808 | bytes 2162690 | tf_op jit(solution)/shard_map/reduce_sum | solution.py:65
  74.5 0.9 broadcast_in_dim.32
  75.3 8.1 %all-to-all-start.1 = ((bf16[8,64,512]{2,1,0:T(8,128)(2,1)}), bf16[8,64,512]{2,1,0:T(8,128)(2,1)S(1)}, u32[]{:S(2)}, u32[]{:S(2)}) async-start(bf16[8,64,512]{2,1,0:T(8,128)(2,1)} %broadcast_in_dim.32), calls=%async_computation.1 | async-start | bytes 1048576 | tf_op jit(solution)/shard_map/all_to_all | solution.py:11
  83.5 3.5 %collective-permute-start.16 = (bf16[64,512]{1,0:T(8,128)(2,1)S(1)}, bf16[64,512]{1,0:T(8,128)(2,1)S(1)}, u32[]{:S(2)}, u32[]{:S(2)}) collective-permute-start(bf16[64,512]{1,0:T(8,128)(2,1)S(1)} %slice_bitcast_fusion), channel_id=1, source_target_pairs={{0,1},{1,2},{2,3},{3,4},{4,5},{5,6},{6,7},{8,9},{9,10},{10,11},{11... | collective-permute-start | bytes 196616 | tf_op jit(solution)/shard_map/ppermute | solution.py:37
  87.0 0.3 fusion.62
  87.3 0.3 fusion.38
  87.6 10.0 %all-to-all-done.1 = bf16[8,64,512]{2,1,0:T(8,128)(2,1)S(1)} async-done(((bf16[8,64,512]{2,1,0:T(8,128)(2,1)}), bf16[8,64,512]{2,1,0:T(8,128)(2,1)S(1)}, u32[]{:S(2)}, u32[]{:S(2)}) %all-to-all-start.1) | async-done | bytes 524320 | tf_op jit(solution)/shard_map/all_to_all | solution.py:11
  97.6 0.1 convert_reduce_fusion
  97.7 0.3 fusion.101
  98.0 10.4 %collective-permute-start.2 = (bf16[64,512]{1,0:T(8,128)(2,1)S(1)}, bf16[64,512]{1,0:T(8,128)(2,1)S(1)}, u32[]{:S(2)}, u32[]{:S(2)}) collective-permute-start(bf16[64,512]{1,0:T(8,128)(2,1)S(1)} %get-tuple-element.2), channel_id=1, source_target_pairs={{0,8},{8,16},{16,24},{24,32},{32,40},{40,48},{48,56},{56,64},{64,7... | collective-permute-start | bytes 196616 | tf_op jit(solution)/shard_map/ppermute | solution.py:26
  108.4 0.3 fusion.60
  108.6 1.9 %collective-permute-start.3 = (bf16[64,512]{1,0:T(8,128)(2,1)S(1)}, bf16[64,512]{1,0:T(8,128)(2,1)S(1)}, u32[]{:S(2)}, u32[]{:S(2)}) collective-permute-start(bf16[64,512]{1,0:T(8,128)(2,1)S(1)} %get-tuple-element.2), channel_id=1, source_target_pairs={{8,0},{16,8},{24,16},{32,24},{40,32},{48,40},{56,48},{64,56},{72,6... | collective-permute-start | bytes 196616 | tf_op jit(solution)/shard_map/ppermute | solution.py:29
  110.6 0.3 fusion.70
  110.9 5.5 %collective-permute-done.3 = bf16[64,512]{1,0:T(8,128)(2,1)S(1)} collective-permute-done((bf16[64,512]{1,0:T(8,128)(2,1)S(1)}, bf16[64,512]{1,0:T(8,128)(2,1)S(1)}, u32[]{:S(2)}, u32[]{:S(2)}) %collective-permute-start.3) | collective-permute-done | bytes 65568 | tf_op jit(solution)/shard_map/ppermute | solution.py:29
  116.3 0.3 fusion.102
  116.6 1.9 %collective-permute-start.4 = (bf16[64,512]{1,0:T(8,128)(2,1)S(1)}, bf16[64,512]{1,0:T(8,128)(2,1)S(1)}, u32[]{:S(2)}, u32[]{:S(2)}) collective-permute-start(bf16[64,512]{1,0:T(8,128)(2,1)S(1)} %get-tuple-element.4), channel_id=1, source_target_pairs={{0,8},{8,16},{16,24},{24,32},{32,40},{40,48},{48,56},{56,64},{64,7... | collective-permute-start | bytes 196616 | tf_op jit(solution)/shard_map/ppermute | solution.py:26
  118.6 0.3 fusion.58
  118.8 2.4 %collective-permute-start.5 = (bf16[64,512]{1,0:T(8,128)(2,1)S(1)}, bf16[64,512]{1,0:T(8,128)(2,1)S(1)}, u32[]{:S(2)}, u32[]{:S(2)}) collective-permute-start(bf16[64,512]{1,0:T(8,128)(2,1)S(1)} %get-tuple-element.4), channel_id=1, source_target_pairs={{8,0},{16,8},{24,16},{32,24},{40,32},{48,40},{56,48},{64,56},{72,6... | collective-permute-start | bytes 196616 | tf_op jit(solution)/shard_map/ppermute | solution.py:29
  121.3 0.3 fusion.32
  121.5 5.0 %collective-permute-done.5 = bf16[64,512]{1,0:T(8,128)(2,1)S(1)} collective-permute-done((bf16[64,512]{1,0:T(8,128)(2,1)S(1)}, bf16[64,512]{1,0:T(8,128)(2,1)S(1)}, u32[]{:S(2)}, u32[]{:S(2)}) %collective-permute-start.5) | collective-permute-done | bytes 65568 | tf_op jit(solution)/shard_map/ppermute | solution.py:29
  126.5 0.3 fusion.103
  126.8 1.9 %collective-permute-start.6 = (bf16[64,512]{1,0:T(8,128)(2,1)S(1)}, bf16[64,512]{1,0:T(8,128)(2,1)S(1)}, u32[]{:S(2)}, u32[]{:S(2)}) collective-permute-start(bf16[64,512]{1,0:T(8,128)(2,1)S(1)} %get-tuple-element.6), channel_id=1, source_target_pairs={{0,8},{8,16},{16,24},{24,32},{32,40},{40,48},{48,56},{56,64},{64,7... | collective-permute-start | bytes 196616 | tf_op jit(solution)/shard_map/ppermute | solution.py:26
  128.8 0.3 fusion.56
  129.0 2.4 %collective-permute-start.7 = (bf16[64,512]{1,0:T(8,128)(2,1)S(1)}, bf16[64,512]{1,0:T(8,128)(2,1)S(1)}, u32[]{:S(2)}, u32[]{:S(2)}) collective-permute-start(bf16[64,512]{1,0:T(8,128)(2,1)S(1)} %get-tuple-element.6), channel_id=1, source_target_pairs={{8,0},{16,8},{24,16},{32,24},{40,32},{48,40},{56,48},{64,56},{72,6... | collective-permute-start | bytes 196616 | tf_op jit(solution)/shard_map/ppermute | solution.py:29
  131.5 0.3 fusion.28
  131.8 5.0 %collective-permute-done.7 = bf16[64,512]{1,0:T(8,128)(2,1)S(1)} collective-permute-done((bf16[64,512]{1,0:T(8,128)(2,1)S(1)}, bf16[64,512]{1,0:T(8,128)(2,1)S(1)}, u32[]{:S(2)}, u32[]{:S(2)}) %collective-permute-start.7) | collective-permute-done | bytes 65568 | tf_op jit(solution)/shard_map/ppermute | solution.py:29
  136.7 0.3 fusion.104
  137.0 1.9 %collective-permute-start.8 = (bf16[64,512]{1,0:T(8,128)(2,1)S(1)}, bf16[64,512]{1,0:T(8,128)(2,1)S(1)}, u32[]{:S(2)}, u32[]{:S(2)}) collective-permute-start(bf16[64,512]{1,0:T(8,128)(2,1)S(1)} %get-tuple-element.8), channel_id=1, source_target_pairs={{0,8},{8,16},{16,24},{24,32},{32,40},{40,48},{48,56},{56,64},{64,7... | collective-permute-start | bytes 196616 | tf_op jit(solution)/shard_map/ppermute | solution.py:26
  139.0 0.3 fusion.54
  139.2 2.4 %collective-permute-start.9 = (bf16[64,512]{1,0:T(8,128)(2,1)S(1)}, bf16[64,512]{1,0:T(8,128)(2,1)S(1)}, u32[]{:S(2)}, u32[]{:S(2)}) collective-permute-start(bf16[64,512]{1,0:T(8,128)(2,1)S(1)} %get-tuple-element.8), channel_id=1, source_target_pairs={{8,0},{16,8},{24,16},{32,24},{40,32},{48,40},{56,48},{64,56},{72,6... | collective-permute-start | bytes 196616 | tf_op jit(solution)/shard_map/ppermute | solution.py:29
  141.7 0.3 fusion.24
  142.0 5.0 %collective-permute-done.9 = bf16[64,512]{1,0:T(8,128)(2,1)S(1)} collective-permute-done((bf16[64,512]{1,0:T(8,128)(2,1)S(1)}, bf16[64,512]{1,0:T(8,128)(2,1)S(1)}, u32[]{:S(2)}, u32[]{:S(2)}) %collective-permute-start.9) | collective-permute-done | bytes 65568 | tf_op jit(solution)/shard_map/ppermute | solution.py:29
  146.9 0.3 fusion.105
  147.2 1.9 %collective-permute-start.10 = (bf16[64,512]{1,0:T(8,128)(2,1)S(1)}, bf16[64,512]{1,0:T(8,128)(2,1)S(1)}, u32[]{:S(2)}, u32[]{:S(2)}) collective-permute-start(bf16[64,512]{1,0:T(8,128)(2,1)S(1)} %get-tuple-element.10), channel_id=1, source_target_pairs={{0,8},{8,16},{16,24},{24,32},{32,40},{40,48},{48,56},{56,64},{64,7... | collective-permute-start | bytes 196616 | tf_op jit(solution)/shard_map/ppermute | solution.py:26
  149.2 0.3 fusion.52
  149.4 2.4 %collective-permute-start.11 = (bf16[64,512]{1,0:T(8,128)(2,1)S(1)}, bf16[64,512]{1,0:T(8,128)(2,1)S(1)}, u32[]{:S(2)}, u32[]{:S(2)}) collective-permute-start(bf16[64,512]{1,0:T(8,128)(2,1)S(1)} %get-tuple-element.10), channel_id=1, source_target_pairs={{8,0},{16,8},{24,16},{32,24},{40,32},{48,40},{56,48},{64,56},{72,6... | collective-permute-start | bytes 196616 | tf_op jit(solution)/shard_map/ppermute | solution.py:29
  151.9 0.3 fusion.20
  152.1 5.0 %collective-permute-done.11 = bf16[64,512]{1,0:T(8,128)(2,1)S(1)} collective-permute-done((bf16[64,512]{1,0:T(8,128)(2,1)S(1)}, bf16[64,512]{1,0:T(8,128)(2,1)S(1)}, u32[]{:S(2)}, u32[]{:S(2)}) %collective-permute-start.11) | collective-permute-done | bytes 65568 | tf_op jit(solution)/shard_map/ppermute | solution.py:29
  157.1 0.3 fusion.106
  157.4 1.9 %collective-permute-start.12 = (bf16[64,512]{1,0:T(8,128)(2,1)S(1)}, bf16[64,512]{1,0:T(8,128)(2,1)S(1)}, u32[]{:S(2)}, u32[]{:S(2)}) collective-permute-start(bf16[64,512]{1,0:T(8,128)(2,1)S(1)} %get-tuple-element.12), channel_id=1, source_target_pairs={{0,8},{8,16},{16,24},{24,32},{32,40},{40,48},{48,56},{56,64},{64,7... | collective-permute-start | bytes 196616 | tf_op jit(solution)/shard_map/ppermute | solution.py:26
  159.4 0.3 fusion.50
  159.6 2.4 %collective-permute-start.13 = (bf16[64,512]{1,0:T(8,128)(2,1)S(1)}, bf16[64,512]{1,0:T(8,128)(2,1)S(1)}, u32[]{:S(2)}, u32[]{:S(2)}) collective-permute-start(bf16[64,512]{1,0:T(8,128)(2,1)S(1)} %get-tuple-element.12), channel_id=1, source_target_pairs={{8,0},{16,8},{24,16},{32,24},{40,32},{48,40},{56,48},{64,56},{72,6... | collective-permute-start | bytes 196616 | tf_op jit(solution)/shard_map/ppermute | solution.py:29
  162.1 0.3 fusion.16
  162.3 5.0 %collective-permute-done.13 = bf16[64,512]{1,0:T(8,128)(2,1)S(1)} collective-permute-done((bf16[64,512]{1,0:T(8,128)(2,1)S(1)}, bf16[64,512]{1,0:T(8,128)(2,1)S(1)}, u32[]{:S(2)}, u32[]{:S(2)}) %collective-permute-start.13) | collective-permute-done | bytes 65568 | tf_op jit(solution)/shard_map/ppermute | solution.py:29
  167.3 0.3 fusion.107
  167.6 2.1 %collective-permute-start.14 = (bf16[64,512]{1,0:T(8,128)(2,1)S(1)}, bf16[64,512]{1,0:T(8,128)(2,1)S(1)}, u32[]{:S(2)}, u32[]{:S(2)}) collective-permute-start(bf16[64,512]{1,0:T(8,128)(2,1)S(1)} %get-tuple-element.14), channel_id=1, source_target_pairs={{0,8},{8,16},{16,24},{24,32},{32,40},{40,48},{48,56},{56,64},{64,7... | collective-permute-start | bytes 196616 | tf_op jit(solution)/shard_map/ppermute | solution.py:26
  169.7 0.3 fusion.48
  170.0 2.4 %collective-permute-start.15 = (bf16[64,512]{1,0:T(8,128)(2,1)S(1)}, bf16[64,512]{1,0:T(8,128)(2,1)S(1)}, u32[]{:S(2)}, u32[]{:S(2)}) collective-permute-start(bf16[64,512]{1,0:T(8,128)(2,1)S(1)} %get-tuple-element.14), channel_id=1, source_target_pairs={{8,0},{16,8},{24,16},{32,24},{40,32},{48,40},{56,48},{64,56},{72,6... | collective-permute-start | bytes 196616 | tf_op jit(solution)/shard_map/ppermute | solution.py:29
  172.4 0.3 fusion.12
  172.7 5.0 %collective-permute-done.15 = bf16[64,512]{1,0:T(8,128)(2,1)S(1)} collective-permute-done((bf16[64,512]{1,0:T(8,128)(2,1)S(1)}, bf16[64,512]{1,0:T(8,128)(2,1)S(1)}, u32[]{:S(2)}, u32[]{:S(2)}) %collective-permute-start.15) | collective-permute-done | bytes 65568 | tf_op jit(solution)/shard_map/ppermute | solution.py:29
  177.7 0.3 fusion.11
  178.0 0.7 pad_maximum_fusion
  (28 shorter events, 0.1 us)
Async XLA Ops:
  18.1 54.5 %all-to-all-start = ((bf16[32,64,512]{2,1,0:T(8,128)(2,1)}), bf16[32,64,512]{2,1,0:T(8,128)(2,1)}, u32[]{:S(2)}, u32[]{:S(2)}) async-start(bf16[32,64,512]{2,1,0:T(8,128)(2,1)} %convolution_convert_fusion), calls=%async_computation | async-start | bytes 4194304 | tf_op jit(solution)/shard_map/all_to_all | solution.py:62
  27.0 56.4 %copy-start.1 = (bf16[4,64,512]{2,1,0:T(8,128)(2,1)S(1)}, bf16[4,64,512]{2,1,0:T(8,128)(2,1)}, u32[]{:S(2)}) copy-start(bf16[4,64,512]{2,1,0:T(8,128)(2,1)} %param.8) | copy-start | bytes 786436
  27.0 59.9 %copy-start = (bf16[3,512,512]{2,1,0:T(8,128)(2,1)S(1)}, bf16[3,512,512]{2,1,0:T(8,128)(2,1)}, u32[]{:S(2)}) copy-start(bf16[3,512,512]{2,1,0:T(8,128)(2,1)} %param.13) | copy-start | bytes 4718596
  27.0 60.2 %collective-permute-start = (bf16[64,512]{1,0:T(8,128)(2,1)S(1)}, bf16[64,512]{1,0:T(8,128)(2,1)S(1)}, u32[]{:S(2)}, u32[]{:S(2)}) collective-permute-start(bf16[64,512]{1,0:T(8,128)(2,1)S(1)} %convert_element_type.45), channel_id=1, source_target_pairs={{0,8},{8,16},{16,24},{24,32},{32,40},{40,48},{48,56},{56,64},{64,7... | collective-permute-start | bytes 196616 | tf_op jit(solution)/shard_map/ppermute | solution.py:26
  30.6 67.1 %collective-permute-start.1 = (bf16[64,512]{1,0:T(8,128)(2,1)S(1)}, bf16[64,512]{1,0:T(8,128)(2,1)S(1)}, u32[]{:S(2)}, u32[]{:S(2)}) collective-permute-start(bf16[64,512]{1,0:T(8,128)(2,1)S(1)} %convert_element_type.45), channel_id=1, source_target_pairs={{8,0},{16,8},{24,16},{32,24},{40,32},{48,40},{56,48},{64,56},{72,6... | collective-permute-start | bytes 196616 | tf_op jit(solution)/shard_map/ppermute | solution.py:29
  74.5 12.8 %copy-start.2 = (f32[512]{0:T(512)S(1)}, f32[512]{0:T(512)}, u32[]{:S(2)}) copy-start(f32[512]{0:T(512)} %param.14) | copy-start | bytes 6148
  75.3 22.2 %all-to-all-start.1 = ((bf16[8,64,512]{2,1,0:T(8,128)(2,1)}), bf16[8,64,512]{2,1,0:T(8,128)(2,1)S(1)}, u32[]{:S(2)}, u32[]{:S(2)}) async-start(bf16[8,64,512]{2,1,0:T(8,128)(2,1)} %broadcast_in_dim.32), calls=%async_computation.1 | async-start | bytes 1048576 | tf_op jit(solution)/shard_map/all_to_all | solution.py:11
  83.5 14.2 %copy-start.3 = (f32[64,512]{1,0:T(8,128)S(1)}, f32[64,512]{1,0:T(8,128)}, u32[]{:S(2)}) copy-start(f32[64,512]{1,0:T(8,128)} %param.15) | copy-start | bytes 393220
  83.5 94.5 %collective-permute-start.16 = (bf16[64,512]{1,0:T(8,128)(2,1)S(1)}, bf16[64,512]{1,0:T(8,128)(2,1)S(1)}, u32[]{:S(2)}, u32[]{:S(2)}) collective-permute-start(bf16[64,512]{1,0:T(8,128)(2,1)S(1)} %slice_bitcast_fusion), channel_id=1, source_target_pairs={{0,1},{1,2},{2,3},{3,4},{4,5},{5,6},{6,7},{8,9},{9,10},{10,11},{11... | collective-permute-start | bytes 196616 | tf_op jit(solution)/shard_map/ppermute | solution.py:37
  98.0 12.6 %collective-permute-start.2 = (bf16[64,512]{1,0:T(8,128)(2,1)S(1)}, bf16[64,512]{1,0:T(8,128)(2,1)S(1)}, u32[]{:S(2)}, u32[]{:S(2)}) collective-permute-start(bf16[64,512]{1,0:T(8,128)(2,1)S(1)} %get-tuple-element.2), channel_id=1, source_target_pairs={{0,8},{8,16},{16,24},{24,32},{32,40},{40,48},{48,56},{56,64},{64,7... | collective-permute-start | bytes 196616 | tf_op jit(solution)/shard_map/ppermute | solution.py:26
  108.6 7.7 %collective-permute-start.3 = (bf16[64,512]{1,0:T(8,128)(2,1)S(1)}, bf16[64,512]{1,0:T(8,128)(2,1)S(1)}, u32[]{:S(2)}, u32[]{:S(2)}) collective-permute-start(bf16[64,512]{1,0:T(8,128)(2,1)S(1)} %get-tuple-element.2), channel_id=1, source_target_pairs={{8,0},{16,8},{24,16},{32,24},{40,32},{48,40},{56,48},{64,56},{72,6... | collective-permute-start | bytes 196616 | tf_op jit(solution)/shard_map/ppermute | solution.py:29
  116.6 4.6 %collective-permute-start.4 = (bf16[64,512]{1,0:T(8,128)(2,1)S(1)}, bf16[64,512]{1,0:T(8,128)(2,1)S(1)}, u32[]{:S(2)}, u32[]{:S(2)}) collective-permute-start(bf16[64,512]{1,0:T(8,128)(2,1)S(1)} %get-tuple-element.4), channel_id=1, source_target_pairs={{0,8},{8,16},{16,24},{24,32},{32,40},{40,48},{48,56},{56,64},{64,7... | collective-permute-start | bytes 196616 | tf_op jit(solution)/shard_map/ppermute | solution.py:26
  118.8 7.7 %collective-permute-start.5 = (bf16[64,512]{1,0:T(8,128)(2,1)S(1)}, bf16[64,512]{1,0:T(8,128)(2,1)S(1)}, u32[]{:S(2)}, u32[]{:S(2)}) collective-permute-start(bf16[64,512]{1,0:T(8,128)(2,1)S(1)} %get-tuple-element.4), channel_id=1, source_target_pairs={{8,0},{16,8},{24,16},{32,24},{40,32},{48,40},{56,48},{64,56},{72,6... | collective-permute-start | bytes 196616 | tf_op jit(solution)/shard_map/ppermute | solution.py:29
  126.8 4.6 %collective-permute-start.6 = (bf16[64,512]{1,0:T(8,128)(2,1)S(1)}, bf16[64,512]{1,0:T(8,128)(2,1)S(1)}, u32[]{:S(2)}, u32[]{:S(2)}) collective-permute-start(bf16[64,512]{1,0:T(8,128)(2,1)S(1)} %get-tuple-element.6), channel_id=1, source_target_pairs={{0,8},{8,16},{16,24},{24,32},{32,40},{40,48},{48,56},{56,64},{64,7... | collective-permute-start | bytes 196616 | tf_op jit(solution)/shard_map/ppermute | solution.py:26
  129.0 7.7 %collective-permute-start.7 = (bf16[64,512]{1,0:T(8,128)(2,1)S(1)}, bf16[64,512]{1,0:T(8,128)(2,1)S(1)}, u32[]{:S(2)}, u32[]{:S(2)}) collective-permute-start(bf16[64,512]{1,0:T(8,128)(2,1)S(1)} %get-tuple-element.6), channel_id=1, source_target_pairs={{8,0},{16,8},{24,16},{32,24},{40,32},{48,40},{56,48},{64,56},{72,6... | collective-permute-start | bytes 196616 | tf_op jit(solution)/shard_map/ppermute | solution.py:29
  137.0 4.6 %collective-permute-start.8 = (bf16[64,512]{1,0:T(8,128)(2,1)S(1)}, bf16[64,512]{1,0:T(8,128)(2,1)S(1)}, u32[]{:S(2)}, u32[]{:S(2)}) collective-permute-start(bf16[64,512]{1,0:T(8,128)(2,1)S(1)} %get-tuple-element.8), channel_id=1, source_target_pairs={{0,8},{8,16},{16,24},{24,32},{32,40},{40,48},{48,56},{56,64},{64,7... | collective-permute-start | bytes 196616 | tf_op jit(solution)/shard_map/ppermute | solution.py:26
  139.2 7.7 %collective-permute-start.9 = (bf16[64,512]{1,0:T(8,128)(2,1)S(1)}, bf16[64,512]{1,0:T(8,128)(2,1)S(1)}, u32[]{:S(2)}, u32[]{:S(2)}) collective-permute-start(bf16[64,512]{1,0:T(8,128)(2,1)S(1)} %get-tuple-element.8), channel_id=1, source_target_pairs={{8,0},{16,8},{24,16},{32,24},{40,32},{48,40},{56,48},{64,56},{72,6... | collective-permute-start | bytes 196616 | tf_op jit(solution)/shard_map/ppermute | solution.py:29
  147.2 4.6 %collective-permute-start.10 = (bf16[64,512]{1,0:T(8,128)(2,1)S(1)}, bf16[64,512]{1,0:T(8,128)(2,1)S(1)}, u32[]{:S(2)}, u32[]{:S(2)}) collective-permute-start(bf16[64,512]{1,0:T(8,128)(2,1)S(1)} %get-tuple-element.10), channel_id=1, source_target_pairs={{0,8},{8,16},{16,24},{24,32},{32,40},{40,48},{48,56},{56,64},{64,7... | collective-permute-start | bytes 196616 | tf_op jit(solution)/shard_map/ppermute | solution.py:26
  149.4 7.7 %collective-permute-start.11 = (bf16[64,512]{1,0:T(8,128)(2,1)S(1)}, bf16[64,512]{1,0:T(8,128)(2,1)S(1)}, u32[]{:S(2)}, u32[]{:S(2)}) collective-permute-start(bf16[64,512]{1,0:T(8,128)(2,1)S(1)} %get-tuple-element.10), channel_id=1, source_target_pairs={{8,0},{16,8},{24,16},{32,24},{40,32},{48,40},{56,48},{64,56},{72,6... | collective-permute-start | bytes 196616 | tf_op jit(solution)/shard_map/ppermute | solution.py:29
  157.4 4.6 %collective-permute-start.12 = (bf16[64,512]{1,0:T(8,128)(2,1)S(1)}, bf16[64,512]{1,0:T(8,128)(2,1)S(1)}, u32[]{:S(2)}, u32[]{:S(2)}) collective-permute-start(bf16[64,512]{1,0:T(8,128)(2,1)S(1)} %get-tuple-element.12), channel_id=1, source_target_pairs={{0,8},{8,16},{16,24},{24,32},{32,40},{40,48},{48,56},{56,64},{64,7... | collective-permute-start | bytes 196616 | tf_op jit(solution)/shard_map/ppermute | solution.py:26
  159.6 7.7 %collective-permute-start.13 = (bf16[64,512]{1,0:T(8,128)(2,1)S(1)}, bf16[64,512]{1,0:T(8,128)(2,1)S(1)}, u32[]{:S(2)}, u32[]{:S(2)}) collective-permute-start(bf16[64,512]{1,0:T(8,128)(2,1)S(1)} %get-tuple-element.12), channel_id=1, source_target_pairs={{8,0},{16,8},{24,16},{32,24},{40,32},{48,40},{56,48},{64,56},{72,6... | collective-permute-start | bytes 196616 | tf_op jit(solution)/shard_map/ppermute | solution.py:29
  167.6 10.4 %slice-start = ((bf16[4,64,512]{2,1,0:T(8,128)(2,1)}), bf16[3,64,512]{2,1,0:T(8,128)(2,1)S(1)}, s32[]{:S(2)}) async-start(bf16[4,64,512]{2,1,0:T(8,128)(2,1)} %param.8), calls=%async_computation.2 | async-start | bytes 393216 | tf_op jit(solution)/shard_map/slice | solution.py:84
  167.6 4.8 %collective-permute-start.14 = (bf16[64,512]{1,0:T(8,128)(2,1)S(1)}, bf16[64,512]{1,0:T(8,128)(2,1)S(1)}, u32[]{:S(2)}, u32[]{:S(2)}) collective-permute-start(bf16[64,512]{1,0:T(8,128)(2,1)S(1)} %get-tuple-element.14), channel_id=1, source_target_pairs={{0,8},{8,16},{16,24},{24,32},{32,40},{40,48},{48,56},{56,64},{64,7... | collective-permute-start | bytes 196616 | tf_op jit(solution)/shard_map/ppermute | solution.py:26
  170.0 7.7 %collective-permute-start.15 = (bf16[64,512]{1,0:T(8,128)(2,1)S(1)}, bf16[64,512]{1,0:T(8,128)(2,1)S(1)}, u32[]{:S(2)}, u32[]{:S(2)}) collective-permute-start(bf16[64,512]{1,0:T(8,128)(2,1)S(1)} %get-tuple-element.14), channel_id=1, source_target_pairs={{8,0},{16,8},{24,16},{32,24},{40,32},{48,40},{56,48},{64,56},{72,6... | collective-permute-start | bytes 196616 | tf_op jit(solution)/shard_map/ppermute | solution.py:29
  178.0 0.8 copy-start.4
where the time goes:
time: 180 us; the launch traced here: 179 us
  waiting for transfers between devices  85.5 us (48%)
  starting transfers between devices  64.3 us (36%)
  matrix products  17.1 us (10%)
  local copies, waits for them, and re-layouts  6 us (3%)
  other arithmetic  4.78 us (3%)
    all_to_all x1, waiting for transfers between devices, per_device(): lax.all_to_all(partial_value.astype(jnp.bfloat16), 'space', split_axis=0,...  40.1 us
    ppermute x8, waiting for transfers between devices, padded_2(): lax.ppermute(lax.slice_in_dim(block, 0, width, axis=dim), axis, backward)  35.4 us
    ppermute x8, starting transfers between devices, padded_2(): lax.ppermute(lax.slice_in_dim(block, block.shape[dim] - width, None, axis...  25.5 us
    ppermute x8, starting transfers between devices, padded_2(): lax.ppermute(lax.slice_in_dim(block, 0, width, axis=dim), axis, backward)  18.3 us
    all_to_all x1, waiting for transfers between devices, from_everyone(): lax.all_to_all(jnp.broadcast_to(shard[None], (devices, *shard.shape)), ax...  9.97 us
    all_to_all x1, starting transfers between devices, per_device(): lax.all_to_all(partial_value.astype(jnp.bfloat16), 'space', split_axis=0,...  8.88 us
    all_to_all x1, starting transfers between devices, from_everyone(): lax.all_to_all(jnp.broadcast_to(shard[None], (devices, *shard.shape)), ax...  8.12 us
    dot_general x24, matrix products, per_device(): lax.dot_general(beside, near_block[offset], (((1,), (1,)), ((), ())), pre...  6.79 us
  transfers between devices with their start and end apart: 19, of which 9 were waited for; matrix products, arithmetic and copies ran while one was open for 5% of the time, Pallas kernels for 0%

commit v1 on v0

v1 whole, which is shorter than its diff:
```python
import functools

import jax
import jax.numpy as jnp
from jax import lax
from jax.experimental import pallas as pl
from jax.experimental.pallas import tpu as pltpu
from jax.sharding import Mesh
from jax.sharding import PartitionSpec as P

SWEEPS = 8
SPACE = ("zl", "x", "c")
HIST = ("zh", "y")


def far_kernel(core_ref, rank_ref, lag_ref, hist_ref, right_ref, left_ref, out_ref, *, ranks):
    group = pl.program_id(0)
    chips, _, depth, width = right_ref.shape
    lags, steps, _ = hist_ref.shape
    total = chips * depth
    lane = lax.broadcasted_iota(jnp.int32, (1, total), 1)
    column = jnp.full((1, total), -1, jnp.int32)
    per = depth // ranks
    for chip in range(chips):
        for k in range(per):
            pair = ((group * chips + chip) * 2 + core_ref[0]) * per + k
            first = (chip * per + k) * ranks
            inside = (lane >= first) & (lane < first + rank_ref[pair])
            column = jnp.where(inside, lag_ref[pair], column)
    right = right_ref[...].reshape(total, width)
    every = lax.dot_general(
        hist_ref[...].reshape(lags * steps, width),
        right,
        (((1,), (1,)), ((), ())),
        preferred_element_type=jnp.float32,
    )
    chosen = jnp.zeros((steps, total), jnp.float32)
    for lag in range(lags):
        chosen = jnp.where(column == lag, every[lag * steps : (lag + 1) * steps], chosen)
    chosen = chosen.astype(jnp.bfloat16)
    left = left_ref[...].reshape(total, width)
    for chip in range(chips):
        first, last = chip * depth, (chip + 1) * depth
        low, high = first // 128 * 128, -(-last // 128) * 128
        part = chosen[:, low:high]
        at = lax.broadcasted_iota(jnp.int32, part.shape, 1) + low
        part = jnp.where((at >= first) & (at < last), part, jnp.zeros_like(part))
        value = jnp.dot(part, left[low:high], preferred_element_type=jnp.float32)
        out_ref[chip] = value.reshape(out_ref.shape[1:]).astype(out_ref.dtype)


def far_half(core, rank, lag, history, right, left, ranks):
    rows, cores, depth, width = right.shape
    lags, steps, _ = history.shape
    groups, chips, cuts = 4, 4, 4
    spec = pl.BlockSpec((chips, 1, depth, width), lambda g, core, *_: (g, core[0], 0, 0))
    return pl.pallas_call(
        functools.partial(far_kernel, ranks=ranks),
        out_shape=jax.ShapeDtypeStruct((chips, cuts, groups, steps // cuts, width), jnp.bfloat16),
        grid_spec=pltpu.PrefetchScalarGridSpec(
            num_scalar_prefetch=3,
            grid=(groups,),
            in_specs=[
                pl.BlockSpec((lags, steps, width), lambda g, *_: (0, 0, 0)),
                spec,
                spec,
            ],
            out_specs=pl.BlockSpec(
                (chips, cuts, 1, steps // cuts, width), lambda g, *_: (0, 0, g, 0, 0)
            ),
        ),
        compiler_params=pltpu.CompilerParams(vmem_limit_bytes=60 * 1024 * 1024),
        cost_estimate=pl.CostEstimate(
            flops=2 * rows * depth * width * (lags + 1) * steps,
            bytes_accessed=rows * depth * width * 4 + rows * steps * width * 2,
            transcendentals=0,
        ),
        name="far_half",
    )(core, rank, lag, history, right, left)


def per_device(
    history, right_factor, left_factor, pair_rank, pair_lag, near_block, self_term, excitation
):
    lags, time_steps, width = history.shape
    pairs, ranks, _ = right_factor.shape
    targets = 32
    depth = pairs // targets * ranks
    right = right_factor.reshape(targets // 2, 2, depth, width)
    left = left_factor.reshape(targets // 2, 2, depth, width)
    rank, lag = pair_rank[:, 0], pair_lag[:, 0]
    core = lax.axis_index("c")
    swap = [(0, 1), (1, 0)]

    def half(which):
        return far_half(which.reshape(1), rank, lag, history, right, left, ranks)

    away = half(1 - core)
    came = lax.ppermute(away, "c", swap)
    mine = half(core)
    partial_value = (mine.astype(jnp.float32) + came.astype(jnp.float32)).astype(jnp.bfloat16)
    arrived = lax.all_to_all(
        partial_value.reshape(16, -1, width), ("x", "y"), 0, 0, tiled=True
    ).reshape(16, 4, -1, width)
    order = [(i, i + 1) for i in range(7)]
    incoming = lax.ppermute(history[-1], HIST, order)
    arrived, incoming = lax.optimization_barrier((arrived, incoming))
    plane = jnp.sum(arrived.astype(jnp.float32), axis=0).astype(jnp.bfloat16)
    twice = jnp.broadcast_to(plane[None], (2, *plane.shape)).reshape(8, -1, width)
    arrived = lax.all_to_all(twice, ("zh", "zl"), 0, 0, tiled=True)
    far_field = jnp.sum(arrived.astype(jnp.float32), axis=0)
    rows = time_steps // 4
    cut = lax.axis_index("y") * rows
    right_side = lax.dynamic_slice_in_dim(excitation, cut, rows, 0) - far_field

    inverse = 1.0 / self_term[None, :]
    near_own = near_block[1]
    near_chip = jnp.where(core == 0, near_block[2], near_block[0])
    near_away = jnp.where(core == 0, near_block[0], near_block[2])
    between = []
    for t in range(1, targets - 1, 2):
        between += [(t, t + 1), (t + 1, t)]

    def product(value, block):
        return lax.dot_general(
            value, block, (((1,), (1,)), ((), ())), preferred_element_type=jnp.float32
        )

    current = right_side * inverse
    for _ in range(SWEEPS - 1):
        rounded = current.astype(jnp.bfloat16)
        far = lax.ppermute(rounded, SPACE, between)
        chip = lax.ppermute(rounded, "c", swap)
        total = product(rounded, near_own) + product(chip, near_chip)
        total = total + product(far, near_away)
        current = (right_side - total) * inverse

    everywhere = lax.all_to_all(
        jnp.broadcast_to(current[None], (4, *current.shape)), "y", 0, 0, tiled=True
    ).reshape(time_steps, width)
    oldest = (lax.axis_index("zh") == 0) & (lax.axis_index("y") == 0)
    newest = jnp.where(oldest, everywhere.astype(jnp.bfloat16), incoming)
    next_history = jnp.concatenate([newest[None], history[:-1]], axis=0)
    return (everywhere, next_history)


def solution(mesh):
    fine = Mesh(mesh.devices.reshape(4, 4, 2, 2, 4), SPACE + HIST)
    in_specs = (
        P(HIST, None, SPACE),
        P(HIST, None, SPACE),
        P(HIST, None, SPACE),
        P(HIST, SPACE),
        P(HIST, SPACE),
        P(None, SPACE, None),
        P(SPACE),
        P(None, SPACE),
    )
    out_specs = (P(None, SPACE), P(HIST, None, SPACE))
    return jax.shard_map(
        per_device, mesh=fine, in_specs=in_specs, out_specs=out_specs, check_vma=False
    )
```

time: 180 us -> 125 us (0.69)
  the two profiles are of different devices: /device:TPU:39 before, /device:TPU:32 now
where the time goes in v1:
time: 125 us; the launch traced here: 124 us
  starting transfers between devices  50.4 us (40%)
  waiting for transfers between devices  49.2 us (39%)
  Pallas kernels  12.5 us (10%)
  matrix products  4.92 us (4%)
  other arithmetic  4.42 us (4%)
  local copies, waits for them, and re-layouts  2.03 us (2%)
    ppermute x7, starting transfers between devices, per_device(): far = lax.ppermute(rounded, SPACE, between)  27.3 us
    ppermute x7, waiting for transfers between devices, per_device(): far = lax.ppermute(rounded, SPACE, between)  21.1 us
    pallas_call x2, Pallas kernels, far_half(): pl.pallas_call(functools.partial(far_kernel, ranks=ranks), out_shape=jax....  12.5 us
    ppermute x1, waiting for transfers between devices, per_device(): incoming = lax.ppermute(history[-1], HIST, order)  9.29 us
    all_to_all x1, starting transfers between devices, per_device(): arrived = lax.all_to_all(twice, ('zh', 'zl'), 0, 0, tiled=True)  8.57 us
    all_to_all x1, waiting for transfers between devices, per_device(): arrived = lax.all_to_all(twice, ('zh', 'zl'), 0, 0, tiled=True)  7.52 us
    all_to_all x1, starting transfers between devices, per_device(): lax.all_to_all(partial_value.reshape(16, -1, width), ('x', 'y'), 0, 0, ti...  7.16 us
    all_to_all x1, waiting for transfers between devices, per_device(): lax.all_to_all(jnp.broadcast_to(current[None], (4, *current.shape)), 'y',...  5.93 us
  transfers between devices with their start and end apart: 19, of which 11 were waited for; matrix products, arithmetic and copies ran while one was open for 3% of the time, Pallas kernels for 5%

profile of v1, /device:TPU:32, one launch (start us, length us, event | category | flops | bytes accessed | tf_op | source)
XLA Modules:
  0.0 124.4 jit_solution(6080981072552667970)
XLA Ops:
  0.6 6.3 %far_half.3 = bf16[4,4,4,16,512]{4,3,2,1,0:T(8,128)(2,1)} custom-call(s32[1]{0:T(128)} %bitcast.5.core_ref, s32[64]{0:T(128)} %bitcast.87, s32[64]{0:T(128)} %bitcast.89, bf16[4,64,512]{2,1,0:T(8,128)(2,1)} %hist_ref.3, bf16[16,2,160,512]{3,2,1,0:T(8,128)(2,1)} %bitcast.81, bf16[16,2,160,512]{3,2,1,0:T(8,128)(2,1)} %bitcast.83), custom_call_target="tpu_custom_call" | custom-call | flops 838860800 | bytes 6291456 | tf_op jit(solution)/shard_map/far_half/pallas_call | solution.py:57
  6.9 0.0 collective-permute-start
  6.9 6.2 %far_half.2 = bf16[4,4,4,16,512]{4,3,2,1,0:T(8,128)(2,1)} custom-call(s32[1]{0:T(128)} %bitcast.core_ref, s32[64]{0:T(128)} %bitcast.88, s32[64]{0:T(128)} %bitcast.90, bf16[4,64,512]{2,1,0:T(8,128)(2,1)} %hist_ref.3, bf16[16,2,160,512]{3,2,1,0:T(8,128)(2,1)} %bitcast.82, bf16[16,2,160,512]{3,2,1,0:T(8,128)(2,1)} %bitcast.84), custom_call_target="tpu_custom_call" | custom-call | flops 838860800 | bytes 6291456 | tf_op jit(solution)/shard_map/far_half/pallas_call | solution.py:57
  13.1 0.0 collective-permute-done
  13.2 2.6 %add_convert_fusion = bf16[4,4,4,16,512]{4,3,2,1,0:T(8,128)(2,1)} fusion(bf16[4,4,4,16,512]{4,3,2,1,0:T(8,128)(2,1)S(1)} %collective-permute-done, bf16[4,4,4,16,512]{4,3,2,1,0:T(8,128)(2,1)} %far_half.2), kind=kLoop, calls=%fused_computation | loop fusion | flops 2097152 | bytes 3145728 | tf_op jit(solution)/shard_map/convert_element_type | solution.py:101
  15.8 7.2 %all-to-all-start = ((bf16[16,64,512]{2,1,0:T(8,128)(2,1)}), bf16[16,64,512]{2,1,0:T(8,128)(2,1)S(1)}, u32[]{:S(2)}, u32[]{:S(2)}) async-start(bf16[16,64,512]{2,1,0:T(8,128)(2,1)} %bitcast.6), calls=%async_computation | async-start | bytes 2097152 | tf_op jit(solution)/shard_map/all_to_all | solution.py:102
  23.0 3.8 %collective-permute-start.1 = (bf16[64,512]{1,0:T(8,128)(2,1)S(1)}, bf16[64,512]{1,0:T(8,128)(2,1)S(1)}, u32[]{:S(2)}, u32[]{:S(2)}) collective-permute-start(bf16[64,512]{1,0:T(8,128)(2,1)S(1)} %slice_bitcast_fusion), channel_id=1, source_target_pairs={{0,1},{1,2},{2,3},{3,4},{4,5},{5,6},{6,7},{8,9},{9,10},{10,11},{11... | collective-permute-start | bytes 196616 | tf_op jit(solution)/shard_map/ppermute | solution.py:106
  26.8 9.3 %collective-permute-done.1 = bf16[64,512]{1,0:T(8,128)(2,1)S(1)} collective-permute-done((bf16[64,512]{1,0:T(8,128)(2,1)S(1)}, bf16[64,512]{1,0:T(8,128)(2,1)S(1)}, u32[]{:S(2)}, u32[]{:S(2)}) %collective-permute-start.1) | collective-permute-done | bytes 65568 | tf_op jit(solution)/shard_map/ppermute | solution.py:106
  36.1 5.3 %all-to-all-done = bf16[16,64,512]{2,1,0:T(8,128)(2,1)S(1)} async-done(((bf16[16,64,512]{2,1,0:T(8,128)(2,1)}), bf16[16,64,512]{2,1,0:T(8,128)(2,1)S(1)}, u32[]{:S(2)}, u32[]{:S(2)}) %all-to-all-start) | async-done | bytes 1048608 | tf_op jit(solution)/shard_map/all_to_all | solution.py:102
  41.4 0.2 reduce_sum.21
  41.6 0.7 broadcast_in_dim.6
  42.3 8.6 %all-to-all-start.1 = ((bf16[8,16,512]{2,1,0:T(8,128)(2,1)}), bf16[8,16,512]{2,1,0:T(8,128)(2,1)S(1)}, u32[]{:S(2)}, u32[]{:S(2)}) async-start(bf16[8,16,512]{2,1,0:T(8,128)(2,1)} %bitcast.9), calls=%async_computation.1 | async-start | bytes 262144 | tf_op jit(solution)/shard_map/all_to_all | solution.py:110
  50.9 0.1 broadcast_select_fusion
  51.0 7.5 %all-to-all-done.1 = bf16[8,16,512]{2,1,0:T(8,128)(2,1)S(1)} async-done(((bf16[8,16,512]{2,1,0:T(8,128)(2,1)}), bf16[8,16,512]{2,1,0:T(8,128)(2,1)S(1)}, u32[]{:S(2)}, u32[]{:S(2)}) %all-to-all-start.1) | async-done | bytes 131104 | tf_op jit(solution)/shard_map/all_to_all | solution.py:110
  58.5 0.8 multiply_convert_fusion
  59.3 0.2 fusion.46
  59.5 3.9 %collective-permute-start.3 = (bf16[16,512]{1,0:T(8,128)(2,1)S(1)}, bf16[16,512]{1,0:T(8,128)(2,1)S(1)}, u32[]{:S(2)}, u32[]{:S(2)}) collective-permute-start(bf16[16,512]{1,0:T(8,128)(2,1)S(1)} %get-tuple-element.6), channel_id=1, source_target_pairs={{8,16},{16,8},{24,32},{32,24},{40,48},{48,40},{56,64},{64,56},{72,... | collective-permute-start | bytes 49160 | tf_op jit(solution)/shard_map/ppermute | solution.py:132
  63.4 0.0 collective-permute-done.2
  63.4 0.2 convolution_add_fusion.13
  63.7 3.0 %collective-permute-done.3 = bf16[16,512]{1,0:T(8,128)(2,1)S(1)} collective-permute-done((bf16[16,512]{1,0:T(8,128)(2,1)S(1)}, bf16[16,512]{1,0:T(8,128)(2,1)S(1)}, u32[]{:S(2)}, u32[]{:S(2)}) %collective-permute-start.3) | collective-permute-done | bytes 16416 | tf_op jit(solution)/shard_map/ppermute | solution.py:132
  66.7 0.2 fusion.19
  66.9 0.0 collective-permute-start.4
  67.0 0.2 fusion.44
  67.2 3.9 %collective-permute-start.5 = (bf16[16,512]{1,0:T(8,128)(2,1)S(1)}, bf16[16,512]{1,0:T(8,128)(2,1)S(1)}, u32[]{:S(2)}, u32[]{:S(2)}) collective-permute-start(bf16[16,512]{1,0:T(8,128)(2,1)S(1)} %fusion.19), channel_id=1, source_target_pairs={{8,16},{16,8},{24,32},{32,24},{40,48},{48,40},{56,64},{64,56},{72,... | collective-permute-start | bytes 49160 | tf_op jit(solution)/shard_map/ppermute | solution.py:132
  71.1 0.0 collective-permute-done.4
  71.1 0.2 convolution_add_fusion.11
  71.3 3.0 %collective-permute-done.5 = bf16[16,512]{1,0:T(8,128)(2,1)S(1)} collective-permute-done((bf16[16,512]{1,0:T(8,128)(2,1)S(1)}, bf16[16,512]{1,0:T(8,128)(2,1)S(1)}, u32[]{:S(2)}, u32[]{:S(2)}) %collective-permute-start.5) | collective-permute-done | bytes 16416 | tf_op jit(solution)/shard_map/ppermute | solution.py:132
  74.4 0.2 fusion.18
  74.6 0.0 collective-permute-start.6
  74.6 0.2 fusion.42
  74.9 3.9 %collective-permute-start.7 = (bf16[16,512]{1,0:T(8,128)(2,1)S(1)}, bf16[16,512]{1,0:T(8,128)(2,1)S(1)}, u32[]{:S(2)}, u32[]{:S(2)}) collective-permute-start(bf16[16,512]{1,0:T(8,128)(2,1)S(1)} %fusion.18), channel_id=1, source_target_pairs={{8,16},{16,8},{24,32},{32,24},{40,48},{48,40},{56,64},{64,56},{72,... | collective-permute-start | bytes 49160 | tf_op jit(solution)/shard_map/ppermute | solution.py:132
  78.8 0.0 collective-permute-done.6
  78.8 0.2 convolution_add_fusion.9
  79.0 3.0 %collective-permute-done.7 = bf16[16,512]{1,0:T(8,128)(2,1)S(1)} collective-permute-done((bf16[16,512]{1,0:T(8,128)(2,1)S(1)}, bf16[16,512]{1,0:T(8,128)(2,1)S(1)}, u32[]{:S(2)}, u32[]{:S(2)}) %collective-permute-start.7) | collective-permute-done | bytes 16416 | tf_op jit(solution)/shard_map/ppermute | solution.py:132
  82.0 0.2 fusion.17
  82.3 0.0 collective-permute-start.8
  82.3 0.2 fusion.40
  82.5 3.9 %collective-permute-start.9 = (bf16[16,512]{1,0:T(8,128)(2,1)S(1)}, bf16[16,512]{1,0:T(8,128)(2,1)S(1)}, u32[]{:S(2)}, u32[]{:S(2)}) collective-permute-start(bf16[16,512]{1,0:T(8,128)(2,1)S(1)} %fusion.17), channel_id=1, source_target_pairs={{8,16},{16,8},{24,32},{32,24},{40,48},{48,40},{56,64},{64,56},{72,... | collective-permute-start | bytes 49160 | tf_op jit(solution)/shard_map/ppermute | solution.py:132
  86.5 0.2 convolution_add_fusion.7
  86.7 3.0 %collective-permute-done.9 = bf16[16,512]{1,0:T(8,128)(2,1)S(1)} collective-permute-done((bf16[16,512]{1,0:T(8,128)(2,1)S(1)}, bf16[16,512]{1,0:T(8,128)(2,1)S(1)}, u32[]{:S(2)}, u32[]{:S(2)}) %collective-permute-start.9) | collective-permute-done | bytes 16416 | tf_op jit(solution)/shard_map/ppermute | solution.py:132
  89.7 0.2 fusion.16
  89.9 0.0 collective-permute-start.10
  90.0 0.2 fusion.38
  90.2 3.9 %collective-permute-start.11 = (bf16[16,512]{1,0:T(8,128)(2,1)S(1)}, bf16[16,512]{1,0:T(8,128)(2,1)S(1)}, u32[]{:S(2)}, u32[]{:S(2)}) collective-permute-start(bf16[16,512]{1,0:T(8,128)(2,1)S(1)} %fusion.16), channel_id=1, source_target_pairs={{8,16},{16,8},{24,32},{32,24},{40,48},{48,40},{56,64},{64,56},{72,... | collective-permute-start | bytes 49160 | tf_op jit(solution)/shard_map/ppermute | solution.py:132
  94.1 0.2 convolution_add_fusion.5
  94.4 3.0 %collective-permute-done.11 = bf16[16,512]{1,0:T(8,128)(2,1)S(1)} collective-permute-done((bf16[16,512]{1,0:T(8,128)(2,1)S(1)}, bf16[16,512]{1,0:T(8,128)(2,1)S(1)}, u32[]{:S(2)}, u32[]{:S(2)}) %collective-permute-start.11) | collective-permute-done | bytes 16416 | tf_op jit(solution)/shard_map/ppermute | solution.py:132
  97.4 0.2 fusion.15
  97.6 0.0 collective-permute-start.12
  97.6 0.2 fusion.36
  97.9 3.9 %collective-permute-start.13 = (bf16[16,512]{1,0:T(8,128)(2,1)S(1)}, bf16[16,512]{1,0:T(8,128)(2,1)S(1)}, u32[]{:S(2)}, u32[]{:S(2)}) collective-permute-start(bf16[16,512]{1,0:T(8,128)(2,1)S(1)} %fusion.15), channel_id=1, source_target_pairs={{8,16},{16,8},{24,32},{32,24},{40,48},{48,40},{56,64},{64,56},{72,... | collective-permute-start | bytes 49160 | tf_op jit(solution)/shard_map/ppermute | solution.py:132
  101.8 0.2 convolution_add_fusion.3
  102.0 3.0 %collective-permute-done.13 = bf16[16,512]{1,0:T(8,128)(2,1)S(1)} collective-permute-done((bf16[16,512]{1,0:T(8,128)(2,1)S(1)}, bf16[16,512]{1,0:T(8,128)(2,1)S(1)}, u32[]{:S(2)}, u32[]{:S(2)}) %collective-permute-start.13) | collective-permute-done | bytes 16416 | tf_op jit(solution)/shard_map/ppermute | solution.py:132
  105.0 0.2 fusion.14
  105.3 0.1 collective-permute-start.14
  105.4 0.2 fusion.34
  105.6 3.9 %collective-permute-start.15 = (bf16[16,512]{1,0:T(8,128)(2,1)S(1)}, bf16[16,512]{1,0:T(8,128)(2,1)S(1)}, u32[]{:S(2)}, u32[]{:S(2)}) collective-permute-start(bf16[16,512]{1,0:T(8,128)(2,1)S(1)} %fusion.14), channel_id=1, source_target_pairs={{8,16},{16,8},{24,32},{32,24},{40,48},{48,40},{56,64},{64,56},{72,... | collective-permute-start | bytes 49160 | tf_op jit(solution)/shard_map/ppermute | solution.py:132
  109.6 0.2 convolution_add_fusion.1
  109.8 3.0 %collective-permute-done.15 = bf16[16,512]{1,0:T(8,128)(2,1)S(1)} collective-permute-done((bf16[16,512]{1,0:T(8,128)(2,1)S(1)}, bf16[16,512]{1,0:T(8,128)(2,1)S(1)}, u32[]{:S(2)}, u32[]{:S(2)}) %collective-permute-start.15) | collective-permute-done | bytes 16416 | tf_op jit(solution)/shard_map/ppermute | solution.py:132
  112.8 0.2 fusion.13
  113.0 0.7 broadcast_in_dim.7
  113.7 3.3 %all-to-all-start.2 = ((f32[4,16,512]{2,1,0:T(8,128)}), f32[4,16,512]{2,1,0:T(8,128)S(1)}, u32[]{:S(2)}, u32[]{:S(2)}) async-start(f32[4,16,512]{2,1,0:T(8,128)} %broadcast_in_dim.7), calls=%async_computation.2 | async-start | bytes 262144 | tf_op jit(solution)/shard_map/all_to_all | solution.py:138
  117.1 5.9 %all-to-all-done.2 = f32[4,16,512]{2,1,0:T(8,128)S(1)} async-done(((f32[4,16,512]{2,1,0:T(8,128)}), f32[4,16,512]{2,1,0:T(8,128)S(1)}, u32[]{:S(2)}, u32[]{:S(2)}) %all-to-all-start.2) | async-done | bytes 131104 | tf_op jit(solution)/shard_map/all_to_all | solution.py:138
  123.0 0.7 pad_maximum_fusion
  123.8 0.7 copy.11
  (17 shorter events, 0.1 us)
Async XLA Ops:
  6.9 6.3 %collective-permute-start = (bf16[4,4,4,16,512]{4,3,2,1,0:T(8,128)(2,1)}, bf16[4,4,4,16,512]{4,3,2,1,0:T(8,128)(2,1)S(1)}, u32[]{:S(2)}, u32[]{:S(2)}) collective-permute-start(bf16[4,4,4,16,512]{4,3,2,1,0:T(8,128)(2,1)} %far_half.3), channel_id=1, source_target_pairs={{0,8},{8,0},{1,9},{9,1},{2,10},{10,2},{3,11},{11,3},{4,12},{12,4},... | collective-permute-start | bytes 3145736 | tf_op jit(solution)/shard_map/ppermute | solution.py:99
  15.8 7.2 %copy-start.1 = (bf16[4,64,512]{2,1,0:T(8,128)(2,1)S(1)}, bf16[4,64,512]{2,1,0:T(8,128)(2,1)}, u32[]{:S(2)}) copy-start(bf16[4,64,512]{2,1,0:T(8,128)(2,1)} %hist_ref.3) | copy-start | bytes 786436
  15.8 35.1 %copy-start = (bf16[3,512,512]{2,1,0:T(8,128)(2,1)S(1)}, bf16[3,512,512]{2,1,0:T(8,128)(2,1)}, u32[]{:S(2)}) copy-start(bf16[3,512,512]{2,1,0:T(8,128)(2,1)} %param.13) | copy-start | bytes 4718596
  15.8 25.6 %all-to-all-start = ((bf16[16,64,512]{2,1,0:T(8,128)(2,1)}), bf16[16,64,512]{2,1,0:T(8,128)(2,1)S(1)}, u32[]{:S(2)}, u32[]{:S(2)}) async-start(bf16[16,64,512]{2,1,0:T(8,128)(2,1)} %bitcast.6), calls=%async_computation | async-start | bytes 2097152 | tf_op jit(solution)/shard_map/all_to_all | solution.py:102
  23.0 13.1 %collective-permute-start.1 = (bf16[64,512]{1,0:T(8,128)(2,1)S(1)}, bf16[64,512]{1,0:T(8,128)(2,1)S(1)}, u32[]{:S(2)}, u32[]{:S(2)}) collective-permute-start(bf16[64,512]{1,0:T(8,128)(2,1)S(1)} %slice_bitcast_fusion), channel_id=1, source_target_pairs={{0,1},{1,2},{2,3},{3,4},{4,5},{5,6},{6,7},{8,9},{9,10},{10,11},{11... | collective-permute-start | bytes 196616 | tf_op jit(solution)/shard_map/ppermute | solution.py:106
  41.4 9.5 %copy-start.2 = (f32[512]{0:T(512)S(1)}, f32[512]{0:T(512)}, u32[]{:S(2)}) copy-start(f32[512]{0:T(512)} %param.14) | copy-start | bytes 6148
  42.3 16.2 %all-to-all-start.1 = ((bf16[8,16,512]{2,1,0:T(8,128)(2,1)}), bf16[8,16,512]{2,1,0:T(8,128)(2,1)S(1)}, u32[]{:S(2)}, u32[]{:S(2)}) async-start(bf16[8,16,512]{2,1,0:T(8,128)(2,1)} %bitcast.9), calls=%async_computation.1 | async-start | bytes 262144 | tf_op jit(solution)/shard_map/all_to_all | solution.py:110
  59.3 4.2 %collective-permute-start.2 = (bf16[16,512]{1,0:T(8,128)(2,1)S(1)}, bf16[16,512]{1,0:T(8,128)(2,1)S(1)}, u32[]{:S(2)}, u32[]{:S(2)}) collective-permute-start(bf16[16,512]{1,0:T(8,128)(2,1)S(1)} %get-tuple-element.6), channel_id=1, source_target_pairs={{0,8},{8,0},{1,9},{9,1},{2,10},{10,2},{3,11},{11,3},{4,12},{12,4},... | collective-permute-start | bytes 49160 | tf_op jit(solution)/shard_map/ppermute | solution.py:133
  59.5 7.2 %collective-permute-start.3 = (bf16[16,512]{1,0:T(8,128)(2,1)S(1)}, bf16[16,512]{1,0:T(8,128)(2,1)S(1)}, u32[]{:S(2)}, u32[]{:S(2)}) collective-permute-start(bf16[16,512]{1,0:T(8,128)(2,1)S(1)} %get-tuple-element.6), channel_id=1, source_target_pairs={{8,16},{16,8},{24,32},{32,24},{40,48},{48,40},{56,64},{64,56},{72,... | collective-permute-start | bytes 49160 | tf_op jit(solution)/shard_map/ppermute | solution.py:132
  66.9 4.2 %collective-permute-start.4 = (bf16[16,512]{1,0:T(8,128)(2,1)S(1)}, bf16[16,512]{1,0:T(8,128)(2,1)S(1)}, u32[]{:S(2)}, u32[]{:S(2)}) collective-permute-start(bf16[16,512]{1,0:T(8,128)(2,1)S(1)} %fusion.19), channel_id=1, source_target_pairs={{0,8},{8,0},{1,9},{9,1},{2,10},{10,2},{3,11},{11,3},{4,12},{12,4},... | collective-permute-start | bytes 49160 | tf_op jit(solution)/shard_map/ppermute | solution.py:133
  67.2 7.2 %collective-permute-start.5 = (bf16[16,512]{1,0:T(8,128)(2,1)S(1)}, bf16[16,512]{1,0:T(8,128)(2,1)S(1)}, u32[]{:S(2)}, u32[]{:S(2)}) collective-permute-start(bf16[16,512]{1,0:T(8,128)(2,1)S(1)} %fusion.19), channel_id=1, source_target_pairs={{8,16},{16,8},{24,32},{32,24},{40,48},{48,40},{56,64},{64,56},{72,... | collective-permute-start | bytes 49160 | tf_op jit(solution)/shard_map/ppermute | solution.py:132
  74.6 4.2 %collective-permute-start.6 = (bf16[16,512]{1,0:T(8,128)(2,1)S(1)}, bf16[16,512]{1,0:T(8,128)(2,1)S(1)}, u32[]{:S(2)}, u32[]{:S(2)}) collective-permute-start(bf16[16,512]{1,0:T(8,128)(2,1)S(1)} %fusion.18), channel_id=1, source_target_pairs={{0,8},{8,0},{1,9},{9,1},{2,10},{10,2},{3,11},{11,3},{4,12},{12,4},... | collective-permute-start | bytes 49160 | tf_op jit(solution)/shard_map/ppermute | solution.py:133
  74.9 7.2 %collective-permute-start.7 = (bf16[16,512]{1,0:T(8,128)(2,1)S(1)}, bf16[16,512]{1,0:T(8,128)(2,1)S(1)}, u32[]{:S(2)}, u32[]{:S(2)}) collective-permute-start(bf16[16,512]{1,0:T(8,128)(2,1)S(1)} %fusion.18), channel_id=1, source_target_pairs={{8,16},{16,8},{24,32},{32,24},{40,48},{48,40},{56,64},{64,56},{72,... | collective-permute-start | bytes 49160 | tf_op jit(solution)/shard_map/ppermute | solution.py:132
  82.3 4.2 %collective-permute-start.8 = (bf16[16,512]{1,0:T(8,128)(2,1)S(1)}, bf16[16,512]{1,0:T(8,128)(2,1)S(1)}, u32[]{:S(2)}, u32[]{:S(2)}) collective-permute-start(bf16[16,512]{1,0:T(8,128)(2,1)S(1)} %fusion.17), channel_id=1, source_target_pairs={{0,8},{8,0},{1,9},{9,1},{2,10},{10,2},{3,11},{11,3},{4,12},{12,4},... | collective-permute-start | bytes 49160 | tf_op jit(solution)/shard_map/ppermute | solution.py:133
  82.5 7.2 %collective-permute-start.9 = (bf16[16,512]{1,0:T(8,128)(2,1)S(1)}, bf16[16,512]{1,0:T(8,128)(2,1)S(1)}, u32[]{:S(2)}, u32[]{:S(2)}) collective-permute-start(bf16[16,512]{1,0:T(8,128)(2,1)S(1)} %fusion.17), channel_id=1, source_target_pairs={{8,16},{16,8},{24,32},{32,24},{40,48},{48,40},{56,64},{64,56},{72,... | collective-permute-start | bytes 49160 | tf_op jit(solution)/shard_map/ppermute | solution.py:132
  89.9 4.2 %collective-permute-start.10 = (bf16[16,512]{1,0:T(8,128)(2,1)S(1)}, bf16[16,512]{1,0:T(8,128)(2,1)S(1)}, u32[]{:S(2)}, u32[]{:S(2)}) collective-permute-start(bf16[16,512]{1,0:T(8,128)(2,1)S(1)} %fusion.16), channel_id=1, source_target_pairs={{0,8},{8,0},{1,9},{9,1},{2,10},{10,2},{3,11},{11,3},{4,12},{12,4},... | collective-permute-start | bytes 49160 | tf_op jit(solution)/shard_map/ppermute | solution.py:133
  90.2 7.2 %collective-permute-start.11 = (bf16[16,512]{1,0:T(8,128)(2,1)S(1)}, bf16[16,512]{1,0:T(8,128)(2,1)S(1)}, u32[]{:S(2)}, u32[]{:S(2)}) collective-permute-start(bf16[16,512]{1,0:T(8,128)(2,1)S(1)} %fusion.16), channel_id=1, source_target_pairs={{8,16},{16,8},{24,32},{32,24},{40,48},{48,40},{56,64},{64,56},{72,... | collective-permute-start | bytes 49160 | tf_op jit(solution)/shard_map/ppermute | solution.py:132
  97.6 4.2 %collective-permute-start.12 = (bf16[16,512]{1,0:T(8,128)(2,1)S(1)}, bf16[16,512]{1,0:T(8,128)(2,1)S(1)}, u32[]{:S(2)}, u32[]{:S(2)}) collective-permute-start(bf16[16,512]{1,0:T(8,128)(2,1)S(1)} %fusion.15), channel_id=1, source_target_pairs={{0,8},{8,0},{1,9},{9,1},{2,10},{10,2},{3,11},{11,3},{4,12},{12,4},... | collective-permute-start | bytes 49160 | tf_op jit(solution)/shard_map/ppermute | solution.py:133
  97.9 7.2 %collective-permute-start.13 = (bf16[16,512]{1,0:T(8,128)(2,1)S(1)}, bf16[16,512]{1,0:T(8,128)(2,1)S(1)}, u32[]{:S(2)}, u32[]{:S(2)}) collective-permute-start(bf16[16,512]{1,0:T(8,128)(2,1)S(1)} %fusion.15), channel_id=1, source_target_pairs={{8,16},{16,8},{24,32},{32,24},{40,48},{48,40},{56,64},{64,56},{72,... | collective-permute-start | bytes 49160 | tf_op jit(solution)/shard_map/ppermute | solution.py:132
  105.3 17.7 %slice-start = ((bf16[4,64,512]{2,1,0:T(8,128)(2,1)}), bf16[3,64,512]{2,1,0:T(8,128)(2,1)S(1)}, s32[]{:S(2)}) async-start(bf16[4,64,512]{2,1,0:T(8,128)(2,1)} %hist_ref.3), calls=%async_computation.3 | async-start | bytes 393216 | tf_op jit(solution)/shard_map/slice | solution.py:143
  105.3 4.2 %collective-permute-start.14 = (bf16[16,512]{1,0:T(8,128)(2,1)S(1)}, bf16[16,512]{1,0:T(8,128)(2,1)S(1)}, u32[]{:S(2)}, u32[]{:S(2)}) collective-permute-start(bf16[16,512]{1,0:T(8,128)(2,1)S(1)} %fusion.14), channel_id=1, source_target_pairs={{0,8},{8,0},{1,9},{9,1},{2,10},{10,2},{3,11},{11,3},{4,12},{12,4},... | collective-permute-start | bytes 49160 | tf_op jit(solution)/shard_map/ppermute | solution.py:133
  105.6 7.2 %collective-permute-start.15 = (bf16[16,512]{1,0:T(8,128)(2,1)S(1)}, bf16[16,512]{1,0:T(8,128)(2,1)S(1)}, u32[]{:S(2)}, u32[]{:S(2)}) collective-permute-start(bf16[16,512]{1,0:T(8,128)(2,1)S(1)} %fusion.14), channel_id=1, source_target_pairs={{8,16},{16,8},{24,32},{32,24},{40,48},{48,40},{56,64},{64,56},{72,... | collective-permute-start | bytes 49160 | tf_op jit(solution)/shard_map/ppermute | solution.py:132
  113.7 9.3 %all-to-all-start.2 = ((f32[4,16,512]{2,1,0:T(8,128)}), f32[4,16,512]{2,1,0:T(8,128)S(1)}, u32[]{:S(2)}, u32[]{:S(2)}) async-start(f32[4,16,512]{2,1,0:T(8,128)} %broadcast_in_dim.7), calls=%async_computation.2 | async-start | bytes 262144 | tf_op jit(solution)/shard_map/all_to_all | solution.py:138

commit v2 on v1

v2 whole, which is shorter than its diff:
```python
import functools

import jax
import jax.numpy as jnp
from jax import lax
from jax.experimental import pallas as pl
from jax.experimental.pallas import tpu as pltpu
from jax.sharding import Mesh
from jax.sharding import PartitionSpec as P


SWEEPS = 8
SPACE = ("zl", "x", "c")
HIST = ("zh", "y")


def far_kernel(
    core_ref, rank_ref, lag_ref, hist_ref, right_ref, left_ref, out_ref,
    hist_buf, right_buf, left_buf, hist_sem, right_sem, left_sem, *, ranks
):
    groups, chips, depth, width = right_buf.shape
    lags, steps, _ = hist_buf.shape
    total = chips * depth
    core = core_ref[0]

    def brought(source, target, sem, group):
        return pltpu.make_async_copy(
            source.at[pl.ds(group * chips, chips), core], target.at[group], sem.at[group]
        )

    whole = pltpu.make_async_copy(hist_ref, hist_buf, hist_sem)
    whole.start()
    rights = [brought(right_ref, right_buf, right_sem, g) for g in range(groups)]
    lefts = [brought(left_ref, left_buf, left_sem, g) for g in range(groups)]
    for g in range(groups):
        rights[g].start()
        lefts[g].start()
    lane = lax.broadcasted_iota(jnp.int32, (1, total), 1)
    per = depth // ranks

    def chosen(group):
        column = jnp.full((1, total), -1, jnp.int32)
        for chip in range(chips):
            for k in range(per):
                pair = ((group * chips + chip) * 2 + core) * per + k
                first = (chip * per + k) * ranks
                inside = (lane >= first) & (lane < first + rank_ref[pair])
                column = jnp.where(inside, lag_ref[pair], column)
        every = lax.dot_general(
            hist_buf[...].reshape(lags * steps, width),
            right_buf[group].reshape(total, width),
            (((1,), (1,)), ((), ())),
            preferred_element_type=jnp.float32,
        )
        value = jnp.zeros((steps, total), jnp.float32)
        for lag in range(lags):
            value = jnp.where(column == lag, every[lag * steps : (lag + 1) * steps], value)
        return value.astype(jnp.bfloat16)

    def far(group, value):
        left = left_buf[group].reshape(total, width)
        for chip in range(chips):
            first, last = chip * depth, (chip + 1) * depth
            low, high = first // 128 * 128, -(-last // 128) * 128
            part = value[:, low:high]
            at = lax.broadcasted_iota(jnp.int32, part.shape, 1) + low
            part = jnp.where((at >= first) & (at < last), part, jnp.zeros_like(part))
            field = jnp.dot(part, left[low:high], preferred_element_type=jnp.float32)
            out_ref[chip, :, group] = field.reshape(out_ref.shape[1], -1, width).astype(out_ref.dtype)

    whole.wait()
    rights[0].wait()
    value = chosen(0)
    for g in range(groups):
        lefts[g].wait()
        ahead = None
        if g + 1 < groups:
            rights[g + 1].wait()
            ahead = chosen(g + 1)
        far(g, value)
        value = ahead


def far_half(core, rank, lag, history, right, left, ranks):
    rows, _, depth, width = right.shape
    lags, steps, _ = history.shape
    groups, chips, cuts = 4, 4, 4
    scalar = pl.BlockSpec(memory_space=pltpu.SMEM)
    outside = pl.BlockSpec(memory_space=pltpu.HBM)
    held = pltpu.VMEM((groups, chips, depth, width), jnp.bfloat16)
    return pl.pallas_call(
        functools.partial(far_kernel, ranks=ranks),
        out_shape=jax.ShapeDtypeStruct((chips, cuts, groups, steps // cuts, width), jnp.bfloat16),
        in_specs=[scalar, scalar, scalar, outside, outside, outside],
        out_specs=pl.BlockSpec(memory_space=pltpu.VMEM),
        scratch_shapes=[
            pltpu.VMEM((lags, steps, width), jnp.bfloat16),
            held,
            held,
            pltpu.SemaphoreType.DMA,
            pltpu.SemaphoreType.DMA((groups,)),
            pltpu.SemaphoreType.DMA((groups,)),
        ],
        compiler_params=pltpu.CompilerParams(vmem_limit_bytes=16 << 20),
        cost_estimate=pl.CostEstimate(
            flops=2 * rows * depth * width * (lags + 1) * steps,
            bytes_accessed=rows * depth * width * 4 + rows * steps * width * 2,
            transcendentals=0,
        ),
        name="far_half",
    )(core, rank, lag, history, right, left)


def per_device(
    history, right_factor, left_factor, pair_rank, pair_lag, near_block, self_term, excitation
):
    _, time_steps, width = history.shape
    pairs, ranks, _ = right_factor.shape
    targets = 32
    depth = pairs // targets * ranks
    right = right_factor.reshape(targets // 2, 2, depth, width)
    left = left_factor.reshape(targets // 2, 2, depth, width)
    rank, lag = pair_rank[:, 0], pair_lag[:, 0]
    history_out, right, left = (
        pltpu.with_memory_space_constraint(v, pltpu.HBM) for v in (history, right, left)
    )
    core = lax.axis_index("c")
    swap = [(0, 1), (1, 0)]

    def half(which):
        return far_half(which.reshape(1), rank, lag, history_out, right, left, ranks)

    away = half(1 - core)
    came = lax.ppermute(away, "c", swap)
    mine = half(core)
    partial_value = (mine.astype(jnp.float32) + came.astype(jnp.float32)).astype(jnp.bfloat16)
    arrived = lax.all_to_all(
        partial_value.reshape(16, -1, width), ("x", "y"), 0, 0, tiled=True
    ).reshape(16, 4, -1, width)
    plane = jnp.sum(arrived.astype(jnp.float32), axis=0).astype(jnp.bfloat16)
    twice = jnp.broadcast_to(plane[None], (2, *plane.shape)).reshape(8, -1, width)
    arrived = lax.all_to_all(twice, ("zh", "zl"), 0, 0, tiled=True)
    incoming = lax.ppermute(history[-1], HIST, [(i, i + 1) for i in range(7)])
    shifted = jnp.concatenate([incoming[None], history[:-1]], axis=0)
    arrived, incoming, shifted = lax.optimization_barrier((arrived, incoming, shifted))
    far_field = jnp.sum(arrived.astype(jnp.float32), axis=0)
    rows = time_steps // 4
    row = lax.axis_index("y")
    right_side = lax.dynamic_slice_in_dim(excitation, row * rows, rows, 0) - far_field

    inverse = 1.0 / self_term[None, :]
    near_own = near_block[1]
    near_chip = jnp.where(core == 0, near_block[2], near_block[0])
    near_away = jnp.where(core == 0, near_block[0], near_block[2])
    between = []
    for t in range(1, targets - 1, 2):
        between += [(t, t + 1), (t + 1, t)]

    def product(value, block):
        return lax.dot_general(
            value, block, (((1,), (1,)), ((), ())), preferred_element_type=jnp.float32
        )

    current = right_side * inverse
    for _ in range(1, SWEEPS):
        rounded = current.astype(jnp.bfloat16)
        away = lax.ppermute(rounded, SPACE, between)
        chip = lax.ppermute(rounded, "c", swap)
        total = product(rounded, near_own)
        total = total + product(chip, near_chip)
        total = total + product(away, near_away)
        current = (right_side - total) * inverse

    pieces = [current]
    for step in (2, 1, 3):
        pieces.append(
            lax.ppermute(current, "y", [(i, (i + step) % 4) for i in range(4)])
        )
    everywhere = []
    for slot in range(4):
        value = pieces[0]
        for step, piece in zip((2, 1, 3), pieces[1:]):
            value = jnp.where(row == (slot + step) % 4, piece, value)
        everywhere.append(value)
    everywhere = jnp.concatenate(everywhere, axis=0)
    oldest = (lax.axis_index("zh") == 0) & (row == 0)
    newest = jnp.where(oldest, everywhere.astype(jnp.bfloat16), incoming)
    next_history = lax.dynamic_update_slice_in_dim(shifted, newest[None], 0, 0)
    return (everywhere, next_history)


def solution(mesh):
    fine = Mesh(mesh.devices.reshape(4, 4, 2, 2, 4), SPACE + HIST)
    in_specs = (
        P(HIST, None, SPACE),
        P(HIST, None, SPACE),
        P(HIST, None, SPACE),
        P(HIST, SPACE),
        P(HIST, SPACE),
        P(None, SPACE, None),
        P(SPACE),
        P(None, SPACE),
    )
    out_specs = (P(None, SPACE), P(HIST, None, SPACE))
    return jax.shard_map(
        per_device, mesh=fine, in_specs=in_specs, out_specs=out_specs, check_vma=False
    )
```

time: 125 us -> 122 us (0.976)
  Pallas kernels: 12.5 us -> 10.5 us
  waiting for transfers between devices: 49.2 us -> 47.9 us
    all_to_all x1, waiting for transfers between devices: 5.32 us -> 14.6 us  [per_device(): lax.all_to_all(partial_value.reshape(16, -1, width), ('x', 'y'), 0, 0, ti...]
    all_to_all x1 -> x0, waiting for transfers between devices: 5.93 us -> none  [per_device(): lax.all_to_all(jnp.broadcast_to(current[None], (4, *current.shape)), 'y',...]
    ppermute x8 -> x11, waiting for transfers between devices: 30.4 us -> 25.8 us  [the longest x7 21.1 us: per_device(): away = lax.ppermute(rounded, SPACE, between)]
    all_to_all x1 -> x0, starting transfers between devices: 3.33 us -> none  [per_device(): lax.all_to_all(jnp.broadcast_to(current[None], (4, *current.shape)), 'y',...]
    ppermute x8 -> x11, starting transfers between devices: 31.2 us -> 33.9 us  [the longest x7 27.3 us: per_device(): away = lax.ppermute(rounded, SPACE, between)]
    pallas_call x2, Pallas kernels: 12.5 us -> 10.5 us  [far_half(): pl.pallas_call(functools.partial(far_kernel, ranks=ranks), out_shape=jax....]
    unnamed x7 -> x16, local copies, waits for them, and re-layouts: 0.67 us -> 2.03 us
  transfers between devices with their start and end apart: 19 -> 21, of which waited for: 11 -> 12; matrix products, arithmetic and copies ran while one was open for 3% -> 4% of each run, Pallas kernels for 5% -> 4%
where the time goes in v2:
time: 122 us; the launch traced here: 121 us
  starting transfers between devices  49.9 us (41%)
  waiting for transfers between devices  47.9 us (39%)
  Pallas kernels  10.5 us (9%)
  matrix products  4.92 us (4%)
  other arithmetic  4.37 us (4%)
  local copies, waits for them, and re-layouts  2.71 us (2%)
    ppermute x7, starting transfers between devices, per_device(): away = lax.ppermute(rounded, SPACE, between)  27.3 us
    ppermute x7, waiting for transfers between devices, per_device(): away = lax.ppermute(rounded, SPACE, between)  21.1 us
    all_to_all x1, waiting for transfers between devices, per_device(): lax.all_to_all(partial_value.reshape(16, -1, width), ('x', 'y'), 0, 0, ti...  14.6 us
    pallas_call x2, Pallas kernels, far_half(): pl.pallas_call(functools.partial(far_kernel, ranks=ranks), out_shape=jax....  10.5 us
    all_to_all x1, starting transfers between devices, per_device(): arrived = lax.all_to_all(twice, ('zh', 'zl'), 0, 0, tiled=True)  8.57 us
    all_to_all x1, waiting for transfers between devices, per_device(): arrived = lax.all_to_all(twice, ('zh', 'zl'), 0, 0, tiled=True)  7.55 us
    all_to_all x1, starting transfers between devices, per_device(): lax.all_to_all(partial_value.reshape(16, -1, width), ('x', 'y'), 0, 0, ti...  7.22 us
    dot_general x21, matrix products, product(): lax.dot_general(value, block, (((1,), (1,)), ((), ())), preferred_element...  4.92 us
  transfers between devices with their start and end apart: 21, of which 12 were waited for; matrix products, arithmetic and copies ran while one was open for 4% of the time, Pallas kernels for 4%

profile of v2, /device:TPU:32, one launch (start us, length us, event | category | flops | bytes accessed | tf_op | source)
XLA Modules:
  0.0 121.3 jit_solution(2260604577297700422)
XLA Ops:
  0.6 0.6 copy-done
  1.3 0.7 copy-done.2
  2.0 5.2 %far_half.3 = bf16[4,4,4,16,512]{4,3,2,1,0:T(8,128)(2,1)S(1)} custom-call(s32[1]{0:T(128)} %bitcast.5.core_ref, s32[64]{0:T(128)S(1)} %bitcast.80, s32[64]{0:T(128)S(1)} %bitcast.82, bf16[4,64,512]{2,1,0:T(8,128)(2,1)} %hist_ref.3, bf16[16,2,160,512]{3,2,1,0:T(8,128)(2,1)} %bitcast.84, bf16[16,2,160,512]{3,2,1,0:T(8,128)(2,1)} %bitcast.86), custom_call_target="tpu_custom_call" | custom-call | flops 838860800 | bytes 6291456 | tf_op jit(solution)/shard_map/far_half/pallas_call | solution.py:91
  7.2 0.1 collective-permute-start
  7.3 5.2 %far_half.2 = bf16[4,4,4,16,512]{4,3,2,1,0:T(8,128)(2,1)S(1)} custom-call(s32[1]{0:T(128)} %bitcast.core_ref, s32[64]{0:T(128)S(1)} %bitcast.81, s32[64]{0:T(128)S(1)} %bitcast.83, bf16[4,64,512]{2,1,0:T(8,128)(2,1)} %hist_ref.3, bf16[16,2,160,512]{3,2,1,0:T(8,128)(2,1)} %bitcast.85, bf16[16,2,160,512]{3,2,1,0:T(8,128)(2,1)} %bitcast.87), custom_call_target="tpu_custom_call" | custom-call | flops 838860800 | bytes 6291456 | tf_op jit(solution)/shard_map/far_half/pallas_call | solution.py:91
  12.6 1.4 %add_convert_fusion = bf16[4,4,4,16,512]{4,3,2,1,0:T(8,128)(2,1)} fusion(bf16[4,4,4,16,512]{4,3,2,1,0:T(8,128)(2,1)S(1)} %collective-permute-done, bf16[4,4,4,16,512]{4,3,2,1,0:T(8,128)(2,1)S(1)} %far_half.2), kind=kLoop, calls=%fused_computation | loop fusion | flops 2097152 | bytes 3145728 | tf_op jit(solution)/shard_map/convert_element_type | solution.py:136
  14.0 7.2 %all-to-all-start = ((bf16[16,64,512]{2,1,0:T(8,128)(2,1)}), bf16[16,64,512]{2,1,0:T(8,128)(2,1)}, u32[]{:S(2)}, u32[]{:S(2)}) async-start(bf16[16,64,512]{2,1,0:T(8,128)(2,1)} %bitcast.6), calls=%async_computation | async-start | bytes 2097152 | tf_op jit(solution)/shard_map/all_to_all | solution.py:137
  21.2 3.8 %collective-permute-start.1 = (bf16[64,512]{1,0:T(8,128)(2,1)S(1)}, bf16[64,512]{1,0:T(8,128)(2,1)S(1)}, u32[]{:S(2)}, u32[]{:S(2)}) collective-permute-start(bf16[64,512]{1,0:T(8,128)(2,1)S(1)} %slice_bitcast_fusion), channel_id=1, source_target_pairs={{0,1},{1,2},{2,3},{3,4},{4,5},{5,6},{6,7},{8,9},{9,10},{10,11},{11... | collective-permute-start | bytes 196616 | tf_op jit(solution)/shard_map/ppermute | solution.py:143
  25.1 0.1 broadcast_select_fusion
  25.1 14.6 %all-to-all-done = bf16[16,64,512]{2,1,0:T(8,128)(2,1)} async-done(((bf16[16,64,512]{2,1,0:T(8,128)(2,1)}), bf16[16,64,512]{2,1,0:T(8,128)(2,1)}, u32[]{:S(2)}, u32[]{:S(2)}) %all-to-all-start) | async-done | bytes 1048608 | tf_op jit(solution)/shard_map/all_to_all | solution.py:137
  39.7 1.4 %reduce_sum.21 = bf16[64,512]{1,0:T(8,128)(2,1)S(1)} reduce(bf16[16,64,512]{2,1,0:T(8,128)(2,1)} %all-to-all-done, bf16[]{:T(256)} %constant.25.clone.1), dimensions={0}, to_apply=%region_0.0 | reduce | flops 491520 | bytes 1114114 | tf_op jit(solution)/shard_map/reduce_sum | solution.py:140
  41.1 0.7 broadcast_in_dim.16
  41.8 8.6 %all-to-all-start.1 = ((bf16[8,16,512]{2,1,0:T(8,128)(2,1)}), bf16[8,16,512]{2,1,0:T(8,128)(2,1)S(1)}, u32[]{:S(2)}, u32[]{:S(2)}) async-start(bf16[8,16,512]{2,1,0:T(8,128)(2,1)} %bitcast.8), calls=%async_computation.1 | async-start | bytes 262144 | tf_op jit(solution)/shard_map/all_to_all | solution.py:142
  50.4 7.6 %all-to-all-done.1 = bf16[8,16,512]{2,1,0:T(8,128)(2,1)S(1)} async-done(((bf16[8,16,512]{2,1,0:T(8,128)(2,1)}), bf16[8,16,512]{2,1,0:T(8,128)(2,1)S(1)}, u32[]{:S(2)}, u32[]{:S(2)}) %all-to-all-start.1) | async-done | bytes 131104 | tf_op jit(solution)/shard_map/all_to_all | solution.py:142
  58.0 0.8 multiply_convert_fusion
  58.8 0.2 fusion.46
  59.0 3.9 %collective-permute-start.3 = (bf16[16,512]{1,0:T(8,128)(2,1)S(1)}, bf16[16,512]{1,0:T(8,128)(2,1)S(1)}, u32[]{:S(2)}, u32[]{:S(2)}) collective-permute-start(bf16[16,512]{1,0:T(8,128)(2,1)S(1)} %get-tuple-element.10), channel_id=1, source_target_pairs={{8,16},{16,8},{24,32},{32,24},{40,48},{48,40},{56,64},{64,56},{72,... | collective-permute-start | bytes 49160 | tf_op jit(solution)/shard_map/ppermute | solution.py:167
  62.9 0.2 convolution_add_fusion.13
  63.1 3.0 %collective-permute-done.3 = bf16[16,512]{1,0:T(8,128)(2,1)S(1)} collective-permute-done((bf16[16,512]{1,0:T(8,128)(2,1)S(1)}, bf16[16,512]{1,0:T(8,128)(2,1)S(1)}, u32[]{:S(2)}, u32[]{:S(2)}) %collective-permute-start.3) | collective-permute-done | bytes 16416 | tf_op jit(solution)/shard_map/ppermute | solution.py:167
  66.2 0.2 fusion.19
  66.4 0.0 collective-permute-start.4
  66.4 0.2 fusion.44
  66.7 3.9 %collective-permute-start.5 = (bf16[16,512]{1,0:T(8,128)(2,1)S(1)}, bf16[16,512]{1,0:T(8,128)(2,1)S(1)}, u32[]{:S(2)}, u32[]{:S(2)}) collective-permute-start(bf16[16,512]{1,0:T(8,128)(2,1)S(1)} %fusion.19), channel_id=1, source_target_pairs={{8,16},{16,8},{24,32},{32,24},{40,48},{48,40},{56,64},{64,56},{72,... | collective-permute-start | bytes 49160 | tf_op jit(solution)/shard_map/ppermute | solution.py:167
  70.6 0.2 convolution_add_fusion.11
  70.8 3.0 %collective-permute-done.5 = bf16[16,512]{1,0:T(8,128)(2,1)S(1)} collective-permute-done((bf16[16,512]{1,0:T(8,128)(2,1)S(1)}, bf16[16,512]{1,0:T(8,128)(2,1)S(1)}, u32[]{:S(2)}, u32[]{:S(2)}) %collective-permute-start.5) | collective-permute-done | bytes 16416 | tf_op jit(solution)/shard_map/ppermute | solution.py:167
  73.8 0.2 fusion.18
  74.1 0.0 collective-permute-start.6
  74.1 0.2 fusion.42
  74.3 3.9 %collective-permute-start.7 = (bf16[16,512]{1,0:T(8,128)(2,1)S(1)}, bf16[16,512]{1,0:T(8,128)(2,1)S(1)}, u32[]{:S(2)}, u32[]{:S(2)}) collective-permute-start(bf16[16,512]{1,0:T(8,128)(2,1)S(1)} %fusion.18), channel_id=1, source_target_pairs={{8,16},{16,8},{24,32},{32,24},{40,48},{48,40},{56,64},{64,56},{72,... | collective-permute-start | bytes 49160 | tf_op jit(solution)/shard_map/ppermute | solution.py:167
  78.3 0.2 convolution_add_fusion.9
  78.5 3.0 %collective-permute-done.7 = bf16[16,512]{1,0:T(8,128)(2,1)S(1)} collective-permute-done((bf16[16,512]{1,0:T(8,128)(2,1)S(1)}, bf16[16,512]{1,0:T(8,128)(2,1)S(1)}, u32[]{:S(2)}, u32[]{:S(2)}) %collective-permute-start.7) | collective-permute-done | bytes 16416 | tf_op jit(solution)/shard_map/ppermute | solution.py:167
  81.5 0.2 fusion.17
  81.7 0.0 collective-permute-start.8
  81.8 0.2 fusion.40
  82.0 3.9 %collective-permute-start.9 = (bf16[16,512]{1,0:T(8,128)(2,1)S(1)}, bf16[16,512]{1,0:T(8,128)(2,1)S(1)}, u32[]{:S(2)}, u32[]{:S(2)}) collective-permute-start(bf16[16,512]{1,0:T(8,128)(2,1)S(1)} %fusion.17), channel_id=1, source_target_pairs={{8,16},{16,8},{24,32},{32,24},{40,48},{48,40},{56,64},{64,56},{72,... | collective-permute-start | bytes 49160 | tf_op jit(solution)/shard_map/ppermute | solution.py:167
  85.9 0.2 convolution_add_fusion.7
  86.2 3.0 %collective-permute-done.9 = bf16[16,512]{1,0:T(8,128)(2,1)S(1)} collective-permute-done((bf16[16,512]{1,0:T(8,128)(2,1)S(1)}, bf16[16,512]{1,0:T(8,128)(2,1)S(1)}, u32[]{:S(2)}, u32[]{:S(2)}) %collective-permute-start.9) | collective-permute-done | bytes 16416 | tf_op jit(solution)/shard_map/ppermute | solution.py:167
  89.2 0.2 fusion.16
  89.4 0.0 collective-permute-start.10
  89.4 0.2 fusion.38
  89.7 3.9 %collective-permute-start.11 = (bf16[16,512]{1,0:T(8,128)(2,1)S(1)}, bf16[16,512]{1,0:T(8,128)(2,1)S(1)}, u32[]{:S(2)}, u32[]{:S(2)}) collective-permute-start(bf16[16,512]{1,0:T(8,128)(2,1)S(1)} %fusion.16), channel_id=1, source_target_pairs={{8,16},{16,8},{24,32},{32,24},{40,48},{48,40},{56,64},{64,56},{72,... | collective-permute-start | bytes 49160 | tf_op jit(solution)/shard_map/ppermute | solution.py:167
  93.6 0.2 convolution_add_fusion.5
  93.8 3.0 %collective-permute-done.11 = bf16[16,512]{1,0:T(8,128)(2,1)S(1)} collective-permute-done((bf16[16,512]{1,0:T(8,128)(2,1)S(1)}, bf16[16,512]{1,0:T(8,128)(2,1)S(1)}, u32[]{:S(2)}, u32[]{:S(2)}) %collective-permute-start.11) | collective-permute-done | bytes 16416 | tf_op jit(solution)/shard_map/ppermute | solution.py:167
  96.9 0.2 fusion.15
  97.1 0.0 collective-permute-start.12
  97.1 0.2 fusion.36
  97.4 3.9 %collective-permute-start.13 = (bf16[16,512]{1,0:T(8,128)(2,1)S(1)}, bf16[16,512]{1,0:T(8,128)(2,1)S(1)}, u32[]{:S(2)}, u32[]{:S(2)}) collective-permute-start(bf16[16,512]{1,0:T(8,128)(2,1)S(1)} %fusion.15), channel_id=1, source_target_pairs={{8,16},{16,8},{24,32},{32,24},{40,48},{48,40},{56,64},{64,56},{72,... | collective-permute-start | bytes 49160 | tf_op jit(solution)/shard_map/ppermute | solution.py:167
  101.3 0.2 convolution_add_fusion.3
  101.5 3.0 %collective-permute-done.13 = bf16[16,512]{1,0:T(8,128)(2,1)S(1)} collective-permute-done((bf16[16,512]{1,0:T(8,128)(2,1)S(1)}, bf16[16,512]{1,0:T(8,128)(2,1)S(1)}, u32[]{:S(2)}, u32[]{:S(2)}) %collective-permute-start.13) | collective-permute-done | bytes 16416 | tf_op jit(solution)/shard_map/ppermute | solution.py:167
  104.5 0.2 fusion.14
  104.8 0.0 collective-permute-start.14
  104.8 0.2 fusion.34
  105.0 3.9 %collective-permute-start.15 = (bf16[16,512]{1,0:T(8,128)(2,1)S(1)}, bf16[16,512]{1,0:T(8,128)(2,1)S(1)}, u32[]{:S(2)}, u32[]{:S(2)}) collective-permute-start(bf16[16,512]{1,0:T(8,128)(2,1)S(1)} %fusion.14), channel_id=1, source_target_pairs={{8,16},{16,8},{24,32},{32,24},{40,48},{48,40},{56,64},{64,56},{72,... | collective-permute-start | bytes 49160 | tf_op jit(solution)/shard_map/ppermute | solution.py:167
  108.9 0.2 convolution_add_fusion.1
  109.2 3.0 %collective-permute-done.15 = bf16[16,512]{1,0:T(8,128)(2,1)S(1)} collective-permute-done((bf16[16,512]{1,0:T(8,128)(2,1)S(1)}, bf16[16,512]{1,0:T(8,128)(2,1)S(1)}, u32[]{:S(2)}, u32[]{:S(2)}) %collective-permute-start.15) | collective-permute-done | bytes 16416 | tf_op jit(solution)/shard_map/ppermute | solution.py:167
  112.2 0.2 fusion.13
  112.4 0.2 collective-permute-start.16
  112.7 1.8 %collective-permute-start.17 = (f32[16,512]{1,0:T(8,128)S(1)}, f32[16,512]{1,0:T(8,128)S(1)}, u32[]{:S(2)}, u32[]{:S(2)}) collective-permute-start(f32[16,512]{1,0:T(8,128)S(1)} %fusion.13), channel_id=1, source_target_pairs={{0,1},{1,2},{2,3},{3,0},{4,5},{5,6},{6,7},{7,4},{8,9},{9,10},{10,1... | collective-permute-start | bytes 98312 | tf_op jit(solution)/shard_map/ppermute | solution.py:177
  114.5 0.8 collective-permute-start.18
  115.3 1.1 collective-permute-done.16
  116.4 1.4 %collective-permute-done.17 = f32[16,512]{1,0:T(8,128)S(1)} collective-permute-done((f32[16,512]{1,0:T(8,128)S(1)}, f32[16,512]{1,0:T(8,128)S(1)}, u32[]{:S(2)}, u32[]{:S(2)}) %collective-permute-start.17) | collective-permute-done | bytes 32800 | tf_op jit(solution)/shard_map/ppermute | solution.py:177
  117.8 2.1 %collective-permute-done.18 = f32[16,512]{1,0:T(8,128)S(1)} collective-permute-done((f32[16,512]{1,0:T(8,128)S(1)}, f32[16,512]{1,0:T(8,128)S(1)}, u32[]{:S(2)}, u32[]{:S(2)}) %collective-permute-start.18) | collective-permute-done | bytes 32800 | tf_op jit(solution)/shard_map/ppermute | solution.py:177
  119.9 0.7 bitcast_dynamic-update-slice_fusion
  120.6 0.7 copy-done.6
  (30 shorter events, 0.1 us)
Async XLA Ops:
  0.6 0.7 copy-start
  1.3 0.7 copy-start.2
  1.9 5.4 %copy-start.1 = (s32[64,1]{0,1:T(1,128)S(1)}, s32[64,1]{0,1:T(1,128)}, u32[]{:S(2)}) copy-start(s32[64,1]{0,1:T(1,128)} %param.11) | copy-start | bytes 772
  2.0 5.4 %copy-start.3 = (s32[64,1]{0,1:T(1,128)S(1)}, s32[64,1]{0,1:T(1,128)}, u32[]{:S(2)}) copy-start(s32[64,1]{0,1:T(1,128)} %param.12) | copy-start | bytes 772
  7.2 5.4 %collective-permute-start = (bf16[4,4,4,16,512]{4,3,2,1,0:T(8,128)(2,1)S(1)}, bf16[4,4,4,16,512]{4,3,2,1,0:T(8,128)(2,1)S(1)}, u32[]{:S(2)}, u32[]{:S(2)}) collective-permute-start(bf16[4,4,4,16,512]{4,3,2,1,0:T(8,128)(2,1)S(1)} %far_half.3), channel_id=1, source_target_pairs={{0,8},{8,0},{1,9},{9,1},{2,10},{10,2},{3,11},{11,3},{4,12},{12,4},... | collective-permute-start | bytes 3145736 | tf_op jit(solution)/shard_map/ppermute | solution.py:134
  14.0 7.2 %copy-start.5 = (bf16[4,64,512]{2,1,0:T(8,128)(2,1)S(1)}, bf16[4,64,512]{2,1,0:T(8,128)(2,1)}, u32[]{:S(2)}) copy-start(bf16[4,64,512]{2,1,0:T(8,128)(2,1)} %hist_ref.3) | copy-start | bytes 786436
  14.0 11.0 %copy-start.4 = (bf16[3,512,512]{2,1,0:T(8,128)(2,1)S(1)}, bf16[3,512,512]{2,1,0:T(8,128)(2,1)}, u32[]{:S(2)}) copy-start(bf16[3,512,512]{2,1,0:T(8,128)(2,1)} %param.13) | copy-start | bytes 4718596
  14.0 25.7 %all-to-all-start = ((bf16[16,64,512]{2,1,0:T(8,128)(2,1)}), bf16[16,64,512]{2,1,0:T(8,128)(2,1)}, u32[]{:S(2)}, u32[]{:S(2)}) async-start(bf16[16,64,512]{2,1,0:T(8,128)(2,1)} %bitcast.6), calls=%async_computation | async-start | bytes 2097152 | tf_op jit(solution)/shard_map/all_to_all | solution.py:137
  21.2 29.1 %collective-permute-start.1 = (bf16[64,512]{1,0:T(8,128)(2,1)S(1)}, bf16[64,512]{1,0:T(8,128)(2,1)S(1)}, u32[]{:S(2)}, u32[]{:S(2)}) collective-permute-start(bf16[64,512]{1,0:T(8,128)(2,1)S(1)} %slice_bitcast_fusion), channel_id=1, source_target_pairs={{0,1},{1,2},{2,3},{3,4},{4,5},{5,6},{6,7},{8,9},{9,10},{10,11},{11... | collective-permute-start | bytes 196616 | tf_op jit(solution)/shard_map/ppermute | solution.py:143
  25.0 25.3 %copy-start.7 = (f32[512]{0:T(512)S(1)}, f32[512]{0:T(512)}, u32[]{:S(2)}) copy-start(f32[512]{0:T(512)} %param.14) | copy-start | bytes 6148
  25.1 25.3 %slice-start = ((bf16[4,64,512]{2,1,0:T(8,128)(2,1)}), bf16[3,64,512]{2,1,0:T(8,128)(2,1)S(1)}, s32[]{:S(2)}) async-start(bf16[4,64,512]{2,1,0:T(8,128)(2,1)} %hist_ref.3), calls=%async_computation.2 | async-start | bytes 393216 | tf_op jit(solution)/shard_map/slice | solution.py:144
  41.8 16.2 %all-to-all-start.1 = ((bf16[8,16,512]{2,1,0:T(8,128)(2,1)}), bf16[8,16,512]{2,1,0:T(8,128)(2,1)S(1)}, u32[]{:S(2)}, u32[]{:S(2)}) async-start(bf16[8,16,512]{2,1,0:T(8,128)(2,1)} %bitcast.8), calls=%async_computation.1 | async-start | bytes 262144 | tf_op jit(solution)/shard_map/all_to_all | solution.py:142
  58.8 4.2 %collective-permute-start.2 = (bf16[16,512]{1,0:T(8,128)(2,1)S(1)}, bf16[16,512]{1,0:T(8,128)(2,1)S(1)}, u32[]{:S(2)}, u32[]{:S(2)}) collective-permute-start(bf16[16,512]{1,0:T(8,128)(2,1)S(1)} %get-tuple-element.10), channel_id=1, source_target_pairs={{0,8},{8,0},{1,9},{9,1},{2,10},{10,2},{3,11},{11,3},{4,12},{12,4},... | collective-permute-start | bytes 49160 | tf_op jit(solution)/shard_map/ppermute | solution.py:168
  59.0 7.2 %collective-permute-start.3 = (bf16[16,512]{1,0:T(8,128)(2,1)S(1)}, bf16[16,512]{1,0:T(8,128)(2,1)S(1)}, u32[]{:S(2)}, u32[]{:S(2)}) collective-permute-start(bf16[16,512]{1,0:T(8,128)(2,1)S(1)} %get-tuple-element.10), channel_id=1, source_target_pairs={{8,16},{16,8},{24,32},{32,24},{40,48},{48,40},{56,64},{64,56},{72,... | collective-permute-start | bytes 49160 | tf_op jit(solution)/shard_map/ppermute | solution.py:167
  66.4 4.2 %collective-permute-start.4 = (bf16[16,512]{1,0:T(8,128)(2,1)S(1)}, bf16[16,512]{1,0:T(8,128)(2,1)S(1)}, u32[]{:S(2)}, u32[]{:S(2)}) collective-permute-start(bf16[16,512]{1,0:T(8,128)(2,1)S(1)} %fusion.19), channel_id=1, source_target_pairs={{0,8},{8,0},{1,9},{9,1},{2,10},{10,2},{3,11},{11,3},{4,12},{12,4},... | collective-permute-start | bytes 49160 | tf_op jit(solution)/shard_map/ppermute | solution.py:168
  66.7 7.2 %collective-permute-start.5 = (bf16[16,512]{1,0:T(8,128)(2,1)S(1)}, bf16[16,512]{1,0:T(8,128)(2,1)S(1)}, u32[]{:S(2)}, u32[]{:S(2)}) collective-permute-start(bf16[16,512]{1,0:T(8,128)(2,1)S(1)} %fusion.19), channel_id=1, source_target_pairs={{8,16},{16,8},{24,32},{32,24},{40,48},{48,40},{56,64},{64,56},{72,... | collective-permute-start | bytes 49160 | tf_op jit(solution)/shard_map/ppermute | solution.py:167
  74.1 4.2 %collective-permute-start.6 = (bf16[16,512]{1,0:T(8,128)(2,1)S(1)}, bf16[16,512]{1,0:T(8,128)(2,1)S(1)}, u32[]{:S(2)}, u32[]{:S(2)}) collective-permute-start(bf16[16,512]{1,0:T(8,128)(2,1)S(1)} %fusion.18), channel_id=1, source_target_pairs={{0,8},{8,0},{1,9},{9,1},{2,10},{10,2},{3,11},{11,3},{4,12},{12,4},... | collective-permute-start | bytes 49160 | tf_op jit(solution)/shard_map/ppermute | solution.py:168
  74.3 7.2 %collective-permute-start.7 = (bf16[16,512]{1,0:T(8,128)(2,1)S(1)}, bf16[16,512]{1,0:T(8,128)(2,1)S(1)}, u32[]{:S(2)}, u32[]{:S(2)}) collective-permute-start(bf16[16,512]{1,0:T(8,128)(2,1)S(1)} %fusion.18), channel_id=1, source_target_pairs={{8,16},{16,8},{24,32},{32,24},{40,48},{48,40},{56,64},{64,56},{72,... | collective-permute-start | bytes 49160 | tf_op jit(solution)/shard_map/ppermute | solution.py:167
  81.7 4.2 %collective-permute-start.8 = (bf16[16,512]{1,0:T(8,128)(2,1)S(1)}, bf16[16,512]{1,0:T(8,128)(2,1)S(1)}, u32[]{:S(2)}, u32[]{:S(2)}) collective-permute-start(bf16[16,512]{1,0:T(8,128)(2,1)S(1)} %fusion.17), channel_id=1, source_target_pairs={{0,8},{8,0},{1,9},{9,1},{2,10},{10,2},{3,11},{11,3},{4,12},{12,4},... | collective-permute-start | bytes 49160 | tf_op jit(solution)/shard_map/ppermute | solution.py:168
  82.0 7.2 %collective-permute-start.9 = (bf16[16,512]{1,0:T(8,128)(2,1)S(1)}, bf16[16,512]{1,0:T(8,128)(2,1)S(1)}, u32[]{:S(2)}, u32[]{:S(2)}) collective-permute-start(bf16[16,512]{1,0:T(8,128)(2,1)S(1)} %fusion.17), channel_id=1, source_target_pairs={{8,16},{16,8},{24,32},{32,24},{40,48},{48,40},{56,64},{64,56},{72,... | collective-permute-start | bytes 49160 | tf_op jit(solution)/shard_map/ppermute | solution.py:167
  89.4 4.2 %collective-permute-start.10 = (bf16[16,512]{1,0:T(8,128)(2,1)S(1)}, bf16[16,512]{1,0:T(8,128)(2,1)S(1)}, u32[]{:S(2)}, u32[]{:S(2)}) collective-permute-start(bf16[16,512]{1,0:T(8,128)(2,1)S(1)} %fusion.16), channel_id=1, source_target_pairs={{0,8},{8,0},{1,9},{9,1},{2,10},{10,2},{3,11},{11,3},{4,12},{12,4},... | collective-permute-start | bytes 49160 | tf_op jit(solution)/shard_map/ppermute | solution.py:168
  89.7 7.2 %collective-permute-start.11 = (bf16[16,512]{1,0:T(8,128)(2,1)S(1)}, bf16[16,512]{1,0:T(8,128)(2,1)S(1)}, u32[]{:S(2)}, u32[]{:S(2)}) collective-permute-start(bf16[16,512]{1,0:T(8,128)(2,1)S(1)} %fusion.16), channel_id=1, source_target_pairs={{8,16},{16,8},{24,32},{32,24},{40,48},{48,40},{56,64},{64,56},{72,... | collective-permute-start | bytes 49160 | tf_op jit(solution)/shard_map/ppermute | solution.py:167
  97.1 4.2 %collective-permute-start.12 = (bf16[16,512]{1,0:T(8,128)(2,1)S(1)}, bf16[16,512]{1,0:T(8,128)(2,1)S(1)}, u32[]{:S(2)}, u32[]{:S(2)}) collective-permute-start(bf16[16,512]{1,0:T(8,128)(2,1)S(1)} %fusion.15), channel_id=1, source_target_pairs={{0,8},{8,0},{1,9},{9,1},{2,10},{10,2},{3,11},{11,3},{4,12},{12,4},... | collective-permute-start | bytes 49160 | tf_op jit(solution)/shard_map/ppermute | solution.py:168
  97.4 7.2 %collective-permute-start.13 = (bf16[16,512]{1,0:T(8,128)(2,1)S(1)}, bf16[16,512]{1,0:T(8,128)(2,1)S(1)}, u32[]{:S(2)}, u32[]{:S(2)}) collective-permute-start(bf16[16,512]{1,0:T(8,128)(2,1)S(1)} %fusion.15), channel_id=1, source_target_pairs={{8,16},{16,8},{24,32},{32,24},{40,48},{48,40},{56,64},{64,56},{72,... | collective-permute-start | bytes 49160 | tf_op jit(solution)/shard_map/ppermute | solution.py:167
  104.8 4.2 %collective-permute-start.14 = (bf16[16,512]{1,0:T(8,128)(2,1)S(1)}, bf16[16,512]{1,0:T(8,128)(2,1)S(1)}, u32[]{:S(2)}, u32[]{:S(2)}) collective-permute-start(bf16[16,512]{1,0:T(8,128)(2,1)S(1)} %fusion.14), channel_id=1, source_target_pairs={{0,8},{8,0},{1,9},{9,1},{2,10},{10,2},{3,11},{11,3},{4,12},{12,4},... | collective-permute-start | bytes 49160 | tf_op jit(solution)/shard_map/ppermute | solution.py:168
  105.0 7.2 %collective-permute-start.15 = (bf16[16,512]{1,0:T(8,128)(2,1)S(1)}, bf16[16,512]{1,0:T(8,128)(2,1)S(1)}, u32[]{:S(2)}, u32[]{:S(2)}) collective-permute-start(bf16[16,512]{1,0:T(8,128)(2,1)S(1)} %fusion.14), channel_id=1, source_target_pairs={{8,16},{16,8},{24,32},{32,24},{40,48},{48,40},{56,64},{64,56},{72,... | collective-permute-start | bytes 49160 | tf_op jit(solution)/shard_map/ppermute | solution.py:167
  112.4 3.9 %collective-permute-start.16 = (f32[16,512]{1,0:T(8,128)S(1)}, f32[16,512]{1,0:T(8,128)S(1)}, u32[]{:S(2)}, u32[]{:S(2)}) collective-permute-start(f32[16,512]{1,0:T(8,128)S(1)} %fusion.13), channel_id=1, source_target_pairs={{0,3},{1,0},{2,1},{3,2},{4,7},{5,4},{6,5},{7,6},{8,11},{9,8},{10,9... | collective-permute-start | bytes 98312 | tf_op jit(solution)/shard_map/ppermute | solution.py:177
  112.7 5.1 %collective-permute-start.17 = (f32[16,512]{1,0:T(8,128)S(1)}, f32[16,512]{1,0:T(8,128)S(1)}, u32[]{:S(2)}, u32[]{:S(2)}) collective-permute-start(f32[16,512]{1,0:T(8,128)S(1)} %fusion.13), channel_id=1, source_target_pairs={{0,1},{1,2},{2,3},{3,0},{4,5},{5,6},{6,7},{7,4},{8,9},{9,10},{10,1... | collective-permute-start | bytes 98312 | tf_op jit(solution)/shard_map/ppermute | solution.py:177
  114.5 5.4 %collective-permute-start.18 = (f32[16,512]{1,0:T(8,128)S(1)}, f32[16,512]{1,0:T(8,128)S(1)}, u32[]{:S(2)}, u32[]{:S(2)}) collective-permute-start(f32[16,512]{1,0:T(8,128)S(1)} %fusion.13), channel_id=1, source_target_pairs={{0,2},{1,3},{2,0},{3,1},{4,6},{5,7},{6,4},{7,5},{8,10},{9,11},{10,... | collective-permute-start | bytes 98312 | tf_op jit(solution)/shard_map/ppermute | solution.py:177
  120.6 0.7 copy-start.6

commit v3 on v2

--- a/solution.py
+++ b/solution.py
@@ -16,7 +16,8 @@
 
 def far_kernel(
     core_ref, rank_ref, lag_ref, hist_ref, right_ref, left_ref, out_ref,
-    hist_buf, right_buf, left_buf, hist_sem, right_sem, left_sem, *, ranks
+    rank_buf, lag_buf, hist_buf, right_buf, left_buf,
+    rank_sem, lag_sem, hist_sem, right_sem, left_sem, *, ranks
 ):
     groups, chips, depth, width = right_buf.shape
     lags, steps, _ = hist_buf.shape
@@ -28,8 +29,13 @@
             source.at[pl.ds(group * chips, chips), core], target.at[group], sem.at[group]
         )
 
-    whole = pltpu.make_async_copy(hist_ref, hist_buf, hist_sem)
-    whole.start()
+    small = [
+        pltpu.make_async_copy(rank_ref, rank_buf, rank_sem),
+        pltpu.make_async_copy(lag_ref, lag_buf, lag_sem),
+        pltpu.make_async_copy(hist_ref, hist_buf, hist_sem),
+    ]
+    for copy in small:
+        copy.start()
     rights = [brought(right_ref, right_buf, right_sem, g) for g in range(groups)]
     lefts = [brought(left_ref, left_buf, left_sem, g) for g in range(groups)]
     for g in range(groups):
@@ -44,8 +50,8 @@
             for k in range(per):
                 pair = ((group * chips + chip) * 2 + core) * per + k
                 first = (chip * per + k) * ranks
-                inside = (lane >= first) & (lane < first + rank_ref[pair])
-                column = jnp.where(inside, lag_ref[pair], column)
+                inside = (lane >= first) & (lane < first + rank_buf[pair])
+                column = jnp.where(inside, lag_buf[pair], column)
         every = lax.dot_general(
             hist_buf[...].reshape(lags * steps, width),
             right_buf[group].reshape(total, width),
@@ -68,7 +74,8 @@
             field = jnp.dot(part, left[low:high], preferred_element_type=jnp.float32)
             out_ref[chip, :, group] = field.reshape(out_ref.shape[1], -1, width).astype(out_ref.dtype)
 
-    whole.wait()
+    for copy in small:
+        copy.wait()
     rights[0].wait()
     value = chosen(0)
     for g in range(groups):
@@ -91,12 +98,16 @@
     return pl.pallas_call(
         functools.partial(far_kernel, ranks=ranks),
         out_shape=jax.ShapeDtypeStruct((chips, cuts, groups, steps // cuts, width), jnp.bfloat16),
-        in_specs=[scalar, scalar, scalar, outside, outside, outside],
+        in_specs=[scalar] + [outside] * 5,
         out_specs=pl.BlockSpec(memory_space=pltpu.VMEM),
         scratch_shapes=[
+            pltpu.SMEM(rank.shape, jnp.int32),
+            pltpu.SMEM(lag.shape, jnp.int32),
             pltpu.VMEM((lags, steps, width), jnp.bfloat16),
             held,
             held,
+            pltpu.SemaphoreType.DMA,
+            pltpu.SemaphoreType.DMA,
             pltpu.SemaphoreType.DMA,
             pltpu.SemaphoreType.DMA((groups,)),
             pltpu.SemaphoreType.DMA((groups,)),
@@ -111,6 +122,32 @@
     )(core, rank, lag, history, right, left)
 
 
+def plane_kernel(in_ref, out_ref):
+    rows = 16
+    for first in range(0, in_ref.shape[1], rows):
+        part = slice(first, first + rows)
+        total = in_ref[0, part].astype(jnp.float32)
+        for source in range(1, in_ref.shape[0]):
+            total = total + in_ref[source, part].astype(jnp.float32)
+        for copy in range(out_ref.shape[0]):
+            out_ref[copy, part] = total.astype(out_ref.dtype)
+
+
+def plane_sum(arrived, copies):
+    inside = pl.BlockSpec(memory_space=pltpu.VMEM)
+    return pl.pallas_call(
+        plane_kernel,
+        out_shape=jax.ShapeDtypeStruct((copies, *arrived.shape[1:]), arrived.dtype),
+        in_specs=[inside],
+        out_specs=inside,
+        compiler_params=pltpu.CompilerParams(vmem_limit_bytes=4 << 20),
+        cost_estimate=pl.CostEstimate(
+            flops=arrived.size, bytes_accessed=2 * arrived.size, transcendentals=0
+        ),
+        name="plane_sum",
+    )(arrived)
+
+
 def per_device(
     history, right_factor, left_factor, pair_rank, pair_lag, near_block, self_term, excitation
 ):
@@ -120,9 +157,9 @@
     depth = pairs // targets * ranks
     right = right_factor.reshape(targets // 2, 2, depth, width)
     left = left_factor.reshape(targets // 2, 2, depth, width)
-    rank, lag = pair_rank[:, 0], pair_lag[:, 0]
-    history_out, right, left = (
-        pltpu.with_memory_space_constraint(v, pltpu.HBM) for v in (history, right, left)
+    history_out, right, left, rank, lag = (
+        pltpu.with_memory_space_constraint(v, pltpu.HBM)
+        for v in (history, right, left, pair_rank[:, 0], pair_lag[:, 0])
     )
     core = lax.axis_index("c")
     swap = [(0, 1), (1, 0)]
@@ -136,11 +173,10 @@
     partial_value = (mine.astype(jnp.float32) + came.astype(jnp.float32)).astype(jnp.bfloat16)
     arrived = lax.all_to_all(
         partial_value.reshape(16, -1, width), ("x", "y"), 0, 0, tiled=True
-    ).reshape(16, 4, -1, width)
-    plane = jnp.sum(arrived.astype(jnp.float32), axis=0).astype(jnp.bfloat16)
-    twice = jnp.broadcast_to(plane[None], (2, *plane.shape)).reshape(8, -1, width)
+    )
+    twice = plane_sum(arrived, 2).reshape(8, -1, width)
     arrived = lax.all_to_all(twice, ("zh", "zl"), 0, 0, tiled=True)
-    incoming = lax.ppermute(history[-1], HIST, [(i, i + 1) for i in range(7)])
+    incoming = lax.ppermute(history[-1], HIST, [(i, (i + 1) % 8) for i in range(8)])
     shifted = jnp.concatenate([incoming[None], history[:-1]], axis=0)
     arrived, incoming, shifted = lax.optimization_barrier((arrived, incoming, shifted))
     far_field = jnp.sum(arrived.astype(jnp.float32), axis=0)
@@ -152,7 +188,9 @@
     near_own = near_block[1]
     near_chip = jnp.where(core == 0, near_block[2], near_block[0])
     near_away = jnp.where(core == 0, near_block[0], near_block[2])
-    between = []
+    block = lax.axis_index(SPACE)
+    near_away = jnp.where((block == 0) | (block == targets - 1), 0.0, near_away)
+    between = [(0, 0), (targets - 1, targets - 1)]
     for t in range(1, targets - 1, 2):
         between += [(t, t + 1), (t + 1, t)]
 

time: 122 us -> 119 us (0.975)
  local copies, waits for them, and re-layouts: 2.71 us -> 0.72 us
  starting transfers between devices: 49.9 us -> 48.1 us
    ppermute x1, starting transfers between devices: 3.78 us -> 2 us  [per_device(): lax.ppermute(history[-1], HIST, [(i, (i + 1) % 8) for i in range(8)])]
    reduce_sum x1 -> x0, other arithmetic: 1.37 us -> none  [per_device(): plane = jnp.sum(arrived.astype(jnp.float32), axis=0).astype(jnp.bfloat16)]
    unnamed x16 -> x8, local copies, waits for them, and re-layouts: 2.03 us -> 0.71 us
    select_n x1, other arithmetic: 0.07 us -> 1.31 us  [per_device(): near_away = jnp.where((block == 0) | (block == targets - 1), 0.0, near_away)]
  transfers between devices with their start and end apart: 21 -> 21, of which waited for: 12 -> 12; matrix products, arithmetic and copies ran while one was open for 4% -> 5% of each run, Pallas kernels for 4% -> 5%
where the time goes in v3:
time: 119 us
  waiting for transfers between devices  48.5 us (41%)
  starting transfers between devices  48.1 us (40%)
  Pallas kernels  10.2 us (9%)
  matrix products  5.96 us (5%)
  other arithmetic  4.26 us (4%)
    ppermute x7, starting transfers between devices, per_device(): away = lax.ppermute(rounded, SPACE, between)  27.3 us
    ppermute x7, waiting for transfers between devices, per_device(): away = lax.ppermute(rounded, SPACE, between)  21.2 us
    all_to_all x1, waiting for transfers between devices, per_device(): lax.all_to_all(partial_value.reshape(16, -1, width), ('x', 'y'), 0, 0, ti...  15.1 us
    pallas_call x2, Pallas kernels, far_half(): pl.pallas_call(functools.partial(far_kernel, ranks=ranks), out_shape=jax....  9.45 us
    all_to_all x1, starting transfers between devices, per_device(): arrived = lax.all_to_all(twice, ('zh', 'zl'), 0, 0, tiled=True)  8.57 us
    all_to_all x1, waiting for transfers between devices, per_device(): arrived = lax.all_to_all(twice, ('zh', 'zl'), 0, 0, tiled=True)  7.55 us
    all_to_all x1, starting transfers between devices, per_device(): lax.all_to_all(partial_value.reshape(16, -1, width), ('x', 'y'), 0, 0, ti...  7.16 us
    dot_general x21, matrix products, product(): lax.dot_general(value, block, (((1,), (1,)), ((), ())), preferred_element...  5.96 us
  transfers between devices with their start and end apart: 21, of which 12 were waited for; matrix products, arithmetic and copies ran while one was open for 5% of the time, Pallas kernels for 5%

profile of v3, /device:TPU:32, one launch (start us, length us, event | category | flops | bytes accessed | tf_op | source)
XLA Modules:
  0.0 118.7 jit_solution(4899456327820718559)
XLA Ops:
  0.6 4.7 %far_half.3 = bf16[4,4,4,16,512]{4,3,2,1,0:T(8,128)(2,1)S(1)} custom-call(s32[1]{0:T(128)} %bitcast.5.core_ref, s32[64]{0:T(128)} %bitcast.84, s32[64]{0:T(128)} %bitcast.86, bf16[4,64,512]{2,1,0:T(8,128)(2,1)} %hist_ref.3, bf16[16,2,160,512]{3,2,1,0:T(8,128)(2,1)} %bitcast.79, bf16[16,2,160,512]{3,2,1,0:T(8,128)(2,1)} %bitcast.81), custom_call_target="tpu_custom_call" | custom-call | flops 838860800 | bytes 6291456 | tf_op jit(solution)/shard_map/far_half/pallas_call | solution.py:98
  5.4 0.1 collective-permute-start
  5.5 4.7 %far_half.2 = bf16[4,4,4,16,512]{4,3,2,1,0:T(8,128)(2,1)S(1)} custom-call(s32[1]{0:T(128)} %bitcast.core_ref, s32[64]{0:T(128)} %bitcast.85, s32[64]{0:T(128)} %bitcast.87, bf16[4,64,512]{2,1,0:T(8,128)(2,1)} %hist_ref.3, bf16[16,2,160,512]{3,2,1,0:T(8,128)(2,1)} %bitcast.80, bf16[16,2,160,512]{3,2,1,0:T(8,128)(2,1)} %bitcast.82), custom_call_target="tpu_custom_call" | custom-call | flops 838860800 | bytes 6291456 | tf_op jit(solution)/shard_map/far_half/pallas_call | solution.py:98
  10.2 1.4 %add_convert_fusion = bf16[4,4,4,16,512]{4,3,2,1,0:T(8,128)(2,1)} fusion(bf16[4,4,4,16,512]{4,3,2,1,0:T(8,128)(2,1)S(1)} %collective-permute-done, bf16[4,4,4,16,512]{4,3,2,1,0:T(8,128)(2,1)S(1)} %far_half.2), kind=kLoop, calls=%fused_computation | loop fusion | flops 2097152 | bytes 3145728 | tf_op jit(solution)/shard_map/convert_element_type | solution.py:173
  11.6 7.2 %all-to-all-start = ((bf16[16,64,512]{2,1,0:T(8,128)(2,1)}), bf16[16,64,512]{2,1,0:T(8,128)(2,1)S(1)}, u32[]{:S(2)}, u32[]{:S(2)}) async-start(bf16[16,64,512]{2,1,0:T(8,128)(2,1)} %bitcast.6), calls=%async_computation | async-start | bytes 2097152 | tf_op jit(solution)/shard_map/all_to_all | solution.py:174
  18.8 2.0 %collective-permute-start.1 = (bf16[64,512]{1,0:T(8,128)(2,1)S(1)}, bf16[64,512]{1,0:T(8,128)(2,1)S(1)}, u32[]{:S(2)}, u32[]{:S(2)}) collective-permute-start(bf16[64,512]{1,0:T(8,128)(2,1)S(1)} %slice_bitcast_fusion), channel_id=1, source_target_pairs={{0,1},{1,2},{2,3},{3,4},{4,5},{5,6},{6,7},{7,0},{8,9},{9,10},{10,1... | collective-permute-start | bytes 196616 | tf_op jit(solution)/shard_map/ppermute | solution.py:179
  20.8 1.3 %select_select_fusion = (bf16[1,512,512]{2,1,0:T(8,128)(2,1)S(1)}, bf16[1,512,512]{2,1,0:T(8,128)(2,1)S(1)}) fusion(pred[]{:T(512)S(6)} %or.3, pred[]{:T(512)S(6)} %eq.17, bf16[3,512,512]{2,1,0:T(8,128)(2,1)} %param.13), kind=kLoop, calls=%fused_computation.63 | loop fusion | flops 786432 | bytes 2097154 | tf_op jit(solution)/shard_map/jit(_where)/select_n | solution.py:192
  22.2 15.1 %all-to-all-done.in_ref = bf16[16,64,512]{2,1,0:T(8,128)(2,1)S(1)} async-done(((bf16[16,64,512]{2,1,0:T(8,128)(2,1)}), bf16[16,64,512]{2,1,0:T(8,128)(2,1)S(1)}, u32[]{:S(2)}, u32[]{:S(2)}) %all-to-all-start) | async-done | bytes 1048608 | tf_op jit(solution)/shard_map/all_to_all | solution.py:174
  37.3 0.8 plane_sum.1
  38.1 8.6 %all-to-all-start.1 = ((bf16[8,16,512]{2,1,0:T(8,128)(2,1)}), bf16[8,16,512]{2,1,0:T(8,128)(2,1)S(1)}, u32[]{:S(2)}, u32[]{:S(2)}) async-start(bf16[8,16,512]{2,1,0:T(8,128)(2,1)} %bitcast.7), calls=%async_computation.1 | async-start | bytes 262144 | tf_op jit(solution)/shard_map/all_to_all | solution.py:178
  46.7 0.0 collective-permute-done.1
  46.7 7.6 %all-to-all-done.1 = bf16[8,16,512]{2,1,0:T(8,128)(2,1)S(1)} async-done(((bf16[8,16,512]{2,1,0:T(8,128)(2,1)}), bf16[8,16,512]{2,1,0:T(8,128)(2,1)S(1)}, u32[]{:S(2)}, u32[]{:S(2)}) %all-to-all-start.1) | async-done | bytes 131104 | tf_op jit(solution)/shard_map/all_to_all | solution.py:178
  54.3 0.8 multiply_convert_fusion
  55.1 0.0 collective-permute-start.2
  55.1 1.3 %fusion.46 = f32[16,512]{1,0:T(8,128)S(1)} fusion(bf16[16,512]{1,0:T(8,128)(2,1)S(1)} %get-tuple-element.10, bf16[3,512,512]{2,1,0:T(8,128)(2,1)} %param.13), kind=kOutput, calls=%fused_computation.61 | convolution fusion | flops 8388608 | bytes 573440 | tf_op jit(solution)/shard_map/dot_general | solution.py:198
  56.4 3.9 %collective-permute-start.3 = (bf16[16,512]{1,0:T(8,128)(2,1)S(1)}, bf16[16,512]{1,0:T(8,128)(2,1)S(1)}, u32[]{:S(2)}, u32[]{:S(2)}) collective-permute-start(bf16[16,512]{1,0:T(8,128)(2,1)S(1)} %get-tuple-element.10), channel_id=1, source_target_pairs={{0,0},{248,248},{8,16},{16,8},{24,32},{32,24},{40,48},{48,40},{56,... | collective-permute-start | bytes 49160 | tf_op jit(solution)/shard_map/ppermute | solution.py:205
  60.3 0.0 collective-permute-done.2
  60.3 0.2 convolution_add_fusion.13
  60.5 3.0 %collective-permute-done.3 = bf16[16,512]{1,0:T(8,128)(2,1)S(1)} collective-permute-done((bf16[16,512]{1,0:T(8,128)(2,1)S(1)}, bf16[16,512]{1,0:T(8,128)(2,1)S(1)}, u32[]{:S(2)}, u32[]{:S(2)}) %collective-permute-start.3) | collective-permute-done | bytes 16416 | tf_op jit(solution)/shard_map/ppermute | solution.py:205
  63.5 0.2 fusion.19
  63.8 0.0 collective-permute-start.4
  63.8 0.2 fusion.44
  64.0 3.9 %collective-permute-start.5 = (bf16[16,512]{1,0:T(8,128)(2,1)S(1)}, bf16[16,512]{1,0:T(8,128)(2,1)S(1)}, u32[]{:S(2)}, u32[]{:S(2)}) collective-permute-start(bf16[16,512]{1,0:T(8,128)(2,1)S(1)} %fusion.19), channel_id=1, source_target_pairs={{0,0},{248,248},{8,16},{16,8},{24,32},{32,24},{40,48},{48,40},{56,... | collective-permute-start | bytes 49160 | tf_op jit(solution)/shard_map/ppermute | solution.py:205
  68.0 0.2 convolution_add_fusion.11
  68.2 3.0 %collective-permute-done.5 = bf16[16,512]{1,0:T(8,128)(2,1)S(1)} collective-permute-done((bf16[16,512]{1,0:T(8,128)(2,1)S(1)}, bf16[16,512]{1,0:T(8,128)(2,1)S(1)}, u32[]{:S(2)}, u32[]{:S(2)}) %collective-permute-start.5) | collective-permute-done | bytes 16416 | tf_op jit(solution)/shard_map/ppermute | solution.py:205
  71.2 0.2 fusion.18
  71.4 0.0 collective-permute-start.6
  71.5 0.2 fusion.42
  71.7 3.9 %collective-permute-start.7 = (bf16[16,512]{1,0:T(8,128)(2,1)S(1)}, bf16[16,512]{1,0:T(8,128)(2,1)S(1)}, u32[]{:S(2)}, u32[]{:S(2)}) collective-permute-start(bf16[16,512]{1,0:T(8,128)(2,1)S(1)} %fusion.18), channel_id=1, source_target_pairs={{0,0},{248,248},{8,16},{16,8},{24,32},{32,24},{40,48},{48,40},{56,... | collective-permute-start | bytes 49160 | tf_op jit(solution)/shard_map/ppermute | solution.py:205
  75.6 0.2 convolution_add_fusion.9
  75.9 3.0 %collective-permute-done.7 = bf16[16,512]{1,0:T(8,128)(2,1)S(1)} collective-permute-done((bf16[16,512]{1,0:T(8,128)(2,1)S(1)}, bf16[16,512]{1,0:T(8,128)(2,1)S(1)}, u32[]{:S(2)}, u32[]{:S(2)}) %collective-permute-start.7) | collective-permute-done | bytes 16416 | tf_op jit(solution)/shard_map/ppermute | solution.py:205
  78.9 0.2 fusion.17
  79.1 0.0 collective-permute-start.8
  79.1 0.2 fusion.40
  79.4 3.9 %collective-permute-start.9 = (bf16[16,512]{1,0:T(8,128)(2,1)S(1)}, bf16[16,512]{1,0:T(8,128)(2,1)S(1)}, u32[]{:S(2)}, u32[]{:S(2)}) collective-permute-start(bf16[16,512]{1,0:T(8,128)(2,1)S(1)} %fusion.17), channel_id=1, source_target_pairs={{0,0},{248,248},{8,16},{16,8},{24,32},{32,24},{40,48},{48,40},{56,... | collective-permute-start | bytes 49160 | tf_op jit(solution)/shard_map/ppermute | solution.py:205
  83.3 0.2 convolution_add_fusion.7
  83.5 3.0 %collective-permute-done.9 = bf16[16,512]{1,0:T(8,128)(2,1)S(1)} collective-permute-done((bf16[16,512]{1,0:T(8,128)(2,1)S(1)}, bf16[16,512]{1,0:T(8,128)(2,1)S(1)}, u32[]{:S(2)}, u32[]{:S(2)}) %collective-permute-start.9) | collective-permute-done | bytes 16416 | tf_op jit(solution)/shard_map/ppermute | solution.py:205
  86.6 0.2 fusion.16
  86.8 0.0 collective-permute-start.10
  86.8 0.2 fusion.38
  87.0 3.9 %collective-permute-start.11 = (bf16[16,512]{1,0:T(8,128)(2,1)S(1)}, bf16[16,512]{1,0:T(8,128)(2,1)S(1)}, u32[]{:S(2)}, u32[]{:S(2)}) collective-permute-start(bf16[16,512]{1,0:T(8,128)(2,1)S(1)} %fusion.16), channel_id=1, source_target_pairs={{0,0},{248,248},{8,16},{16,8},{24,32},{32,24},{40,48},{48,40},{56,... | collective-permute-start | bytes 49160 | tf_op jit(solution)/shard_map/ppermute | solution.py:205
  91.0 0.2 convolution_add_fusion.5
  91.2 3.0 %collective-permute-done.11 = bf16[16,512]{1,0:T(8,128)(2,1)S(1)} collective-permute-done((bf16[16,512]{1,0:T(8,128)(2,1)S(1)}, bf16[16,512]{1,0:T(8,128)(2,1)S(1)}, u32[]{:S(2)}, u32[]{:S(2)}) %collective-permute-start.11) | collective-permute-done | bytes 16416 | tf_op jit(solution)/shard_map/ppermute | solution.py:205
  94.2 0.2 fusion.15
  94.5 0.0 collective-permute-start.12
  94.5 0.2 fusion.36
  94.7 3.9 %collective-permute-start.13 = (bf16[16,512]{1,0:T(8,128)(2,1)S(1)}, bf16[16,512]{1,0:T(8,128)(2,1)S(1)}, u32[]{:S(2)}, u32[]{:S(2)}) collective-permute-start(bf16[16,512]{1,0:T(8,128)(2,1)S(1)} %fusion.15), channel_id=1, source_target_pairs={{0,0},{248,248},{8,16},{16,8},{24,32},{32,24},{40,48},{48,40},{56,... | collective-permute-start | bytes 49160 | tf_op jit(solution)/shard_map/ppermute | solution.py:205
  98.6 0.2 convolution_add_fusion.3
  98.9 3.0 %collective-permute-done.13 = bf16[16,512]{1,0:T(8,128)(2,1)S(1)} collective-permute-done((bf16[16,512]{1,0:T(8,128)(2,1)S(1)}, bf16[16,512]{1,0:T(8,128)(2,1)S(1)}, u32[]{:S(2)}, u32[]{:S(2)}) %collective-permute-start.13) | collective-permute-done | bytes 16416 | tf_op jit(solution)/shard_map/ppermute | solution.py:205
  101.9 0.2 fusion.14
  102.1 0.0 collective-permute-start.14
  102.2 0.2 fusion.34
  102.4 3.9 %collective-permute-start.15 = (bf16[16,512]{1,0:T(8,128)(2,1)S(1)}, bf16[16,512]{1,0:T(8,128)(2,1)S(1)}, u32[]{:S(2)}, u32[]{:S(2)}) collective-permute-start(bf16[16,512]{1,0:T(8,128)(2,1)S(1)} %fusion.14), channel_id=1, source_target_pairs={{0,0},{248,248},{8,16},{16,8},{24,32},{32,24},{40,48},{48,40},{56,... | collective-permute-start | bytes 49160 | tf_op jit(solution)/shard_map/ppermute | solution.py:205
  106.3 0.2 convolution_add_fusion.1
  106.5 3.0 %collective-permute-done.15 = bf16[16,512]{1,0:T(8,128)(2,1)S(1)} collective-permute-done((bf16[16,512]{1,0:T(8,128)(2,1)S(1)}, bf16[16,512]{1,0:T(8,128)(2,1)S(1)}, u32[]{:S(2)}, u32[]{:S(2)}) %collective-permute-start.15) | collective-permute-done | bytes 16416 | tf_op jit(solution)/shard_map/ppermute | solution.py:205
  109.6 0.2 fusion.13
  109.8 0.2 collective-permute-start.16
  110.0 1.8 %collective-permute-start.17 = (f32[16,512]{1,0:T(8,128)S(1)}, f32[16,512]{1,0:T(8,128)S(1)}, u32[]{:S(2)}, u32[]{:S(2)}) collective-permute-start(f32[16,512]{1,0:T(8,128)S(1)} %fusion.13), channel_id=1, source_target_pairs={{0,1},{1,2},{2,3},{3,0},{4,5},{5,6},{6,7},{7,4},{8,9},{9,10},{10,1... | collective-permute-start | bytes 98312 | tf_op jit(solution)/shard_map/ppermute | solution.py:215
  111.8 0.8 collective-permute-start.18
  112.7 1.1 collective-permute-done.16
  113.7 1.4 %collective-permute-done.17 = f32[16,512]{1,0:T(8,128)S(1)} collective-permute-done((f32[16,512]{1,0:T(8,128)S(1)}, f32[16,512]{1,0:T(8,128)S(1)}, u32[]{:S(2)}, u32[]{:S(2)}) %collective-permute-start.17) | collective-permute-done | bytes 32800 | tf_op jit(solution)/shard_map/ppermute | solution.py:215
  115.1 2.1 %collective-permute-done.18 = f32[16,512]{1,0:T(8,128)S(1)} collective-permute-done((f32[16,512]{1,0:T(8,128)S(1)}, f32[16,512]{1,0:T(8,128)S(1)}, u32[]{:S(2)}, u32[]{:S(2)}) %collective-permute-start.18) | collective-permute-done | bytes 32800 | tf_op jit(solution)/shard_map/ppermute | solution.py:215
  117.3 0.7 bitcast_dynamic-update-slice_fusion
  118.0 0.7 copy-done.2
  (21 shorter events, 0.1 us)
Async XLA Ops:
  5.4 4.8 %collective-permute-start = (bf16[4,4,4,16,512]{4,3,2,1,0:T(8,128)(2,1)S(1)}, bf16[4,4,4,16,512]{4,3,2,1,0:T(8,128)(2,1)S(1)}, u32[]{:S(2)}, u32[]{:S(2)}) collective-permute-start(bf16[4,4,4,16,512]{4,3,2,1,0:T(8,128)(2,1)S(1)} %far_half.3), channel_id=1, source_target_pairs={{0,8},{8,0},{1,9},{9,1},{2,10},{10,2},{3,11},{11,3},{4,12},{12,4},... | collective-permute-start | bytes 3145736 | tf_op jit(solution)/shard_map/ppermute | solution.py:171
  11.6 7.2 %copy-start.1 = (bf16[4,64,512]{2,1,0:T(8,128)(2,1)S(1)}, bf16[4,64,512]{2,1,0:T(8,128)(2,1)}, u32[]{:S(2)}) copy-start(bf16[4,64,512]{2,1,0:T(8,128)(2,1)} %hist_ref.3) | copy-start | bytes 786436
  11.6 25.6 %all-to-all-start = ((bf16[16,64,512]{2,1,0:T(8,128)(2,1)}), bf16[16,64,512]{2,1,0:T(8,128)(2,1)S(1)}, u32[]{:S(2)}, u32[]{:S(2)}) async-start(bf16[16,64,512]{2,1,0:T(8,128)(2,1)} %bitcast.6), calls=%async_computation | async-start | bytes 2097152 | tf_op jit(solution)/shard_map/all_to_all | solution.py:174
  18.8 27.8 %collective-permute-start.1 = (bf16[64,512]{1,0:T(8,128)(2,1)S(1)}, bf16[64,512]{1,0:T(8,128)(2,1)S(1)}, u32[]{:S(2)}, u32[]{:S(2)}) collective-permute-start(bf16[64,512]{1,0:T(8,128)(2,1)S(1)} %slice_bitcast_fusion), channel_id=1, source_target_pairs={{0,1},{1,2},{2,3},{3,4},{4,5},{5,6},{6,7},{7,0},{8,9},{9,10},{10,1... | collective-permute-start | bytes 196616 | tf_op jit(solution)/shard_map/ppermute | solution.py:179
  20.8 25.8 %copy-start.3 = (f32[512]{0:T(512)S(1)}, f32[512]{0:T(512)}, u32[]{:S(2)}) copy-start(f32[512]{0:T(512)} %param.14) | copy-start | bytes 6148
  20.8 25.8 %slice-start = ((bf16[4,64,512]{2,1,0:T(8,128)(2,1)}), bf16[3,64,512]{2,1,0:T(8,128)(2,1)S(1)}, s32[]{:S(2)}) async-start(bf16[4,64,512]{2,1,0:T(8,128)(2,1)} %hist_ref.3), calls=%async_computation.2 | async-start | bytes 393216 | tf_op jit(solution)/shard_map/slice | solution.py:180
  38.1 16.2 %all-to-all-start.1 = ((bf16[8,16,512]{2,1,0:T(8,128)(2,1)}), bf16[8,16,512]{2,1,0:T(8,128)(2,1)S(1)}, u32[]{:S(2)}, u32[]{:S(2)}) async-start(bf16[8,16,512]{2,1,0:T(8,128)(2,1)} %bitcast.7), calls=%async_computation.1 | async-start | bytes 262144 | tf_op jit(solution)/shard_map/all_to_all | solution.py:178
  46.6 17.1 %copy-start = (bf16[3,512,512]{2,1,0:T(8,128)(2,1)S(1)}, bf16[3,512,512]{2,1,0:T(8,128)(2,1)}, u32[]{:S(2)}) copy-start(bf16[3,512,512]{2,1,0:T(8,128)(2,1)} %param.13) | copy-start | bytes 4718596
  55.1 5.2 %collective-permute-start.2 = (bf16[16,512]{1,0:T(8,128)(2,1)S(1)}, bf16[16,512]{1,0:T(8,128)(2,1)S(1)}, u32[]{:S(2)}, u32[]{:S(2)}) collective-permute-start(bf16[16,512]{1,0:T(8,128)(2,1)S(1)} %get-tuple-element.10), channel_id=1, source_target_pairs={{0,8},{8,0},{1,9},{9,1},{2,10},{10,2},{3,11},{11,3},{4,12},{12,4},... | collective-permute-start | bytes 49160 | tf_op jit(solution)/shard_map/ppermute | solution.py:206
  56.4 7.2 %collective-permute-start.3 = (bf16[16,512]{1,0:T(8,128)(2,1)S(1)}, bf16[16,512]{1,0:T(8,128)(2,1)S(1)}, u32[]{:S(2)}, u32[]{:S(2)}) collective-permute-start(bf16[16,512]{1,0:T(8,128)(2,1)S(1)} %get-tuple-element.10), channel_id=1, source_target_pairs={{0,0},{248,248},{8,16},{16,8},{24,32},{32,24},{40,48},{48,40},{56,... | collective-permute-start | bytes 49160 | tf_op jit(solution)/shard_map/ppermute | solution.py:205
  63.8 4.2 %collective-permute-start.4 = (bf16[16,512]{1,0:T(8,128)(2,1)S(1)}, bf16[16,512]{1,0:T(8,128)(2,1)S(1)}, u32[]{:S(2)}, u32[]{:S(2)}) collective-permute-start(bf16[16,512]{1,0:T(8,128)(2,1)S(1)} %fusion.19), channel_id=1, source_target_pairs={{0,8},{8,0},{1,9},{9,1},{2,10},{10,2},{3,11},{11,3},{4,12},{12,4},... | collective-permute-start | bytes 49160 | tf_op jit(solution)/shard_map/ppermute | solution.py:206
  64.0 7.2 %collective-permute-start.5 = (bf16[16,512]{1,0:T(8,128)(2,1)S(1)}, bf16[16,512]{1,0:T(8,128)(2,1)S(1)}, u32[]{:S(2)}, u32[]{:S(2)}) collective-permute-start(bf16[16,512]{1,0:T(8,128)(2,1)S(1)} %fusion.19), channel_id=1, source_target_pairs={{0,0},{248,248},{8,16},{16,8},{24,32},{32,24},{40,48},{48,40},{56,... | collective-permute-start | bytes 49160 | tf_op jit(solution)/shard_map/ppermute | solution.py:205
  71.4 4.2 %collective-permute-start.6 = (bf16[16,512]{1,0:T(8,128)(2,1)S(1)}, bf16[16,512]{1,0:T(8,128)(2,1)S(1)}, u32[]{:S(2)}, u32[]{:S(2)}) collective-permute-start(bf16[16,512]{1,0:T(8,128)(2,1)S(1)} %fusion.18), channel_id=1, source_target_pairs={{0,8},{8,0},{1,9},{9,1},{2,10},{10,2},{3,11},{11,3},{4,12},{12,4},... | collective-permute-start | bytes 49160 | tf_op jit(solution)/shard_map/ppermute | solution.py:206
  71.7 7.2 %collective-permute-start.7 = (bf16[16,512]{1,0:T(8,128)(2,1)S(1)}, bf16[16,512]{1,0:T(8,128)(2,1)S(1)}, u32[]{:S(2)}, u32[]{:S(2)}) collective-permute-start(bf16[16,512]{1,0:T(8,128)(2,1)S(1)} %fusion.18), channel_id=1, source_target_pairs={{0,0},{248,248},{8,16},{16,8},{24,32},{32,24},{40,48},{48,40},{56,... | collective-permute-start | bytes 49160 | tf_op jit(solution)/shard_map/ppermute | solution.py:205
  79.1 4.2 %collective-permute-start.8 = (bf16[16,512]{1,0:T(8,128)(2,1)S(1)}, bf16[16,512]{1,0:T(8,128)(2,1)S(1)}, u32[]{:S(2)}, u32[]{:S(2)}) collective-permute-start(bf16[16,512]{1,0:T(8,128)(2,1)S(1)} %fusion.17), channel_id=1, source_target_pairs={{0,8},{8,0},{1,9},{9,1},{2,10},{10,2},{3,11},{11,3},{4,12},{12,4},... | collective-permute-start | bytes 49160 | tf_op jit(solution)/shard_map/ppermute | solution.py:206
  79.4 7.2 %collective-permute-start.9 = (bf16[16,512]{1,0:T(8,128)(2,1)S(1)}, bf16[16,512]{1,0:T(8,128)(2,1)S(1)}, u32[]{:S(2)}, u32[]{:S(2)}) collective-permute-start(bf16[16,512]{1,0:T(8,128)(2,1)S(1)} %fusion.17), channel_id=1, source_target_pairs={{0,0},{248,248},{8,16},{16,8},{24,32},{32,24},{40,48},{48,40},{56,... | collective-permute-start | bytes 49160 | tf_op jit(solution)/shard_map/ppermute | solution.py:205
  86.8 4.2 %collective-permute-start.10 = (bf16[16,512]{1,0:T(8,128)(2,1)S(1)}, bf16[16,512]{1,0:T(8,128)(2,1)S(1)}, u32[]{:S(2)}, u32[]{:S(2)}) collective-permute-start(bf16[16,512]{1,0:T(8,128)(2,1)S(1)} %fusion.16), channel_id=1, source_target_pairs={{0,8},{8,0},{1,9},{9,1},{2,10},{10,2},{3,11},{11,3},{4,12},{12,4},... | collective-permute-start | bytes 49160 | tf_op jit(solution)/shard_map/ppermute | solution.py:206
  87.0 7.2 %collective-permute-start.11 = (bf16[16,512]{1,0:T(8,128)(2,1)S(1)}, bf16[16,512]{1,0:T(8,128)(2,1)S(1)}, u32[]{:S(2)}, u32[]{:S(2)}) collective-permute-start(bf16[16,512]{1,0:T(8,128)(2,1)S(1)} %fusion.16), channel_id=1, source_target_pairs={{0,0},{248,248},{8,16},{16,8},{24,32},{32,24},{40,48},{48,40},{56,... | collective-permute-start | bytes 49160 | tf_op jit(solution)/shard_map/ppermute | solution.py:205
  94.5 4.2 %collective-permute-start.12 = (bf16[16,512]{1,0:T(8,128)(2,1)S(1)}, bf16[16,512]{1,0:T(8,128)(2,1)S(1)}, u32[]{:S(2)}, u32[]{:S(2)}) collective-permute-start(bf16[16,512]{1,0:T(8,128)(2,1)S(1)} %fusion.15), channel_id=1, source_target_pairs={{0,8},{8,0},{1,9},{9,1},{2,10},{10,2},{3,11},{11,3},{4,12},{12,4},... | collective-permute-start | bytes 49160 | tf_op jit(solution)/shard_map/ppermute | solution.py:206
  94.7 7.2 %collective-permute-start.13 = (bf16[16,512]{1,0:T(8,128)(2,1)S(1)}, bf16[16,512]{1,0:T(8,128)(2,1)S(1)}, u32[]{:S(2)}, u32[]{:S(2)}) collective-permute-start(bf16[16,512]{1,0:T(8,128)(2,1)S(1)} %fusion.15), channel_id=1, source_target_pairs={{0,0},{248,248},{8,16},{16,8},{24,32},{32,24},{40,48},{48,40},{56,... | collective-permute-start | bytes 49160 | tf_op jit(solution)/shard_map/ppermute | solution.py:205
  102.1 4.2 %collective-permute-start.14 = (bf16[16,512]{1,0:T(8,128)(2,1)S(1)}, bf16[16,512]{1,0:T(8,128)(2,1)S(1)}, u32[]{:S(2)}, u32[]{:S(2)}) collective-permute-start(bf16[16,512]{1,0:T(8,128)(2,1)S(1)} %fusion.14), channel_id=1, source_target_pairs={{0,8},{8,0},{1,9},{9,1},{2,10},{10,2},{3,11},{11,3},{4,12},{12,4},... | collective-permute-start | bytes 49160 | tf_op jit(solution)/shard_map/ppermute | solution.py:206
  102.4 7.2 %collective-permute-start.15 = (bf16[16,512]{1,0:T(8,128)(2,1)S(1)}, bf16[16,512]{1,0:T(8,128)(2,1)S(1)}, u32[]{:S(2)}, u32[]{:S(2)}) collective-permute-start(bf16[16,512]{1,0:T(8,128)(2,1)S(1)} %fusion.14), channel_id=1, source_target_pairs={{0,0},{248,248},{8,16},{16,8},{24,32},{32,24},{40,48},{48,40},{56,... | collective-permute-start | bytes 49160 | tf_op jit(solution)/shard_map/ppermute | solution.py:205
  109.8 3.9 %collective-permute-start.16 = (f32[16,512]{1,0:T(8,128)S(1)}, f32[16,512]{1,0:T(8,128)S(1)}, u32[]{:S(2)}, u32[]{:S(2)}) collective-permute-start(f32[16,512]{1,0:T(8,128)S(1)} %fusion.13), channel_id=1, source_target_pairs={{0,3},{1,0},{2,1},{3,2},{4,7},{5,4},{6,5},{7,6},{8,11},{9,8},{10,9... | collective-permute-start | bytes 98312 | tf_op jit(solution)/shard_map/ppermute | solution.py:215
  110.0 5.1 %collective-permute-start.17 = (f32[16,512]{1,0:T(8,128)S(1)}, f32[16,512]{1,0:T(8,128)S(1)}, u32[]{:S(2)}, u32[]{:S(2)}) collective-permute-start(f32[16,512]{1,0:T(8,128)S(1)} %fusion.13), channel_id=1, source_target_pairs={{0,1},{1,2},{2,3},{3,0},{4,5},{5,6},{6,7},{7,4},{8,9},{9,10},{10,1... | collective-permute-start | bytes 98312 | tf_op jit(solution)/shard_map/ppermute | solution.py:215
  111.8 5.4 %collective-permute-start.18 = (f32[16,512]{1,0:T(8,128)S(1)}, f32[16,512]{1,0:T(8,128)S(1)}, u32[]{:S(2)}, u32[]{:S(2)}) collective-permute-start(f32[16,512]{1,0:T(8,128)S(1)} %fusion.13), channel_id=1, source_target_pairs={{0,2},{1,3},{2,0},{3,1},{4,6},{5,7},{6,4},{7,5},{8,10},{9,11},{10,... | collective-permute-start | bytes 98312 | tf_op jit(solution)/shard_map/ppermute | solution.py:215
  118.0 0.7 copy-start.2

commit v4 on v3

--- a/solution.py
+++ b/solution.py
@@ -148,6 +148,49 @@
     )(arrived)
 
 
+def last_kernel(
+    where_ref, own_ref, second_ref, first_ref, third_ref, incoming_ref, shifted_ref,
+    out_ref, next_ref, whole_ref, front_ref, out_sem, next_sem
+):
+    row = where_ref[0]
+    rows = own_ref.shape[0]
+    for turn, piece in enumerate((own_ref, first_ref, second_ref, third_ref)):
+        slot = lax.rem(row + 4 - turn, 4)
+        at = pl.ds(pl.multiple_of(slot * rows, rows), rows)
+        whole_ref[at] = piece[...]
+        front_ref[at] = piece[...].astype(front_ref.dtype)
+    whole = pltpu.make_async_copy(whole_ref, out_ref, out_sem)
+    whole.start()
+    front_ref[...] = jnp.where(where_ref[1] == 1, front_ref[...], incoming_ref[...])
+    front = pltpu.make_async_copy(front_ref, next_ref.at[0], next_sem)
+    front.start()
+    whole.wait()
+    front.wait()
+
+
+def finish(where, pieces, incoming, shifted):
+    steps, width = incoming.shape
+    inside, outside = (pl.BlockSpec(memory_space=m) for m in (pltpu.VMEM, pltpu.HBM))
+    return pl.pallas_call(
+        last_kernel,
+        out_shape=(
+            jax.ShapeDtypeStruct((steps, width), jnp.float32),
+            jax.ShapeDtypeStruct(shifted.shape, shifted.dtype),
+        ),
+        in_specs=[pl.BlockSpec(memory_space=pltpu.SMEM)] + [inside] * 5 + [outside],
+        out_specs=(outside, outside),
+        scratch_shapes=[
+            pltpu.VMEM((steps, width), jnp.float32),
+            pltpu.VMEM((steps, width), jnp.bfloat16),
+            pltpu.SemaphoreType.DMA,
+            pltpu.SemaphoreType.DMA,
+        ],
+        input_output_aliases={6: 1},
+        compiler_params=pltpu.CompilerParams(vmem_limit_bytes=4 << 20),
+        name="finish",
+    )(where, *pieces, incoming, shifted)
+
+
 def per_device(
     history, right_factor, left_factor, pair_rank, pair_lag, near_block, self_term, excitation
 ):
@@ -190,9 +233,13 @@
     near_away = jnp.where(core == 0, near_block[0], near_block[2])
     block = lax.axis_index(SPACE)
     near_away = jnp.where((block == 0) | (block == targets - 1), 0.0, near_away)
-    between = [(0, 0), (targets - 1, targets - 1)]
+    partner = {0: 0, targets - 1: targets - 1}
     for t in range(1, targets - 1, 2):
-        between += [(t, t + 1), (t + 1, t)]
+        partner[t], partner[t + 1] = t + 1, t
+    between = []
+    for t, other in partner.items():
+        for y in range(4):
+            between.append((t * 4 + y, other * 4 + (y ^ 1 if other == t else y)))
 
     def product(value, block):
         return lax.dot_general(
@@ -202,7 +249,7 @@
     current = right_side * inverse
     for _ in range(1, SWEEPS):
         rounded = current.astype(jnp.bfloat16)
-        away = lax.ppermute(rounded, SPACE, between)
+        away = lax.ppermute(rounded, SPACE + ("y",), between)
         chip = lax.ppermute(rounded, "c", swap)
         total = product(rounded, near_own)
         total = total + product(chip, near_chip)
@@ -214,17 +261,8 @@
         pieces.append(
             lax.ppermute(current, "y", [(i, (i + step) % 4) for i in range(4)])
         )
-    everywhere = []
-    for slot in range(4):
-        value = pieces[0]
-        for step, piece in zip((2, 1, 3), pieces[1:]):
-            value = jnp.where(row == (slot + step) % 4, piece, value)
-        everywhere.append(value)
-    everywhere = jnp.concatenate(everywhere, axis=0)
-    oldest = (lax.axis_index("zh") == 0) & (row == 0)
-    newest = jnp.where(oldest, everywhere.astype(jnp.bfloat16), incoming)
-    next_history = lax.dynamic_update_slice_in_dim(shifted, newest[None], 0, 0)
-    return (everywhere, next_history)
+    oldest = ((lax.axis_index("zh") == 0) & (row == 0)).astype(jnp.int32)
+    return finish(jnp.stack([row, oldest]), pieces, incoming, shifted)
 
 
 def solution(mesh):

time: 119 us -> 105 us (0.88)
  the two profiles are of different devices: /device:TPU:32 before, /device:TPU:56 now
where the time goes in v4:
time: 105 us; the launch traced here: 104 us
  starting transfers between devices  41.4 us (39%)
  waiting for transfers between devices  40.2 us (38%)
  Pallas kernels  11.5 us (11%)
  matrix products  5.96 us (6%)
  other arithmetic  4.36 us (4%)
    ppermute x7, waiting for transfers between devices, per_device(): away = lax.ppermute(rounded, SPACE + ('y',), between)  21.2 us
    ppermute x7, starting transfers between devices, per_device(): away = lax.ppermute(rounded, SPACE + ('y',), between)  14.3 us
    pallas_call x2, Pallas kernels, far_half(): pl.pallas_call(functools.partial(far_kernel, ranks=ranks), out_shape=jax....  9.45 us
    all_to_all x1, starting transfers between devices, per_device(): arrived = lax.all_to_all(twice, ('zh', 'zl'), 0, 0, tiled=True)  8.57 us
    all_to_all x1, waiting for transfers between devices, per_device(): lax.all_to_all(partial_value.reshape(16, -1, width), ('x', 'y'), 0, 0, ti...  8.29 us
    all_to_all x1, starting transfers between devices, per_device(): lax.all_to_all(partial_value.reshape(16, -1, width), ('x', 'y'), 0, 0, ti...  7.3 us
    all_to_all x1, waiting for transfers between devices, per_device(): arrived = lax.all_to_all(twice, ('zh', 'zl'), 0, 0, tiled=True)  6.85 us
    dot_general x21, matrix products, product(): lax.dot_general(value, block, (((1,), (1,)), ((), ())), preferred_element...  5.96 us
  transfers between devices with their start and end apart: 21, of which 12 were waited for; matrix products, arithmetic and copies ran while one was open for 6% of the time, Pallas kernels for 5%

profile of v4, /device:TPU:56, one launch (start us, length us, event | category | flops | bytes accessed | tf_op | source)
XLA Modules:
  0.0 104.4 jit_solution(18369204364552750800)
XLA Ops:
  0.6 4.7 %far_half.3 = bf16[4,4,4,16,512]{4,3,2,1,0:T(8,128)(2,1)S(1)} custom-call(s32[1]{0:T(128)} %bitcast.7.core_ref, s32[64]{0:T(128)} %bitcast.84, s32[64]{0:T(128)} %bitcast.86, bf16[4,64,512]{2,1,0:T(8,128)(2,1)} %hist_ref.3, bf16[16,2,160,512]{3,2,1,0:T(8,128)(2,1)} %bitcast.80, bf16[16,2,160,512]{3,2,1,0:T(8,128)(2,1)} %bitcast.82), custom_call_target="tpu_custom_call" | custom-call | flops 838860800 | bytes 6291456 | tf_op jit(solution)/shard_map/far_half/pallas_call | solution.py:98
  5.4 0.1 collective-permute-start
  5.5 4.7 %far_half.2 = bf16[4,4,4,16,512]{4,3,2,1,0:T(8,128)(2,1)S(1)} custom-call(s32[1]{0:T(128)} %bitcast.2.core_ref, s32[64]{0:T(128)} %bitcast.85, s32[64]{0:T(128)} %bitcast.87, bf16[4,64,512]{2,1,0:T(8,128)(2,1)} %hist_ref.3, bf16[16,2,160,512]{3,2,1,0:T(8,128)(2,1)} %bitcast.81, bf16[16,2,160,512]{3,2,1,0:T(8,128)(2,1)} %bitcast.83), custom_call_target="tpu_custom_call" | custom-call | flops 838860800 | bytes 6291456 | tf_op jit(solution)/shard_map/far_half/pallas_call | solution.py:98
  10.2 1.5 %add_convert_fusion = bf16[4,4,4,16,512]{4,3,2,1,0:T(8,128)(2,1)} fusion(bf16[4,4,4,16,512]{4,3,2,1,0:T(8,128)(2,1)S(1)} %collective-permute-done, bf16[4,4,4,16,512]{4,3,2,1,0:T(8,128)(2,1)S(1)} %far_half.2), kind=kLoop, calls=%fused_computation | loop fusion | flops 2097152 | bytes 3145728 | tf_op jit(solution)/shard_map/convert_element_type | solution.py:216
  11.7 7.3 %all-to-all-start = ((bf16[16,64,512]{2,1,0:T(8,128)(2,1)}), bf16[16,64,512]{2,1,0:T(8,128)(2,1)S(1)}, u32[]{:S(2)}, u32[]{:S(2)}) async-start(bf16[16,64,512]{2,1,0:T(8,128)(2,1)} %bitcast.8), calls=%async_computation | async-start | bytes 2097152 | tf_op jit(solution)/shard_map/all_to_all | solution.py:217
  19.0 5.9 %collective-permute-start.1 = (bf16[64,512]{1,0:T(8,128)(2,1)S(1)}, bf16[64,512]{1,0:T(8,128)(2,1)S(1)}, u32[]{:S(2)}, u32[]{:S(2)}) collective-permute-start(bf16[64,512]{1,0:T(8,128)(2,1)S(1)} %slice_bitcast_fusion), channel_id=1, source_target_pairs={{0,1},{1,2},{2,3},{3,4},{4,5},{5,6},{6,7},{7,0},{8,9},{9,10},{10,1... | collective-permute-start | bytes 196616 | tf_op jit(solution)/shard_map/ppermute | solution.py:222
  24.9 1.3 %select_select_fusion = (bf16[1,512,512]{2,1,0:T(8,128)(2,1)S(1)}, bf16[1,512,512]{2,1,0:T(8,128)(2,1)S(1)}) fusion(pred[]{:T(512)S(6)} %or.3, pred[]{:T(512)S(6)} %eq.18, bf16[3,512,512]{2,1,0:T(8,128)(2,1)} %param.13), kind=kLoop, calls=%fused_computation.63 | loop fusion | flops 786432 | bytes 2097154 | tf_op jit(solution)/shard_map/jit(_where)/select_n | solution.py:235
  26.2 8.3 %all-to-all-done.in_ref = bf16[16,64,512]{2,1,0:T(8,128)(2,1)S(1)} async-done(((bf16[16,64,512]{2,1,0:T(8,128)(2,1)}), bf16[16,64,512]{2,1,0:T(8,128)(2,1)S(1)}, u32[]{:S(2)}, u32[]{:S(2)}) %all-to-all-start) | async-done | bytes 1048608 | tf_op jit(solution)/shard_map/all_to_all | solution.py:217
  34.5 0.8 plane_sum.1
  35.3 8.6 %all-to-all-start.1 = ((bf16[8,16,512]{2,1,0:T(8,128)(2,1)}), bf16[8,16,512]{2,1,0:T(8,128)(2,1)S(1)}, u32[]{:S(2)}, u32[]{:S(2)}) async-start(bf16[8,16,512]{2,1,0:T(8,128)(2,1)} %bitcast.9), calls=%async_computation.1 | async-start | bytes 262144 | tf_op jit(solution)/shard_map/all_to_all | solution.py:221
  43.9 0.0 collective-permute-done.1.incoming_ref
  43.9 0.7 pad_maximum_fusion.shifted_ref
  44.6 6.8 %all-to-all-done.1 = bf16[8,16,512]{2,1,0:T(8,128)(2,1)S(1)} async-done(((bf16[8,16,512]{2,1,0:T(8,128)(2,1)}), bf16[8,16,512]{2,1,0:T(8,128)(2,1)S(1)}, u32[]{:S(2)}, u32[]{:S(2)}) %all-to-all-start.1) | async-done | bytes 131104 | tf_op jit(solution)/shard_map/all_to_all | solution.py:221
  51.5 0.8 multiply_convert_fusion
  52.3 0.0 collective-permute-start.2
  52.3 1.3 %fusion.46 = f32[16,512]{1,0:T(8,128)S(1)} fusion(bf16[16,512]{1,0:T(8,128)(2,1)S(1)} %get-tuple-element.8, bf16[3,512,512]{2,1,0:T(8,128)(2,1)} %param.13), kind=kOutput, calls=%fused_computation.61 | convolution fusion | flops 8388608 | bytes 573440 | tf_op jit(solution)/shard_map/dot_general | solution.py:245
  53.6 2.0 %collective-permute-start.3 = (bf16[16,512]{1,0:T(8,128)(2,1)S(1)}, bf16[16,512]{1,0:T(8,128)(2,1)S(1)}, u32[]{:S(2)}, u32[]{:S(2)}) collective-permute-start(bf16[16,512]{1,0:T(8,128)(2,1)S(1)} %get-tuple-element.8), channel_id=1, source_target_pairs={{0,1},{1,0},{2,3},{3,2},{248,249},{249,248},{250,251},{251,250},{8... | collective-permute-start | bytes 49160 | tf_op jit(solution)/shard_map/ppermute | solution.py:252
  55.6 0.2 convolution_add_fusion.13
  55.8 3.0 %collective-permute-done.3 = bf16[16,512]{1,0:T(8,128)(2,1)S(1)} collective-permute-done((bf16[16,512]{1,0:T(8,128)(2,1)S(1)}, bf16[16,512]{1,0:T(8,128)(2,1)S(1)}, u32[]{:S(2)}, u32[]{:S(2)}) %collective-permute-start.3) | collective-permute-done | bytes 16416 | tf_op jit(solution)/shard_map/ppermute | solution.py:252
  58.9 0.2 fusion.19
  59.1 0.0 collective-permute-start.4
  59.1 0.2 fusion.44
  59.4 2.0 %collective-permute-start.5 = (bf16[16,512]{1,0:T(8,128)(2,1)S(1)}, bf16[16,512]{1,0:T(8,128)(2,1)S(1)}, u32[]{:S(2)}, u32[]{:S(2)}) collective-permute-start(bf16[16,512]{1,0:T(8,128)(2,1)S(1)} %fusion.19), channel_id=1, source_target_pairs={{0,1},{1,0},{2,3},{3,2},{248,249},{249,248},{250,251},{251,250},{8... | collective-permute-start | bytes 49160 | tf_op jit(solution)/shard_map/ppermute | solution.py:252
  61.4 0.2 convolution_add_fusion.11
  61.6 3.0 %collective-permute-done.5 = bf16[16,512]{1,0:T(8,128)(2,1)S(1)} collective-permute-done((bf16[16,512]{1,0:T(8,128)(2,1)S(1)}, bf16[16,512]{1,0:T(8,128)(2,1)S(1)}, u32[]{:S(2)}, u32[]{:S(2)}) %collective-permute-start.5) | collective-permute-done | bytes 16416 | tf_op jit(solution)/shard_map/ppermute | solution.py:252
  64.7 0.2 fusion.18
  64.9 0.0 collective-permute-start.6
  64.9 0.2 fusion.42
  65.2 2.0 %collective-permute-start.7 = (bf16[16,512]{1,0:T(8,128)(2,1)S(1)}, bf16[16,512]{1,0:T(8,128)(2,1)S(1)}, u32[]{:S(2)}, u32[]{:S(2)}) collective-permute-start(bf16[16,512]{1,0:T(8,128)(2,1)S(1)} %fusion.18), channel_id=1, source_target_pairs={{0,1},{1,0},{2,3},{3,2},{248,249},{249,248},{250,251},{251,250},{8... | collective-permute-start | bytes 49160 | tf_op jit(solution)/shard_map/ppermute | solution.py:252
  67.2 0.2 convolution_add_fusion.9
  67.4 3.0 %collective-permute-done.7 = bf16[16,512]{1,0:T(8,128)(2,1)S(1)} collective-permute-done((bf16[16,512]{1,0:T(8,128)(2,1)S(1)}, bf16[16,512]{1,0:T(8,128)(2,1)S(1)}, u32[]{:S(2)}, u32[]{:S(2)}) %collective-permute-start.7) | collective-permute-done | bytes 16416 | tf_op jit(solution)/shard_map/ppermute | solution.py:252
  70.5 0.2 fusion.17
  70.7 0.0 collective-permute-start.8
  70.7 0.2 fusion.40
  70.9 2.0 %collective-permute-start.9 = (bf16[16,512]{1,0:T(8,128)(2,1)S(1)}, bf16[16,512]{1,0:T(8,128)(2,1)S(1)}, u32[]{:S(2)}, u32[]{:S(2)}) collective-permute-start(bf16[16,512]{1,0:T(8,128)(2,1)S(1)} %fusion.17), channel_id=1, source_target_pairs={{0,1},{1,0},{2,3},{3,2},{248,249},{249,248},{250,251},{251,250},{8... | collective-permute-start | bytes 49160 | tf_op jit(solution)/shard_map/ppermute | solution.py:252
  73.0 0.2 convolution_add_fusion.7
  73.2 3.0 %collective-permute-done.9 = bf16[16,512]{1,0:T(8,128)(2,1)S(1)} collective-permute-done((bf16[16,512]{1,0:T(8,128)(2,1)S(1)}, bf16[16,512]{1,0:T(8,128)(2,1)S(1)}, u32[]{:S(2)}, u32[]{:S(2)}) %collective-permute-start.9) | collective-permute-done | bytes 16416 | tf_op jit(solution)/shard_map/ppermute | solution.py:252
  76.2 0.2 fusion.16
  76.5 0.0 collective-permute-start.10
  76.5 0.2 fusion.38
  76.7 2.2 %collective-permute-start.11 = (bf16[16,512]{1,0:T(8,128)(2,1)S(1)}, bf16[16,512]{1,0:T(8,128)(2,1)S(1)}, u32[]{:S(2)}, u32[]{:S(2)}) collective-permute-start(bf16[16,512]{1,0:T(8,128)(2,1)S(1)} %fusion.16), channel_id=1, source_target_pairs={{0,1},{1,0},{2,3},{3,2},{248,249},{249,248},{250,251},{251,250},{8... | collective-permute-start | bytes 49160 | tf_op jit(solution)/shard_map/ppermute | solution.py:252
  78.9 0.2 convolution_add_fusion.5
  79.1 3.0 %collective-permute-done.11 = bf16[16,512]{1,0:T(8,128)(2,1)S(1)} collective-permute-done((bf16[16,512]{1,0:T(8,128)(2,1)S(1)}, bf16[16,512]{1,0:T(8,128)(2,1)S(1)}, u32[]{:S(2)}, u32[]{:S(2)}) %collective-permute-start.11) | collective-permute-done | bytes 16416 | tf_op jit(solution)/shard_map/ppermute | solution.py:252
  82.2 0.2 fusion.15
  82.4 0.0 collective-permute-start.12
  82.4 0.2 fusion.36
  82.7 2.0 %collective-permute-start.13 = (bf16[16,512]{1,0:T(8,128)(2,1)S(1)}, bf16[16,512]{1,0:T(8,128)(2,1)S(1)}, u32[]{:S(2)}, u32[]{:S(2)}) collective-permute-start(bf16[16,512]{1,0:T(8,128)(2,1)S(1)} %fusion.15), channel_id=1, source_target_pairs={{0,1},{1,0},{2,3},{3,2},{248,249},{249,248},{250,251},{251,250},{8... | collective-permute-start | bytes 49160 | tf_op jit(solution)/shard_map/ppermute | solution.py:252
  84.7 0.2 convolution_add_fusion.3
  84.9 3.0 %collective-permute-done.13 = bf16[16,512]{1,0:T(8,128)(2,1)S(1)} collective-permute-done((bf16[16,512]{1,0:T(8,128)(2,1)S(1)}, bf16[16,512]{1,0:T(8,128)(2,1)S(1)}, u32[]{:S(2)}, u32[]{:S(2)}) %collective-permute-start.13) | collective-permute-done | bytes 16416 | tf_op jit(solution)/shard_map/ppermute | solution.py:252
  88.0 0.2 fusion.14
  88.2 0.0 collective-permute-start.14
  88.2 0.2 fusion.34
  88.5 2.0 %collective-permute-start.15 = (bf16[16,512]{1,0:T(8,128)(2,1)S(1)}, bf16[16,512]{1,0:T(8,128)(2,1)S(1)}, u32[]{:S(2)}, u32[]{:S(2)}) collective-permute-start(bf16[16,512]{1,0:T(8,128)(2,1)S(1)} %fusion.14), channel_id=1, source_target_pairs={{0,1},{1,0},{2,3},{3,2},{248,249},{249,248},{250,251},{251,250},{8... | collective-permute-start | bytes 49160 | tf_op jit(solution)/shard_map/ppermute | solution.py:252
  90.5 0.2 convolution_add_fusion.1
  90.7 3.0 %collective-permute-done.15 = bf16[16,512]{1,0:T(8,128)(2,1)S(1)} collective-permute-done((bf16[16,512]{1,0:T(8,128)(2,1)S(1)}, bf16[16,512]{1,0:T(8,128)(2,1)S(1)}, u32[]{:S(2)}, u32[]{:S(2)}) %collective-permute-start.15) | collective-permute-done | bytes 16416 | tf_op jit(solution)/shard_map/ppermute | solution.py:252
  93.8 0.2 fusion.13.own_ref
  94.0 3.1 %collective-permute-start.16 = (f32[16,512]{1,0:T(8,128)S(1)}, f32[16,512]{1,0:T(8,128)S(1)}, u32[]{:S(2)}, u32[]{:S(2)}) collective-permute-start(f32[16,512]{1,0:T(8,128)S(1)} %fusion.13.own_ref), channel_id=1, source_target_pairs={{0,2},{1,3},{2,0},{3,1},{4,6},{5,7},{6,4},{7,5},{8,10},{9,11},{10,... | collective-permute-start | bytes 98312 | tf_op jit(solution)/shard_map/ppermute | solution.py:262
  97.0 0.8 collective-permute-start.17
  97.9 1.2 %collective-permute-start.18 = (f32[16,512]{1,0:T(8,128)S(1)}, f32[16,512]{1,0:T(8,128)S(1)}, u32[]{:S(2)}, u32[]{:S(2)}) collective-permute-start(f32[16,512]{1,0:T(8,128)S(1)} %fusion.13.own_ref), channel_id=1, source_target_pairs={{0,3},{1,0},{2,1},{3,2},{4,7},{5,4},{6,5},{7,6},{8,11},{9,8},{10,9... | collective-permute-start | bytes 98312 | tf_op jit(solution)/shard_map/ppermute | solution.py:262
  99.1 0.1 pad_add_fusion.where_ref
  99.2 0.3 collective-permute-done.16.second_ref
  99.4 1.5 %collective-permute-done.17.first_ref = f32[16,512]{1,0:T(8,128)S(1)} collective-permute-done((f32[16,512]{1,0:T(8,128)S(1)}, f32[16,512]{1,0:T(8,128)S(1)}, u32[]{:S(2)}, u32[]{:S(2)}) %collective-permute-start.17) | collective-permute-done | bytes 32800 | tf_op jit(solution)/shard_map/ppermute | solution.py:262
  101.0 2.0 %collective-permute-done.18.third_ref = f32[16,512]{1,0:T(8,128)S(1)} collective-permute-done((f32[16,512]{1,0:T(8,128)S(1)}, f32[16,512]{1,0:T(8,128)S(1)}, u32[]{:S(2)}, u32[]{:S(2)}) %collective-permute-start.18) | collective-permute-done | bytes 32800 | tf_op jit(solution)/shard_map/ppermute | solution.py:262
  103.0 1.2 %finish.1 = (f32[64,512]{1,0:T(8,128)}, bf16[4,64,512]{2,1,0:T(8,128)(2,1)}) custom-call(s32[2]{0:T(128)S(1)} %pad_add_fusion.where_ref, f32[16,512]{1,0:T(8,128)S(1)} %fusion.13.own_ref, f32[16,512]{1,0:T(8,128)S(1)} %collective-permute-done.16.second_ref, f32[16,512]{1,0:T(8,128)S(1)} %collective-permute-done.17.first_ref, ...), custom_call_target="tpu_custom_call", output_to_operand_aliasing={{1}: (6, {})} | custom-call | tf_op jit(solution)/shard_map/finish/pallas_call | solution.py:174
  (19 shorter events, 0.1 us)
Async XLA Ops:
  5.4 4.8 %collective-permute-start = (bf16[4,4,4,16,512]{4,3,2,1,0:T(8,128)(2,1)S(1)}, bf16[4,4,4,16,512]{4,3,2,1,0:T(8,128)(2,1)S(1)}, u32[]{:S(2)}, u32[]{:S(2)}) collective-permute-start(bf16[4,4,4,16,512]{4,3,2,1,0:T(8,128)(2,1)S(1)} %far_half.3), channel_id=1, source_target_pairs={{0,8},{8,0},{1,9},{9,1},{2,10},{10,2},{3,11},{11,3},{4,12},{12,4},... | collective-permute-start | bytes 3145736 | tf_op jit(solution)/shard_map/ppermute | solution.py:214
  11.7 7.3 %copy-start.1 = (bf16[4,64,512]{2,1,0:T(8,128)(2,1)S(1)}, bf16[4,64,512]{2,1,0:T(8,128)(2,1)}, u32[]{:S(2)}) copy-start(bf16[4,64,512]{2,1,0:T(8,128)(2,1)} %hist_ref.3) | copy-start | bytes 786436
  11.7 22.8 %all-to-all-start = ((bf16[16,64,512]{2,1,0:T(8,128)(2,1)}), bf16[16,64,512]{2,1,0:T(8,128)(2,1)S(1)}, u32[]{:S(2)}, u32[]{:S(2)}) async-start(bf16[16,64,512]{2,1,0:T(8,128)(2,1)} %bitcast.8), calls=%async_computation | async-start | bytes 2097152 | tf_op jit(solution)/shard_map/all_to_all | solution.py:217
  19.0 24.9 %collective-permute-start.1 = (bf16[64,512]{1,0:T(8,128)(2,1)S(1)}, bf16[64,512]{1,0:T(8,128)(2,1)S(1)}, u32[]{:S(2)}, u32[]{:S(2)}) collective-permute-start(bf16[64,512]{1,0:T(8,128)(2,1)S(1)} %slice_bitcast_fusion), channel_id=1, source_target_pairs={{0,1},{1,2},{2,3},{3,4},{4,5},{5,6},{6,7},{7,0},{8,9},{9,10},{10,1... | collective-permute-start | bytes 196616 | tf_op jit(solution)/shard_map/ppermute | solution.py:222
  24.9 19.0 %copy-start.2 = (f32[512]{0:T(512)S(1)}, f32[512]{0:T(512)}, u32[]{:S(2)}) copy-start(f32[512]{0:T(512)} %param.14) | copy-start | bytes 6148
  24.9 19.0 %slice-start = ((bf16[4,64,512]{2,1,0:T(8,128)(2,1)}), bf16[3,64,512]{2,1,0:T(8,128)(2,1)S(1)}, s32[]{:S(2)}) async-start(bf16[4,64,512]{2,1,0:T(8,128)(2,1)} %hist_ref.3), calls=%async_computation.2 | async-start | bytes 393216 | tf_op jit(solution)/shard_map/slice | solution.py:223
  35.3 16.2 %all-to-all-start.1 = ((bf16[8,16,512]{2,1,0:T(8,128)(2,1)}), bf16[8,16,512]{2,1,0:T(8,128)(2,1)S(1)}, u32[]{:S(2)}, u32[]{:S(2)}) async-start(bf16[8,16,512]{2,1,0:T(8,128)(2,1)} %bitcast.9), calls=%async_computation.1 | async-start | bytes 262144 | tf_op jit(solution)/shard_map/all_to_all | solution.py:221
  43.9 15.3 %copy-start = (bf16[3,512,512]{2,1,0:T(8,128)(2,1)S(1)}, bf16[3,512,512]{2,1,0:T(8,128)(2,1)}, u32[]{:S(2)}) copy-start(bf16[3,512,512]{2,1,0:T(8,128)(2,1)} %param.13) | copy-start | bytes 4718596
  52.3 3.3 %collective-permute-start.2 = (bf16[16,512]{1,0:T(8,128)(2,1)S(1)}, bf16[16,512]{1,0:T(8,128)(2,1)S(1)}, u32[]{:S(2)}, u32[]{:S(2)}) collective-permute-start(bf16[16,512]{1,0:T(8,128)(2,1)S(1)} %get-tuple-element.8), channel_id=1, source_target_pairs={{0,8},{8,0},{1,9},{9,1},{2,10},{10,2},{3,11},{11,3},{4,12},{12,4},... | collective-permute-start | bytes 49160 | tf_op jit(solution)/shard_map/ppermute | solution.py:253
  53.6 5.3 %collective-permute-start.3 = (bf16[16,512]{1,0:T(8,128)(2,1)S(1)}, bf16[16,512]{1,0:T(8,128)(2,1)S(1)}, u32[]{:S(2)}, u32[]{:S(2)}) collective-permute-start(bf16[16,512]{1,0:T(8,128)(2,1)S(1)} %get-tuple-element.8), channel_id=1, source_target_pairs={{0,1},{1,0},{2,3},{3,2},{248,249},{249,248},{250,251},{251,250},{8... | collective-permute-start | bytes 49160 | tf_op jit(solution)/shard_map/ppermute | solution.py:252
  59.1 2.3 %collective-permute-start.4 = (bf16[16,512]{1,0:T(8,128)(2,1)S(1)}, bf16[16,512]{1,0:T(8,128)(2,1)S(1)}, u32[]{:S(2)}, u32[]{:S(2)}) collective-permute-start(bf16[16,512]{1,0:T(8,128)(2,1)S(1)} %fusion.19), channel_id=1, source_target_pairs={{0,8},{8,0},{1,9},{9,1},{2,10},{10,2},{3,11},{11,3},{4,12},{12,4},... | collective-permute-start | bytes 49160 | tf_op jit(solution)/shard_map/ppermute | solution.py:253
  59.4 5.3 %collective-permute-start.5 = (bf16[16,512]{1,0:T(8,128)(2,1)S(1)}, bf16[16,512]{1,0:T(8,128)(2,1)S(1)}, u32[]{:S(2)}, u32[]{:S(2)}) collective-permute-start(bf16[16,512]{1,0:T(8,128)(2,1)S(1)} %fusion.19), channel_id=1, source_target_pairs={{0,1},{1,0},{2,3},{3,2},{248,249},{249,248},{250,251},{251,250},{8... | collective-permute-start | bytes 49160 | tf_op jit(solution)/shard_map/ppermute | solution.py:252
  64.9 2.3 %collective-permute-start.6 = (bf16[16,512]{1,0:T(8,128)(2,1)S(1)}, bf16[16,512]{1,0:T(8,128)(2,1)S(1)}, u32[]{:S(2)}, u32[]{:S(2)}) collective-permute-start(bf16[16,512]{1,0:T(8,128)(2,1)S(1)} %fusion.18), channel_id=1, source_target_pairs={{0,8},{8,0},{1,9},{9,1},{2,10},{10,2},{3,11},{11,3},{4,12},{12,4},... | collective-permute-start | bytes 49160 | tf_op jit(solution)/shard_map/ppermute | solution.py:253
  65.2 5.3 %collective-permute-start.7 = (bf16[16,512]{1,0:T(8,128)(2,1)S(1)}, bf16[16,512]{1,0:T(8,128)(2,1)S(1)}, u32[]{:S(2)}, u32[]{:S(2)}) collective-permute-start(bf16[16,512]{1,0:T(8,128)(2,1)S(1)} %fusion.18), channel_id=1, source_target_pairs={{0,1},{1,0},{2,3},{3,2},{248,249},{249,248},{250,251},{251,250},{8... | collective-permute-start | bytes 49160 | tf_op jit(solution)/shard_map/ppermute | solution.py:252
  70.7 2.3 %collective-permute-start.8 = (bf16[16,512]{1,0:T(8,128)(2,1)S(1)}, bf16[16,512]{1,0:T(8,128)(2,1)S(1)}, u32[]{:S(2)}, u32[]{:S(2)}) collective-permute-start(bf16[16,512]{1,0:T(8,128)(2,1)S(1)} %fusion.17), channel_id=1, source_target_pairs={{0,8},{8,0},{1,9},{9,1},{2,10},{10,2},{3,11},{11,3},{4,12},{12,4},... | collective-permute-start | bytes 49160 | tf_op jit(solution)/shard_map/ppermute | solution.py:253
  70.9 5.3 %collective-permute-start.9 = (bf16[16,512]{1,0:T(8,128)(2,1)S(1)}, bf16[16,512]{1,0:T(8,128)(2,1)S(1)}, u32[]{:S(2)}, u32[]{:S(2)}) collective-permute-start(bf16[16,512]{1,0:T(8,128)(2,1)S(1)} %fusion.17), channel_id=1, source_target_pairs={{0,1},{1,0},{2,3},{3,2},{248,249},{249,248},{250,251},{251,250},{8... | collective-permute-start | bytes 49160 | tf_op jit(solution)/shard_map/ppermute | solution.py:252
  76.5 2.4 %collective-permute-start.10 = (bf16[16,512]{1,0:T(8,128)(2,1)S(1)}, bf16[16,512]{1,0:T(8,128)(2,1)S(1)}, u32[]{:S(2)}, u32[]{:S(2)}) collective-permute-start(bf16[16,512]{1,0:T(8,128)(2,1)S(1)} %fusion.16), channel_id=1, source_target_pairs={{0,8},{8,0},{1,9},{9,1},{2,10},{10,2},{3,11},{11,3},{4,12},{12,4},... | collective-permute-start | bytes 49160 | tf_op jit(solution)/shard_map/ppermute | solution.py:253
  76.7 5.4 %collective-permute-start.11 = (bf16[16,512]{1,0:T(8,128)(2,1)S(1)}, bf16[16,512]{1,0:T(8,128)(2,1)S(1)}, u32[]{:S(2)}, u32[]{:S(2)}) collective-permute-start(bf16[16,512]{1,0:T(8,128)(2,1)S(1)} %fusion.16), channel_id=1, source_target_pairs={{0,1},{1,0},{2,3},{3,2},{248,249},{249,248},{250,251},{251,250},{8... | collective-permute-start | bytes 49160 | tf_op jit(solution)/shard_map/ppermute | solution.py:252
  82.4 2.3 %collective-permute-start.12 = (bf16[16,512]{1,0:T(8,128)(2,1)S(1)}, bf16[16,512]{1,0:T(8,128)(2,1)S(1)}, u32[]{:S(2)}, u32[]{:S(2)}) collective-permute-start(bf16[16,512]{1,0:T(8,128)(2,1)S(1)} %fusion.15), channel_id=1, source_target_pairs={{0,8},{8,0},{1,9},{9,1},{2,10},{10,2},{3,11},{11,3},{4,12},{12,4},... | collective-permute-start | bytes 49160 | tf_op jit(solution)/shard_map/ppermute | solution.py:253
  82.7 5.3 %collective-permute-start.13 = (bf16[16,512]{1,0:T(8,128)(2,1)S(1)}, bf16[16,512]{1,0:T(8,128)(2,1)S(1)}, u32[]{:S(2)}, u32[]{:S(2)}) collective-permute-start(bf16[16,512]{1,0:T(8,128)(2,1)S(1)} %fusion.15), channel_id=1, source_target_pairs={{0,1},{1,0},{2,3},{3,2},{248,249},{249,248},{250,251},{251,250},{8... | collective-permute-start | bytes 49160 | tf_op jit(solution)/shard_map/ppermute | solution.py:252
  88.2 2.3 %collective-permute-start.14 = (bf16[16,512]{1,0:T(8,128)(2,1)S(1)}, bf16[16,512]{1,0:T(8,128)(2,1)S(1)}, u32[]{:S(2)}, u32[]{:S(2)}) collective-permute-start(bf16[16,512]{1,0:T(8,128)(2,1)S(1)} %fusion.14), channel_id=1, source_target_pairs={{0,8},{8,0},{1,9},{9,1},{2,10},{10,2},{3,11},{11,3},{4,12},{12,4},... | collective-permute-start | bytes 49160 | tf_op jit(solution)/shard_map/ppermute | solution.py:253
  88.5 5.3 %collective-permute-start.15 = (bf16[16,512]{1,0:T(8,128)(2,1)S(1)}, bf16[16,512]{1,0:T(8,128)(2,1)S(1)}, u32[]{:S(2)}, u32[]{:S(2)}) collective-permute-start(bf16[16,512]{1,0:T(8,128)(2,1)S(1)} %fusion.14), channel_id=1, source_target_pairs={{0,1},{1,0},{2,3},{3,2},{248,249},{249,248},{250,251},{251,250},{8... | collective-permute-start | bytes 49160 | tf_op jit(solution)/shard_map/ppermute | solution.py:252
  94.0 5.4 %collective-permute-start.16 = (f32[16,512]{1,0:T(8,128)S(1)}, f32[16,512]{1,0:T(8,128)S(1)}, u32[]{:S(2)}, u32[]{:S(2)}) collective-permute-start(f32[16,512]{1,0:T(8,128)S(1)} %fusion.13.own_ref), channel_id=1, source_target_pairs={{0,2},{1,3},{2,0},{3,1},{4,6},{5,7},{6,4},{7,5},{8,10},{9,11},{10,... | collective-permute-start | bytes 98312 | tf_op jit(solution)/shard_map/ppermute | solution.py:262
  97.0 3.9 %collective-permute-start.17 = (f32[16,512]{1,0:T(8,128)S(1)}, f32[16,512]{1,0:T(8,128)S(1)}, u32[]{:S(2)}, u32[]{:S(2)}) collective-permute-start(f32[16,512]{1,0:T(8,128)S(1)} %fusion.13.own_ref), channel_id=1, source_target_pairs={{0,1},{1,2},{2,3},{3,0},{4,5},{5,6},{6,7},{7,4},{8,9},{9,10},{10,1... | collective-permute-start | bytes 98312 | tf_op jit(solution)/shard_map/ppermute | solution.py:262
  97.9 5.1 %collective-permute-start.18 = (f32[16,512]{1,0:T(8,128)S(1)}, f32[16,512]{1,0:T(8,128)S(1)}, u32[]{:S(2)}, u32[]{:S(2)}) collective-permute-start(f32[16,512]{1,0:T(8,128)S(1)} %fusion.13.own_ref), channel_id=1, source_target_pairs={{0,3},{1,0},{2,1},{3,2},{4,7},{5,4},{6,5},{7,6},{8,11},{9,8},{10,9... | collective-permute-start | bytes 98312 | tf_op jit(solution)/shard_map/ppermute | solution.py:262

commit v5 on v4

--- a/solution.py
+++ b/solution.py
@@ -191,6 +191,66 @@
     )(where, *pieces, incoming, shifted)
 
 
+def times(value, block_ref):
+    return lax.dot_general(
+        value, block_ref, (((1,), (1,)), ((), ())), preferred_element_type=jnp.float32
+    )
+
+
+def begin_kernel(c_ref, c_u_ref, inv_ref, own_ref, chip_ref, pack_ref, p_ref):
+    value = c_ref[...].astype(jnp.bfloat16)
+    beside = c_u_ref[...].astype(jnp.bfloat16)
+    part = c_ref[...] - inv_ref[...] * (times(value, own_ref[...]) + times(beside, chip_ref[...]))
+    pack_ref[0] = value
+    pack_ref[1] = part.astype(jnp.bfloat16)
+    p_ref[...] = part
+
+
+def first_kernel(pack_ref, p_ref, got_ref, inv_ref, away_ref, back_ref, next_ref):
+    mine = p_ref[...] - inv_ref[...] * times(got_ref[0], away_ref[...])
+    other = got_ref[1].astype(jnp.float32) - times(pack_ref[0], back_ref[...])
+    next_ref[0] = mine.astype(jnp.bfloat16)
+    next_ref[1] = other.astype(jnp.bfloat16)
+
+
+def second_kernel(
+    next_ref, got_ref, c_ref, c_u_ref, inv_ref, inv_u_ref, own_ref, chip_ref, away_ref,
+    own_u_ref, chip_u_ref, away_u_ref, pack_ref, p_ref
+):
+    mine, mine_away, other, other_away = next_ref[0], next_ref[1], got_ref[0], got_ref[1]
+    total = times(mine, own_ref[...]) + times(other, chip_ref[...]) + times(mine_away, away_ref[...])
+    total_u = (
+        times(other, own_u_ref[...]) + times(mine, chip_u_ref[...]) + times(other_away, away_u_ref[...])
+    )
+    value = (c_ref[...] - inv_ref[...] * total).astype(jnp.bfloat16)
+    beside = (c_u_ref[...] - inv_u_ref[...] * total_u).astype(jnp.bfloat16)
+    part = c_ref[...] - inv_ref[...] * (times(value, own_ref[...]) + times(beside, chip_ref[...]))
+    pack_ref[0] = value
+    pack_ref[1] = part.astype(jnp.bfloat16)
+    p_ref[...] = part
+
+
+def end_kernel(p_ref, got_ref, inv_ref, away_ref, out_ref):
+    out_ref[...] = p_ref[...] - inv_ref[...] * times(got_ref[0], away_ref[...])
+
+
+def small_call(kernel, products, outs, *operands):
+    inside = pl.BlockSpec(memory_space=pltpu.VMEM)
+    rows, width = outs[0].shape[-2:]
+    return pl.pallas_call(
+        kernel,
+        out_shape=outs,
+        in_specs=[inside] * len(operands),
+        out_specs=[inside] * len(outs),
+        compiler_params=pltpu.CompilerParams(vmem_limit_bytes=8 << 20),
+        cost_estimate=pl.CostEstimate(
+            flops=2 * products * rows * width * width,
+            bytes_accessed=2 * products * width * width,
+            transcendentals=0,
+        ),
+    )(*operands)
+
+
 def per_device(
     history, right_factor, left_factor, pair_rank, pair_lag, near_block, self_term, excitation
 ):
@@ -214,25 +274,29 @@
     came = lax.ppermute(away, "c", swap)
     mine = half(core)
     partial_value = (mine.astype(jnp.float32) + came.astype(jnp.float32)).astype(jnp.bfloat16)
-    arrived = lax.all_to_all(
-        partial_value.reshape(16, -1, width), ("x", "y"), 0, 0, tiled=True
-    )
-    twice = plane_sum(arrived, 2).reshape(8, -1, width)
-    arrived = lax.all_to_all(twice, ("zh", "zl"), 0, 0, tiled=True)
+    arrived = lax.all_to_all(partial_value.reshape(16, -1, width), ("x", "y"), 0, 0, tiled=True)
     incoming = lax.ppermute(history[-1], HIST, [(i, (i + 1) % 8) for i in range(8)])
+    near_u = lax.ppermute(near_block, "c", swap)
+    self_u = lax.ppermute(self_term[None, :], "c", swap)
+
+    block = lax.axis_index(SPACE)
+    inverse, inverse_u = 1.0 / self_term[None, :], 1.0 / self_u
+
+    def sides(blocks, even, at):
+        chip = jnp.where(even, blocks[2], blocks[0])
+        away = jnp.where(even, blocks[0], blocks[2])
+        away = jnp.where((at == 0) | (at == targets - 1), 0.0, away)
+        return chip, away
+
+    near_own = near_block[1]
+    near_chip, near_away = sides(near_block, core == 0, block)
+    toward = (inverse.reshape(width, 1) * near_away).astype(jnp.bfloat16)
+    arrived, incoming, near_u, self_u, near_chip, near_away, toward = lax.optimization_barrier(
+        (arrived, incoming, near_u, self_u, near_chip, near_away, toward)
+    )
+    inverse_u = 1.0 / self_u
+    chip_u, away_u = sides(near_u, core == 1, block + 1 - 2 * core)
     shifted = jnp.concatenate([incoming[None], history[:-1]], axis=0)
-    arrived, incoming, shifted = lax.optimization_barrier((arrived, incoming, shifted))
-    far_field = jnp.sum(arrived.astype(jnp.float32), axis=0)
-    rows = time_steps // 4
-    row = lax.axis_index("y")
-    right_side = lax.dynamic_slice_in_dim(excitation, row * rows, rows, 0) - far_field
-
-    inverse = 1.0 / self_term[None, :]
-    near_own = near_block[1]
-    near_chip = jnp.where(core == 0, near_block[2], near_block[0])
-    near_away = jnp.where(core == 0, near_block[0], near_block[2])
-    block = lax.axis_index(SPACE)
-    near_away = jnp.where((block == 0) | (block == targets - 1), 0.0, near_away)
     partner = {0: 0, targets - 1: targets - 1}
     for t in range(1, targets - 1, 2):
         partner[t], partner[t + 1] = t + 1, t
@@ -241,20 +305,37 @@
         for y in range(4):
             between.append((t * 4 + y, other * 4 + (y ^ 1 if other == t else y)))
 
-    def product(value, block):
-        return lax.dot_general(
-            value, block, (((1,), (1,)), ((), ())), preferred_element_type=jnp.float32
+    def off_chip(value):
+        return lax.ppermute(value, SPACE + ("y",), between)
+
+    twice = plane_sum(arrived, 2).reshape(8, -1, width)
+    arrived = lax.all_to_all(twice, ("zh", "zl"), 0, 0, tiled=True)
+    back = off_chip(toward)
+    back = jnp.where((block == 0) | (block == targets - 1), 0.0, back)
+    arrived, incoming, shifted, chip_u, away_u = lax.optimization_barrier(
+        (arrived, incoming, shifted, chip_u, away_u)
+    )
+    far_field = jnp.sum(arrived.astype(jnp.float32), axis=0)
+    rows = time_steps // 4
+    row = lax.axis_index("y")
+    right_side = lax.dynamic_slice_in_dim(excitation, row * rows, rows, 0) - far_field
+
+    c = right_side * inverse
+    c_u = lax.ppermute(c, "c", swap)
+    packed = jax.ShapeDtypeStruct((2, rows, width), jnp.bfloat16)
+    single = jax.ShapeDtypeStruct((rows, width), jnp.float32)
+    pack, part = small_call(begin_kernel, 2, (packed, single), c, c_u, inverse, near_own, near_chip)
+    for _ in range((SWEEPS - 1) // 2):
+        got = off_chip(pack)
+        (both,) = small_call(first_kernel, 2, (packed,), pack, part, got, inverse, near_away, back)
+        over = lax.ppermute(both, "c", swap)
+        pack, part = small_call(
+            second_kernel, 8, (packed, single),
+            both, over, c, c_u, inverse, inverse_u, near_own, near_chip, near_away,
+            near_u[1], chip_u, away_u,
         )
-
-    current = right_side * inverse
-    for _ in range(1, SWEEPS):
-        rounded = current.astype(jnp.bfloat16)
-        away = lax.ppermute(rounded, SPACE + ("y",), between)
-        chip = lax.ppermute(rounded, "c", swap)
-        total = product(rounded, near_own)
-        total = total + product(chip, near_chip)
-        total = total + product(away, near_away)
-        current = (right_side - total) * inverse
+    got = off_chip(pack)
+    (current,) = small_call(end_kernel, 1, (single,), part, got, inverse, near_away)
 
     pieces = [current]
     for step in (2, 1, 3):

time: 105 us -> 96.7 us (0.921)
  the two profiles are of different devices: /device:TPU:56 before, /device:TPU:32 now
where the time goes in v5:
time: 96.7 us; the launch traced here: 96.3 us
  waiting for transfers between devices  40.8 us (42%)
  starting transfers between devices  28.3 us (29%)
  Pallas kernels  16.9 us (17%)
  other arithmetic  9.25 us (10%)
  between operations  0.97 us (1%)
    ppermute x5, waiting for transfers between devices, off_chip(): return lax.ppermute(value, SPACE + ('y',), between)  13.7 us
    pallas_call x2, Pallas kernels, far_half(): pl.pallas_call(functools.partial(far_kernel, ranks=ranks), out_shape=jax....  9.44 us
    all_to_all x1, starting transfers between devices, per_device(): arrived = lax.all_to_all(twice, ('zh', 'zl'), 0, 0, tiled=True)  8.57 us
    ppermute x5, starting transfers between devices, off_chip(): return lax.ppermute(value, SPACE + ('y',), between)  7.07 us
    all_to_all x1, starting transfers between devices, per_device(): lax.all_to_all(partial_value.reshape(16, -1, width), ('x', 'y'), 0, 0, ti...  7.04 us
    ppermute x1, waiting for transfers between devices, per_device(): lax.ppermute(history[-1], HIST, [(i, (i + 1) % 8) for i in range(8)])  6.53 us
    all_to_all x1, waiting for transfers between devices, per_device(): lax.all_to_all(partial_value.reshape(16, -1, width), ('x', 'y'), 0, 0, ti...  5.71 us
    pallas_call x8, Pallas kernels, small_call(): pl.pallas_call(kernel, out_shape=outs, in_specs=[inside] * len(operands),...  5.42 us
  transfers between devices with their start and end apart: 18, of which 14 were waited for; matrix products, arithmetic and copies ran while one was open for 10% of the time, Pallas kernels for 5%

profile of v5, /device:TPU:32, one launch (start us, length us, event | category | flops | bytes accessed | tf_op | source)
XLA Modules:
  0.0 96.3 jit_solution(13451317809564278884)
XLA Ops:
  0.6 4.7 %far_half.3 = bf16[4,4,4,16,512]{4,3,2,1,0:T(8,128)(2,1)S(1)} custom-call(s32[1]{0:T(128)} %bitcast.7.core_ref, s32[64]{0:T(128)} %bitcast.41, s32[64]{0:T(128)} %bitcast.43, bf16[4,64,512]{2,1,0:T(8,128)(2,1)} %hist_ref.3, bf16[16,2,160,512]{3,2,1,0:T(8,128)(2,1)} %bitcast.37, bf16[16,2,160,512]{3,2,1,0:T(8,128)(2,1)} %bitcast.39), custom_call_target="tpu_custom_call" | custom-call | flops 838860800 | bytes 6291456 | tf_op jit(solution)/shard_map/far_half/pallas_call | solution.py:98
  5.4 0.1 collective-permute-start
  5.5 0.5 collective-permute-start.2
  6.0 4.7 %far_half.2 = bf16[4,4,4,16,512]{4,3,2,1,0:T(8,128)(2,1)S(1)} custom-call(s32[1]{0:T(128)} %bitcast.2.core_ref, s32[64]{0:T(128)} %bitcast.42, s32[64]{0:T(128)} %bitcast.44, bf16[4,64,512]{2,1,0:T(8,128)(2,1)} %hist_ref.3, bf16[16,2,160,512]{3,2,1,0:T(8,128)(2,1)} %bitcast.38, bf16[16,2,160,512]{3,2,1,0:T(8,128)(2,1)} %bitcast.40), custom_call_target="tpu_custom_call" | custom-call | flops 838860800 | bytes 6291456 | tf_op jit(solution)/shard_map/far_half/pallas_call | solution.py:98
  10.7 0.0 copy-start.1
  10.7 0.0 copy-start
  10.7 0.0 collective-permute-done
  10.7 1.4 %add_convert_fusion = bf16[4,4,4,16,512]{4,3,2,1,0:T(8,128)(2,1)} fusion(bf16[4,4,4,16,512]{4,3,2,1,0:T(8,128)(2,1)S(1)} %collective-permute-done, bf16[4,4,4,16,512]{4,3,2,1,0:T(8,128)(2,1)S(1)} %far_half.2), kind=kLoop, calls=%fused_computation | loop fusion | flops 2097152 | bytes 3145728 | tf_op jit(solution)/shard_map/convert_element_type | solution.py:276
  12.1 7.0 %all-to-all-start = ((bf16[16,64,512]{2,1,0:T(8,128)(2,1)}), bf16[16,64,512]{2,1,0:T(8,128)(2,1)S(1)}, u32[]{:S(2)}, u32[]{:S(2)}) async-start(bf16[16,64,512]{2,1,0:T(8,128)(2,1)} %bitcast.8), calls=%async_computation | async-start | bytes 2097152 | tf_op jit(solution)/shard_map/all_to_all | solution.py:277
  19.2 0.0 copy-done.1
  19.2 0.1 collective-permute-start.3
  19.3 0.0 copy-done
  19.3 2.0 %collective-permute-start.1 = (bf16[64,512]{1,0:T(8,128)(2,1)S(1)}, bf16[64,512]{1,0:T(8,128)(2,1)S(1)}, u32[]{:S(2)}, u32[]{:S(2)}) collective-permute-start(bf16[64,512]{1,0:T(8,128)(2,1)S(1)} %slice_bitcast_fusion.2), channel_id=1, source_target_pairs={{0,1},{1,2},{2,3},{3,4},{4,5},{5,6},{6,7},{7,0},{8,9},{9,10},{10,1... | collective-permute-start | bytes 196616 | tf_op jit(solution)/shard_map/ppermute | solution.py:278
  21.3 2.2 %multiply_convert_fusion = (bf16[512,512]{1,0:T(8,128)(2,1)}, bf16[512,512]{1,0:T(8,128)(2,1)S(1)}) fusion(f32[512]{0:T(512)S(1)} %broadcast_divide_fusion.1, bf16[3,512,512]{2,1,0:T(8,128)(2,1)} %param.13, pred[]{:T(512)S(6)} %eq.28, pred[]{:T(512)S(6)} %or.7), kind=kLoop, calls=%fused_computation.1 | loop fusion | flops 1310720 | bytes 2099202 | tf_op jit(solution)/shard_map/convert_element_type | solution.py:293
  23.5 1.4 %slice_bitcast_fusion.1 = (bf16[512,512]{1,0:T(8,128)(2,1)S(1)}, bf16[512,512]{1,0:T(8,128)(2,1)S(1)}) fusion(bf16[3,512,512]{2,1,0:T(8,128)(2,1)} %param.13, pred[]{:T(512)S(6)} %eq.28), kind=kLoop, calls=%fused_computation.3 | loop fusion | flops 262144 | bytes 2621441 | tf_op jit(solution)/shard_map/squeeze | solution.py:291
  25.0 0.0 collective-permute-done.3
  25.0 6.5 %collective-permute-done.1.incoming_ref = bf16[64,512]{1,0:T(8,128)(2,1)S(1)} collective-permute-done((bf16[64,512]{1,0:T(8,128)(2,1)S(1)}, bf16[64,512]{1,0:T(8,128)(2,1)S(1)}, u32[]{:S(2)}, u32[]{:S(2)}) %collective-permute-start.1) | collective-permute-done | bytes 65568 | tf_op jit(solution)/shard_map/ppermute | solution.py:278
  31.6 0.0 collective-permute-done.2
  31.6 5.7 %all-to-all-done.in_ref = bf16[16,64,512]{2,1,0:T(8,128)(2,1)S(1)} async-done(((bf16[16,64,512]{2,1,0:T(8,128)(2,1)}), bf16[16,64,512]{2,1,0:T(8,128)(2,1)S(1)}, u32[]{:S(2)}, u32[]{:S(2)}) %all-to-all-start) | async-done | bytes 1048608 | tf_op jit(solution)/shard_map/all_to_all | solution.py:277
  37.3 0.0 slice-start
  37.3 0.8 plane_sum.1
  38.1 8.6 %all-to-all-start.1 = ((bf16[8,16,512]{2,1,0:T(8,128)(2,1)}), bf16[8,16,512]{2,1,0:T(8,128)(2,1)S(1)}, u32[]{:S(2)}, u32[]{:S(2)}) async-start(bf16[8,16,512]{2,1,0:T(8,128)(2,1)} %bitcast.13), calls=%async_computation.1 | async-start | bytes 262144 | tf_op jit(solution)/shard_map/all_to_all | solution.py:312
  46.6 0.0 collective-permute-start.6
  46.6 1.5 %slice_bitcast_fusion = (bf16[512,512]{1,0:T(8,128)(2,1)S(1)}, bf16[512,512]{1,0:T(8,128)(2,1)S(1)}, bf16[512,512]{1,0:T(8,128)(2,1)S(1)}) fusion(bf16[3,512,512]{2,1,0:T(8,128)(2,1)} %collective-permute-done.2, pred[]{:T(512)S(6)} %eq.31, pred[]{:T(512)S(6)} %or.8), kind=kLoop, calls=%fused_computation.2 | loop fusion | flops 786432 | bytes 3145730 | tf_op jit(solution)/shard_map/squeeze | solution.py:335
  48.1 0.0 slice-done
  48.1 0.7 pad_maximum_fusion.shifted_ref
  48.8 5.4 %all-to-all-done.1 = bf16[8,16,512]{2,1,0:T(8,128)(2,1)S(1)} async-done(((bf16[8,16,512]{2,1,0:T(8,128)(2,1)}), bf16[8,16,512]{2,1,0:T(8,128)(2,1)S(1)}, u32[]{:S(2)}, u32[]{:S(2)}) %all-to-all-start.1) | async-done | bytes 131104 | tf_op jit(solution)/shard_map/all_to_all | solution.py:312
  54.3 0.8 subtract_multiply_fusion.c_ref
  55.1 0.0 collective-permute-start.4
  55.1 1.2 %collective-permute-done.4.c_u_ref = f32[16,512]{1,0:T(8,128)S(1)} collective-permute-done((f32[16,512]{1,0:T(8,128)S(1)}, f32[16,512]{1,0:T(8,128)S(1)}, u32[]{:S(2)}, u32[]{:S(2)}) %collective-permute-start.4) | collective-permute-done | bytes 32800 | tf_op jit(solution)/shard_map/ppermute | solution.py:324
  56.3 0.4 shard_map.95
  56.6 1.8 %collective-permute-start.5 = (bf16[2,16,512]{2,1,0:T(8,128)(2,1)S(1)}, bf16[2,16,512]{2,1,0:T(8,128)(2,1)S(1)}, u32[]{:S(2)}, u32[]{:S(2)}) collective-permute-start(bf16[2,16,512]{2,1,0:T(8,128)(2,1)S(1)} %get-tuple-element.27.pack_ref), channel_id=1, source_target_pairs={{0,1},{1,0},{2,3},{3,2},{248,249},{249,248},{250,251},{251,250},{8... | collective-permute-start | bytes 98312 | tf_op jit(solution)/shard_map/ppermute | solution.py:309
  58.4 0.0 collective-permute-done.6
  58.4 1.1 %broadcast_select_fusion.back_ref = bf16[512,512]{1,0:T(8,128)(2,1)S(1)} fusion(bf16[512,512]{1,0:T(8,128)(2,1)} %collective-permute-done.6, pred[]{:T(512)S(6)} %or.7), kind=kLoop, calls=%fused_computation.8 | loop fusion | flops 262144 | bytes 1048577 | tf_op jit(solution)/shard_map/jit(_where)/select_n | solution.py:314
  59.5 2.6 %collective-permute-done.5.got_ref = bf16[2,16,512]{2,1,0:T(8,128)(2,1)S(1)} collective-permute-done((bf16[2,16,512]{2,1,0:T(8,128)(2,1)S(1)}, bf16[2,16,512]{2,1,0:T(8,128)(2,1)S(1)}, u32[]{:S(2)}, u32[]{:S(2)}) %collective-permute-start.5) | collective-permute-done | bytes 32800 | tf_op jit(solution)/shard_map/ppermute | solution.py:309
  62.1 0.4 shard_map.96.next_ref
  62.5 0.0 collective-permute-start.7
  62.5 1.2 %collective-permute-done.7.got_ref = bf16[2,16,512]{2,1,0:T(8,128)(2,1)S(1)} collective-permute-done((bf16[2,16,512]{2,1,0:T(8,128)(2,1)S(1)}, bf16[2,16,512]{2,1,0:T(8,128)(2,1)S(1)}, u32[]{:S(2)}, u32[]{:S(2)}) %collective-permute-start.7) | collective-permute-done | bytes 32800 | tf_op jit(solution)/shard_map/ppermute | solution.py:331
  63.7 1.2 %shard_map.97 = (bf16[2,16,512]{2,1,0:T(8,128)(2,1)S(1)}, f32[16,512]{1,0:T(8,128)S(1)}) custom-call(bf16[2,16,512]{2,1,0:T(8,128)(2,1)S(1)} %shard_map.96.next_ref, bf16[2,16,512]{2,1,0:T(8,128)(2,1)S(1)} %collective-permute-done.7.got_ref, f32[16,512]{1,0:T(8,128)S(1)} %subtract_multiply_fusion.c_ref, f32[16,512]{1,0:T(8,128)S(1)} %collective-permute-done.4.c_u_ref, ...), custom_call_target="tpu_custom_call" | custom-call | flops 67108864 | bytes 4194304 | tf_op jit(solution)/shard_map/pallas_call | solution.py:240
  64.9 1.8 %collective-permute-start.8 = (bf16[2,16,512]{2,1,0:T(8,128)(2,1)S(1)}, bf16[2,16,512]{2,1,0:T(8,128)(2,1)S(1)}, u32[]{:S(2)}, u32[]{:S(2)}) collective-permute-start(bf16[2,16,512]{2,1,0:T(8,128)(2,1)S(1)} %get-tuple-element.34.pack_ref), channel_id=1, source_target_pairs={{0,1},{1,0},{2,3},{3,2},{248,249},{249,248},{250,251},{251,250},{8... | collective-permute-start | bytes 98312 | tf_op jit(solution)/shard_map/ppermute | solution.py:309
  66.7 3.7 %collective-permute-done.8.got_ref = bf16[2,16,512]{2,1,0:T(8,128)(2,1)S(1)} collective-permute-done((bf16[2,16,512]{2,1,0:T(8,128)(2,1)S(1)}, bf16[2,16,512]{2,1,0:T(8,128)(2,1)S(1)}, u32[]{:S(2)}, u32[]{:S(2)}) %collective-permute-start.8) | collective-permute-done | bytes 32800 | tf_op jit(solution)/shard_map/ppermute | solution.py:309
  70.4 0.4 shard_map.98.next_ref
  70.8 0.2 collective-permute-start.9
  71.0 1.2 %collective-permute-done.9.got_ref = bf16[2,16,512]{2,1,0:T(8,128)(2,1)S(1)} collective-permute-done((bf16[2,16,512]{2,1,0:T(8,128)(2,1)S(1)}, bf16[2,16,512]{2,1,0:T(8,128)(2,1)S(1)}, u32[]{:S(2)}, u32[]{:S(2)}) %collective-permute-start.9) | collective-permute-done | bytes 32800 | tf_op jit(solution)/shard_map/ppermute | solution.py:331
  72.2 1.2 %shard_map.99 = (bf16[2,16,512]{2,1,0:T(8,128)(2,1)S(1)}, f32[16,512]{1,0:T(8,128)S(1)}) custom-call(bf16[2,16,512]{2,1,0:T(8,128)(2,1)S(1)} %shard_map.98.next_ref, bf16[2,16,512]{2,1,0:T(8,128)(2,1)S(1)} %collective-permute-done.9.got_ref, f32[16,512]{1,0:T(8,128)S(1)} %subtract_multiply_fusion.c_ref, f32[16,512]{1,0:T(8,128)S(1)} %collective-permute-done.4.c_u_ref, ...), custom_call_target="tpu_custom_call" | custom-call | flops 67108864 | bytes 4194304 | tf_op jit(solution)/shard_map/pallas_call | solution.py:240
  73.4 1.8 %collective-permute-start.10 = (bf16[2,16,512]{2,1,0:T(8,128)(2,1)S(1)}, bf16[2,16,512]{2,1,0:T(8,128)(2,1)S(1)}, u32[]{:S(2)}, u32[]{:S(2)}) collective-permute-start(bf16[2,16,512]{2,1,0:T(8,128)(2,1)S(1)} %get-tuple-element.36.pack_ref), channel_id=1, source_target_pairs={{0,1},{1,0},{2,3},{3,2},{248,249},{249,248},{250,251},{251,250},{8... | collective-permute-start | bytes 98312 | tf_op jit(solution)/shard_map/ppermute | solution.py:309
  75.2 3.7 %collective-permute-done.10.got_ref = bf16[2,16,512]{2,1,0:T(8,128)(2,1)S(1)} collective-permute-done((bf16[2,16,512]{2,1,0:T(8,128)(2,1)S(1)}, bf16[2,16,512]{2,1,0:T(8,128)(2,1)S(1)}, u32[]{:S(2)}, u32[]{:S(2)}) %collective-permute-start.10) | collective-permute-done | bytes 32800 | tf_op jit(solution)/shard_map/ppermute | solution.py:309
  78.9 0.4 shard_map.100.next_ref
  79.2 0.0 collective-permute-start.11
  79.2 1.2 %collective-permute-done.11.got_ref = bf16[2,16,512]{2,1,0:T(8,128)(2,1)S(1)} collective-permute-done((bf16[2,16,512]{2,1,0:T(8,128)(2,1)S(1)}, bf16[2,16,512]{2,1,0:T(8,128)(2,1)S(1)}, u32[]{:S(2)}, u32[]{:S(2)}) %collective-permute-start.11) | collective-permute-done | bytes 32800 | tf_op jit(solution)/shard_map/ppermute | solution.py:331
  80.5 1.2 %shard_map.101 = (bf16[2,16,512]{2,1,0:T(8,128)(2,1)S(1)}, f32[16,512]{1,0:T(8,128)S(1)}) custom-call(bf16[2,16,512]{2,1,0:T(8,128)(2,1)S(1)} %shard_map.100.next_ref, bf16[2,16,512]{2,1,0:T(8,128)(2,1)S(1)} %collective-permute-done.11.got_ref, f32[16,512]{1,0:T(8,128)S(1)} %subtract_multiply_fusion.c_ref, f32[16,512]{1,0:T(8,128)S(1)} %collective-permute-done.4.c_u_ref, ...), custom_call_target="tpu_custom_call" | custom-call | flops 67108864 | bytes 4194304 | tf_op jit(solution)/shard_map/pallas_call | solution.py:240
  81.7 1.8 %collective-permute-start.12 = (bf16[2,16,512]{2,1,0:T(8,128)(2,1)S(1)}, bf16[2,16,512]{2,1,0:T(8,128)(2,1)S(1)}, u32[]{:S(2)}, u32[]{:S(2)}) collective-permute-start(bf16[2,16,512]{2,1,0:T(8,128)(2,1)S(1)} %get-tuple-element.39), channel_id=1, source_target_pairs={{0,1},{1,0},{2,3},{3,2},{248,249},{249,248},{250,251},{251,250},{8... | collective-permute-start | bytes 98312 | tf_op jit(solution)/shard_map/ppermute | solution.py:309
  83.5 3.7 %collective-permute-done.12.got_ref = bf16[2,16,512]{2,1,0:T(8,128)(2,1)S(1)} collective-permute-done((bf16[2,16,512]{2,1,0:T(8,128)(2,1)S(1)}, bf16[2,16,512]{2,1,0:T(8,128)(2,1)S(1)}, u32[]{:S(2)}, u32[]{:S(2)}) %collective-permute-start.12) | collective-permute-done | bytes 32800 | tf_op jit(solution)/shard_map/ppermute | solution.py:309
  87.2 0.2 shard_map.102.own_ref
  87.4 0.2 collective-permute-start.15
  87.6 1.9 %collective-permute-start.14 = (f32[16,512]{1,0:T(8,128)S(1)}, f32[16,512]{1,0:T(8,128)S(1)}, u32[]{:S(2)}, u32[]{:S(2)}) collective-permute-start(f32[16,512]{1,0:T(8,128)S(1)} %shard_map.102.own_ref), channel_id=1, source_target_pairs={{0,1},{1,2},{2,3},{3,0},{4,5},{5,6},{6,7},{7,4},{8,9},{9,10},{10,1... | collective-permute-start | bytes 98312 | tf_op jit(solution)/shard_map/ppermute | solution.py:343
  89.4 0.8 collective-permute-start.13
  90.2 0.1 pad_add_fusion.where_ref
  90.3 1.0 %collective-permute-done.15.third_ref = f32[16,512]{1,0:T(8,128)S(1)} collective-permute-done((f32[16,512]{1,0:T(8,128)S(1)}, f32[16,512]{1,0:T(8,128)S(1)}, u32[]{:S(2)}, u32[]{:S(2)}) %collective-permute-start.15) | collective-permute-done | bytes 32800 | tf_op jit(solution)/shard_map/ppermute | solution.py:343
  91.3 1.4 %collective-permute-done.14.first_ref = f32[16,512]{1,0:T(8,128)S(1)} collective-permute-done((f32[16,512]{1,0:T(8,128)S(1)}, f32[16,512]{1,0:T(8,128)S(1)}, u32[]{:S(2)}, u32[]{:S(2)}) %collective-permute-start.14) | collective-permute-done | bytes 32800 | tf_op jit(solution)/shard_map/ppermute | solution.py:343
  92.7 2.2 %collective-permute-done.13.second_ref = f32[16,512]{1,0:T(8,128)S(1)} collective-permute-done((f32[16,512]{1,0:T(8,128)S(1)}, f32[16,512]{1,0:T(8,128)S(1)}, u32[]{:S(2)}, u32[]{:S(2)}) %collective-permute-start.13) | collective-permute-done | bytes 32800 | tf_op jit(solution)/shard_map/ppermute | solution.py:343
  94.9 1.2 %finish.1 = (f32[64,512]{1,0:T(8,128)}, bf16[4,64,512]{2,1,0:T(8,128)(2,1)}) custom-call(s32[2]{0:T(128)S(1)} %pad_add_fusion.where_ref, f32[16,512]{1,0:T(8,128)S(1)} %shard_map.102.own_ref, f32[16,512]{1,0:T(8,128)S(1)} %collective-permute-done.13.second_ref, f32[16,512]{1,0:T(8,128)S(1)} %collective-permute-done.14.first_ref, ...), custom_call_target="tpu_custom_call", output_to_operand_aliasing={{1}: (6, {})} | custom-call | tf_op jit(solution)/shard_map/finish/pallas_call | solution.py:174
  (4 shorter events, 0.0 us)
Async XLA Ops:
  5.4 5.3 %collective-permute-start = (bf16[4,4,4,16,512]{4,3,2,1,0:T(8,128)(2,1)S(1)}, bf16[4,4,4,16,512]{4,3,2,1,0:T(8,128)(2,1)S(1)}, u32[]{:S(2)}, u32[]{:S(2)}) collective-permute-start(bf16[4,4,4,16,512]{4,3,2,1,0:T(8,128)(2,1)S(1)} %far_half.3), channel_id=1, source_target_pairs={{0,8},{8,0},{1,9},{9,1},{2,10},{10,2},{3,11},{11,3},{4,12},{12,4},... | collective-permute-start | bytes 3145736 | tf_op jit(solution)/shard_map/ppermute | solution.py:274
  5.5 26.1 %collective-permute-start.2 = (bf16[3,512,512]{2,1,0:T(8,128)(2,1)}, bf16[3,512,512]{2,1,0:T(8,128)(2,1)}, u32[]{:S(2)}, u32[]{:S(2)}) collective-permute-start(bf16[3,512,512]{2,1,0:T(8,128)(2,1)} %param.13), channel_id=1, source_target_pairs={{0,8},{8,0},{1,9},{9,1},{2,10},{10,2},{3,11},{11,3},{4,12},{12,4},... | collective-permute-start | bytes 4718600 | tf_op jit(solution)/shard_map/ppermute | solution.py:279
  10.7 8.5 %copy-start.1 = (f32[512]{0:T(512)S(1)}, f32[512]{0:T(512)}, u32[]{:S(2)}) copy-start(f32[512]{0:T(512)} %param.14) | copy-start | bytes 6148
  10.7 8.6 %copy-start = (bf16[4,64,512]{2,1,0:T(8,128)(2,1)S(1)}, bf16[4,64,512]{2,1,0:T(8,128)(2,1)}, u32[]{:S(2)}) copy-start(bf16[4,64,512]{2,1,0:T(8,128)(2,1)} %hist_ref.3) | copy-start | bytes 786436
  12.1 25.1 %all-to-all-start = ((bf16[16,64,512]{2,1,0:T(8,128)(2,1)}), bf16[16,64,512]{2,1,0:T(8,128)(2,1)S(1)}, u32[]{:S(2)}, u32[]{:S(2)}) async-start(bf16[16,64,512]{2,1,0:T(8,128)(2,1)} %bitcast.8), calls=%async_computation | async-start | bytes 2097152 | tf_op jit(solution)/shard_map/all_to_all | solution.py:277
  19.2 5.8 %collective-permute-start.3 = (f32[1,512]{1,0:T(1,128)S(1)}, f32[1,512]{1,0:T(1,128)S(1)}, u32[]{:S(2)}, u32[]{:S(2)}) collective-permute-start(f32[1,512]{1,0:T(1,128)S(1)} %bitcast.45), channel_id=1, source_target_pairs={{0,8},{8,0},{1,9},{9,1},{2,10},{10,2},{3,11},{11,3},{4,12},{12,4},... | collective-permute-start | bytes 6152 | tf_op jit(solution)/shard_map/ppermute | solution.py:280
  19.3 12.2 %collective-permute-start.1 = (bf16[64,512]{1,0:T(8,128)(2,1)S(1)}, bf16[64,512]{1,0:T(8,128)(2,1)S(1)}, u32[]{:S(2)}, u32[]{:S(2)}) collective-permute-start(bf16[64,512]{1,0:T(8,128)(2,1)S(1)} %slice_bitcast_fusion.2), channel_id=1, source_target_pairs={{0,1},{1,2},{2,3},{3,4},{4,5},{5,6},{6,7},{7,0},{8,9},{9,10},{10,1... | collective-permute-start | bytes 196616 | tf_op jit(solution)/shard_map/ppermute | solution.py:278
  37.3 10.8 %slice-start = ((bf16[4,64,512]{2,1,0:T(8,128)(2,1)}), bf16[3,64,512]{2,1,0:T(8,128)(2,1)S(1)}, s32[]{:S(2)}) async-start(bf16[4,64,512]{2,1,0:T(8,128)(2,1)} %hist_ref.3), calls=%async_computation.2 | async-start | bytes 393216 | tf_op jit(solution)/shard_map/slice | solution.py:299
  38.1 16.2 %all-to-all-start.1 = ((bf16[8,16,512]{2,1,0:T(8,128)(2,1)}), bf16[8,16,512]{2,1,0:T(8,128)(2,1)S(1)}, u32[]{:S(2)}, u32[]{:S(2)}) async-start(bf16[8,16,512]{2,1,0:T(8,128)(2,1)} %bitcast.13), calls=%async_computation.1 | async-start | bytes 262144 | tf_op jit(solution)/shard_map/all_to_all | solution.py:312
  46.6 11.8 %collective-permute-start.6 = (bf16[512,512]{1,0:T(8,128)(2,1)}, bf16[512,512]{1,0:T(8,128)(2,1)}, u32[]{:S(2)}, u32[]{:S(2)}) collective-permute-start(bf16[512,512]{1,0:T(8,128)(2,1)} %get-tuple-element.30), channel_id=1, source_target_pairs={{0,1},{1,0},{2,3},{3,2},{248,249},{249,248},{250,251},{251,250},{8... | collective-permute-start | bytes 1572872 | tf_op jit(solution)/shard_map/ppermute | solution.py:309
  55.1 1.2 %collective-permute-start.4 = (f32[16,512]{1,0:T(8,128)S(1)}, f32[16,512]{1,0:T(8,128)S(1)}, u32[]{:S(2)}, u32[]{:S(2)}) collective-permute-start(f32[16,512]{1,0:T(8,128)S(1)} %subtract_multiply_fusion.c_ref), channel_id=1, source_target_pairs={{0,8},{8,0},{1,9},{9,1},{2,10},{10,2},{3,11},{11,3},{4,12},{12,4},... | collective-permute-start | bytes 98312 | tf_op jit(solution)/shard_map/ppermute | solution.py:324
  56.6 5.5 %collective-permute-start.5 = (bf16[2,16,512]{2,1,0:T(8,128)(2,1)S(1)}, bf16[2,16,512]{2,1,0:T(8,128)(2,1)S(1)}, u32[]{:S(2)}, u32[]{:S(2)}) collective-permute-start(bf16[2,16,512]{2,1,0:T(8,128)(2,1)S(1)} %get-tuple-element.27.pack_ref), channel_id=1, source_target_pairs={{0,1},{1,0},{2,3},{3,2},{248,249},{249,248},{250,251},{251,250},{8... | collective-permute-start | bytes 98312 | tf_op jit(solution)/shard_map/ppermute | solution.py:309
  62.5 1.2 %collective-permute-start.7 = (bf16[2,16,512]{2,1,0:T(8,128)(2,1)S(1)}, bf16[2,16,512]{2,1,0:T(8,128)(2,1)S(1)}, u32[]{:S(2)}, u32[]{:S(2)}) collective-permute-start(bf16[2,16,512]{2,1,0:T(8,128)(2,1)S(1)} %shard_map.96.next_ref), channel_id=1, source_target_pairs={{0,8},{8,0},{1,9},{9,1},{2,10},{10,2},{3,11},{11,3},{4,12},{12,4},... | collective-permute-start | bytes 98312 | tf_op jit(solution)/shard_map/ppermute | solution.py:331
  64.9 5.5 %collective-permute-start.8 = (bf16[2,16,512]{2,1,0:T(8,128)(2,1)S(1)}, bf16[2,16,512]{2,1,0:T(8,128)(2,1)S(1)}, u32[]{:S(2)}, u32[]{:S(2)}) collective-permute-start(bf16[2,16,512]{2,1,0:T(8,128)(2,1)S(1)} %get-tuple-element.34.pack_ref), channel_id=1, source_target_pairs={{0,1},{1,0},{2,3},{3,2},{248,249},{249,248},{250,251},{251,250},{8... | collective-permute-start | bytes 98312 | tf_op jit(solution)/shard_map/ppermute | solution.py:309
  70.8 1.4 %collective-permute-start.9 = (bf16[2,16,512]{2,1,0:T(8,128)(2,1)S(1)}, bf16[2,16,512]{2,1,0:T(8,128)(2,1)S(1)}, u32[]{:S(2)}, u32[]{:S(2)}) collective-permute-start(bf16[2,16,512]{2,1,0:T(8,128)(2,1)S(1)} %shard_map.98.next_ref), channel_id=1, source_target_pairs={{0,8},{8,0},{1,9},{9,1},{2,10},{10,2},{3,11},{11,3},{4,12},{12,4},... | collective-permute-start | bytes 98312 | tf_op jit(solution)/shard_map/ppermute | solution.py:331
  73.4 5.5 %collective-permute-start.10 = (bf16[2,16,512]{2,1,0:T(8,128)(2,1)S(1)}, bf16[2,16,512]{2,1,0:T(8,128)(2,1)S(1)}, u32[]{:S(2)}, u32[]{:S(2)}) collective-permute-start(bf16[2,16,512]{2,1,0:T(8,128)(2,1)S(1)} %get-tuple-element.36.pack_ref), channel_id=1, source_target_pairs={{0,1},{1,0},{2,3},{3,2},{248,249},{249,248},{250,251},{251,250},{8... | collective-permute-start | bytes 98312 | tf_op jit(solution)/shard_map/ppermute | solution.py:309
  79.2 1.2 %collective-permute-start.11 = (bf16[2,16,512]{2,1,0:T(8,128)(2,1)S(1)}, bf16[2,16,512]{2,1,0:T(8,128)(2,1)S(1)}, u32[]{:S(2)}, u32[]{:S(2)}) collective-permute-start(bf16[2,16,512]{2,1,0:T(8,128)(2,1)S(1)} %shard_map.100.next_ref), channel_id=1, source_target_pairs={{0,8},{8,0},{1,9},{9,1},{2,10},{10,2},{3,11},{11,3},{4,12},{12,4},... | collective-permute-start | bytes 98312 | tf_op jit(solution)/shard_map/ppermute | solution.py:331
  81.7 5.5 %collective-permute-start.12 = (bf16[2,16,512]{2,1,0:T(8,128)(2,1)S(1)}, bf16[2,16,512]{2,1,0:T(8,128)(2,1)S(1)}, u32[]{:S(2)}, u32[]{:S(2)}) collective-permute-start(bf16[2,16,512]{2,1,0:T(8,128)(2,1)S(1)} %get-tuple-element.39), channel_id=1, source_target_pairs={{0,1},{1,0},{2,3},{3,2},{248,249},{249,248},{250,251},{251,250},{8... | collective-permute-start | bytes 98312 | tf_op jit(solution)/shard_map/ppermute | solution.py:309
  87.4 3.9 %collective-permute-start.15 = (f32[16,512]{1,0:T(8,128)S(1)}, f32[16,512]{1,0:T(8,128)S(1)}, u32[]{:S(2)}, u32[]{:S(2)}) collective-permute-start(f32[16,512]{1,0:T(8,128)S(1)} %shard_map.102.own_ref), channel_id=1, source_target_pairs={{0,3},{1,0},{2,1},{3,2},{4,7},{5,4},{6,5},{7,6},{8,11},{9,8},{10,9... | collective-permute-start | bytes 98312 | tf_op jit(solution)/shard_map/ppermute | solution.py:343
  87.6 5.1 %collective-permute-start.14 = (f32[16,512]{1,0:T(8,128)S(1)}, f32[16,512]{1,0:T(8,128)S(1)}, u32[]{:S(2)}, u32[]{:S(2)}) collective-permute-start(f32[16,512]{1,0:T(8,128)S(1)} %shard_map.102.own_ref), channel_id=1, source_target_pairs={{0,1},{1,2},{2,3},{3,0},{4,5},{5,6},{6,7},{7,4},{8,9},{9,10},{10,1... | collective-permute-start | bytes 98312 | tf_op jit(solution)/shard_map/ppermute | solution.py:343
  89.4 5.4 %collective-permute-start.13 = (f32[16,512]{1,0:T(8,128)S(1)}, f32[16,512]{1,0:T(8,128)S(1)}, u32[]{:S(2)}, u32[]{:S(2)}) collective-permute-start(f32[16,512]{1,0:T(8,128)S(1)} %shard_map.102.own_ref), channel_id=1, source_target_pairs={{0,2},{1,3},{2,0},{3,1},{4,6},{5,7},{6,4},{7,5},{8,10},{9,11},{10,... | collective-permute-start | bytes 98312 | tf_op jit(solution)/shard_map/ppermute | solution.py:343

commit v6 on v5

--- a/solution.py
+++ b/solution.py
@@ -197,41 +197,77 @@
     )
 
 
-def begin_kernel(c_ref, c_u_ref, inv_ref, own_ref, chip_ref, pack_ref, p_ref):
-    value = c_ref[...].astype(jnp.bfloat16)
-    beside = c_u_ref[...].astype(jnp.bfloat16)
+def right_kernel(arrived_ref, given_ref, inv_ref, c_ref, value_ref):
+    total = arrived_ref[0].astype(jnp.float32)
+    for source in range(1, arrived_ref.shape[0]):
+        total = total + arrived_ref[source].astype(jnp.float32)
+    c = given_ref[...] - inv_ref[...] * total
+    c_ref[...] = c
+    value_ref[...] = c.astype(jnp.bfloat16)
+
+
+def inner_kernel(value_ref, beside_ref, c_ref, inv_ref, own_ref, chip_ref, part_ref):
+    beside = beside_ref[...].astype(jnp.bfloat16)
+    total = times(value_ref[...], own_ref[...]) + times(beside, chip_ref[...])
+    part_ref[...] = c_ref[...] - inv_ref[...] * total
+
+
+def simple_kernel(part_ref, got_ref, inv_ref, away_ref, value_ref):
+    value = part_ref[...] - inv_ref[...] * times(got_ref[...], away_ref[...])
+    value_ref[...] = value.astype(jnp.bfloat16)
+
+
+def one_kernel(value_ref, c_ref, inv_ref, own_ref, part_ref):
+    part_ref[...] = c_ref[...] - inv_ref[...] * times(value_ref[...], own_ref[...])
+
+
+def begin_kernel(value_ref, part_ref, beside_ref, inv_ref, chip_ref, pack_ref, p_ref):
+    part = part_ref[...] - inv_ref[...] * times(beside_ref[...], chip_ref[...])
+    pack_ref[0] = value_ref[...]
+    pack_ref[1] = part.astype(jnp.bfloat16)
+    p_ref[...] = part
+
+
+def ahead_kernel(pack_ref, back_ref, out_ref):
+    out_ref[...] = times(pack_ref[0], back_ref[...])
+
+
+def first_kernel(known_ref, p_ref, got_ref, inv_ref, away_ref, next_ref):
+    mine = p_ref[...] - inv_ref[...] * times(got_ref[0], away_ref[...])
+    other = got_ref[1].astype(jnp.float32) - known_ref[...]
+    next_ref[0] = mine.astype(jnp.bfloat16)
+    next_ref[1] = other.astype(jnp.bfloat16)
+
+
+def under_kernel(
+    next_ref, c_ref, c_u_ref, inv_ref, inv_u_ref, own_ref, away_ref, chip_u_ref, part_ref, part_u_ref
+):
+    total = times(next_ref[0], own_ref[...]) + times(next_ref[1], away_ref[...])
+    part_ref[...] = c_ref[...] - inv_ref[...] * total
+    part_u_ref[...] = c_u_ref[...] - inv_u_ref[...] * times(next_ref[0], chip_u_ref[...])
+
+
+def second_kernel(
+    got_ref, part_ref, part_u_ref, c_ref, inv_ref, inv_u_ref, own_ref, chip_ref, own_u_ref,
+    away_u_ref, pack_ref, p_ref
+):
+    value = part_ref[...] - inv_ref[...] * times(got_ref[0], chip_ref[...])
+    total_u = times(got_ref[0], own_u_ref[...]) + times(got_ref[1], away_u_ref[...])
+    value = value.astype(jnp.bfloat16)
+    beside = (part_u_ref[...] - inv_u_ref[...] * total_u).astype(jnp.bfloat16)
     part = c_ref[...] - inv_ref[...] * (times(value, own_ref[...]) + times(beside, chip_ref[...]))
     pack_ref[0] = value
     pack_ref[1] = part.astype(jnp.bfloat16)
     p_ref[...] = part
 
 
-def first_kernel(pack_ref, p_ref, got_ref, inv_ref, away_ref, back_ref, next_ref):
-    mine = p_ref[...] - inv_ref[...] * times(got_ref[0], away_ref[...])
-    other = got_ref[1].astype(jnp.float32) - times(pack_ref[0], back_ref[...])
-    next_ref[0] = mine.astype(jnp.bfloat16)
-    next_ref[1] = other.astype(jnp.bfloat16)
-
-
-def second_kernel(
-    next_ref, got_ref, c_ref, c_u_ref, inv_ref, inv_u_ref, own_ref, chip_ref, away_ref,
-    own_u_ref, chip_u_ref, away_u_ref, pack_ref, p_ref
-):
-    mine, mine_away, other, other_away = next_ref[0], next_ref[1], got_ref[0], got_ref[1]
-    total = times(mine, own_ref[...]) + times(other, chip_ref[...]) + times(mine_away, away_ref[...])
-    total_u = (
-        times(other, own_u_ref[...]) + times(mine, chip_u_ref[...]) + times(other_away, away_u_ref[...])
-    )
-    value = (c_ref[...] - inv_ref[...] * total).astype(jnp.bfloat16)
-    beside = (c_u_ref[...] - inv_u_ref[...] * total_u).astype(jnp.bfloat16)
-    part = c_ref[...] - inv_ref[...] * (times(value, own_ref[...]) + times(beside, chip_ref[...]))
-    pack_ref[0] = value
-    pack_ref[1] = part.astype(jnp.bfloat16)
-    p_ref[...] = part
-
-
-def end_kernel(p_ref, got_ref, inv_ref, away_ref, out_ref):
-    out_ref[...] = p_ref[...] - inv_ref[...] * times(got_ref[0], away_ref[...])
+def last_under_kernel(next_ref, c_ref, inv_ref, own_ref, away_ref, part_ref):
+    total = times(next_ref[0], own_ref[...]) + times(next_ref[1], away_ref[...])
+    part_ref[...] = c_ref[...] - inv_ref[...] * total
+
+
+def end_kernel(part_ref, got_ref, inv_ref, chip_ref, out_ref):
+    out_ref[...] = part_ref[...] - inv_ref[...] * times(got_ref[0], chip_ref[...])
 
 
 def small_call(kernel, products, outs, *operands):
@@ -308,34 +344,49 @@
     def off_chip(value):
         return lax.ppermute(value, SPACE + ("y",), between)
 
+    rows = time_steps // 4
+    row = lax.axis_index("y")
+    given = lax.dynamic_slice_in_dim(excitation, row * rows, rows, 0) * inverse
     twice = plane_sum(arrived, 2).reshape(8, -1, width)
     arrived = lax.all_to_all(twice, ("zh", "zl"), 0, 0, tiled=True)
     back = off_chip(toward)
     back = jnp.where((block == 0) | (block == targets - 1), 0.0, back)
-    arrived, incoming, shifted, chip_u, away_u = lax.optimization_barrier(
-        (arrived, incoming, shifted, chip_u, away_u)
-    )
-    far_field = jnp.sum(arrived.astype(jnp.float32), axis=0)
-    rows = time_steps // 4
-    row = lax.axis_index("y")
-    right_side = lax.dynamic_slice_in_dim(excitation, row * rows, rows, 0) - far_field
-
-    c = right_side * inverse
-    c_u = lax.ppermute(c, "c", swap)
+    arrived, incoming, shifted, chip_u, away_u, given = lax.optimization_barrier(
+        (arrived, incoming, shifted, chip_u, away_u, given)
+    )
     packed = jax.ShapeDtypeStruct((2, rows, width), jnp.bfloat16)
     single = jax.ShapeDtypeStruct((rows, width), jnp.float32)
-    pack, part = small_call(begin_kernel, 2, (packed, single), c, c_u, inverse, near_own, near_chip)
-    for _ in range((SWEEPS - 1) // 2):
+    rounded = jax.ShapeDtypeStruct((rows, width), jnp.bfloat16)
+    c, value = small_call(right_kernel, 0, (single, rounded), arrived, given, inverse)
+    got = off_chip(value)
+    c_u = lax.ppermute(c, "c", swap)
+    (part,) = small_call(inner_kernel, 2, (single,), value, c_u, c, inverse, near_own, near_chip)
+    (value,) = small_call(simple_kernel, 1, (rounded,), part, got, inverse, near_away)
+    beside = lax.ppermute(value, "c", swap)
+    (part,) = small_call(one_kernel, 1, (single,), value, c, inverse, near_own)
+    pack, part = small_call(
+        begin_kernel, 1, (packed, single), value, part, beside, inverse, near_chip
+    )
+    for sweep in range(2, SWEEPS, 2):
         got = off_chip(pack)
-        (both,) = small_call(first_kernel, 2, (packed,), pack, part, got, inverse, near_away, back)
+        (known,) = small_call(ahead_kernel, 1, (single,), pack, back)
+        (both,) = small_call(first_kernel, 1, (packed,), known, part, got, inverse, near_away)
         over = lax.ppermute(both, "c", swap)
+        if sweep + 2 >= SWEEPS:
+            (part,) = small_call(
+                last_under_kernel, 2, (single,),
+                both, c, inverse, near_own, near_away,
+            )
+            (current,) = small_call(end_kernel, 1, (single,), part, over, inverse, near_chip)
+            break
+        part, part_u = small_call(
+            under_kernel, 3, (single, single),
+            both, c, c_u, inverse, inverse_u, near_own, near_away, chip_u,
+        )
         pack, part = small_call(
-            second_kernel, 8, (packed, single),
-            both, over, c, c_u, inverse, inverse_u, near_own, near_chip, near_away,
-            near_u[1], chip_u, away_u,
+            second_kernel, 5, (packed, single),
+            over, part, part_u, c, inverse, inverse_u, near_own, near_chip, near_u[1], away_u,
         )
-    got = off_chip(pack)
-    (current,) = small_call(end_kernel, 1, (single,), part, got, inverse, near_away)
 
     pieces = [current]
     for step in (2, 1, 3):

time: 96.7 us -> 93.9 us (0.971)
  the two profiles are of different devices: /device:TPU:32 before, /device:TPU:56 now
where the time goes in v6:
time: 93.9 us; the launch traced here: 93.4 us
  starting transfers between devices  37.7 us (40%)
  waiting for transfers between devices  28.2 us (30%)
  Pallas kernels  17.3 us (18%)
  other arithmetic  9.23 us (10%)
  between operations  1.01 us (1%)
    ppermute x5, waiting for transfers between devices, off_chip(): return lax.ppermute(value, SPACE + ('y',), between)  10.9 us
    ppermute x5, starting transfers between devices, off_chip(): return lax.ppermute(value, SPACE + ('y',), between)  9.62 us
    pallas_call x2, Pallas kernels, far_half(): pl.pallas_call(functools.partial(far_kernel, ranks=ranks), out_shape=jax....  9.44 us
    all_to_all x1, starting transfers between devices, per_device(): arrived = lax.all_to_all(twice, ('zh', 'zl'), 0, 0, tiled=True)  9.03 us
    all_to_all x1, starting transfers between devices, per_device(): lax.all_to_all(partial_value.reshape(16, -1, width), ('x', 'y'), 0, 0, ti...  7.17 us
    ppermute x1, starting transfers between devices, per_device(): lax.ppermute(history[-1], HIST, [(i, (i + 1) % 8) for i in range(8)])  5.9 us
    pallas_call x17, Pallas kernels, small_call(): pl.pallas_call(kernel, out_shape=outs, in_specs=[inside] * len(operands),...  5.79 us
    all_to_all x1, waiting for transfers between devices, per_device(): arrived = lax.all_to_all(twice, ('zh', 'zl'), 0, 0, tiled=True)  5.56 us
  transfers between devices with their start and end apart: 19, of which 13 were waited for; matrix products, arithmetic and copies ran while one was open for 10% of the time, Pallas kernels for 9%

profile of v6, /device:TPU:56, one launch (start us, length us, event | category | flops | bytes accessed | tf_op | source)
XLA Modules:
  0.0 93.4 jit_solution(9414035877204459392)
XLA Ops:
  0.6 4.7 %far_half.3 = bf16[4,4,4,16,512]{4,3,2,1,0:T(8,128)(2,1)S(1)} custom-call(s32[1]{0:T(128)} %bitcast.7.core_ref, s32[64]{0:T(128)} %bitcast.47, s32[64]{0:T(128)} %bitcast.49, bf16[4,64,512]{2,1,0:T(8,128)(2,1)} %hist_ref.3, bf16[16,2,160,512]{3,2,1,0:T(8,128)(2,1)} %bitcast.43, bf16[16,2,160,512]{3,2,1,0:T(8,128)(2,1)} %bitcast.45), custom_call_target="tpu_custom_call" | custom-call | flops 838860800 | bytes 6291456 | tf_op jit(solution)/shard_map/far_half/pallas_call | solution.py:98
  5.4 0.1 collective-permute-start
  5.5 0.5 collective-permute-start.2
  6.0 4.7 %far_half.2 = bf16[4,4,4,16,512]{4,3,2,1,0:T(8,128)(2,1)S(1)} custom-call(s32[1]{0:T(128)} %bitcast.2.core_ref, s32[64]{0:T(128)} %bitcast.48, s32[64]{0:T(128)} %bitcast.50, bf16[4,64,512]{2,1,0:T(8,128)(2,1)} %hist_ref.3, bf16[16,2,160,512]{3,2,1,0:T(8,128)(2,1)} %bitcast.44, bf16[16,2,160,512]{3,2,1,0:T(8,128)(2,1)} %bitcast.46), custom_call_target="tpu_custom_call" | custom-call | flops 838860800 | bytes 6291456 | tf_op jit(solution)/shard_map/far_half/pallas_call | solution.py:98
  10.7 0.0 copy-start
  10.7 0.0 copy-start.1
  10.7 0.0 collective-permute-done
  10.7 1.4 %add_convert_fusion = bf16[4,4,4,16,512]{4,3,2,1,0:T(8,128)(2,1)} fusion(bf16[4,4,4,16,512]{4,3,2,1,0:T(8,128)(2,1)S(1)} %collective-permute-done, bf16[4,4,4,16,512]{4,3,2,1,0:T(8,128)(2,1)S(1)} %far_half.2), kind=kLoop, calls=%fused_computation | loop fusion | flops 2097152 | bytes 3145728 | tf_op jit(solution)/shard_map/convert_element_type | solution.py:312
  12.2 7.2 %all-to-all-start = ((bf16[16,64,512]{2,1,0:T(8,128)(2,1)}), bf16[16,64,512]{2,1,0:T(8,128)(2,1)S(1)}, u32[]{:S(2)}, u32[]{:S(2)}) async-start(bf16[16,64,512]{2,1,0:T(8,128)(2,1)} %bitcast.8), calls=%async_computation | async-start | bytes 2097152 | tf_op jit(solution)/shard_map/all_to_all | solution.py:313
  19.3 5.9 %collective-permute-start.1 = (bf16[64,512]{1,0:T(8,128)(2,1)S(1)}, bf16[64,512]{1,0:T(8,128)(2,1)S(1)}, u32[]{:S(2)}, u32[]{:S(2)}) collective-permute-start(bf16[64,512]{1,0:T(8,128)(2,1)S(1)} %slice_bitcast_fusion.2), channel_id=1, source_target_pairs={{0,1},{1,2},{2,3},{3,4},{4,5},{5,6},{6,7},{7,0},{8,9},{9,10},{10,1... | collective-permute-start | bytes 196616 | tf_op jit(solution)/shard_map/ppermute | solution.py:314
  25.2 0.0 collective-permute-start.3
  25.3 2.2 %multiply_convert_fusion = (bf16[512,512]{1,0:T(8,128)(2,1)}, bf16[512,512]{1,0:T(8,128)(2,1)S(1)}) fusion(f32[512]{0:T(512)S(1)} %broadcast_divide_fusion.1, bf16[3,512,512]{2,1,0:T(8,128)(2,1)} %param.13, pred[]{:T(512)S(6)} %eq.28, pred[]{:T(512)S(6)} %or.7), kind=kLoop, calls=%fused_computation.1 | loop fusion | flops 1310720 | bytes 2099202 | tf_op jit(solution)/shard_map/convert_element_type | solution.py:329
  27.5 1.5 %slice_bitcast_fusion.1 = (bf16[512,512]{1,0:T(8,128)(2,1)S(1)}, bf16[512,512]{1,0:T(8,128)(2,1)S(1)}) fusion(bf16[3,512,512]{2,1,0:T(8,128)(2,1)} %param.13, pred[]{:T(512)S(6)} %eq.28), kind=kLoop, calls=%fused_computation.3 | loop fusion | flops 262144 | bytes 2621441 | tf_op jit(solution)/shard_map/squeeze | solution.py:327
  29.0 0.0 collective-permute-done.3
  29.0 0.0 collective-permute-done.1.incoming_ref
  29.0 0.0 collective-permute-done.2
  29.0 5.4 %all-to-all-done.in_ref = bf16[16,64,512]{2,1,0:T(8,128)(2,1)S(1)} async-done(((bf16[16,64,512]{2,1,0:T(8,128)(2,1)}), bf16[16,64,512]{2,1,0:T(8,128)(2,1)S(1)}, u32[]{:S(2)}, u32[]{:S(2)}) %all-to-all-start) | async-done | bytes 1048608 | tf_op jit(solution)/shard_map/all_to_all | solution.py:313
  34.4 0.7 collective-permute-start.7
  35.1 0.8 dynamic-slice_multiply_fusion.given_ref
  35.9 0.8 plane_sum.1
  36.7 9.0 %all-to-all-start.1 = ((bf16[8,16,512]{2,1,0:T(8,128)(2,1)}), bf16[8,16,512]{2,1,0:T(8,128)(2,1)S(1)}, u32[]{:S(2)}, u32[]{:S(2)}) async-start(bf16[8,16,512]{2,1,0:T(8,128)(2,1)} %bitcast.13), calls=%async_computation.1 | async-start | bytes 262144 | tf_op jit(solution)/shard_map/all_to_all | solution.py:351
  45.7 0.7 pad_maximum_fusion.shifted_ref
  46.5 1.5 %slice_bitcast_fusion = (bf16[512,512]{1,0:T(8,128)(2,1)S(1)}, bf16[512,512]{1,0:T(8,128)(2,1)S(1)}, bf16[512,512]{1,0:T(8,128)(2,1)S(1)}) fusion(bf16[3,512,512]{2,1,0:T(8,128)(2,1)} %collective-permute-done.2, pred[]{:T(512)S(6)} %eq.31, pred[]{:T(512)S(6)} %or.8), kind=kLoop, calls=%fused_computation.2 | loop fusion | flops 786432 | bytes 3145730 | tf_op jit(solution)/shard_map/squeeze | solution.py:388
  47.9 5.6 %all-to-all-done.1.arrived_ref = bf16[8,16,512]{2,1,0:T(8,128)(2,1)S(1)} async-done(((bf16[8,16,512]{2,1,0:T(8,128)(2,1)}), bf16[8,16,512]{2,1,0:T(8,128)(2,1)S(1)}, u32[]{:S(2)}, u32[]{:S(2)}) %all-to-all-start.1) | async-done | bytes 131104 | tf_op jit(solution)/shard_map/all_to_all | solution.py:351
  53.5 0.1 collective-permute-start.4
  53.6 2.2 %collective-permute-start.5 = (bf16[16,512]{1,0:T(8,128)(2,1)S(1)}, bf16[16,512]{1,0:T(8,128)(2,1)S(1)}, u32[]{:S(2)}, u32[]{:S(2)}) collective-permute-start(bf16[16,512]{1,0:T(8,128)(2,1)S(1)} %get-tuple-element.32.value_ref), channel_id=1, source_target_pairs={{0,1},{1,0},{2,3},{3,2},{248,249},{249,248},{250,251},{251,250},{8... | collective-permute-start | bytes 49160 | tf_op jit(solution)/shard_map/ppermute | solution.py:345
  55.9 0.0 collective-permute-done.4.beside_ref.c_u_ref
  55.9 0.4 shard_map.96.part_ref
  56.2 2.8 %collective-permute-done.5.got_ref = bf16[16,512]{1,0:T(8,128)(2,1)S(1)} collective-permute-done((bf16[16,512]{1,0:T(8,128)(2,1)S(1)}, bf16[16,512]{1,0:T(8,128)(2,1)S(1)}, u32[]{:S(2)}, u32[]{:S(2)}) %collective-permute-start.5) | collective-permute-done | bytes 16416 | tf_op jit(solution)/shard_map/ppermute | solution.py:345
  59.0 0.2 shard_map.97.value_ref
  59.2 0.2 shard_map.98.part_ref
  59.5 0.9 %collective-permute-done.6.beside_ref = bf16[16,512]{1,0:T(8,128)(2,1)S(1)} collective-permute-done((bf16[16,512]{1,0:T(8,128)(2,1)S(1)}, bf16[16,512]{1,0:T(8,128)(2,1)S(1)}, u32[]{:S(2)}, u32[]{:S(2)}) %collective-permute-start.6) | collective-permute-done | bytes 16416 | tf_op jit(solution)/shard_map/ppermute | solution.py:365
  60.4 0.2 shard_map.99
  60.7 2.2 %collective-permute-start.8 = (bf16[2,16,512]{2,1,0:T(8,128)(2,1)S(1)}, bf16[2,16,512]{2,1,0:T(8,128)(2,1)S(1)}, u32[]{:S(2)}, u32[]{:S(2)}) collective-permute-start(bf16[2,16,512]{2,1,0:T(8,128)(2,1)S(1)} %get-tuple-element.36.pack_ref), channel_id=1, source_target_pairs={{0,1},{1,0},{2,3},{3,2},{248,249},{249,248},{250,251},{251,250},{8... | collective-permute-start | bytes 98312 | tf_op jit(solution)/shard_map/ppermute | solution.py:345
  62.8 1.1 %broadcast_select_fusion.back_ref = bf16[512,512]{1,0:T(8,128)(2,1)S(1)} fusion(bf16[512,512]{1,0:T(8,128)(2,1)} %collective-permute-done.7, pred[]{:T(512)S(6)} %or.7), kind=kLoop, calls=%fused_computation.8 | loop fusion | flops 262144 | bytes 1048577 | tf_op jit(solution)/shard_map/jit(_where)/select_n | solution.py:353
  63.9 0.2 shard_map.100.known_ref
  64.1 2.0 %collective-permute-done.8.got_ref = bf16[2,16,512]{2,1,0:T(8,128)(2,1)S(1)} collective-permute-done((bf16[2,16,512]{2,1,0:T(8,128)(2,1)S(1)}, bf16[2,16,512]{2,1,0:T(8,128)(2,1)S(1)}, u32[]{:S(2)}, u32[]{:S(2)}) %collective-permute-start.8) | collective-permute-done | bytes 32800 | tf_op jit(solution)/shard_map/ppermute | solution.py:345
  66.1 0.2 shard_map.101.next_ref
  66.4 0.5 shard_map.102
  66.9 0.7 collective-permute-done.9.got_ref
  67.6 0.8 shard_map.103
  68.4 2.3 %collective-permute-start.10 = (bf16[2,16,512]{2,1,0:T(8,128)(2,1)S(1)}, bf16[2,16,512]{2,1,0:T(8,128)(2,1)S(1)}, u32[]{:S(2)}, u32[]{:S(2)}) collective-permute-start(bf16[2,16,512]{2,1,0:T(8,128)(2,1)S(1)} %get-tuple-element.44.pack_ref), channel_id=1, source_target_pairs={{0,1},{1,0},{2,3},{3,2},{248,249},{249,248},{250,251},{251,250},{8... | collective-permute-start | bytes 98312 | tf_op jit(solution)/shard_map/ppermute | solution.py:345
  70.7 0.2 shard_map.104.known_ref
  71.0 3.1 %collective-permute-done.10.got_ref = bf16[2,16,512]{2,1,0:T(8,128)(2,1)S(1)} collective-permute-done((bf16[2,16,512]{2,1,0:T(8,128)(2,1)S(1)}, bf16[2,16,512]{2,1,0:T(8,128)(2,1)S(1)}, u32[]{:S(2)}, u32[]{:S(2)}) %collective-permute-start.10) | collective-permute-done | bytes 32800 | tf_op jit(solution)/shard_map/ppermute | solution.py:345
  74.0 0.2 shard_map.105.next_ref
  74.3 0.0 collective-permute-start.11
  74.3 0.5 shard_map.106
  74.8 0.7 collective-permute-done.11.got_ref
  75.5 0.8 shard_map.107
  76.3 2.2 %collective-permute-start.12 = (bf16[2,16,512]{2,1,0:T(8,128)(2,1)S(1)}, bf16[2,16,512]{2,1,0:T(8,128)(2,1)S(1)}, u32[]{:S(2)}, u32[]{:S(2)}) collective-permute-start(bf16[2,16,512]{2,1,0:T(8,128)(2,1)S(1)} %get-tuple-element.48.pack_ref), channel_id=1, source_target_pairs={{0,1},{1,0},{2,3},{3,2},{248,249},{249,248},{250,251},{251,250},{8... | collective-permute-start | bytes 98312 | tf_op jit(solution)/shard_map/ppermute | solution.py:345
  78.5 0.2 shard_map.108.known_ref
  78.7 3.1 %collective-permute-done.12.got_ref = bf16[2,16,512]{2,1,0:T(8,128)(2,1)S(1)} collective-permute-done((bf16[2,16,512]{2,1,0:T(8,128)(2,1)S(1)}, bf16[2,16,512]{2,1,0:T(8,128)(2,1)S(1)}, u32[]{:S(2)}, u32[]{:S(2)}) %collective-permute-start.12) | collective-permute-done | bytes 32800 | tf_op jit(solution)/shard_map/ppermute | solution.py:345
  81.8 0.2 shard_map.109.next_ref
  82.1 0.4 shard_map.110.part_ref
  82.4 0.8 collective-permute-done.13.got_ref
  83.3 0.2 shard_map.111.own_ref
  83.5 3.2 %collective-permute-start.14 = (f32[16,512]{1,0:T(8,128)S(1)}, f32[16,512]{1,0:T(8,128)S(1)}, u32[]{:S(2)}, u32[]{:S(2)}) collective-permute-start(f32[16,512]{1,0:T(8,128)S(1)} %shard_map.111.own_ref), channel_id=1, source_target_pairs={{0,2},{1,3},{2,0},{3,1},{4,6},{5,7},{6,4},{7,5},{8,10},{9,11},{10,... | collective-permute-start | bytes 98312 | tf_op jit(solution)/shard_map/ppermute | solution.py:394
  86.7 0.2 collective-permute-start.15
  86.9 1.9 %collective-permute-start.16 = (f32[16,512]{1,0:T(8,128)S(1)}, f32[16,512]{1,0:T(8,128)S(1)}, u32[]{:S(2)}, u32[]{:S(2)}) collective-permute-start(f32[16,512]{1,0:T(8,128)S(1)} %shard_map.111.own_ref), channel_id=1, source_target_pairs={{0,3},{1,0},{2,1},{3,2},{4,7},{5,4},{6,5},{7,6},{8,11},{9,8},{10,9... | collective-permute-start | bytes 98312 | tf_op jit(solution)/shard_map/ppermute | solution.py:394
  88.8 0.1 pad_add_fusion.where_ref
  88.8 0.1 collective-permute-done.14.second_ref
  88.9 1.7 %collective-permute-done.15.first_ref = f32[16,512]{1,0:T(8,128)S(1)} collective-permute-done((f32[16,512]{1,0:T(8,128)S(1)}, f32[16,512]{1,0:T(8,128)S(1)}, u32[]{:S(2)}, u32[]{:S(2)}) %collective-permute-start.15) | collective-permute-done | bytes 32800 | tf_op jit(solution)/shard_map/ppermute | solution.py:394
  90.7 1.4 %collective-permute-done.16.third_ref = f32[16,512]{1,0:T(8,128)S(1)} collective-permute-done((f32[16,512]{1,0:T(8,128)S(1)}, f32[16,512]{1,0:T(8,128)S(1)}, u32[]{:S(2)}, u32[]{:S(2)}) %collective-permute-start.16) | collective-permute-done | bytes 32800 | tf_op jit(solution)/shard_map/ppermute | solution.py:394
  92.0 1.2 %finish.1 = (f32[64,512]{1,0:T(8,128)}, bf16[4,64,512]{2,1,0:T(8,128)(2,1)}) custom-call(s32[2]{0:T(128)S(1)} %pad_add_fusion.where_ref, f32[16,512]{1,0:T(8,128)S(1)} %shard_map.111.own_ref, f32[16,512]{1,0:T(8,128)S(1)} %collective-permute-done.14.second_ref, f32[16,512]{1,0:T(8,128)S(1)} %collective-permute-done.15.first_ref, ...), custom_call_target="tpu_custom_call", output_to_operand_aliasing={{1}: (6, {})} | custom-call | tf_op jit(solution)/shard_map/finish/pallas_call | solution.py:174
  (12 shorter events, 0.1 us)
Async XLA Ops:
  5.4 5.3 %collective-permute-start = (bf16[4,4,4,16,512]{4,3,2,1,0:T(8,128)(2,1)S(1)}, bf16[4,4,4,16,512]{4,3,2,1,0:T(8,128)(2,1)S(1)}, u32[]{:S(2)}, u32[]{:S(2)}) collective-permute-start(bf16[4,4,4,16,512]{4,3,2,1,0:T(8,128)(2,1)S(1)} %far_half.3), channel_id=1, source_target_pairs={{0,8},{8,0},{1,9},{9,1},{2,10},{10,2},{3,11},{11,3},{4,12},{12,4},... | collective-permute-start | bytes 3145736 | tf_op jit(solution)/shard_map/ppermute | solution.py:310
  5.5 23.5 %collective-permute-start.2 = (bf16[3,512,512]{2,1,0:T(8,128)(2,1)}, bf16[3,512,512]{2,1,0:T(8,128)(2,1)}, u32[]{:S(2)}, u32[]{:S(2)}) collective-permute-start(bf16[3,512,512]{2,1,0:T(8,128)(2,1)} %param.13), channel_id=1, source_target_pairs={{0,8},{8,0},{1,9},{9,1},{2,10},{10,2},{3,11},{11,3},{4,12},{12,4},... | collective-permute-start | bytes 4718600 | tf_op jit(solution)/shard_map/ppermute | solution.py:315
  10.7 8.6 %copy-start = (bf16[4,64,512]{2,1,0:T(8,128)(2,1)S(1)}, bf16[4,64,512]{2,1,0:T(8,128)(2,1)}, u32[]{:S(2)}) copy-start(bf16[4,64,512]{2,1,0:T(8,128)(2,1)} %hist_ref.3) | copy-start | bytes 786436
  10.7 14.5 %copy-start.1 = (f32[512]{0:T(512)S(1)}, f32[512]{0:T(512)}, u32[]{:S(2)}) copy-start(f32[512]{0:T(512)} %param.14) | copy-start | bytes 6148
  12.2 22.3 %all-to-all-start = ((bf16[16,64,512]{2,1,0:T(8,128)(2,1)}), bf16[16,64,512]{2,1,0:T(8,128)(2,1)S(1)}, u32[]{:S(2)}, u32[]{:S(2)}) async-start(bf16[16,64,512]{2,1,0:T(8,128)(2,1)} %bitcast.8), calls=%async_computation | async-start | bytes 2097152 | tf_op jit(solution)/shard_map/all_to_all | solution.py:313
  19.3 9.6 %collective-permute-start.1 = (bf16[64,512]{1,0:T(8,128)(2,1)S(1)}, bf16[64,512]{1,0:T(8,128)(2,1)S(1)}, u32[]{:S(2)}, u32[]{:S(2)}) collective-permute-start(bf16[64,512]{1,0:T(8,128)(2,1)S(1)} %slice_bitcast_fusion.2), channel_id=1, source_target_pairs={{0,1},{1,2},{2,3},{3,4},{4,5},{5,6},{6,7},{7,0},{8,9},{9,10},{10,1... | collective-permute-start | bytes 196616 | tf_op jit(solution)/shard_map/ppermute | solution.py:314
  25.2 3.7 %collective-permute-start.3 = (f32[1,512]{1,0:T(1,128)S(1)}, f32[1,512]{1,0:T(1,128)S(1)}, u32[]{:S(2)}, u32[]{:S(2)}) collective-permute-start(f32[1,512]{1,0:T(1,128)S(1)} %bitcast.51), channel_id=1, source_target_pairs={{0,8},{8,0},{1,9},{9,1},{2,10},{10,2},{3,11},{11,3},{4,12},{12,4},... | collective-permute-start | bytes 6152 | tf_op jit(solution)/shard_map/ppermute | solution.py:316
  27.5 18.3 %slice-start = ((bf16[4,64,512]{2,1,0:T(8,128)(2,1)}), bf16[3,64,512]{2,1,0:T(8,128)(2,1)S(1)}, s32[]{:S(2)}) async-start(bf16[4,64,512]{2,1,0:T(8,128)(2,1)} %hist_ref.3), calls=%async_computation.2 | async-start | bytes 393216 | tf_op jit(solution)/shard_map/slice | solution.py:335
  34.4 28.4 %collective-permute-start.7 = (bf16[512,512]{1,0:T(8,128)(2,1)}, bf16[512,512]{1,0:T(8,128)(2,1)}, u32[]{:S(2)}, u32[]{:S(2)}) collective-permute-start(bf16[512,512]{1,0:T(8,128)(2,1)} %get-tuple-element.37), channel_id=1, source_target_pairs={{0,1},{1,0},{2,3},{3,2},{248,249},{249,248},{250,251},{251,250},{8... | collective-permute-start | bytes 1572872 | tf_op jit(solution)/shard_map/ppermute | solution.py:345
  36.7 16.8 %all-to-all-start.1 = ((bf16[8,16,512]{2,1,0:T(8,128)(2,1)}), bf16[8,16,512]{2,1,0:T(8,128)(2,1)S(1)}, u32[]{:S(2)}, u32[]{:S(2)}) async-start(bf16[8,16,512]{2,1,0:T(8,128)(2,1)} %bitcast.13), calls=%async_computation.1 | async-start | bytes 262144 | tf_op jit(solution)/shard_map/all_to_all | solution.py:351
  53.5 2.3 %collective-permute-start.4 = (f32[16,512]{1,0:T(8,128)S(1)}, f32[16,512]{1,0:T(8,128)S(1)}, u32[]{:S(2)}, u32[]{:S(2)}) collective-permute-start(f32[16,512]{1,0:T(8,128)S(1)} %get-tuple-element.33.c_ref), channel_id=1, source_target_pairs={{0,8},{8,0},{1,9},{9,1},{2,10},{10,2},{3,11},{11,3},{4,12},{12,4},... | collective-permute-start | bytes 98312 | tf_op jit(solution)/shard_map/ppermute | solution.py:362
  53.6 5.4 %collective-permute-start.5 = (bf16[16,512]{1,0:T(8,128)(2,1)S(1)}, bf16[16,512]{1,0:T(8,128)(2,1)S(1)}, u32[]{:S(2)}, u32[]{:S(2)}) collective-permute-start(bf16[16,512]{1,0:T(8,128)(2,1)S(1)} %get-tuple-element.32.value_ref), channel_id=1, source_target_pairs={{0,1},{1,0},{2,3},{3,2},{248,249},{249,248},{250,251},{251,250},{8... | collective-permute-start | bytes 49160 | tf_op jit(solution)/shard_map/ppermute | solution.py:345
  59.2 1.2 %collective-permute-start.6 = (bf16[16,512]{1,0:T(8,128)(2,1)S(1)}, bf16[16,512]{1,0:T(8,128)(2,1)S(1)}, u32[]{:S(2)}, u32[]{:S(2)}) collective-permute-start(bf16[16,512]{1,0:T(8,128)(2,1)S(1)} %shard_map.97.value_ref), channel_id=1, source_target_pairs={{0,8},{8,0},{1,9},{9,1},{2,10},{10,2},{3,11},{11,3},{4,12},{12,4},... | collective-permute-start | bytes 49160 | tf_op jit(solution)/shard_map/ppermute | solution.py:365
  60.7 5.5 %collective-permute-start.8 = (bf16[2,16,512]{2,1,0:T(8,128)(2,1)S(1)}, bf16[2,16,512]{2,1,0:T(8,128)(2,1)S(1)}, u32[]{:S(2)}, u32[]{:S(2)}) collective-permute-start(bf16[2,16,512]{2,1,0:T(8,128)(2,1)S(1)} %get-tuple-element.36.pack_ref), channel_id=1, source_target_pairs={{0,1},{1,0},{2,3},{3,2},{248,249},{249,248},{250,251},{251,250},{8... | collective-permute-start | bytes 98312 | tf_op jit(solution)/shard_map/ppermute | solution.py:345
  66.4 1.2 %collective-permute-start.9 = (bf16[2,16,512]{2,1,0:T(8,128)(2,1)S(1)}, bf16[2,16,512]{2,1,0:T(8,128)(2,1)S(1)}, u32[]{:S(2)}, u32[]{:S(2)}) collective-permute-start(bf16[2,16,512]{2,1,0:T(8,128)(2,1)S(1)} %shard_map.101.next_ref), channel_id=1, source_target_pairs={{0,8},{8,0},{1,9},{9,1},{2,10},{10,2},{3,11},{11,3},{4,12},{12,4},... | collective-permute-start | bytes 98312 | tf_op jit(solution)/shard_map/ppermute | solution.py:374
  68.4 5.6 %collective-permute-start.10 = (bf16[2,16,512]{2,1,0:T(8,128)(2,1)S(1)}, bf16[2,16,512]{2,1,0:T(8,128)(2,1)S(1)}, u32[]{:S(2)}, u32[]{:S(2)}) collective-permute-start(bf16[2,16,512]{2,1,0:T(8,128)(2,1)S(1)} %get-tuple-element.44.pack_ref), channel_id=1, source_target_pairs={{0,1},{1,0},{2,3},{3,2},{248,249},{249,248},{250,251},{251,250},{8... | collective-permute-start | bytes 98312 | tf_op jit(solution)/shard_map/ppermute | solution.py:345
  74.3 1.2 %collective-permute-start.11 = (bf16[2,16,512]{2,1,0:T(8,128)(2,1)S(1)}, bf16[2,16,512]{2,1,0:T(8,128)(2,1)S(1)}, u32[]{:S(2)}, u32[]{:S(2)}) collective-permute-start(bf16[2,16,512]{2,1,0:T(8,128)(2,1)S(1)} %shard_map.105.next_ref), channel_id=1, source_target_pairs={{0,8},{8,0},{1,9},{9,1},{2,10},{10,2},{3,11},{11,3},{4,12},{12,4},... | collective-permute-start | bytes 98312 | tf_op jit(solution)/shard_map/ppermute | solution.py:374
  76.3 5.5 %collective-permute-start.12 = (bf16[2,16,512]{2,1,0:T(8,128)(2,1)S(1)}, bf16[2,16,512]{2,1,0:T(8,128)(2,1)S(1)}, u32[]{:S(2)}, u32[]{:S(2)}) collective-permute-start(bf16[2,16,512]{2,1,0:T(8,128)(2,1)S(1)} %get-tuple-element.48.pack_ref), channel_id=1, source_target_pairs={{0,1},{1,0},{2,3},{3,2},{248,249},{249,248},{250,251},{251,250},{8... | collective-permute-start | bytes 98312 | tf_op jit(solution)/shard_map/ppermute | solution.py:345
  82.0 1.2 %collective-permute-start.13 = (bf16[2,16,512]{2,1,0:T(8,128)(2,1)S(1)}, bf16[2,16,512]{2,1,0:T(8,128)(2,1)S(1)}, u32[]{:S(2)}, u32[]{:S(2)}) collective-permute-start(bf16[2,16,512]{2,1,0:T(8,128)(2,1)S(1)} %shard_map.109.next_ref), channel_id=1, source_target_pairs={{0,8},{8,0},{1,9},{9,1},{2,10},{10,2},{3,11},{11,3},{4,12},{12,4},... | collective-permute-start | bytes 98312 | tf_op jit(solution)/shard_map/ppermute | solution.py:374
  83.5 5.4 %collective-permute-start.14 = (f32[16,512]{1,0:T(8,128)S(1)}, f32[16,512]{1,0:T(8,128)S(1)}, u32[]{:S(2)}, u32[]{:S(2)}) collective-permute-start(f32[16,512]{1,0:T(8,128)S(1)} %shard_map.111.own_ref), channel_id=1, source_target_pairs={{0,2},{1,3},{2,0},{3,1},{4,6},{5,7},{6,4},{7,5},{8,10},{9,11},{10,... | collective-permute-start | bytes 98312 | tf_op jit(solution)/shard_map/ppermute | solution.py:394
  86.7 3.9 %collective-permute-start.15 = (f32[16,512]{1,0:T(8,128)S(1)}, f32[16,512]{1,0:T(8,128)S(1)}, u32[]{:S(2)}, u32[]{:S(2)}) collective-permute-start(f32[16,512]{1,0:T(8,128)S(1)} %shard_map.111.own_ref), channel_id=1, source_target_pairs={{0,1},{1,2},{2,3},{3,0},{4,5},{5,6},{6,7},{7,4},{8,9},{9,10},{10,1... | collective-permute-start | bytes 98312 | tf_op jit(solution)/shard_map/ppermute | solution.py:394
  86.9 5.1 %collective-permute-start.16 = (f32[16,512]{1,0:T(8,128)S(1)}, f32[16,512]{1,0:T(8,128)S(1)}, u32[]{:S(2)}, u32[]{:S(2)}) collective-permute-start(f32[16,512]{1,0:T(8,128)S(1)} %shard_map.111.own_ref), channel_id=1, source_target_pairs={{0,3},{1,0},{2,1},{3,2},{4,7},{5,4},{6,5},{7,6},{8,11},{9,8},{10,9... | collective-permute-start | bytes 98312 | tf_op jit(solution)/shard_map/ppermute | solution.py:394

commit v7 on v6

--- a/solution.py
+++ b/solution.py
@@ -72,7 +72,8 @@
             at = lax.broadcasted_iota(jnp.int32, part.shape, 1) + low
             part = jnp.where((at >= first) & (at < last), part, jnp.zeros_like(part))
             field = jnp.dot(part, left[low:high], preferred_element_type=jnp.float32)
-            out_ref[chip, :, group] = field.reshape(out_ref.shape[1], -1, width).astype(out_ref.dtype)
+            at = group * (chips // 4) + chip // 4
+            out_ref[chip % 4, :, at] = field.reshape(out_ref.shape[1], -1, width).astype(out_ref.dtype)
 
     for copy in small:
         copy.wait()
@@ -91,13 +92,13 @@
 def far_half(core, rank, lag, history, right, left, ranks):
     rows, _, depth, width = right.shape
     lags, steps, _ = history.shape
-    groups, chips, cuts = 4, 4, 4
+    groups, chips, cuts = 2, 16 // 2, 4
     scalar = pl.BlockSpec(memory_space=pltpu.SMEM)
     outside = pl.BlockSpec(memory_space=pltpu.HBM)
     held = pltpu.VMEM((groups, chips, depth, width), jnp.bfloat16)
     return pl.pallas_call(
         functools.partial(far_kernel, ranks=ranks),
-        out_shape=jax.ShapeDtypeStruct((chips, cuts, groups, steps // cuts, width), jnp.bfloat16),
+        out_shape=jax.ShapeDtypeStruct((4, cuts, 4, steps // cuts, width), jnp.bfloat16),
         in_specs=[scalar] + [outside] * 5,
         out_specs=pl.BlockSpec(memory_space=pltpu.VMEM),
         scratch_shapes=[
@@ -122,6 +123,37 @@
     )(core, rank, lag, history, right, left)
 
 
+def halves_kernel(mine_ref, came_ref, out_ref, held_ref, sem):
+    copies = []
+    for piece in range(mine_ref.shape[0]):
+        held_ref[piece] = mine_ref[piece] + came_ref[piece]
+        copies.append(
+            pltpu.make_async_copy(held_ref.at[piece], out_ref.at[piece], sem.at[piece])
+        )
+        copies[-1].start()
+    for copy in copies:
+        copy.wait()
+
+
+def halves_sum(mine, came):
+    inside = pl.BlockSpec(memory_space=pltpu.VMEM)
+    return pl.pallas_call(
+        halves_kernel,
+        out_shape=jax.ShapeDtypeStruct(mine.shape, mine.dtype),
+        in_specs=[inside, inside],
+        out_specs=pl.BlockSpec(memory_space=pltpu.HBM),
+        scratch_shapes=[
+            pltpu.VMEM(mine.shape, mine.dtype),
+            pltpu.SemaphoreType.DMA((mine.shape[0],)),
+        ],
+        compiler_params=pltpu.CompilerParams(vmem_limit_bytes=4 << 20),
+        cost_estimate=pl.CostEstimate(
+            flops=mine.size, bytes_accessed=6 * mine.size, transcendentals=0
+        ),
+        name="halves_sum",
+    )(mine, came)
+
+
 def plane_kernel(in_ref, out_ref):
     rows = 16
     for first in range(0, in_ref.shape[1], rows):
@@ -150,22 +182,21 @@
 
 def last_kernel(
     where_ref, own_ref, second_ref, first_ref, third_ref, incoming_ref, shifted_ref,
-    out_ref, next_ref, whole_ref, front_ref, out_sem, next_sem
+    out_ref, next_ref, front_ref, out_sem, next_sem
 ):
     row = where_ref[0]
     rows = own_ref.shape[0]
+    copies = []
     for turn, piece in enumerate((own_ref, first_ref, second_ref, third_ref)):
-        slot = lax.rem(row + 4 - turn, 4)
-        at = pl.ds(pl.multiple_of(slot * rows, rows), rows)
-        whole_ref[at] = piece[...]
+        at = pl.ds(pl.multiple_of(lax.rem(row + 4 - turn, 4) * rows, rows), rows)
+        copies.append(pltpu.make_async_copy(piece, out_ref.at[at], out_sem.at[turn]))
+        copies[-1].start()
         front_ref[at] = piece[...].astype(front_ref.dtype)
-    whole = pltpu.make_async_copy(whole_ref, out_ref, out_sem)
-    whole.start()
     front_ref[...] = jnp.where(where_ref[1] == 1, front_ref[...], incoming_ref[...])
-    front = pltpu.make_async_copy(front_ref, next_ref.at[0], next_sem)
-    front.start()
-    whole.wait()
-    front.wait()
+    copies.append(pltpu.make_async_copy(front_ref, next_ref.at[0], next_sem))
+    copies[-1].start()
+    for copy in copies:
+        copy.wait()
 
 
 def finish(where, pieces, incoming, shifted):
@@ -180,9 +211,8 @@
         in_specs=[pl.BlockSpec(memory_space=pltpu.SMEM)] + [inside] * 5 + [outside],
         out_specs=(outside, outside),
         scratch_shapes=[
-            pltpu.VMEM((steps, width), jnp.float32),
             pltpu.VMEM((steps, width), jnp.bfloat16),
-            pltpu.SemaphoreType.DMA,
+            pltpu.SemaphoreType.DMA((4,)),
             pltpu.SemaphoreType.DMA,
         ],
         input_output_aliases={6: 1},
@@ -309,7 +339,7 @@
     away = half(1 - core)
     came = lax.ppermute(away, "c", swap)
     mine = half(core)
-    partial_value = (mine.astype(jnp.float32) + came.astype(jnp.float32)).astype(jnp.bfloat16)
+    partial_value = halves_sum(mine, came)
     arrived = lax.all_to_all(partial_value.reshape(16, -1, width), ("x", "y"), 0, 0, tiled=True)
     incoming = lax.ppermute(history[-1], HIST, [(i, (i + 1) % 8) for i in range(8)])
     near_u = lax.ppermute(near_block, "c", swap)
@@ -327,11 +357,16 @@
     near_own = near_block[1]
     near_chip, near_away = sides(near_block, core == 0, block)
     toward = (inverse.reshape(width, 1) * near_away).astype(jnp.bfloat16)
-    arrived, incoming, near_u, self_u, near_chip, near_away, toward = lax.optimization_barrier(
-        (arrived, incoming, near_u, self_u, near_chip, near_away, toward)
-    )
-    inverse_u = 1.0 / self_u
+    rows = time_steps // 4
+    row = lax.axis_index("y")
+    given = lax.dynamic_slice_in_dim(excitation, row * rows, rows, 0) * inverse
+    (
+        arrived, incoming, near_u, inverse_u, near_chip, near_away, toward, given
+    ) = lax.optimization_barrier(
+        (arrived, incoming, near_u, inverse_u, near_chip, near_away, toward, given)
+    )
     chip_u, away_u = sides(near_u, core == 1, block + 1 - 2 * core)
+    own_u = near_u[1]
     shifted = jnp.concatenate([incoming[None], history[:-1]], axis=0)
     partner = {0: 0, targets - 1: targets - 1}
     for t in range(1, targets - 1, 2):
@@ -344,15 +379,12 @@
     def off_chip(value):
         return lax.ppermute(value, SPACE + ("y",), between)
 
-    rows = time_steps // 4
-    row = lax.axis_index("y")
-    given = lax.dynamic_slice_in_dim(excitation, row * rows, rows, 0) * inverse
     twice = plane_sum(arrived, 2).reshape(8, -1, width)
     arrived = lax.all_to_all(twice, ("zh", "zl"), 0, 0, tiled=True)
     back = off_chip(toward)
     back = jnp.where((block == 0) | (block == targets - 1), 0.0, back)
-    arrived, incoming, shifted, chip_u, away_u, given = lax.optimization_barrier(
-        (arrived, incoming, shifted, chip_u, away_u, given)
+    arrived, incoming, shifted, chip_u, away_u = lax.optimization_barrier(
+        (arrived, incoming, shifted, chip_u, away_u)
     )
     packed = jax.ShapeDtypeStruct((2, rows, width), jnp.bfloat16)
     single = jax.ShapeDtypeStruct((rows, width), jnp.float32)
@@ -385,7 +417,7 @@
         )
         pack, part = small_call(
             second_kernel, 5, (packed, single),
-            over, part, part_u, c, inverse, inverse_u, near_own, near_chip, near_u[1], away_u,
+            over, part, part_u, c, inverse, inverse_u, near_own, near_chip, own_u, away_u,
         )
 
     pieces = [current]

time: 93.9 us -> 94.3 us (level)
  the two profiles are of different devices: /device:TPU:56 before, /device:TPU:32 now
where the time goes in v7:
time: 94.3 us; the launch traced here: 93.9 us
  waiting for transfers between devices  36.6 us (39%)
  starting transfers between devices  31.3 us (33%)
  Pallas kernels  17.1 us (18%)
  other arithmetic  7.8 us (8%)
  between operations  1.03 us (1%)
    all_to_all x1, waiting for transfers between devices, per_device(): lax.all_to_all(partial_value.reshape(16, -1, width), ('x', 'y'), 0, 0, ti...  13.6 us
    all_to_all x1, starting transfers between devices, per_device(): lax.all_to_all(partial_value.reshape(16, -1, width), ('x', 'y'), 0, 0, ti...  11.2 us
    ppermute x5, waiting for transfers between devices, off_chip(): return lax.ppermute(value, SPACE + ('y',), between)  10.6 us
    ppermute x5, starting transfers between devices, off_chip(): return lax.ppermute(value, SPACE + ('y',), between)  9.05 us
    pallas_call x2, Pallas kernels, far_half(): pl.pallas_call(functools.partial(far_kernel, ranks=ranks), out_shape=jax....  8.22 us
    pallas_call x17, Pallas kernels, small_call(): pl.pallas_call(kernel, out_shape=outs, in_specs=[inside] * len(operands),...  5.8 us
    all_to_all x1, waiting for transfers between devices, per_device(): arrived = lax.all_to_all(twice, ('zh', 'zl'), 0, 0, tiled=True)  5.45 us
    all_to_all x1, starting transfers between devices, per_device(): arrived = lax.all_to_all(twice, ('zh', 'zl'), 0, 0, tiled=True)  4.85 us
  transfers between devices with their start and end apart: 19, of which 13 were waited for; matrix products, arithmetic and copies ran while one was open for 8% of the time, Pallas kernels for 9%

profile of v7, /device:TPU:32, one launch (start us, length us, event | category | flops | bytes accessed | tf_op | source)
XLA Modules:
  0.0 93.9 jit_solution(6561828012281629088)
XLA Ops:
  0.6 0.0 copy-start
  0.7 4.4 %far_half.3 = bf16[4,4,4,16,512]{4,3,2,1,0:T(8,128)(2,1)S(1)} custom-call(s32[1]{0:T(128)} %bitcast.7.core_ref, s32[64]{0:T(128)} %bitcast.47, s32[64]{0:T(128)} %bitcast.49, bf16[4,64,512]{2,1,0:T(8,128)(2,1)} %hist_ref.3, bf16[16,2,160,512]{3,2,1,0:T(8,128)(2,1)} %bitcast.43, bf16[16,2,160,512]{3,2,1,0:T(8,128)(2,1)} %bitcast.45), custom_call_target="tpu_custom_call" | custom-call | flops 838860800 | bytes 6291456 | tf_op jit(solution)/shard_map/far_half/pallas_call | solution.py:99
  5.1 0.1 collective-permute-start
  5.2 0.5 collective-permute-start.2
  5.7 0.1 collective-permute-start.3
  5.8 1.7 %collective-permute-start.1 = (bf16[64,512]{1,0:T(8,128)(2,1)S(1)}, bf16[64,512]{1,0:T(8,128)(2,1)S(1)}, u32[]{:S(2)}, u32[]{:S(2)}) collective-permute-start(bf16[64,512]{1,0:T(8,128)(2,1)S(1)} %slice_bitcast_fusion.2), channel_id=1, source_target_pairs={{0,1},{1,2},{2,3},{3,4},{4,5},{5,6},{6,7},{7,0},{8,9},{9,10},{10,1... | collective-permute-start | bytes 196616 | tf_op jit(solution)/shard_map/ppermute | solution.py:344
  7.4 3.8 %far_half.2.mine_ref = bf16[4,4,4,16,512]{4,3,2,1,0:T(8,128)(2,1)S(1)} custom-call(s32[1]{0:T(128)} %bitcast.2.core_ref, s32[64]{0:T(128)} %bitcast.48, s32[64]{0:T(128)} %bitcast.50, bf16[4,64,512]{2,1,0:T(8,128)(2,1)} %hist_ref.3, bf16[16,2,160,512]{3,2,1,0:T(8,128)(2,1)} %bitcast.44, bf16[16,2,160,512]{3,2,1,0:T(8,128)(2,1)} %bitcast.46), custom_call_target="tpu_custom_call" | custom-call | flops 838860800 | bytes 6291456 | tf_op jit(solution)/shard_map/far_half/pallas_call | solution.py:99
  11.3 0.0 collective-permute-done.came_ref
  11.3 1.1 %halves_sum.1 = bf16[4,4,4,16,512]{4,3,2,1,0:T(8,128)(2,1)} custom-call(bf16[4,4,4,16,512]{4,3,2,1,0:T(8,128)(2,1)S(1)} %far_half.2.mine_ref, bf16[4,4,4,16,512]{4,3,2,1,0:T(8,128)(2,1)S(1)} %collective-permute-done.came_ref), custom_call_target="tpu_custom_call" | custom-call | flops 524288 | bytes 3145728 | tf_op jit(solution)/shard_map/halves_sum/pallas_call | solution.py:140
  12.3 11.2 %all-to-all-start = ((bf16[16,64,512]{2,1,0:T(8,128)(2,1)}), bf16[16,64,512]{2,1,0:T(8,128)(2,1)S(1)}, u32[]{:S(2)}, u32[]{:S(2)}) async-start(bf16[16,64,512]{2,1,0:T(8,128)(2,1)} %bitcast.8), calls=%async_computation | async-start | bytes 2097152 | tf_op jit(solution)/shard_map/all_to_all | solution.py:343
  23.6 1.5 %slice_bitcast_fusion.1 = (bf16[512,512]{1,0:T(8,128)(2,1)S(1)}, bf16[512,512]{1,0:T(8,128)(2,1)S(1)}) fusion(bf16[3,512,512]{2,1,0:T(8,128)(2,1)} %param.13, pred[]{:T(512)S(6)} %eq.28), kind=kLoop, calls=%fused_computation.2 | loop fusion | flops 262144 | bytes 2621441 | tf_op jit(solution)/shard_map/squeeze | solution.py:357
  25.1 0.0 slice-start
  25.1 2.2 %multiply_convert_fusion = (bf16[512,512]{1,0:T(8,128)(2,1)}, bf16[512,512]{1,0:T(8,128)(2,1)S(1)}) fusion(f32[512]{0:T(512)S(1)} %broadcast_divide_fusion, bf16[3,512,512]{2,1,0:T(8,128)(2,1)} %param.13, pred[]{:T(512)S(6)} %eq.28, pred[]{:T(512)S(6)} %or.7), kind=kLoop, calls=%fused_computation | loop fusion | flops 1310720 | bytes 2099202 | tf_op jit(solution)/shard_map/convert_element_type | solution.py:359
  27.3 0.8 dynamic-slice_multiply_fusion.given_ref
  28.1 0.0 collective-permute-done.3
  28.1 0.0 collective-permute-done.2
  28.1 13.6 %all-to-all-done.in_ref = bf16[16,64,512]{2,1,0:T(8,128)(2,1)S(1)} async-done(((bf16[16,64,512]{2,1,0:T(8,128)(2,1)}), bf16[16,64,512]{2,1,0:T(8,128)(2,1)S(1)}, u32[]{:S(2)}, u32[]{:S(2)}) %all-to-all-start) | async-done | bytes 1048608 | tf_op jit(solution)/shard_map/all_to_all | solution.py:343
  41.7 0.0 collective-permute-start.7
  41.7 0.8 plane_sum.1
  42.5 4.8 %all-to-all-start.1 = ((bf16[8,16,512]{2,1,0:T(8,128)(2,1)}), bf16[8,16,512]{2,1,0:T(8,128)(2,1)S(1)}, u32[]{:S(2)}, u32[]{:S(2)}) async-start(bf16[8,16,512]{2,1,0:T(8,128)(2,1)} %bitcast.13), calls=%async_computation.1 | async-start | bytes 262144 | tf_op jit(solution)/shard_map/all_to_all | solution.py:383
  47.3 0.7 pad_maximum_fusion.shifted_ref
  48.1 1.5 %slice_bitcast_fusion = (bf16[512,512]{1,0:T(8,128)(2,1)S(1)}, bf16[512,512]{1,0:T(8,128)(2,1)S(1)}, bf16[512,512]{1,0:T(8,128)(2,1)S(1)}) fusion(bf16[3,512,512]{2,1,0:T(8,128)(2,1)} %collective-permute-done.2, pred[]{:T(512)S(6)} %eq.31, pred[]{:T(512)S(6)} %or.8), kind=kLoop, calls=%fused_computation.1 | loop fusion | flops 786432 | bytes 3145730 | tf_op jit(solution)/shard_map/squeeze | solution.py:369
  49.5 5.5 %all-to-all-done.1.arrived_ref = bf16[8,16,512]{2,1,0:T(8,128)(2,1)S(1)} async-done(((bf16[8,16,512]{2,1,0:T(8,128)(2,1)}), bf16[8,16,512]{2,1,0:T(8,128)(2,1)S(1)}, u32[]{:S(2)}, u32[]{:S(2)}) %all-to-all-start.1) | async-done | bytes 131104 | tf_op jit(solution)/shard_map/all_to_all | solution.py:383
  55.0 0.1 collective-permute-start.4
  55.1 2.3 %collective-permute-start.5 = (bf16[16,512]{1,0:T(8,128)(2,1)S(1)}, bf16[16,512]{1,0:T(8,128)(2,1)S(1)}, u32[]{:S(2)}, u32[]{:S(2)}) collective-permute-start(bf16[16,512]{1,0:T(8,128)(2,1)S(1)} %get-tuple-element.32.value_ref), channel_id=1, source_target_pairs={{0,1},{1,0},{2,3},{3,2},{248,249},{249,248},{250,251},{251,250},{8... | collective-permute-start | bytes 49160 | tf_op jit(solution)/shard_map/ppermute | solution.py:380
  57.4 0.4 shard_map.96.part_ref
  57.8 2.7 %collective-permute-done.5.got_ref = bf16[16,512]{1,0:T(8,128)(2,1)S(1)} collective-permute-done((bf16[16,512]{1,0:T(8,128)(2,1)S(1)}, bf16[16,512]{1,0:T(8,128)(2,1)S(1)}, u32[]{:S(2)}, u32[]{:S(2)}) %collective-permute-start.5) | collective-permute-done | bytes 16416 | tf_op jit(solution)/shard_map/ppermute | solution.py:380
  60.5 0.2 shard_map.97.value_ref
  60.7 0.0 collective-permute-start.6
  60.7 0.2 shard_map.98.part_ref
  61.0 0.9 %collective-permute-done.6.beside_ref = bf16[16,512]{1,0:T(8,128)(2,1)S(1)} collective-permute-done((bf16[16,512]{1,0:T(8,128)(2,1)S(1)}, bf16[16,512]{1,0:T(8,128)(2,1)S(1)}, u32[]{:S(2)}, u32[]{:S(2)}) %collective-permute-start.6) | collective-permute-done | bytes 16416 | tf_op jit(solution)/shard_map/ppermute | solution.py:397
  61.9 0.2 shard_map.99
  62.1 2.2 %collective-permute-start.8 = (bf16[2,16,512]{2,1,0:T(8,128)(2,1)S(1)}, bf16[2,16,512]{2,1,0:T(8,128)(2,1)S(1)}, u32[]{:S(2)}, u32[]{:S(2)}) collective-permute-start(bf16[2,16,512]{2,1,0:T(8,128)(2,1)S(1)} %get-tuple-element.36.pack_ref), channel_id=1, source_target_pairs={{0,1},{1,0},{2,3},{3,2},{248,249},{249,248},{250,251},{251,250},{8... | collective-permute-start | bytes 98312 | tf_op jit(solution)/shard_map/ppermute | solution.py:380
  64.4 0.0 collective-permute-done.7
  64.4 1.1 %broadcast_select_fusion.back_ref = bf16[512,512]{1,0:T(8,128)(2,1)S(1)} fusion(bf16[512,512]{1,0:T(8,128)(2,1)} %collective-permute-done.7, pred[]{:T(512)S(6)} %or.7), kind=kLoop, calls=%fused_computation.7 | loop fusion | flops 262144 | bytes 1048577 | tf_op jit(solution)/shard_map/jit(_where)/select_n | solution.py:385
  65.5 0.2 shard_map.100.known_ref
  65.7 1.9 %collective-permute-done.8.got_ref = bf16[2,16,512]{2,1,0:T(8,128)(2,1)S(1)} collective-permute-done((bf16[2,16,512]{2,1,0:T(8,128)(2,1)S(1)}, bf16[2,16,512]{2,1,0:T(8,128)(2,1)S(1)}, u32[]{:S(2)}, u32[]{:S(2)}) %collective-permute-start.8) | collective-permute-done | bytes 32800 | tf_op jit(solution)/shard_map/ppermute | solution.py:380
  67.6 0.2 shard_map.101.next_ref
  67.9 0.5 shard_map.102
  68.4 0.7 collective-permute-done.9.got_ref
  69.1 0.8 shard_map.103
  69.9 2.2 %collective-permute-start.10 = (bf16[2,16,512]{2,1,0:T(8,128)(2,1)S(1)}, bf16[2,16,512]{2,1,0:T(8,128)(2,1)S(1)}, u32[]{:S(2)}, u32[]{:S(2)}) collective-permute-start(bf16[2,16,512]{2,1,0:T(8,128)(2,1)S(1)} %get-tuple-element.44.pack_ref), channel_id=1, source_target_pairs={{0,1},{1,0},{2,3},{3,2},{248,249},{249,248},{250,251},{251,250},{8... | collective-permute-start | bytes 98312 | tf_op jit(solution)/shard_map/ppermute | solution.py:380
  72.1 0.2 shard_map.104.known_ref
  72.4 3.0 %collective-permute-done.10.got_ref = bf16[2,16,512]{2,1,0:T(8,128)(2,1)S(1)} collective-permute-done((bf16[2,16,512]{2,1,0:T(8,128)(2,1)S(1)}, bf16[2,16,512]{2,1,0:T(8,128)(2,1)S(1)}, u32[]{:S(2)}, u32[]{:S(2)}) %collective-permute-start.10) | collective-permute-done | bytes 32800 | tf_op jit(solution)/shard_map/ppermute | solution.py:380
  75.4 0.2 shard_map.105.next_ref
  75.6 0.2 collective-permute-start.11
  75.8 0.5 shard_map.106
  76.3 0.7 collective-permute-done.11.got_ref
  77.0 0.8 shard_map.107
  77.8 2.2 %collective-permute-start.12 = (bf16[2,16,512]{2,1,0:T(8,128)(2,1)S(1)}, bf16[2,16,512]{2,1,0:T(8,128)(2,1)S(1)}, u32[]{:S(2)}, u32[]{:S(2)}) collective-permute-start(bf16[2,16,512]{2,1,0:T(8,128)(2,1)S(1)} %get-tuple-element.48.pack_ref), channel_id=1, source_target_pairs={{0,1},{1,0},{2,3},{3,2},{248,249},{249,248},{250,251},{251,250},{8... | collective-permute-start | bytes 98312 | tf_op jit(solution)/shard_map/ppermute | solution.py:380
  80.1 0.2 shard_map.108.known_ref
  80.3 3.0 %collective-permute-done.12.got_ref = bf16[2,16,512]{2,1,0:T(8,128)(2,1)S(1)} collective-permute-done((bf16[2,16,512]{2,1,0:T(8,128)(2,1)S(1)}, bf16[2,16,512]{2,1,0:T(8,128)(2,1)S(1)}, u32[]{:S(2)}, u32[]{:S(2)}) %collective-permute-start.12) | collective-permute-done | bytes 32800 | tf_op jit(solution)/shard_map/ppermute | solution.py:380
  83.3 0.2 shard_map.109.next_ref
  83.5 0.4 shard_map.110.part_ref
  83.9 0.8 collective-permute-done.13.got_ref
  84.7 0.2 shard_map.111.own_ref
  85.0 0.4 collective-permute-start.16
  85.4 1.6 %collective-permute-start.15 = (f32[16,512]{1,0:T(8,128)S(1)}, f32[16,512]{1,0:T(8,128)S(1)}, u32[]{:S(2)}, u32[]{:S(2)}) collective-permute-start(f32[16,512]{1,0:T(8,128)S(1)} %shard_map.111.own_ref), channel_id=1, source_target_pairs={{0,1},{1,2},{2,3},{3,0},{4,5},{5,6},{6,7},{7,4},{8,9},{9,10},{10,1... | collective-permute-start | bytes 98312 | tf_op jit(solution)/shard_map/ppermute | solution.py:426
  87.0 1.5 %collective-permute-start.14 = (f32[16,512]{1,0:T(8,128)S(1)}, f32[16,512]{1,0:T(8,128)S(1)}, u32[]{:S(2)}, u32[]{:S(2)}) collective-permute-start(f32[16,512]{1,0:T(8,128)S(1)} %shard_map.111.own_ref), channel_id=1, source_target_pairs={{0,2},{1,3},{2,0},{3,1},{4,6},{5,7},{6,4},{7,5},{8,10},{9,11},{10,... | collective-permute-start | bytes 98312 | tf_op jit(solution)/shard_map/ppermute | solution.py:426
  88.5 0.1 pad_add_fusion.where_ref
  88.6 0.3 collective-permute-done.16.third_ref
  88.9 1.6 %collective-permute-done.15.first_ref = f32[16,512]{1,0:T(8,128)S(1)} collective-permute-done((f32[16,512]{1,0:T(8,128)S(1)}, f32[16,512]{1,0:T(8,128)S(1)}, u32[]{:S(2)}, u32[]{:S(2)}) %collective-permute-start.15) | collective-permute-done | bytes 32800 | tf_op jit(solution)/shard_map/ppermute | solution.py:426
  90.5 1.9 %collective-permute-done.14.second_ref = f32[16,512]{1,0:T(8,128)S(1)} collective-permute-done((f32[16,512]{1,0:T(8,128)S(1)}, f32[16,512]{1,0:T(8,128)S(1)}, u32[]{:S(2)}, u32[]{:S(2)}) %collective-permute-start.14) | collective-permute-done | bytes 32800 | tf_op jit(solution)/shard_map/ppermute | solution.py:426
  92.4 1.3 %finish.1 = (f32[64,512]{1,0:T(8,128)}, bf16[4,64,512]{2,1,0:T(8,128)(2,1)}) custom-call(s32[2]{0:T(128)S(1)} %pad_add_fusion.where_ref, f32[16,512]{1,0:T(8,128)S(1)} %shard_map.111.own_ref, f32[16,512]{1,0:T(8,128)S(1)} %collective-permute-done.14.second_ref, f32[16,512]{1,0:T(8,128)S(1)} %collective-permute-done.15.first_ref, ...), custom_call_target="tpu_custom_call", output_to_operand_aliasing={{1}: (6, {})} | custom-call | tf_op jit(solution)/shard_map/finish/pallas_call | solution.py:205
  (12 shorter events, 0.1 us)
Async XLA Ops:
  0.6 5.0 %copy-start.1 = (f32[512]{0:T(512)S(1)}, f32[512]{0:T(512)}, u32[]{:S(2)}) copy-start(f32[512]{0:T(512)} %param.14) | copy-start | bytes 6148
  0.6 5.1 %copy-start = (bf16[4,64,512]{2,1,0:T(8,128)(2,1)S(1)}, bf16[4,64,512]{2,1,0:T(8,128)(2,1)}, u32[]{:S(2)}) copy-start(bf16[4,64,512]{2,1,0:T(8,128)(2,1)} %hist_ref.3) | copy-start | bytes 786436
  5.1 6.2 %collective-permute-start = (bf16[4,4,4,16,512]{4,3,2,1,0:T(8,128)(2,1)S(1)}, bf16[4,4,4,16,512]{4,3,2,1,0:T(8,128)(2,1)S(1)}, u32[]{:S(2)}, u32[]{:S(2)}) collective-permute-start(bf16[4,4,4,16,512]{4,3,2,1,0:T(8,128)(2,1)S(1)} %far_half.3), channel_id=1, source_target_pairs={{0,8},{8,0},{1,9},{9,1},{2,10},{10,2},{3,11},{11,3},{4,12},{12,4},... | collective-permute-start | bytes 3145736 | tf_op jit(solution)/shard_map/ppermute | solution.py:340
  5.2 22.9 %collective-permute-start.2 = (bf16[3,512,512]{2,1,0:T(8,128)(2,1)}, bf16[3,512,512]{2,1,0:T(8,128)(2,1)}, u32[]{:S(2)}, u32[]{:S(2)}) collective-permute-start(bf16[3,512,512]{2,1,0:T(8,128)(2,1)} %param.13), channel_id=1, source_target_pairs={{0,8},{8,0},{1,9},{9,1},{2,10},{10,2},{3,11},{11,3},{4,12},{12,4},... | collective-permute-start | bytes 4718600 | tf_op jit(solution)/shard_map/ppermute | solution.py:345
  5.7 22.4 %collective-permute-start.3 = (f32[1,512]{1,0:T(1,128)S(1)}, f32[1,512]{1,0:T(1,128)S(1)}, u32[]{:S(2)}, u32[]{:S(2)}) collective-permute-start(f32[1,512]{1,0:T(1,128)S(1)} %bitcast.51), channel_id=1, source_target_pairs={{0,8},{8,0},{1,9},{9,1},{2,10},{10,2},{3,11},{11,3},{4,12},{12,4},... | collective-permute-start | bytes 6152 | tf_op jit(solution)/shard_map/ppermute | solution.py:346
  5.8 22.3 %collective-permute-start.1 = (bf16[64,512]{1,0:T(8,128)(2,1)S(1)}, bf16[64,512]{1,0:T(8,128)(2,1)S(1)}, u32[]{:S(2)}, u32[]{:S(2)}) collective-permute-start(bf16[64,512]{1,0:T(8,128)(2,1)S(1)} %slice_bitcast_fusion.2), channel_id=1, source_target_pairs={{0,1},{1,2},{2,3},{3,4},{4,5},{5,6},{6,7},{7,0},{8,9},{9,10},{10,1... | collective-permute-start | bytes 196616 | tf_op jit(solution)/shard_map/ppermute | solution.py:344
  12.3 29.3 %all-to-all-start = ((bf16[16,64,512]{2,1,0:T(8,128)(2,1)}), bf16[16,64,512]{2,1,0:T(8,128)(2,1)S(1)}, u32[]{:S(2)}, u32[]{:S(2)}) async-start(bf16[16,64,512]{2,1,0:T(8,128)(2,1)} %bitcast.8), calls=%async_computation | async-start | bytes 2097152 | tf_op jit(solution)/shard_map/all_to_all | solution.py:343
  25.1 22.3 %slice-start = ((bf16[4,64,512]{2,1,0:T(8,128)(2,1)}), bf16[3,64,512]{2,1,0:T(8,128)(2,1)S(1)}, s32[]{:S(2)}) async-start(bf16[4,64,512]{2,1,0:T(8,128)(2,1)} %hist_ref.3), calls=%async_computation.2 | async-start | bytes 393216 | tf_op jit(solution)/shard_map/slice | solution.py:370
  41.7 22.7 %collective-permute-start.7 = (bf16[512,512]{1,0:T(8,128)(2,1)}, bf16[512,512]{1,0:T(8,128)(2,1)}, u32[]{:S(2)}, u32[]{:S(2)}) collective-permute-start(bf16[512,512]{1,0:T(8,128)(2,1)} %get-tuple-element.37), channel_id=1, source_target_pairs={{0,1},{1,0},{2,3},{3,2},{248,249},{249,248},{250,251},{251,250},{8... | collective-permute-start | bytes 1572872 | tf_op jit(solution)/shard_map/ppermute | solution.py:380
  42.5 12.5 %all-to-all-start.1 = ((bf16[8,16,512]{2,1,0:T(8,128)(2,1)}), bf16[8,16,512]{2,1,0:T(8,128)(2,1)S(1)}, u32[]{:S(2)}, u32[]{:S(2)}) async-start(bf16[8,16,512]{2,1,0:T(8,128)(2,1)} %bitcast.13), calls=%async_computation.1 | async-start | bytes 262144 | tf_op jit(solution)/shard_map/all_to_all | solution.py:383
  55.0 2.4 %collective-permute-start.4 = (f32[16,512]{1,0:T(8,128)S(1)}, f32[16,512]{1,0:T(8,128)S(1)}, u32[]{:S(2)}, u32[]{:S(2)}) collective-permute-start(f32[16,512]{1,0:T(8,128)S(1)} %get-tuple-element.33.c_ref), channel_id=1, source_target_pairs={{0,8},{8,0},{1,9},{9,1},{2,10},{10,2},{3,11},{11,3},{4,12},{12,4},... | collective-permute-start | bytes 98312 | tf_op jit(solution)/shard_map/ppermute | solution.py:394
  55.1 5.4 %collective-permute-start.5 = (bf16[16,512]{1,0:T(8,128)(2,1)S(1)}, bf16[16,512]{1,0:T(8,128)(2,1)S(1)}, u32[]{:S(2)}, u32[]{:S(2)}) collective-permute-start(bf16[16,512]{1,0:T(8,128)(2,1)S(1)} %get-tuple-element.32.value_ref), channel_id=1, source_target_pairs={{0,1},{1,0},{2,3},{3,2},{248,249},{249,248},{250,251},{251,250},{8... | collective-permute-start | bytes 49160 | tf_op jit(solution)/shard_map/ppermute | solution.py:380
  60.7 1.2 %collective-permute-start.6 = (bf16[16,512]{1,0:T(8,128)(2,1)S(1)}, bf16[16,512]{1,0:T(8,128)(2,1)S(1)}, u32[]{:S(2)}, u32[]{:S(2)}) collective-permute-start(bf16[16,512]{1,0:T(8,128)(2,1)S(1)} %shard_map.97.value_ref), channel_id=1, source_target_pairs={{0,8},{8,0},{1,9},{9,1},{2,10},{10,2},{3,11},{11,3},{4,12},{12,4},... | collective-permute-start | bytes 49160 | tf_op jit(solution)/shard_map/ppermute | solution.py:397
  62.1 5.5 %collective-permute-start.8 = (bf16[2,16,512]{2,1,0:T(8,128)(2,1)S(1)}, bf16[2,16,512]{2,1,0:T(8,128)(2,1)S(1)}, u32[]{:S(2)}, u32[]{:S(2)}) collective-permute-start(bf16[2,16,512]{2,1,0:T(8,128)(2,1)S(1)} %get-tuple-element.36.pack_ref), channel_id=1, source_target_pairs={{0,1},{1,0},{2,3},{3,2},{248,249},{249,248},{250,251},{251,250},{8... | collective-permute-start | bytes 98312 | tf_op jit(solution)/shard_map/ppermute | solution.py:380
  67.8 1.2 %collective-permute-start.9 = (bf16[2,16,512]{2,1,0:T(8,128)(2,1)S(1)}, bf16[2,16,512]{2,1,0:T(8,128)(2,1)S(1)}, u32[]{:S(2)}, u32[]{:S(2)}) collective-permute-start(bf16[2,16,512]{2,1,0:T(8,128)(2,1)S(1)} %shard_map.101.next_ref), channel_id=1, source_target_pairs={{0,8},{8,0},{1,9},{9,1},{2,10},{10,2},{3,11},{11,3},{4,12},{12,4},... | collective-permute-start | bytes 98312 | tf_op jit(solution)/shard_map/ppermute | solution.py:406
  69.9 5.5 %collective-permute-start.10 = (bf16[2,16,512]{2,1,0:T(8,128)(2,1)S(1)}, bf16[2,16,512]{2,1,0:T(8,128)(2,1)S(1)}, u32[]{:S(2)}, u32[]{:S(2)}) collective-permute-start(bf16[2,16,512]{2,1,0:T(8,128)(2,1)S(1)} %get-tuple-element.44.pack_ref), channel_id=1, source_target_pairs={{0,1},{1,0},{2,3},{3,2},{248,249},{249,248},{250,251},{251,250},{8... | collective-permute-start | bytes 98312 | tf_op jit(solution)/shard_map/ppermute | solution.py:380
  75.6 1.4 %collective-permute-start.11 = (bf16[2,16,512]{2,1,0:T(8,128)(2,1)S(1)}, bf16[2,16,512]{2,1,0:T(8,128)(2,1)S(1)}, u32[]{:S(2)}, u32[]{:S(2)}) collective-permute-start(bf16[2,16,512]{2,1,0:T(8,128)(2,1)S(1)} %shard_map.105.next_ref), channel_id=1, source_target_pairs={{0,8},{8,0},{1,9},{9,1},{2,10},{10,2},{3,11},{11,3},{4,12},{12,4},... | collective-permute-start | bytes 98312 | tf_op jit(solution)/shard_map/ppermute | solution.py:406
  77.8 5.5 %collective-permute-start.12 = (bf16[2,16,512]{2,1,0:T(8,128)(2,1)S(1)}, bf16[2,16,512]{2,1,0:T(8,128)(2,1)S(1)}, u32[]{:S(2)}, u32[]{:S(2)}) collective-permute-start(bf16[2,16,512]{2,1,0:T(8,128)(2,1)S(1)} %get-tuple-element.48.pack_ref), channel_id=1, source_target_pairs={{0,1},{1,0},{2,3},{3,2},{248,249},{249,248},{250,251},{251,250},{8... | collective-permute-start | bytes 98312 | tf_op jit(solution)/shard_map/ppermute | solution.py:380
  83.5 1.2 %collective-permute-start.13 = (bf16[2,16,512]{2,1,0:T(8,128)(2,1)S(1)}, bf16[2,16,512]{2,1,0:T(8,128)(2,1)S(1)}, u32[]{:S(2)}, u32[]{:S(2)}) collective-permute-start(bf16[2,16,512]{2,1,0:T(8,128)(2,1)S(1)} %shard_map.109.next_ref), channel_id=1, source_target_pairs={{0,8},{8,0},{1,9},{9,1},{2,10},{10,2},{3,11},{11,3},{4,12},{12,4},... | collective-permute-start | bytes 98312 | tf_op jit(solution)/shard_map/ppermute | solution.py:406
  85.0 3.9 %collective-permute-start.16 = (f32[16,512]{1,0:T(8,128)S(1)}, f32[16,512]{1,0:T(8,128)S(1)}, u32[]{:S(2)}, u32[]{:S(2)}) collective-permute-start(f32[16,512]{1,0:T(8,128)S(1)} %shard_map.111.own_ref), channel_id=1, source_target_pairs={{0,3},{1,0},{2,1},{3,2},{4,7},{5,4},{6,5},{7,6},{8,11},{9,8},{10,9... | collective-permute-start | bytes 98312 | tf_op jit(solution)/shard_map/ppermute | solution.py:426
  85.4 5.1 %collective-permute-start.15 = (f32[16,512]{1,0:T(8,128)S(1)}, f32[16,512]{1,0:T(8,128)S(1)}, u32[]{:S(2)}, u32[]{:S(2)}) collective-permute-start(f32[16,512]{1,0:T(8,128)S(1)} %shard_map.111.own_ref), channel_id=1, source_target_pairs={{0,1},{1,2},{2,3},{3,0},{4,5},{5,6},{6,7},{7,4},{8,9},{9,10},{10,1... | collective-permute-start | bytes 98312 | tf_op jit(solution)/shard_map/ppermute | solution.py:426
  87.0 5.4 %collective-permute-start.14 = (f32[16,512]{1,0:T(8,128)S(1)}, f32[16,512]{1,0:T(8,128)S(1)}, u32[]{:S(2)}, u32[]{:S(2)}) collective-permute-start(f32[16,512]{1,0:T(8,128)S(1)} %shard_map.111.own_ref), channel_id=1, source_target_pairs={{0,2},{1,3},{2,0},{3,1},{4,6},{5,7},{6,4},{7,5},{8,10},{9,11},{10,... | collective-permute-start | bytes 98312 | tf_op jit(solution)/shard_map/ppermute | solution.py:426

commit v8 on v7

--- a/solution.py
+++ b/solution.py
@@ -154,24 +154,37 @@
     )(mine, came)
 
 
-def plane_kernel(in_ref, out_ref):
-    rows = 16
-    for first in range(0, in_ref.shape[1], rows):
-        part = slice(first, first + rows)
+def plane_kernel(in_ref, out_ref, held_ref, sem):
+    copies = []
+    pieces, rows, _ = held_ref.shape
+    for piece in range(pieces):
+        part = slice(piece * rows, (piece + 1) * rows)
         total = in_ref[0, part].astype(jnp.float32)
         for source in range(1, in_ref.shape[0]):
             total = total + in_ref[source, part].astype(jnp.float32)
-        for copy in range(out_ref.shape[0]):
-            out_ref[copy, part] = total.astype(out_ref.dtype)
+        held_ref[piece] = total.astype(held_ref.dtype)
+        for twin in range(out_ref.shape[0]):
+            copies.append(
+                pltpu.make_async_copy(
+                    held_ref.at[piece], out_ref.at[twin, part], sem.at[twin, piece]
+                )
+            )
+            copies[-1].start()
+    for copy in copies:
+        copy.wait()
 
 
 def plane_sum(arrived, copies):
-    inside = pl.BlockSpec(memory_space=pltpu.VMEM)
+    pieces = 4
     return pl.pallas_call(
         plane_kernel,
         out_shape=jax.ShapeDtypeStruct((copies, *arrived.shape[1:]), arrived.dtype),
-        in_specs=[inside],
-        out_specs=inside,
+        in_specs=[pl.BlockSpec(memory_space=pltpu.VMEM)],
+        out_specs=pl.BlockSpec(memory_space=pltpu.HBM),
+        scratch_shapes=[
+            pltpu.VMEM((pieces, arrived.shape[1] // pieces, arrived.shape[2]), arrived.dtype),
+            pltpu.SemaphoreType.DMA((copies, pieces)),
+        ],
         compiler_params=pltpu.CompilerParams(vmem_limit_bytes=4 << 20),
         cost_estimate=pl.CostEstimate(
             flops=arrived.size, bytes_accessed=2 * arrived.size, transcendentals=0

time: 94.3 us -> 94.4 us (level)
  no operation moved by 1% of the time
where the time goes in v8:
time: 94.4 us; the launch traced here: 93.9 us
  waiting for transfers between devices  36.6 us (39%)
  starting transfers between devices  31.3 us (33%)
  Pallas kernels  17.2 us (18%)
  other arithmetic  7.8 us (8%)
  between operations  1.03 us (1%)
    all_to_all x1, waiting for transfers between devices, per_device(): lax.all_to_all(partial_value.reshape(16, -1, width), ('x', 'y'), 0, 0, ti...  13.6 us
    all_to_all x1, starting transfers between devices, per_device(): lax.all_to_all(partial_value.reshape(16, -1, width), ('x', 'y'), 0, 0, ti...  11.2 us
    ppermute x5, waiting for transfers between devices, off_chip(): return lax.ppermute(value, SPACE + ('y',), between)  10.6 us
    ppermute x5, starting transfers between devices, off_chip(): return lax.ppermute(value, SPACE + ('y',), between)  9.05 us
    pallas_call x2, Pallas kernels, far_half(): pl.pallas_call(functools.partial(far_kernel, ranks=ranks), out_shape=jax....  8.22 us
    pallas_call x17, Pallas kernels, small_call(): pl.pallas_call(kernel, out_shape=outs, in_specs=[inside] * len(operands),...  5.8 us
    all_to_all x1, waiting for transfers between devices, per_device(): arrived = lax.all_to_all(twice, ('zh', 'zl'), 0, 0, tiled=True)  5.45 us
    all_to_all x1, starting transfers between devices, per_device(): arrived = lax.all_to_all(twice, ('zh', 'zl'), 0, 0, tiled=True)  4.86 us
  transfers between devices with their start and end apart: 19, of which 13 were waited for; matrix products, arithmetic and copies ran while one was open for 8% of the time, Pallas kernels for 9%

profile of v8, /device:TPU:32, one launch (start us, length us, event | category | flops | bytes accessed | tf_op | source)
XLA Modules:
  0.0 93.9 jit_solution(11375357669603963183)
XLA Ops:
  0.6 0.0 copy-start
  0.7 4.4 %far_half.3 = bf16[4,4,4,16,512]{4,3,2,1,0:T(8,128)(2,1)S(1)} custom-call(s32[1]{0:T(128)} %bitcast.7.core_ref, s32[64]{0:T(128)} %bitcast.47, s32[64]{0:T(128)} %bitcast.49, bf16[4,64,512]{2,1,0:T(8,128)(2,1)} %hist_ref.3, bf16[16,2,160,512]{3,2,1,0:T(8,128)(2,1)} %bitcast.43, bf16[16,2,160,512]{3,2,1,0:T(8,128)(2,1)} %bitcast.45), custom_call_target="tpu_custom_call" | custom-call | flops 838860800 | bytes 6291456 | tf_op jit(solution)/shard_map/far_half/pallas_call | solution.py:99
  5.1 0.1 collective-permute-start
  5.2 0.5 collective-permute-start.2
  5.7 0.1 collective-permute-start.3
  5.8 1.7 %collective-permute-start.1 = (bf16[64,512]{1,0:T(8,128)(2,1)S(1)}, bf16[64,512]{1,0:T(8,128)(2,1)S(1)}, u32[]{:S(2)}, u32[]{:S(2)}) collective-permute-start(bf16[64,512]{1,0:T(8,128)(2,1)S(1)} %slice_bitcast_fusion.2), channel_id=1, source_target_pairs={{0,1},{1,2},{2,3},{3,4},{4,5},{5,6},{6,7},{7,0},{8,9},{9,10},{10,1... | collective-permute-start | bytes 196616 | tf_op jit(solution)/shard_map/ppermute | solution.py:357
  7.4 3.8 %far_half.2.mine_ref = bf16[4,4,4,16,512]{4,3,2,1,0:T(8,128)(2,1)S(1)} custom-call(s32[1]{0:T(128)} %bitcast.2.core_ref, s32[64]{0:T(128)} %bitcast.48, s32[64]{0:T(128)} %bitcast.50, bf16[4,64,512]{2,1,0:T(8,128)(2,1)} %hist_ref.3, bf16[16,2,160,512]{3,2,1,0:T(8,128)(2,1)} %bitcast.44, bf16[16,2,160,512]{3,2,1,0:T(8,128)(2,1)} %bitcast.46), custom_call_target="tpu_custom_call" | custom-call | flops 838860800 | bytes 6291456 | tf_op jit(solution)/shard_map/far_half/pallas_call | solution.py:99
  11.3 0.0 collective-permute-done.came_ref
  11.3 1.1 %halves_sum.1 = bf16[4,4,4,16,512]{4,3,2,1,0:T(8,128)(2,1)} custom-call(bf16[4,4,4,16,512]{4,3,2,1,0:T(8,128)(2,1)S(1)} %far_half.2.mine_ref, bf16[4,4,4,16,512]{4,3,2,1,0:T(8,128)(2,1)S(1)} %collective-permute-done.came_ref), custom_call_target="tpu_custom_call" | custom-call | flops 524288 | bytes 3145728 | tf_op jit(solution)/shard_map/halves_sum/pallas_call | solution.py:140
  12.3 11.2 %all-to-all-start = ((bf16[16,64,512]{2,1,0:T(8,128)(2,1)}), bf16[16,64,512]{2,1,0:T(8,128)(2,1)S(1)}, u32[]{:S(2)}, u32[]{:S(2)}) async-start(bf16[16,64,512]{2,1,0:T(8,128)(2,1)} %bitcast.8), calls=%async_computation | async-start | bytes 2097152 | tf_op jit(solution)/shard_map/all_to_all | solution.py:356
  23.6 1.5 %slice_bitcast_fusion.1 = (bf16[512,512]{1,0:T(8,128)(2,1)S(1)}, bf16[512,512]{1,0:T(8,128)(2,1)S(1)}) fusion(bf16[3,512,512]{2,1,0:T(8,128)(2,1)} %param.13, pred[]{:T(512)S(6)} %eq.28), kind=kLoop, calls=%fused_computation.2 | loop fusion | flops 262144 | bytes 2621441 | tf_op jit(solution)/shard_map/squeeze | solution.py:370
  25.1 0.0 slice-start
  25.1 2.2 %multiply_convert_fusion = (bf16[512,512]{1,0:T(8,128)(2,1)}, bf16[512,512]{1,0:T(8,128)(2,1)S(1)}) fusion(f32[512]{0:T(512)S(1)} %broadcast_divide_fusion, bf16[3,512,512]{2,1,0:T(8,128)(2,1)} %param.13, pred[]{:T(512)S(6)} %eq.28, pred[]{:T(512)S(6)} %or.7), kind=kLoop, calls=%fused_computation | loop fusion | flops 1310720 | bytes 2099202 | tf_op jit(solution)/shard_map/convert_element_type | solution.py:372
  27.3 0.8 dynamic-slice_multiply_fusion.given_ref
  28.1 0.0 collective-permute-done.3
  28.1 0.0 collective-permute-done.2
  28.1 13.6 %all-to-all-done.in_ref = bf16[16,64,512]{2,1,0:T(8,128)(2,1)S(1)} async-done(((bf16[16,64,512]{2,1,0:T(8,128)(2,1)}), bf16[16,64,512]{2,1,0:T(8,128)(2,1)S(1)}, u32[]{:S(2)}, u32[]{:S(2)}) %all-to-all-start) | async-done | bytes 1048608 | tf_op jit(solution)/shard_map/all_to_all | solution.py:356
  41.7 0.0 collective-permute-start.7
  41.7 0.8 plane_sum.1
  42.5 4.9 %all-to-all-start.1 = ((bf16[8,16,512]{2,1,0:T(8,128)(2,1)}), bf16[8,16,512]{2,1,0:T(8,128)(2,1)S(1)}, u32[]{:S(2)}, u32[]{:S(2)}) async-start(bf16[8,16,512]{2,1,0:T(8,128)(2,1)} %bitcast.13), calls=%async_computation.1 | async-start | bytes 262144 | tf_op jit(solution)/shard_map/all_to_all | solution.py:396
  47.4 0.7 pad_maximum_fusion.shifted_ref
  48.1 1.5 %slice_bitcast_fusion = (bf16[512,512]{1,0:T(8,128)(2,1)S(1)}, bf16[512,512]{1,0:T(8,128)(2,1)S(1)}, bf16[512,512]{1,0:T(8,128)(2,1)S(1)}) fusion(bf16[3,512,512]{2,1,0:T(8,128)(2,1)} %collective-permute-done.2, pred[]{:T(512)S(6)} %eq.31, pred[]{:T(512)S(6)} %or.8), kind=kLoop, calls=%fused_computation.1 | loop fusion | flops 786432 | bytes 3145730 | tf_op jit(solution)/shard_map/squeeze | solution.py:382
  49.6 5.5 %all-to-all-done.1.arrived_ref = bf16[8,16,512]{2,1,0:T(8,128)(2,1)S(1)} async-done(((bf16[8,16,512]{2,1,0:T(8,128)(2,1)}), bf16[8,16,512]{2,1,0:T(8,128)(2,1)S(1)}, u32[]{:S(2)}, u32[]{:S(2)}) %all-to-all-start.1) | async-done | bytes 131104 | tf_op jit(solution)/shard_map/all_to_all | solution.py:396
  55.0 0.1 collective-permute-start.4
  55.1 2.3 %collective-permute-start.5 = (bf16[16,512]{1,0:T(8,128)(2,1)S(1)}, bf16[16,512]{1,0:T(8,128)(2,1)S(1)}, u32[]{:S(2)}, u32[]{:S(2)}) collective-permute-start(bf16[16,512]{1,0:T(8,128)(2,1)S(1)} %get-tuple-element.32.value_ref), channel_id=1, source_target_pairs={{0,1},{1,0},{2,3},{3,2},{248,249},{249,248},{250,251},{251,250},{8... | collective-permute-start | bytes 49160 | tf_op jit(solution)/shard_map/ppermute | solution.py:393
  57.5 0.4 shard_map.96.part_ref
  57.8 2.7 %collective-permute-done.5.got_ref = bf16[16,512]{1,0:T(8,128)(2,1)S(1)} collective-permute-done((bf16[16,512]{1,0:T(8,128)(2,1)S(1)}, bf16[16,512]{1,0:T(8,128)(2,1)S(1)}, u32[]{:S(2)}, u32[]{:S(2)}) %collective-permute-start.5) | collective-permute-done | bytes 16416 | tf_op jit(solution)/shard_map/ppermute | solution.py:393
  60.5 0.2 shard_map.97.value_ref
  60.8 0.2 shard_map.98.part_ref
  61.0 0.9 %collective-permute-done.6.beside_ref = bf16[16,512]{1,0:T(8,128)(2,1)S(1)} collective-permute-done((bf16[16,512]{1,0:T(8,128)(2,1)S(1)}, bf16[16,512]{1,0:T(8,128)(2,1)S(1)}, u32[]{:S(2)}, u32[]{:S(2)}) %collective-permute-start.6) | collective-permute-done | bytes 16416 | tf_op jit(solution)/shard_map/ppermute | solution.py:410
  61.9 0.2 shard_map.99
  62.2 2.2 %collective-permute-start.8 = (bf16[2,16,512]{2,1,0:T(8,128)(2,1)S(1)}, bf16[2,16,512]{2,1,0:T(8,128)(2,1)S(1)}, u32[]{:S(2)}, u32[]{:S(2)}) collective-permute-start(bf16[2,16,512]{2,1,0:T(8,128)(2,1)S(1)} %get-tuple-element.36.pack_ref), channel_id=1, source_target_pairs={{0,1},{1,0},{2,3},{3,2},{248,249},{249,248},{250,251},{251,250},{8... | collective-permute-start | bytes 98312 | tf_op jit(solution)/shard_map/ppermute | solution.py:393
  64.4 0.0 collective-permute-done.7
  64.4 1.1 %broadcast_select_fusion.back_ref = bf16[512,512]{1,0:T(8,128)(2,1)S(1)} fusion(bf16[512,512]{1,0:T(8,128)(2,1)} %collective-permute-done.7, pred[]{:T(512)S(6)} %or.7), kind=kLoop, calls=%fused_computation.7 | loop fusion | flops 262144 | bytes 1048577 | tf_op jit(solution)/shard_map/jit(_where)/select_n | solution.py:398
  65.5 0.2 shard_map.100.known_ref
  65.7 1.9 %collective-permute-done.8.got_ref = bf16[2,16,512]{2,1,0:T(8,128)(2,1)S(1)} collective-permute-done((bf16[2,16,512]{2,1,0:T(8,128)(2,1)S(1)}, bf16[2,16,512]{2,1,0:T(8,128)(2,1)S(1)}, u32[]{:S(2)}, u32[]{:S(2)}) %collective-permute-start.8) | collective-permute-done | bytes 32800 | tf_op jit(solution)/shard_map/ppermute | solution.py:393
  67.7 0.2 shard_map.101.next_ref
  67.9 0.0 collective-permute-start.9
  67.9 0.5 shard_map.102
  68.4 0.7 collective-permute-done.9.got_ref
  69.1 0.8 shard_map.103
  69.9 2.2 %collective-permute-start.10 = (bf16[2,16,512]{2,1,0:T(8,128)(2,1)S(1)}, bf16[2,16,512]{2,1,0:T(8,128)(2,1)S(1)}, u32[]{:S(2)}, u32[]{:S(2)}) collective-permute-start(bf16[2,16,512]{2,1,0:T(8,128)(2,1)S(1)} %get-tuple-element.44.pack_ref), channel_id=1, source_target_pairs={{0,1},{1,0},{2,3},{3,2},{248,249},{249,248},{250,251},{251,250},{8... | collective-permute-start | bytes 98312 | tf_op jit(solution)/shard_map/ppermute | solution.py:393
  72.2 0.2 shard_map.104.known_ref
  72.4 3.0 %collective-permute-done.10.got_ref = bf16[2,16,512]{2,1,0:T(8,128)(2,1)S(1)} collective-permute-done((bf16[2,16,512]{2,1,0:T(8,128)(2,1)S(1)}, bf16[2,16,512]{2,1,0:T(8,128)(2,1)S(1)}, u32[]{:S(2)}, u32[]{:S(2)}) %collective-permute-start.10) | collective-permute-done | bytes 32800 | tf_op jit(solution)/shard_map/ppermute | solution.py:393
  75.4 0.2 shard_map.105.next_ref
  75.6 0.2 collective-permute-start.11
  75.8 0.5 shard_map.106
  76.3 0.7 collective-permute-done.11.got_ref
  77.0 0.8 shard_map.107
  77.9 2.2 %collective-permute-start.12 = (bf16[2,16,512]{2,1,0:T(8,128)(2,1)S(1)}, bf16[2,16,512]{2,1,0:T(8,128)(2,1)S(1)}, u32[]{:S(2)}, u32[]{:S(2)}) collective-permute-start(bf16[2,16,512]{2,1,0:T(8,128)(2,1)S(1)} %get-tuple-element.48.pack_ref), channel_id=1, source_target_pairs={{0,1},{1,0},{2,3},{3,2},{248,249},{249,248},{250,251},{251,250},{8... | collective-permute-start | bytes 98312 | tf_op jit(solution)/shard_map/ppermute | solution.py:393
  80.1 0.2 shard_map.108.known_ref
  80.3 3.0 %collective-permute-done.12.got_ref = bf16[2,16,512]{2,1,0:T(8,128)(2,1)S(1)} collective-permute-done((bf16[2,16,512]{2,1,0:T(8,128)(2,1)S(1)}, bf16[2,16,512]{2,1,0:T(8,128)(2,1)S(1)}, u32[]{:S(2)}, u32[]{:S(2)}) %collective-permute-start.12) | collective-permute-done | bytes 32800 | tf_op jit(solution)/shard_map/ppermute | solution.py:393
  83.3 0.2 shard_map.109.next_ref
  83.6 0.4 shard_map.110.part_ref
  84.0 0.8 collective-permute-done.13.got_ref
  84.8 0.2 shard_map.111.own_ref
  85.0 0.4 collective-permute-start.16
  85.5 1.6 %collective-permute-start.15 = (f32[16,512]{1,0:T(8,128)S(1)}, f32[16,512]{1,0:T(8,128)S(1)}, u32[]{:S(2)}, u32[]{:S(2)}) collective-permute-start(f32[16,512]{1,0:T(8,128)S(1)} %shard_map.111.own_ref), channel_id=1, source_target_pairs={{0,1},{1,2},{2,3},{3,0},{4,5},{5,6},{6,7},{7,4},{8,9},{9,10},{10,1... | collective-permute-start | bytes 98312 | tf_op jit(solution)/shard_map/ppermute | solution.py:439
  87.1 1.5 %collective-permute-start.14 = (f32[16,512]{1,0:T(8,128)S(1)}, f32[16,512]{1,0:T(8,128)S(1)}, u32[]{:S(2)}, u32[]{:S(2)}) collective-permute-start(f32[16,512]{1,0:T(8,128)S(1)} %shard_map.111.own_ref), channel_id=1, source_target_pairs={{0,2},{1,3},{2,0},{3,1},{4,6},{5,7},{6,4},{7,5},{8,10},{9,11},{10,... | collective-permute-start | bytes 98312 | tf_op jit(solution)/shard_map/ppermute | solution.py:439
  88.6 0.1 pad_add_fusion.where_ref
  88.7 0.3 collective-permute-done.16.third_ref
  89.0 1.6 %collective-permute-done.15.first_ref = f32[16,512]{1,0:T(8,128)S(1)} collective-permute-done((f32[16,512]{1,0:T(8,128)S(1)}, f32[16,512]{1,0:T(8,128)S(1)}, u32[]{:S(2)}, u32[]{:S(2)}) %collective-permute-start.15) | collective-permute-done | bytes 32800 | tf_op jit(solution)/shard_map/ppermute | solution.py:439
  90.6 1.9 %collective-permute-done.14.second_ref = f32[16,512]{1,0:T(8,128)S(1)} collective-permute-done((f32[16,512]{1,0:T(8,128)S(1)}, f32[16,512]{1,0:T(8,128)S(1)}, u32[]{:S(2)}, u32[]{:S(2)}) %collective-permute-start.14) | collective-permute-done | bytes 32800 | tf_op jit(solution)/shard_map/ppermute | solution.py:439
  92.5 1.3 %finish.1 = (f32[64,512]{1,0:T(8,128)}, bf16[4,64,512]{2,1,0:T(8,128)(2,1)}) custom-call(s32[2]{0:T(128)S(1)} %pad_add_fusion.where_ref, f32[16,512]{1,0:T(8,128)S(1)} %shard_map.111.own_ref, f32[16,512]{1,0:T(8,128)S(1)} %collective-permute-done.14.second_ref, f32[16,512]{1,0:T(8,128)S(1)} %collective-permute-done.15.first_ref, ...), custom_call_target="tpu_custom_call", output_to_operand_aliasing={{1}: (6, {})} | custom-call | tf_op jit(solution)/shard_map/finish/pallas_call | solution.py:218
  (12 shorter events, 0.1 us)
Async XLA Ops:
  0.6 5.0 %copy-start.1 = (f32[512]{0:T(512)S(1)}, f32[512]{0:T(512)}, u32[]{:S(2)}) copy-start(f32[512]{0:T(512)} %param.14) | copy-start | bytes 6148
  0.6 5.1 %copy-start = (bf16[4,64,512]{2,1,0:T(8,128)(2,1)S(1)}, bf16[4,64,512]{2,1,0:T(8,128)(2,1)}, u32[]{:S(2)}) copy-start(bf16[4,64,512]{2,1,0:T(8,128)(2,1)} %hist_ref.3) | copy-start | bytes 786436
  5.1 6.2 %collective-permute-start = (bf16[4,4,4,16,512]{4,3,2,1,0:T(8,128)(2,1)S(1)}, bf16[4,4,4,16,512]{4,3,2,1,0:T(8,128)(2,1)S(1)}, u32[]{:S(2)}, u32[]{:S(2)}) collective-permute-start(bf16[4,4,4,16,512]{4,3,2,1,0:T(8,128)(2,1)S(1)} %far_half.3), channel_id=1, source_target_pairs={{0,8},{8,0},{1,9},{9,1},{2,10},{10,2},{3,11},{11,3},{4,12},{12,4},... | collective-permute-start | bytes 3145736 | tf_op jit(solution)/shard_map/ppermute | solution.py:353
  5.2 22.9 %collective-permute-start.2 = (bf16[3,512,512]{2,1,0:T(8,128)(2,1)}, bf16[3,512,512]{2,1,0:T(8,128)(2,1)}, u32[]{:S(2)}, u32[]{:S(2)}) collective-permute-start(bf16[3,512,512]{2,1,0:T(8,128)(2,1)} %param.13), channel_id=1, source_target_pairs={{0,8},{8,0},{1,9},{9,1},{2,10},{10,2},{3,11},{11,3},{4,12},{12,4},... | collective-permute-start | bytes 4718600 | tf_op jit(solution)/shard_map/ppermute | solution.py:358
  5.7 22.4 %collective-permute-start.3 = (f32[1,512]{1,0:T(1,128)S(1)}, f32[1,512]{1,0:T(1,128)S(1)}, u32[]{:S(2)}, u32[]{:S(2)}) collective-permute-start(f32[1,512]{1,0:T(1,128)S(1)} %bitcast.51), channel_id=1, source_target_pairs={{0,8},{8,0},{1,9},{9,1},{2,10},{10,2},{3,11},{11,3},{4,12},{12,4},... | collective-permute-start | bytes 6152 | tf_op jit(solution)/shard_map/ppermute | solution.py:359
  5.8 22.3 %collective-permute-start.1 = (bf16[64,512]{1,0:T(8,128)(2,1)S(1)}, bf16[64,512]{1,0:T(8,128)(2,1)S(1)}, u32[]{:S(2)}, u32[]{:S(2)}) collective-permute-start(bf16[64,512]{1,0:T(8,128)(2,1)S(1)} %slice_bitcast_fusion.2), channel_id=1, source_target_pairs={{0,1},{1,2},{2,3},{3,4},{4,5},{5,6},{6,7},{7,0},{8,9},{9,10},{10,1... | collective-permute-start | bytes 196616 | tf_op jit(solution)/shard_map/ppermute | solution.py:357
  12.3 29.3 %all-to-all-start = ((bf16[16,64,512]{2,1,0:T(8,128)(2,1)}), bf16[16,64,512]{2,1,0:T(8,128)(2,1)S(1)}, u32[]{:S(2)}, u32[]{:S(2)}) async-start(bf16[16,64,512]{2,1,0:T(8,128)(2,1)} %bitcast.8), calls=%async_computation | async-start | bytes 2097152 | tf_op jit(solution)/shard_map/all_to_all | solution.py:356
  25.1 22.3 %slice-start = ((bf16[4,64,512]{2,1,0:T(8,128)(2,1)}), bf16[3,64,512]{2,1,0:T(8,128)(2,1)S(1)}, s32[]{:S(2)}) async-start(bf16[4,64,512]{2,1,0:T(8,128)(2,1)} %hist_ref.3), calls=%async_computation.2 | async-start | bytes 393216 | tf_op jit(solution)/shard_map/slice | solution.py:383
  41.7 22.8 %collective-permute-start.7 = (bf16[512,512]{1,0:T(8,128)(2,1)}, bf16[512,512]{1,0:T(8,128)(2,1)}, u32[]{:S(2)}, u32[]{:S(2)}) collective-permute-start(bf16[512,512]{1,0:T(8,128)(2,1)} %get-tuple-element.37), channel_id=1, source_target_pairs={{0,1},{1,0},{2,3},{3,2},{248,249},{249,248},{250,251},{251,250},{8... | collective-permute-start | bytes 1572872 | tf_op jit(solution)/shard_map/ppermute | solution.py:393
  42.5 12.5 %all-to-all-start.1 = ((bf16[8,16,512]{2,1,0:T(8,128)(2,1)}), bf16[8,16,512]{2,1,0:T(8,128)(2,1)S(1)}, u32[]{:S(2)}, u32[]{:S(2)}) async-start(bf16[8,16,512]{2,1,0:T(8,128)(2,1)} %bitcast.13), calls=%async_computation.1 | async-start | bytes 262144 | tf_op jit(solution)/shard_map/all_to_all | solution.py:396
  55.0 2.4 %collective-permute-start.4 = (f32[16,512]{1,0:T(8,128)S(1)}, f32[16,512]{1,0:T(8,128)S(1)}, u32[]{:S(2)}, u32[]{:S(2)}) collective-permute-start(f32[16,512]{1,0:T(8,128)S(1)} %get-tuple-element.33.c_ref), channel_id=1, source_target_pairs={{0,8},{8,0},{1,9},{9,1},{2,10},{10,2},{3,11},{11,3},{4,12},{12,4},... | collective-permute-start | bytes 98312 | tf_op jit(solution)/shard_map/ppermute | solution.py:407
  55.1 5.4 %collective-permute-start.5 = (bf16[16,512]{1,0:T(8,128)(2,1)S(1)}, bf16[16,512]{1,0:T(8,128)(2,1)S(1)}, u32[]{:S(2)}, u32[]{:S(2)}) collective-permute-start(bf16[16,512]{1,0:T(8,128)(2,1)S(1)} %get-tuple-element.32.value_ref), channel_id=1, source_target_pairs={{0,1},{1,0},{2,3},{3,2},{248,249},{249,248},{250,251},{251,250},{8... | collective-permute-start | bytes 49160 | tf_op jit(solution)/shard_map/ppermute | solution.py:393
  60.7 1.2 %collective-permute-start.6 = (bf16[16,512]{1,0:T(8,128)(2,1)S(1)}, bf16[16,512]{1,0:T(8,128)(2,1)S(1)}, u32[]{:S(2)}, u32[]{:S(2)}) collective-permute-start(bf16[16,512]{1,0:T(8,128)(2,1)S(1)} %shard_map.97.value_ref), channel_id=1, source_target_pairs={{0,8},{8,0},{1,9},{9,1},{2,10},{10,2},{3,11},{11,3},{4,12},{12,4},... | collective-permute-start | bytes 49160 | tf_op jit(solution)/shard_map/ppermute | solution.py:410
  62.2 5.5 %collective-permute-start.8 = (bf16[2,16,512]{2,1,0:T(8,128)(2,1)S(1)}, bf16[2,16,512]{2,1,0:T(8,128)(2,1)S(1)}, u32[]{:S(2)}, u32[]{:S(2)}) collective-permute-start(bf16[2,16,512]{2,1,0:T(8,128)(2,1)S(1)} %get-tuple-element.36.pack_ref), channel_id=1, source_target_pairs={{0,1},{1,0},{2,3},{3,2},{248,249},{249,248},{250,251},{251,250},{8... | collective-permute-start | bytes 98312 | tf_op jit(solution)/shard_map/ppermute | solution.py:393
  67.9 1.2 %collective-permute-start.9 = (bf16[2,16,512]{2,1,0:T(8,128)(2,1)S(1)}, bf16[2,16,512]{2,1,0:T(8,128)(2,1)S(1)}, u32[]{:S(2)}, u32[]{:S(2)}) collective-permute-start(bf16[2,16,512]{2,1,0:T(8,128)(2,1)S(1)} %shard_map.101.next_ref), channel_id=1, source_target_pairs={{0,8},{8,0},{1,9},{9,1},{2,10},{10,2},{3,11},{11,3},{4,12},{12,4},... | collective-permute-start | bytes 98312 | tf_op jit(solution)/shard_map/ppermute | solution.py:419
  69.9 5.5 %collective-permute-start.10 = (bf16[2,16,512]{2,1,0:T(8,128)(2,1)S(1)}, bf16[2,16,512]{2,1,0:T(8,128)(2,1)S(1)}, u32[]{:S(2)}, u32[]{:S(2)}) collective-permute-start(bf16[2,16,512]{2,1,0:T(8,128)(2,1)S(1)} %get-tuple-element.44.pack_ref), channel_id=1, source_target_pairs={{0,1},{1,0},{2,3},{3,2},{248,249},{249,248},{250,251},{251,250},{8... | collective-permute-start | bytes 98312 | tf_op jit(solution)/shard_map/ppermute | solution.py:393
  75.6 1.4 %collective-permute-start.11 = (bf16[2,16,512]{2,1,0:T(8,128)(2,1)S(1)}, bf16[2,16,512]{2,1,0:T(8,128)(2,1)S(1)}, u32[]{:S(2)}, u32[]{:S(2)}) collective-permute-start(bf16[2,16,512]{2,1,0:T(8,128)(2,1)S(1)} %shard_map.105.next_ref), channel_id=1, source_target_pairs={{0,8},{8,0},{1,9},{9,1},{2,10},{10,2},{3,11},{11,3},{4,12},{12,4},... | collective-permute-start | bytes 98312 | tf_op jit(solution)/shard_map/ppermute | solution.py:419
  77.9 5.5 %collective-permute-start.12 = (bf16[2,16,512]{2,1,0:T(8,128)(2,1)S(1)}, bf16[2,16,512]{2,1,0:T(8,128)(2,1)S(1)}, u32[]{:S(2)}, u32[]{:S(2)}) collective-permute-start(bf16[2,16,512]{2,1,0:T(8,128)(2,1)S(1)} %get-tuple-element.48.pack_ref), channel_id=1, source_target_pairs={{0,1},{1,0},{2,3},{3,2},{248,249},{249,248},{250,251},{251,250},{8... | collective-permute-start | bytes 98312 | tf_op jit(solution)/shard_map/ppermute | solution.py:393
  83.6 1.2 %collective-permute-start.13 = (bf16[2,16,512]{2,1,0:T(8,128)(2,1)S(1)}, bf16[2,16,512]{2,1,0:T(8,128)(2,1)S(1)}, u32[]{:S(2)}, u32[]{:S(2)}) collective-permute-start(bf16[2,16,512]{2,1,0:T(8,128)(2,1)S(1)} %shard_map.109.next_ref), channel_id=1, source_target_pairs={{0,8},{8,0},{1,9},{9,1},{2,10},{10,2},{3,11},{11,3},{4,12},{12,4},... | collective-permute-start | bytes 98312 | tf_op jit(solution)/shard_map/ppermute | solution.py:419
  85.0 3.9 %collective-permute-start.16 = (f32[16,512]{1,0:T(8,128)S(1)}, f32[16,512]{1,0:T(8,128)S(1)}, u32[]{:S(2)}, u32[]{:S(2)}) collective-permute-start(f32[16,512]{1,0:T(8,128)S(1)} %shard_map.111.own_ref), channel_id=1, source_target_pairs={{0,3},{1,0},{2,1},{3,2},{4,7},{5,4},{6,5},{7,6},{8,11},{9,8},{10,9... | collective-permute-start | bytes 98312 | tf_op jit(solution)/shard_map/ppermute | solution.py:439
  85.5 5.1 %collective-permute-start.15 = (f32[16,512]{1,0:T(8,128)S(1)}, f32[16,512]{1,0:T(8,128)S(1)}, u32[]{:S(2)}, u32[]{:S(2)}) collective-permute-start(f32[16,512]{1,0:T(8,128)S(1)} %shard_map.111.own_ref), channel_id=1, source_target_pairs={{0,1},{1,2},{2,3},{3,0},{4,5},{5,6},{6,7},{7,4},{8,9},{9,10},{10,1... | collective-permute-start | bytes 98312 | tf_op jit(solution)/shard_map/ppermute | solution.py:439
  87.1 5.4 %collective-permute-start.14 = (f32[16,512]{1,0:T(8,128)S(1)}, f32[16,512]{1,0:T(8,128)S(1)}, u32[]{:S(2)}, u32[]{:S(2)}) collective-permute-start(f32[16,512]{1,0:T(8,128)S(1)} %shard_map.111.own_ref), channel_id=1, source_target_pairs={{0,2},{1,3},{2,0},{3,1},{4,6},{5,7},{6,4},{7,5},{8,10},{9,11},{10,... | collective-permute-start | bytes 98312 | tf_op jit(solution)/shard_map/ppermute | solution.py:439

commit v9 on v8

--- a/solution.py
+++ b/solution.py
@@ -14,113 +14,189 @@
 HIST = ("zh", "y")
 
 
-def far_kernel(
-    core_ref, rank_ref, lag_ref, hist_ref, right_ref, left_ref, out_ref,
-    rank_buf, lag_buf, hist_buf, right_buf, left_buf,
-    rank_sem, lag_sem, hist_sem, right_sem, left_sem, *, ranks
+GROUPS = 2
+
+
+def brought(source, target, sem, group, core):
+    chips = target.shape[0]
+    return pltpu.make_async_copy(source.at[pl.ds(group * chips, chips), core], target, sem)
+
+
+def column_of(group, core, rank_ref, lag_ref, chips, depth, ranks):
+    lane = lax.broadcasted_iota(jnp.int32, (1, chips * depth), 1)
+    column = jnp.full((1, chips * depth), -1, jnp.int32)
+    per = depth // ranks
+    for chip in range(chips):
+        for k in range(per):
+            pair = ((group * chips + chip) * 2 + core) * per + k
+            first = (chip * per + k) * ranks
+            inside = (lane >= first) & (lane < first + rank_ref[pair])
+            column = jnp.where(inside, lag_ref[pair], column)
+    return column
+
+
+def chosen(hist_ref, right_ref, column):
+    lags, steps, width = hist_ref.shape
+    every = lax.dot_general(
+        hist_ref[...].reshape(lags * steps, width),
+        right_ref[...].reshape(-1, width),
+        (((1,), (1,)), ((), ())),
+        preferred_element_type=jnp.float32,
+    )
+    value = jnp.zeros((steps, every.shape[1]), jnp.float32)
+    for lag in range(lags):
+        value = jnp.where(column == lag, every[lag * steps : (lag + 1) * steps], value)
+    return value.astype(jnp.bfloat16)
+
+
+def far(group, value, left_ref, out_ref):
+    chips, depth, width = left_ref.shape
+    left = left_ref[...].reshape(chips * depth, width)
+    for chip in range(chips):
+        first, last = chip * depth, (chip + 1) * depth
+        low, high = first // 128 * 128, -(-last // 128) * 128
+        part = value[:, low:high]
+        at = lax.broadcasted_iota(jnp.int32, part.shape, 1) + low
+        part = jnp.where((at >= first) & (at < last), part, jnp.zeros_like(part))
+        field = jnp.dot(part, left[low:high], preferred_element_type=jnp.float32)
+        line = group * (chips // 4) + chip // 4
+        out_ref[chip % 4, :, line] = field.reshape(out_ref.shape[1], -1, width).astype(out_ref.dtype)
+
+
+def away_kernel(
+    core_ref, rank_ref, lag_ref, hist_ref, right_ref, left_ref,
+    out_ref, hist_buf, right_own, left_own, columns_ref,
+    rank_buf, lag_buf, right_buf, left_buf, small_sem, right_sem, left_sem, *, ranks
 ):
-    groups, chips, depth, width = right_buf.shape
-    lags, steps, _ = hist_buf.shape
-    total = chips * depth
+    groups, chips, depth, _ = right_buf.shape
     core = core_ref[0]
-
-    def brought(source, target, sem, group):
-        return pltpu.make_async_copy(
-            source.at[pl.ds(group * chips, chips), core], target.at[group], sem.at[group]
-        )
-
+    other = 1 - core
     small = [
-        pltpu.make_async_copy(rank_ref, rank_buf, rank_sem),
-        pltpu.make_async_copy(lag_ref, lag_buf, lag_sem),
-        pltpu.make_async_copy(hist_ref, hist_buf, hist_sem),
+        pltpu.make_async_copy(rank_ref, rank_buf, small_sem.at[0]),
+        pltpu.make_async_copy(lag_ref, lag_buf, small_sem.at[1]),
+        pltpu.make_async_copy(hist_ref, hist_buf, small_sem.at[2]),
     ]
     for copy in small:
         copy.start()
-    rights = [brought(right_ref, right_buf, right_sem, g) for g in range(groups)]
-    lefts = [brought(left_ref, left_buf, left_sem, g) for g in range(groups)]
+    rights = [
+        brought(right_ref, right_buf.at[g], right_sem.at[g], g, other) for g in range(groups)
+    ]
+    lefts = [brought(left_ref, left_buf.at[g], left_sem.at[g], g, other) for g in range(groups)]
     for g in range(groups):
         rights[g].start()
         lefts[g].start()
-    lane = lax.broadcasted_iota(jnp.int32, (1, total), 1)
-    per = depth // ranks
-
-    def chosen(group):
-        column = jnp.full((1, total), -1, jnp.int32)
-        for chip in range(chips):
-            for k in range(per):
-                pair = ((group * chips + chip) * 2 + core) * per + k
-                first = (chip * per + k) * ranks
-                inside = (lane >= first) & (lane < first + rank_buf[pair])
-                column = jnp.where(inside, lag_buf[pair], column)
-        every = lax.dot_general(
-            hist_buf[...].reshape(lags * steps, width),
-            right_buf[group].reshape(total, width),
-            (((1,), (1,)), ((), ())),
-            preferred_element_type=jnp.float32,
-        )
-        value = jnp.zeros((steps, total), jnp.float32)
-        for lag in range(lags):
-            value = jnp.where(column == lag, every[lag * steps : (lag + 1) * steps], value)
-        return value.astype(jnp.bfloat16)
-
-    def far(group, value):
-        left = left_buf[group].reshape(total, width)
-        for chip in range(chips):
-            first, last = chip * depth, (chip + 1) * depth
-            low, high = first // 128 * 128, -(-last // 128) * 128
-            part = value[:, low:high]
-            at = lax.broadcasted_iota(jnp.int32, part.shape, 1) + low
-            part = jnp.where((at >= first) & (at < last), part, jnp.zeros_like(part))
-            field = jnp.dot(part, left[low:high], preferred_element_type=jnp.float32)
-            at = group * (chips // 4) + chip // 4
-            out_ref[chip % 4, :, at] = field.reshape(out_ref.shape[1], -1, width).astype(out_ref.dtype)
-
-    for copy in small:
-        copy.wait()
+    late = [
+        brought(right_ref, right_own, right_sem.at[groups], 0, core),
+        brought(left_ref, left_own, left_sem.at[groups], 0, core),
+    ]
+    for copy in late:
+        copy.start()
+    small[0].wait()
+    small[1].wait()
+    columns = []
+    for g in range(groups):
+        columns.append(column_of(g, other, rank_buf, lag_buf, chips, depth, ranks))
+        columns_ref[g : g + 1] = column_of(g, core, rank_buf, lag_buf, chips, depth, ranks)
+    small[2].wait()
     rights[0].wait()
-    value = chosen(0)
+    value = chosen(hist_buf, right_buf.at[0], columns[0])
     for g in range(groups):
         lefts[g].wait()
         ahead = None
         if g + 1 < groups:
             rights[g + 1].wait()
-            ahead = chosen(g + 1)
-        far(g, value)
+            ahead = chosen(hist_buf, right_buf.at[g + 1], columns[g + 1])
+        far(g, value, left_buf.at[g], out_ref)
         value = ahead
-
-
-def far_half(core, rank, lag, history, right, left, ranks):
+    for copy in late:
+        copy.wait()
+
+
+def own_kernel(
+    core_ref, hist_ref, right_own, left_own, columns_ref, right_ref, left_ref, out_ref,
+    right_buf, left_buf, right_sem, left_sem
+):
+    core = core_ref[0]
+    groups = right_buf.shape[0] + 1
+    rights = [
+        brought(right_ref, right_buf.at[g], right_sem.at[g], g + 1, core) for g in range(groups - 1)
+    ]
+    lefts = [
+        brought(left_ref, left_buf.at[g], left_sem.at[g], g + 1, core) for g in range(groups - 1)
+    ]
+    for g in range(groups - 1):
+        rights[g].start()
+        lefts[g].start()
+    value = chosen(hist_ref, right_own, columns_ref[0:1])
+    for g in range(groups):
+        if g > 0:
+            lefts[g - 1].wait()
+        ahead = None
+        if g + 1 < groups:
+            rights[g].wait()
+            ahead = chosen(hist_ref, right_buf.at[g], columns_ref[g + 1 : g + 2])
+        far(g, value, left_own if g == 0 else left_buf.at[g - 1], out_ref)
+        value = ahead
+
+
+def far_halves(core, rank, lag, history, right, left, ranks):
     rows, _, depth, width = right.shape
     lags, steps, _ = history.shape
-    groups, chips, cuts = 2, 16 // 2, 4
+    chips = rows // GROUPS
+    field = jax.ShapeDtypeStruct((4, 4, 4, steps // 4, width), jnp.bfloat16)
+    block = (chips, depth, width)
     scalar = pl.BlockSpec(memory_space=pltpu.SMEM)
+    inside = pl.BlockSpec(memory_space=pltpu.VMEM)
     outside = pl.BlockSpec(memory_space=pltpu.HBM)
-    held = pltpu.VMEM((groups, chips, depth, width), jnp.bfloat16)
-    return pl.pallas_call(
-        functools.partial(far_kernel, ranks=ranks),
-        out_shape=jax.ShapeDtypeStruct((4, cuts, 4, steps // cuts, width), jnp.bfloat16),
+    cost = pl.CostEstimate(
+        flops=2 * rows * depth * width * (lags + 1) * steps,
+        bytes_accessed=rows * depth * width * 4 + rows * steps * width * 2,
+        transcendentals=0,
+    )
+    semaphores = pltpu.SemaphoreType.DMA
+    away, hist_buf, right_own, left_own, columns = pl.pallas_call(
+        functools.partial(away_kernel, ranks=ranks),
+        out_shape=(
+            field,
+            jax.ShapeDtypeStruct(history.shape, history.dtype),
+            jax.ShapeDtypeStruct(block, right.dtype),
+            jax.ShapeDtypeStruct(block, left.dtype),
+            jax.ShapeDtypeStruct((GROUPS, chips * depth), jnp.int32),
+        ),
         in_specs=[scalar] + [outside] * 5,
-        out_specs=pl.BlockSpec(memory_space=pltpu.VMEM),
+        out_specs=[inside] * 5,
         scratch_shapes=[
             pltpu.SMEM(rank.shape, jnp.int32),
             pltpu.SMEM(lag.shape, jnp.int32),
-            pltpu.VMEM((lags, steps, width), jnp.bfloat16),
-            held,
-            held,
-            pltpu.SemaphoreType.DMA,
-            pltpu.SemaphoreType.DMA,
-            pltpu.SemaphoreType.DMA,
-            pltpu.SemaphoreType.DMA((groups,)),
-            pltpu.SemaphoreType.DMA((groups,)),
+            pltpu.VMEM((GROUPS, *block), right.dtype),
+            pltpu.VMEM((GROUPS, *block), left.dtype),
+            semaphores((3,)),
+            semaphores((GROUPS + 1,)),
+            semaphores((GROUPS + 1,)),
         ],
         compiler_params=pltpu.CompilerParams(vmem_limit_bytes=16 << 20),
-        cost_estimate=pl.CostEstimate(
-            flops=2 * rows * depth * width * (lags + 1) * steps,
-            bytes_accessed=rows * depth * width * 4 + rows * steps * width * 2,
-            transcendentals=0,
-        ),
-        name="far_half",
+        cost_estimate=cost,
+        name="far_away",
     )(core, rank, lag, history, right, left)
+
+    def own():
+        return pl.pallas_call(
+            own_kernel,
+            out_shape=field,
+            in_specs=[scalar] + [inside] * 4 + [outside] * 2,
+            out_specs=inside,
+            scratch_shapes=[
+                pltpu.VMEM((GROUPS - 1, *block), right.dtype),
+                pltpu.VMEM((GROUPS - 1, *block), left.dtype),
+                semaphores((GROUPS - 1,)),
+                semaphores((GROUPS - 1,)),
+            ],
+            compiler_params=pltpu.CompilerParams(vmem_limit_bytes=16 << 20),
+            cost_estimate=cost,
+            name="far_own",
+        )(core, hist_buf, right_own, left_own, columns, right, left)
+
+    return away, own
 
 
 def halves_kernel(mine_ref, came_ref, out_ref, held_ref, sem):
@@ -346,12 +422,9 @@
     core = lax.axis_index("c")
     swap = [(0, 1), (1, 0)]
 
-    def half(which):
-        return far_half(which.reshape(1), rank, lag, history_out, right, left, ranks)
-
-    away = half(1 - core)
+    away, own_half = far_halves(core.reshape(1), rank, lag, history_out, right, left, ranks)
     came = lax.ppermute(away, "c", swap)
-    mine = half(core)
+    mine = own_half()
     partial_value = halves_sum(mine, came)
     arrived = lax.all_to_all(partial_value.reshape(16, -1, width), ("x", "y"), 0, 0, tiled=True)
     incoming = lax.ppermute(history[-1], HIST, [(i, (i + 1) % 8) for i in range(8)])

time: 94.4 us -> 93.7 us (level)
  the two profiles are of different devices: /device:TPU:32 before, /device:TPU:56 now
where the time goes in v9:
time: 93.7 us; the launch traced here: 93.2 us
  waiting for transfers between devices  35.5 us (38%)
  starting transfers between devices  31.9 us (34%)
  Pallas kernels  17 us (18%)
  other arithmetic  7.81 us (8%)
  between operations  1.02 us (1%)
    ppermute x5, waiting for transfers between devices, off_chip(): return lax.ppermute(value, SPACE + ('y',), between)  12.5 us
    all_to_all x1, waiting for transfers between devices, per_device(): lax.all_to_all(partial_value.reshape(16, -1, width), ('x', 'y'), 0, 0, ti...  11 us
    ppermute x5, starting transfers between devices, off_chip(): return lax.ppermute(value, SPACE + ('y',), between)  7.35 us
    all_to_all x1, starting transfers between devices, per_device(): lax.all_to_all(partial_value.reshape(16, -1, width), ('x', 'y'), 0, 0, ti...  7 us
    ppermute x1, starting transfers between devices, per_device(): lax.ppermute(history[-1], HIST, [(i, (i + 1) % 8) for i in range(8)])  6.03 us
    pallas_call x17, Pallas kernels, small_call(): pl.pallas_call(kernel, out_shape=outs, in_specs=[inside] * len(operands),...  5.8 us
    all_to_all x1, waiting for transfers between devices, per_device(): arrived = lax.all_to_all(twice, ('zh', 'zl'), 0, 0, tiled=True)  5.45 us
    ppermute x3, starting transfers between devices, per_device(): lax.ppermute(current, 'y', [(i, (i + step) % 4) for i in range(4)])  5.37 us
  transfers between devices with their start and end apart: 19, of which 12 were waited for; matrix products, arithmetic and copies ran while one was open for 8% of the time, Pallas kernels for 8%

profile of v9, /device:TPU:56, one launch (start us, length us, event | category | flops | bytes accessed | tf_op | source)
XLA Modules:
  0.0 93.2 jit_solution(8090344236097997493)
XLA Ops:
  0.6 0.0 copy-start
  0.7 5.2 %far_away.1 = (bf16[4,4,4,16,512]{4,3,2,1,0:T(8,128)(2,1)S(1)}, bf16[4,64,512]{2,1,0:T(8,128)(2,1)S(1)}, bf16[8,160,512]{2,1,0:T(8,128)(2,1)S(1)}, bf16[8,160,512]{2,1,0:T(8,128)(2,1)S(1)}, s32[2,1280]{1,0:T(2,128)S(1)}) custom-call(s32[1]{0:T(128)} %bitcast.2.core_ref, s32[64]{0:T(128)} %bitcast.47, s32[64]{0:T(128)} %bitcast.48, ...), custom_call_target="tpu_custom_call" | custom-call | flops 838860800 | bytes 6291456 | tf_op jit(solution)/shard_map/far_away/pallas_call | solution.py:157
  5.9 0.1 collective-permute-start
  6.0 0.5 collective-permute-start.2
  6.5 6.0 %collective-permute-start.1 = (bf16[64,512]{1,0:T(8,128)(2,1)S(1)}, bf16[64,512]{1,0:T(8,128)(2,1)S(1)}, u32[]{:S(2)}, u32[]{:S(2)}) collective-permute-start(bf16[64,512]{1,0:T(8,128)(2,1)S(1)} %slice_bitcast_fusion.2), channel_id=1, source_target_pairs={{0,1},{1,2},{2,3},{3,4},{4,5},{5,6},{6,7},{7,0},{8,9},{9,10},{10,1... | collective-permute-start | bytes 196616 | tf_op jit(solution)/shard_map/ppermute | solution.py:430
  12.5 0.0 collective-permute-start.3
  12.5 2.8 %far_own.1.mine_ref = bf16[4,4,4,16,512]{4,3,2,1,0:T(8,128)(2,1)S(1)} custom-call(s32[1]{0:T(128)} %bitcast.2.core_ref, bf16[4,64,512]{2,1,0:T(8,128)(2,1)S(1)} %get-tuple-element.32.hist_ref, bf16[8,160,512]{2,1,0:T(8,128)(2,1)S(1)} %get-tuple-element.33.right_own, bf16[8,160,512]{2,1,0:T(8,128)(2,1)S(1)} %get-tuple-element.34.left_own, ...), custom_call_target="tpu_custom_call" | custom-call | flops 838860800 | bytes 6291456 | tf_op jit(solution)/shard_map/far_own/pallas_call | solution.py:183
  15.3 0.0 collective-permute-done.came_ref
  15.3 1.1 %halves_sum.1 = bf16[4,4,4,16,512]{4,3,2,1,0:T(8,128)(2,1)} custom-call(bf16[4,4,4,16,512]{4,3,2,1,0:T(8,128)(2,1)S(1)} %far_own.1.mine_ref, bf16[4,4,4,16,512]{4,3,2,1,0:T(8,128)(2,1)S(1)} %collective-permute-done.came_ref), custom_call_target="tpu_custom_call" | custom-call | flops 524288 | bytes 3145728 | tf_op jit(solution)/shard_map/halves_sum/pallas_call | solution.py:216
  16.4 7.0 %all-to-all-start = ((bf16[16,64,512]{2,1,0:T(8,128)(2,1)}), bf16[16,64,512]{2,1,0:T(8,128)(2,1)S(1)}, u32[]{:S(2)}, u32[]{:S(2)}) async-start(bf16[16,64,512]{2,1,0:T(8,128)(2,1)} %bitcast.7), calls=%async_computation | async-start | bytes 2097152 | tf_op jit(solution)/shard_map/all_to_all | solution.py:429
  23.5 1.5 %slice_bitcast_fusion.1 = (bf16[512,512]{1,0:T(8,128)(2,1)S(1)}, bf16[512,512]{1,0:T(8,128)(2,1)S(1)}) fusion(bf16[3,512,512]{2,1,0:T(8,128)(2,1)} %param.13, pred[]{:T(512)S(6)} %eq.28), kind=kLoop, calls=%fused_computation.2 | loop fusion | flops 262144 | bytes 2621441 | tf_op jit(solution)/shard_map/squeeze | solution.py:443
  24.9 0.0 slice-start
  24.9 2.2 %multiply_convert_fusion = (bf16[512,512]{1,0:T(8,128)(2,1)}, bf16[512,512]{1,0:T(8,128)(2,1)S(1)}) fusion(f32[512]{0:T(512)S(1)} %broadcast_divide_fusion, bf16[3,512,512]{2,1,0:T(8,128)(2,1)} %param.13, pred[]{:T(512)S(6)} %eq.28, pred[]{:T(512)S(6)} %or.7), kind=kLoop, calls=%fused_computation | loop fusion | flops 1310720 | bytes 2099202 | tf_op jit(solution)/shard_map/convert_element_type | solution.py:445
  27.2 0.8 dynamic-slice_multiply_fusion.given_ref
  27.9 0.0 collective-permute-done.3
  27.9 0.0 collective-permute-done.1.incoming_ref
  28.0 11.0 %all-to-all-done.in_ref = bf16[16,64,512]{2,1,0:T(8,128)(2,1)S(1)} async-done(((bf16[16,64,512]{2,1,0:T(8,128)(2,1)}), bf16[16,64,512]{2,1,0:T(8,128)(2,1)S(1)}, u32[]{:S(2)}, u32[]{:S(2)}) %all-to-all-start) | async-done | bytes 1048608 | tf_op jit(solution)/shard_map/all_to_all | solution.py:429
  39.0 0.2 collective-permute-start.7
  39.2 0.8 plane_sum.1
  40.0 5.3 %all-to-all-start.1 = ((bf16[8,16,512]{2,1,0:T(8,128)(2,1)}), bf16[8,16,512]{2,1,0:T(8,128)(2,1)S(1)}, u32[]{:S(2)}, u32[]{:S(2)}) async-start(bf16[8,16,512]{2,1,0:T(8,128)(2,1)} %bitcast.12), calls=%async_computation.1 | async-start | bytes 262144 | tf_op jit(solution)/shard_map/all_to_all | solution.py:469
  45.3 0.7 pad_maximum_fusion.shifted_ref
  46.0 1.5 %slice_bitcast_fusion = (bf16[512,512]{1,0:T(8,128)(2,1)S(1)}, bf16[512,512]{1,0:T(8,128)(2,1)S(1)}, bf16[512,512]{1,0:T(8,128)(2,1)S(1)}) fusion(bf16[3,512,512]{2,1,0:T(8,128)(2,1)} %collective-permute-done.2, pred[]{:T(512)S(6)} %eq.31, pred[]{:T(512)S(6)} %or.8), kind=kLoop, calls=%fused_computation.1 | loop fusion | flops 786432 | bytes 3145730 | tf_op jit(solution)/shard_map/squeeze | solution.py:455
  47.5 5.5 %all-to-all-done.1.arrived_ref = bf16[8,16,512]{2,1,0:T(8,128)(2,1)S(1)} async-done(((bf16[8,16,512]{2,1,0:T(8,128)(2,1)}), bf16[8,16,512]{2,1,0:T(8,128)(2,1)S(1)}, u32[]{:S(2)}, u32[]{:S(2)}) %all-to-all-start.1) | async-done | bytes 131104 | tf_op jit(solution)/shard_map/all_to_all | solution.py:469
  52.9 0.1 collective-permute-start.4
  53.0 1.8 %collective-permute-start.5 = (bf16[16,512]{1,0:T(8,128)(2,1)S(1)}, bf16[16,512]{1,0:T(8,128)(2,1)S(1)}, u32[]{:S(2)}, u32[]{:S(2)}) collective-permute-start(bf16[16,512]{1,0:T(8,128)(2,1)S(1)} %get-tuple-element.42.value_ref), channel_id=1, source_target_pairs={{0,1},{1,0},{2,3},{3,2},{248,249},{249,248},{250,251},{251,250},{8... | collective-permute-start | bytes 49160 | tf_op jit(solution)/shard_map/ppermute | solution.py:466
  54.9 0.0 collective-permute-done.4.beside_ref.c_u_ref
  54.9 0.4 shard_map.96.part_ref
  55.3 3.1 %collective-permute-done.5.got_ref = bf16[16,512]{1,0:T(8,128)(2,1)S(1)} collective-permute-done((bf16[16,512]{1,0:T(8,128)(2,1)S(1)}, bf16[16,512]{1,0:T(8,128)(2,1)S(1)}, u32[]{:S(2)}, u32[]{:S(2)}) %collective-permute-start.5) | collective-permute-done | bytes 16416 | tf_op jit(solution)/shard_map/ppermute | solution.py:466
  58.4 0.2 shard_map.97.value_ref
  58.6 0.0 collective-permute-start.6
  58.7 0.2 shard_map.98.part_ref
  58.9 0.9 %collective-permute-done.6.beside_ref = bf16[16,512]{1,0:T(8,128)(2,1)S(1)} collective-permute-done((bf16[16,512]{1,0:T(8,128)(2,1)S(1)}, bf16[16,512]{1,0:T(8,128)(2,1)S(1)}, u32[]{:S(2)}, u32[]{:S(2)}) %collective-permute-start.6) | collective-permute-done | bytes 16416 | tf_op jit(solution)/shard_map/ppermute | solution.py:483
  59.8 0.2 shard_map.99
  60.1 1.8 %collective-permute-start.8 = (bf16[2,16,512]{2,1,0:T(8,128)(2,1)S(1)}, bf16[2,16,512]{2,1,0:T(8,128)(2,1)S(1)}, u32[]{:S(2)}, u32[]{:S(2)}) collective-permute-start(bf16[2,16,512]{2,1,0:T(8,128)(2,1)S(1)} %get-tuple-element.46.pack_ref), channel_id=1, source_target_pairs={{0,1},{1,0},{2,3},{3,2},{248,249},{249,248},{250,251},{251,250},{8... | collective-permute-start | bytes 98312 | tf_op jit(solution)/shard_map/ppermute | solution.py:466
  61.9 1.1 %broadcast_select_fusion.back_ref = bf16[512,512]{1,0:T(8,128)(2,1)S(1)} fusion(bf16[512,512]{1,0:T(8,128)(2,1)} %collective-permute-done.7, pred[]{:T(512)S(6)} %or.7), kind=kLoop, calls=%fused_computation.7 | loop fusion | flops 262144 | bytes 1048577 | tf_op jit(solution)/shard_map/jit(_where)/select_n | solution.py:471
  62.9 0.2 shard_map.100.known_ref
  63.2 2.4 %collective-permute-done.8.got_ref = bf16[2,16,512]{2,1,0:T(8,128)(2,1)S(1)} collective-permute-done((bf16[2,16,512]{2,1,0:T(8,128)(2,1)S(1)}, bf16[2,16,512]{2,1,0:T(8,128)(2,1)S(1)}, u32[]{:S(2)}, u32[]{:S(2)}) %collective-permute-start.8) | collective-permute-done | bytes 32800 | tf_op jit(solution)/shard_map/ppermute | solution.py:466
  65.5 0.2 shard_map.101.next_ref
  65.8 0.5 shard_map.102
  66.3 0.7 collective-permute-done.9.got_ref
  67.0 0.8 shard_map.103
  67.8 1.8 %collective-permute-start.10 = (bf16[2,16,512]{2,1,0:T(8,128)(2,1)S(1)}, bf16[2,16,512]{2,1,0:T(8,128)(2,1)S(1)}, u32[]{:S(2)}, u32[]{:S(2)}) collective-permute-start(bf16[2,16,512]{2,1,0:T(8,128)(2,1)S(1)} %get-tuple-element.54.pack_ref), channel_id=1, source_target_pairs={{0,1},{1,0},{2,3},{3,2},{248,249},{249,248},{250,251},{251,250},{8... | collective-permute-start | bytes 98312 | tf_op jit(solution)/shard_map/ppermute | solution.py:466
  69.6 0.2 shard_map.104.known_ref
  69.8 3.5 %collective-permute-done.10.got_ref = bf16[2,16,512]{2,1,0:T(8,128)(2,1)S(1)} collective-permute-done((bf16[2,16,512]{2,1,0:T(8,128)(2,1)S(1)}, bf16[2,16,512]{2,1,0:T(8,128)(2,1)S(1)}, u32[]{:S(2)}, u32[]{:S(2)}) %collective-permute-start.10) | collective-permute-done | bytes 32800 | tf_op jit(solution)/shard_map/ppermute | solution.py:466
  73.3 0.2 shard_map.105.next_ref
  73.5 0.2 collective-permute-start.11
  73.7 0.5 shard_map.106
  74.2 0.7 collective-permute-done.11.got_ref
  74.9 0.8 shard_map.107
  75.8 1.8 %collective-permute-start.12 = (bf16[2,16,512]{2,1,0:T(8,128)(2,1)S(1)}, bf16[2,16,512]{2,1,0:T(8,128)(2,1)S(1)}, u32[]{:S(2)}, u32[]{:S(2)}) collective-permute-start(bf16[2,16,512]{2,1,0:T(8,128)(2,1)S(1)} %get-tuple-element.58.pack_ref), channel_id=1, source_target_pairs={{0,1},{1,0},{2,3},{3,2},{248,249},{249,248},{250,251},{251,250},{8... | collective-permute-start | bytes 98312 | tf_op jit(solution)/shard_map/ppermute | solution.py:466
  77.5 0.2 shard_map.108.known_ref
  77.8 3.5 %collective-permute-done.12.got_ref = bf16[2,16,512]{2,1,0:T(8,128)(2,1)S(1)} collective-permute-done((bf16[2,16,512]{2,1,0:T(8,128)(2,1)S(1)}, bf16[2,16,512]{2,1,0:T(8,128)(2,1)S(1)}, u32[]{:S(2)}, u32[]{:S(2)}) %collective-permute-start.12) | collective-permute-done | bytes 32800 | tf_op jit(solution)/shard_map/ppermute | solution.py:466
  81.2 0.2 shard_map.109.next_ref
  81.5 0.4 shard_map.110.part_ref
  81.9 0.8 collective-permute-done.13.got_ref
  82.7 0.2 shard_map.111.own_ref
  82.9 3.3 %collective-permute-start.14 = (f32[16,512]{1,0:T(8,128)S(1)}, f32[16,512]{1,0:T(8,128)S(1)}, u32[]{:S(2)}, u32[]{:S(2)}) collective-permute-start(f32[16,512]{1,0:T(8,128)S(1)} %shard_map.111.own_ref), channel_id=1, source_target_pairs={{0,2},{1,3},{2,0},{3,1},{4,6},{5,7},{6,4},{7,5},{8,10},{9,11},{10,... | collective-permute-start | bytes 98312 | tf_op jit(solution)/shard_map/ppermute | solution.py:512
  86.3 0.4 collective-permute-start.15
  86.7 1.6 %collective-permute-start.16 = (f32[16,512]{1,0:T(8,128)S(1)}, f32[16,512]{1,0:T(8,128)S(1)}, u32[]{:S(2)}, u32[]{:S(2)}) collective-permute-start(f32[16,512]{1,0:T(8,128)S(1)} %shard_map.111.own_ref), channel_id=1, source_target_pairs={{0,3},{1,0},{2,1},{3,2},{4,7},{5,4},{6,5},{7,6},{8,11},{9,8},{10,9... | collective-permute-start | bytes 98312 | tf_op jit(solution)/shard_map/ppermute | solution.py:512
  88.3 0.1 pad_add_fusion.where_ref
  88.4 0.0 collective-permute-done.14.second_ref
  88.4 1.8 %collective-permute-done.15.first_ref = f32[16,512]{1,0:T(8,128)S(1)} collective-permute-done((f32[16,512]{1,0:T(8,128)S(1)}, f32[16,512]{1,0:T(8,128)S(1)}, u32[]{:S(2)}, u32[]{:S(2)}) %collective-permute-start.15) | collective-permute-done | bytes 32800 | tf_op jit(solution)/shard_map/ppermute | solution.py:512
  90.2 1.6 %collective-permute-done.16.third_ref = f32[16,512]{1,0:T(8,128)S(1)} collective-permute-done((f32[16,512]{1,0:T(8,128)S(1)}, f32[16,512]{1,0:T(8,128)S(1)}, u32[]{:S(2)}, u32[]{:S(2)}) %collective-permute-start.16) | collective-permute-done | bytes 32800 | tf_op jit(solution)/shard_map/ppermute | solution.py:512
  91.8 1.3 %finish.1 = (f32[64,512]{1,0:T(8,128)}, bf16[4,64,512]{2,1,0:T(8,128)(2,1)}) custom-call(s32[2]{0:T(128)S(1)} %pad_add_fusion.where_ref, f32[16,512]{1,0:T(8,128)S(1)} %shard_map.111.own_ref, f32[16,512]{1,0:T(8,128)S(1)} %collective-permute-done.14.second_ref, f32[16,512]{1,0:T(8,128)S(1)} %collective-permute-done.15.first_ref, ...), custom_call_target="tpu_custom_call", output_to_operand_aliasing={{1}: (6, {})} | custom-call | tf_op jit(solution)/shard_map/finish/pallas_call | solution.py:294
  (12 shorter events, 0.1 us)
Async XLA Ops:
  0.6 5.9 %copy-start = (bf16[4,64,512]{2,1,0:T(8,128)(2,1)S(1)}, bf16[4,64,512]{2,1,0:T(8,128)(2,1)}, u32[]{:S(2)}) copy-start(bf16[4,64,512]{2,1,0:T(8,128)(2,1)} %hist_ref.1) | copy-start | bytes 786436
  0.6 11.9 %copy-start.1 = (f32[512]{0:T(512)S(1)}, f32[512]{0:T(512)}, u32[]{:S(2)}) copy-start(f32[512]{0:T(512)} %param.14) | copy-start | bytes 6148
  5.9 9.4 %collective-permute-start = (bf16[4,4,4,16,512]{4,3,2,1,0:T(8,128)(2,1)S(1)}, bf16[4,4,4,16,512]{4,3,2,1,0:T(8,128)(2,1)S(1)}, u32[]{:S(2)}, u32[]{:S(2)}) collective-permute-start(bf16[4,4,4,16,512]{4,3,2,1,0:T(8,128)(2,1)S(1)} %get-tuple-element.36), channel_id=1, source_target_pairs={{0,8},{8,0},{1,9},{9,1},{2,10},{10,2},{3,11},{11,3},{4,12},{12,4},... | collective-permute-start | bytes 3145736 | tf_op jit(solution)/shard_map/ppermute | solution.py:426
  6.0 22.0 %collective-permute-start.2 = (bf16[3,512,512]{2,1,0:T(8,128)(2,1)}, bf16[3,512,512]{2,1,0:T(8,128)(2,1)}, u32[]{:S(2)}, u32[]{:S(2)}) collective-permute-start(bf16[3,512,512]{2,1,0:T(8,128)(2,1)} %param.13), channel_id=1, source_target_pairs={{0,8},{8,0},{1,9},{9,1},{2,10},{10,2},{3,11},{11,3},{4,12},{12,4},... | collective-permute-start | bytes 4718600 | tf_op jit(solution)/shard_map/ppermute | solution.py:431
  6.5 21.4 %collective-permute-start.1 = (bf16[64,512]{1,0:T(8,128)(2,1)S(1)}, bf16[64,512]{1,0:T(8,128)(2,1)S(1)}, u32[]{:S(2)}, u32[]{:S(2)}) collective-permute-start(bf16[64,512]{1,0:T(8,128)(2,1)S(1)} %slice_bitcast_fusion.2), channel_id=1, source_target_pairs={{0,1},{1,2},{2,3},{3,4},{4,5},{5,6},{6,7},{7,0},{8,9},{9,10},{10,1... | collective-permute-start | bytes 196616 | tf_op jit(solution)/shard_map/ppermute | solution.py:430
  12.5 15.4 %collective-permute-start.3 = (f32[1,512]{1,0:T(1,128)S(1)}, f32[1,512]{1,0:T(1,128)S(1)}, u32[]{:S(2)}, u32[]{:S(2)}) collective-permute-start(f32[1,512]{1,0:T(1,128)S(1)} %bitcast.46), channel_id=1, source_target_pairs={{0,8},{8,0},{1,9},{9,1},{2,10},{10,2},{3,11},{11,3},{4,12},{12,4},... | collective-permute-start | bytes 6152 | tf_op jit(solution)/shard_map/ppermute | solution.py:432
  16.4 22.5 %all-to-all-start = ((bf16[16,64,512]{2,1,0:T(8,128)(2,1)}), bf16[16,64,512]{2,1,0:T(8,128)(2,1)S(1)}, u32[]{:S(2)}, u32[]{:S(2)}) async-start(bf16[16,64,512]{2,1,0:T(8,128)(2,1)} %bitcast.7), calls=%async_computation | async-start | bytes 2097152 | tf_op jit(solution)/shard_map/all_to_all | solution.py:429
  24.9 20.4 %slice-start = ((bf16[4,64,512]{2,1,0:T(8,128)(2,1)}), bf16[3,64,512]{2,1,0:T(8,128)(2,1)S(1)}, s32[]{:S(2)}) async-start(bf16[4,64,512]{2,1,0:T(8,128)(2,1)} %hist_ref.1), calls=%async_computation.2 | async-start | bytes 393216 | tf_op jit(solution)/shard_map/slice | solution.py:456
  39.0 22.9 %collective-permute-start.7 = (bf16[512,512]{1,0:T(8,128)(2,1)}, bf16[512,512]{1,0:T(8,128)(2,1)}, u32[]{:S(2)}, u32[]{:S(2)}) collective-permute-start(bf16[512,512]{1,0:T(8,128)(2,1)} %get-tuple-element.47), channel_id=1, source_target_pairs={{0,1},{1,0},{2,3},{3,2},{248,249},{249,248},{250,251},{251,250},{8... | collective-permute-start | bytes 1572872 | tf_op jit(solution)/shard_map/ppermute | solution.py:466
  40.0 12.9 %all-to-all-start.1 = ((bf16[8,16,512]{2,1,0:T(8,128)(2,1)}), bf16[8,16,512]{2,1,0:T(8,128)(2,1)S(1)}, u32[]{:S(2)}, u32[]{:S(2)}) async-start(bf16[8,16,512]{2,1,0:T(8,128)(2,1)} %bitcast.12), calls=%async_computation.1 | async-start | bytes 262144 | tf_op jit(solution)/shard_map/all_to_all | solution.py:469
  52.9 1.9 %collective-permute-start.4 = (f32[16,512]{1,0:T(8,128)S(1)}, f32[16,512]{1,0:T(8,128)S(1)}, u32[]{:S(2)}, u32[]{:S(2)}) collective-permute-start(f32[16,512]{1,0:T(8,128)S(1)} %get-tuple-element.43.c_ref), channel_id=1, source_target_pairs={{0,8},{8,0},{1,9},{9,1},{2,10},{10,2},{3,11},{11,3},{4,12},{12,4},... | collective-permute-start | bytes 98312 | tf_op jit(solution)/shard_map/ppermute | solution.py:480
  53.0 5.4 %collective-permute-start.5 = (bf16[16,512]{1,0:T(8,128)(2,1)S(1)}, bf16[16,512]{1,0:T(8,128)(2,1)S(1)}, u32[]{:S(2)}, u32[]{:S(2)}) collective-permute-start(bf16[16,512]{1,0:T(8,128)(2,1)S(1)} %get-tuple-element.42.value_ref), channel_id=1, source_target_pairs={{0,1},{1,0},{2,3},{3,2},{248,249},{249,248},{250,251},{251,250},{8... | collective-permute-start | bytes 49160 | tf_op jit(solution)/shard_map/ppermute | solution.py:466
  58.6 1.2 %collective-permute-start.6 = (bf16[16,512]{1,0:T(8,128)(2,1)S(1)}, bf16[16,512]{1,0:T(8,128)(2,1)S(1)}, u32[]{:S(2)}, u32[]{:S(2)}) collective-permute-start(bf16[16,512]{1,0:T(8,128)(2,1)S(1)} %shard_map.97.value_ref), channel_id=1, source_target_pairs={{0,8},{8,0},{1,9},{9,1},{2,10},{10,2},{3,11},{11,3},{4,12},{12,4},... | collective-permute-start | bytes 49160 | tf_op jit(solution)/shard_map/ppermute | solution.py:483
  60.1 5.5 %collective-permute-start.8 = (bf16[2,16,512]{2,1,0:T(8,128)(2,1)S(1)}, bf16[2,16,512]{2,1,0:T(8,128)(2,1)S(1)}, u32[]{:S(2)}, u32[]{:S(2)}) collective-permute-start(bf16[2,16,512]{2,1,0:T(8,128)(2,1)S(1)} %get-tuple-element.46.pack_ref), channel_id=1, source_target_pairs={{0,1},{1,0},{2,3},{3,2},{248,249},{249,248},{250,251},{251,250},{8... | collective-permute-start | bytes 98312 | tf_op jit(solution)/shard_map/ppermute | solution.py:466
  65.8 1.2 %collective-permute-start.9 = (bf16[2,16,512]{2,1,0:T(8,128)(2,1)S(1)}, bf16[2,16,512]{2,1,0:T(8,128)(2,1)S(1)}, u32[]{:S(2)}, u32[]{:S(2)}) collective-permute-start(bf16[2,16,512]{2,1,0:T(8,128)(2,1)S(1)} %shard_map.101.next_ref), channel_id=1, source_target_pairs={{0,8},{8,0},{1,9},{9,1},{2,10},{10,2},{3,11},{11,3},{4,12},{12,4},... | collective-permute-start | bytes 98312 | tf_op jit(solution)/shard_map/ppermute | solution.py:492
  67.8 5.5 %collective-permute-start.10 = (bf16[2,16,512]{2,1,0:T(8,128)(2,1)S(1)}, bf16[2,16,512]{2,1,0:T(8,128)(2,1)S(1)}, u32[]{:S(2)}, u32[]{:S(2)}) collective-permute-start(bf16[2,16,512]{2,1,0:T(8,128)(2,1)S(1)} %get-tuple-element.54.pack_ref), channel_id=1, source_target_pairs={{0,1},{1,0},{2,3},{3,2},{248,249},{249,248},{250,251},{251,250},{8... | collective-permute-start | bytes 98312 | tf_op jit(solution)/shard_map/ppermute | solution.py:466
  73.5 1.4 %collective-permute-start.11 = (bf16[2,16,512]{2,1,0:T(8,128)(2,1)S(1)}, bf16[2,16,512]{2,1,0:T(8,128)(2,1)S(1)}, u32[]{:S(2)}, u32[]{:S(2)}) collective-permute-start(bf16[2,16,512]{2,1,0:T(8,128)(2,1)S(1)} %shard_map.105.next_ref), channel_id=1, source_target_pairs={{0,8},{8,0},{1,9},{9,1},{2,10},{10,2},{3,11},{11,3},{4,12},{12,4},... | collective-permute-start | bytes 98312 | tf_op jit(solution)/shard_map/ppermute | solution.py:492
  75.8 5.5 %collective-permute-start.12 = (bf16[2,16,512]{2,1,0:T(8,128)(2,1)S(1)}, bf16[2,16,512]{2,1,0:T(8,128)(2,1)S(1)}, u32[]{:S(2)}, u32[]{:S(2)}) collective-permute-start(bf16[2,16,512]{2,1,0:T(8,128)(2,1)S(1)} %get-tuple-element.58.pack_ref), channel_id=1, source_target_pairs={{0,1},{1,0},{2,3},{3,2},{248,249},{249,248},{250,251},{251,250},{8... | collective-permute-start | bytes 98312 | tf_op jit(solution)/shard_map/ppermute | solution.py:466
  81.5 1.2 %collective-permute-start.13 = (bf16[2,16,512]{2,1,0:T(8,128)(2,1)S(1)}, bf16[2,16,512]{2,1,0:T(8,128)(2,1)S(1)}, u32[]{:S(2)}, u32[]{:S(2)}) collective-permute-start(bf16[2,16,512]{2,1,0:T(8,128)(2,1)S(1)} %shard_map.109.next_ref), channel_id=1, source_target_pairs={{0,8},{8,0},{1,9},{9,1},{2,10},{10,2},{3,11},{11,3},{4,12},{12,4},... | collective-permute-start | bytes 98312 | tf_op jit(solution)/shard_map/ppermute | solution.py:492
  82.9 5.5 %collective-permute-start.14 = (f32[16,512]{1,0:T(8,128)S(1)}, f32[16,512]{1,0:T(8,128)S(1)}, u32[]{:S(2)}, u32[]{:S(2)}) collective-permute-start(f32[16,512]{1,0:T(8,128)S(1)} %shard_map.111.own_ref), channel_id=1, source_target_pairs={{0,2},{1,3},{2,0},{3,1},{4,6},{5,7},{6,4},{7,5},{8,10},{9,11},{10,... | collective-permute-start | bytes 98312 | tf_op jit(solution)/shard_map/ppermute | solution.py:512
  86.3 3.9 %collective-permute-start.15 = (f32[16,512]{1,0:T(8,128)S(1)}, f32[16,512]{1,0:T(8,128)S(1)}, u32[]{:S(2)}, u32[]{:S(2)}) collective-permute-start(f32[16,512]{1,0:T(8,128)S(1)} %shard_map.111.own_ref), channel_id=1, source_target_pairs={{0,1},{1,2},{2,3},{3,0},{4,5},{5,6},{6,7},{7,4},{8,9},{9,10},{10,1... | collective-permute-start | bytes 98312 | tf_op jit(solution)/shard_map/ppermute | solution.py:512
  86.7 5.1 %collective-permute-start.16 = (f32[16,512]{1,0:T(8,128)S(1)}, f32[16,512]{1,0:T(8,128)S(1)}, u32[]{:S(2)}, u32[]{:S(2)}) collective-permute-start(f32[16,512]{1,0:T(8,128)S(1)} %shard_map.111.own_ref), channel_id=1, source_target_pairs={{0,3},{1,0},{2,1},{3,2},{4,7},{5,4},{6,5},{7,6},{8,11},{9,8},{10,9... | collective-permute-start | bytes 98312 | tf_op jit(solution)/shard_map/ppermute | solution.py:512

commit v10 on v9

--- a/solution.py
+++ b/solution.py
@@ -65,7 +65,7 @@
 
 def away_kernel(
     core_ref, rank_ref, lag_ref, hist_ref, right_ref, left_ref,
-    out_ref, hist_buf, right_own, left_own, columns_ref,
+    out_ref, hist_buf, right_own, columns_ref,
     rank_buf, lag_buf, right_buf, left_buf, small_sem, right_sem, left_sem, *, ranks
 ):
     groups, chips, depth, _ = right_buf.shape
@@ -85,12 +85,8 @@
     for g in range(groups):
         rights[g].start()
         lefts[g].start()
-    late = [
-        brought(right_ref, right_own, right_sem.at[groups], 0, core),
-        brought(left_ref, left_own, left_sem.at[groups], 0, core),
-    ]
-    for copy in late:
-        copy.start()
+    late = brought(right_ref, right_own, right_sem.at[groups], 0, core)
+    late.start()
     small[0].wait()
     small[1].wait()
     columns = []
@@ -108,34 +104,31 @@
             ahead = chosen(hist_buf, right_buf.at[g + 1], columns[g + 1])
         far(g, value, left_buf.at[g], out_ref)
         value = ahead
-    for copy in late:
-        copy.wait()
+    late.wait()
 
 
 def own_kernel(
-    core_ref, hist_ref, right_own, left_own, columns_ref, right_ref, left_ref, out_ref,
+    core_ref, hist_ref, right_own, columns_ref, right_ref, left_ref, out_ref,
     right_buf, left_buf, right_sem, left_sem
 ):
     core = core_ref[0]
-    groups = right_buf.shape[0] + 1
+    groups = left_buf.shape[0]
+    lefts = [brought(left_ref, left_buf.at[g], left_sem.at[g], g, core) for g in range(groups)]
     rights = [
         brought(right_ref, right_buf.at[g], right_sem.at[g], g + 1, core) for g in range(groups - 1)
     ]
-    lefts = [
-        brought(left_ref, left_buf.at[g], left_sem.at[g], g + 1, core) for g in range(groups - 1)
-    ]
-    for g in range(groups - 1):
-        rights[g].start()
+    for g in range(groups):
         lefts[g].start()
+        if g + 1 < groups:
+            rights[g].start()
     value = chosen(hist_ref, right_own, columns_ref[0:1])
     for g in range(groups):
-        if g > 0:
-            lefts[g - 1].wait()
+        lefts[g].wait()
         ahead = None
         if g + 1 < groups:
             rights[g].wait()
             ahead = chosen(hist_ref, right_buf.at[g], columns_ref[g + 1 : g + 2])
-        far(g, value, left_own if g == 0 else left_buf.at[g - 1], out_ref)
+        far(g, value, left_buf.at[g], out_ref)
         value = ahead
 
 
@@ -154,17 +147,16 @@
         transcendentals=0,
     )
     semaphores = pltpu.SemaphoreType.DMA
-    away, hist_buf, right_own, left_own, columns = pl.pallas_call(
+    away, hist_buf, right_own, columns = pl.pallas_call(
         functools.partial(away_kernel, ranks=ranks),
         out_shape=(
             field,
             jax.ShapeDtypeStruct(history.shape, history.dtype),
             jax.ShapeDtypeStruct(block, right.dtype),
-            jax.ShapeDtypeStruct(block, left.dtype),
             jax.ShapeDtypeStruct((GROUPS, chips * depth), jnp.int32),
         ),
         in_specs=[scalar] + [outside] * 5,
-        out_specs=[inside] * 5,
+        out_specs=[inside] * 4,
         scratch_shapes=[
             pltpu.SMEM(rank.shape, jnp.int32),
             pltpu.SMEM(lag.shape, jnp.int32),
@@ -172,7 +164,7 @@
             pltpu.VMEM((GROUPS, *block), left.dtype),
             semaphores((3,)),
             semaphores((GROUPS + 1,)),
-            semaphores((GROUPS + 1,)),
+            semaphores((GROUPS,)),
         ],
         compiler_params=pltpu.CompilerParams(vmem_limit_bytes=16 << 20),
         cost_estimate=cost,
@@ -183,18 +175,18 @@
         return pl.pallas_call(
             own_kernel,
             out_shape=field,
-            in_specs=[scalar] + [inside] * 4 + [outside] * 2,
+            in_specs=[scalar] + [inside] * 3 + [outside] * 2,
             out_specs=inside,
             scratch_shapes=[
                 pltpu.VMEM((GROUPS - 1, *block), right.dtype),
-                pltpu.VMEM((GROUPS - 1, *block), left.dtype),
+                pltpu.VMEM((GROUPS, *block), left.dtype),
                 semaphores((GROUPS - 1,)),
-                semaphores((GROUPS - 1,)),
+                semaphores((GROUPS,)),
             ],
             compiler_params=pltpu.CompilerParams(vmem_limit_bytes=16 << 20),
             cost_estimate=cost,
             name="far_own",
-        )(core, hist_buf, right_own, left_own, columns, right, left)
+        )(core, hist_buf, right_own, columns, right, left)
 
     return away, own
 
@@ -467,8 +459,6 @@
 
     twice = plane_sum(arrived, 2).reshape(8, -1, width)
     arrived = lax.all_to_all(twice, ("zh", "zl"), 0, 0, tiled=True)
-    back = off_chip(toward)
-    back = jnp.where((block == 0) | (block == targets - 1), 0.0, back)
     arrived, incoming, shifted, chip_u, away_u = lax.optimization_barrier(
         (arrived, incoming, shifted, chip_u, away_u)
     )
@@ -478,6 +468,8 @@
     c, value = small_call(right_kernel, 0, (single, rounded), arrived, given, inverse)
     got = off_chip(value)
     c_u = lax.ppermute(c, "c", swap)
+    back = off_chip(toward)
+    back = jnp.where((block == 0) | (block == targets - 1), 0.0, back)
     (part,) = small_call(inner_kernel, 2, (single,), value, c_u, c, inverse, near_own, near_chip)
     (value,) = small_call(simple_kernel, 1, (rounded,), part, got, inverse, near_away)
     beside = lax.ppermute(value, "c", swap)

time: 93.7 us -> 93.8 us (level)
  transfers between devices with their start and end apart: 19 -> 19, of which waited for: 12 -> 12; matrix products, arithmetic and copies ran while one was open for 8% -> 8% of each run, Pallas kernels for 8% -> 9%
where the time goes in v10:
time: 93.8 us; the launch traced here: 93.3 us
  waiting for transfers between devices  35.5 us (38%)
  starting transfers between devices  31.9 us (34%)
  Pallas kernels  17 us (18%)
  other arithmetic  7.81 us (8%)
  between operations  1.02 us (1%)
    ppermute x5, waiting for transfers between devices, off_chip(): return lax.ppermute(value, SPACE + ('y',), between)  12.5 us
    all_to_all x1, waiting for transfers between devices, per_device(): lax.all_to_all(partial_value.reshape(16, -1, width), ('x', 'y'), 0, 0, ti...  11 us
    ppermute x5, starting transfers between devices, off_chip(): return lax.ppermute(value, SPACE + ('y',), between)  7.36 us
    all_to_all x1, starting transfers between devices, per_device(): lax.all_to_all(partial_value.reshape(16, -1, width), ('x', 'y'), 0, 0, ti...  7 us
    ppermute x1, starting transfers between devices, per_device(): lax.ppermute(history[-1], HIST, [(i, (i + 1) % 8) for i in range(8)])  6.02 us
    pallas_call x17, Pallas kernels, small_call(): pl.pallas_call(kernel, out_shape=outs, in_specs=[inside] * len(operands),...  5.8 us
    all_to_all x1, waiting for transfers between devices, per_device(): arrived = lax.all_to_all(twice, ('zh', 'zl'), 0, 0, tiled=True)  5.45 us
    ppermute x3, starting transfers between devices, per_device(): lax.ppermute(current, 'y', [(i, (i + step) % 4) for i in range(4)])  5.37 us
  transfers between devices with their start and end apart: 19, of which 12 were waited for; matrix products, arithmetic and copies ran while one was open for 8% of the time, Pallas kernels for 9%

profile of v10, /device:TPU:56, one launch (start us, length us, event | category | flops | bytes accessed | tf_op | source)
XLA Modules:
  0.0 93.3 jit_solution(11042264420847029091)
XLA Ops:
  0.6 0.0 copy-start
  0.7 4.9 %far_away.1 = (bf16[4,4,4,16,512]{4,3,2,1,0:T(8,128)(2,1)S(1)}, bf16[4,64,512]{2,1,0:T(8,128)(2,1)S(1)}, bf16[8,160,512]{2,1,0:T(8,128)(2,1)S(1)}, s32[2,1280]{1,0:T(2,128)S(1)}) custom-call(s32[1]{0:T(128)} %bitcast.2.core_ref, s32[64]{0:T(128)} %bitcast.47, s32[64]{0:T(128)} %bitcast.48, bf16[4,64,512]{2,1,0:T(8,128)(2,1)} %hist_ref.1, ...), custom_call_target="tpu_custom_call" | custom-call | flops 838860800 | bytes 6291456 | tf_op jit(solution)/shard_map/far_away/pallas_call | solution.py:150
  5.6 0.1 collective-permute-start
  5.7 0.5 collective-permute-start.2
  6.2 6.0 %collective-permute-start.1 = (bf16[64,512]{1,0:T(8,128)(2,1)S(1)}, bf16[64,512]{1,0:T(8,128)(2,1)S(1)}, u32[]{:S(2)}, u32[]{:S(2)}) collective-permute-start(bf16[64,512]{1,0:T(8,128)(2,1)S(1)} %slice_bitcast_fusion.2), channel_id=1, source_target_pairs={{0,1},{1,2},{2,3},{3,4},{4,5},{5,6},{6,7},{7,0},{8,9},{9,10},{10,1... | collective-permute-start | bytes 196616 | tf_op jit(solution)/shard_map/ppermute | solution.py:422
  12.2 0.0 collective-permute-start.3
  12.2 3.2 %far_own.1.mine_ref = bf16[4,4,4,16,512]{4,3,2,1,0:T(8,128)(2,1)S(1)} custom-call(s32[1]{0:T(128)} %bitcast.2.core_ref, bf16[4,64,512]{2,1,0:T(8,128)(2,1)S(1)} %get-tuple-element.31.hist_ref, bf16[8,160,512]{2,1,0:T(8,128)(2,1)S(1)} %get-tuple-element.32.right_own, s32[2,1280]{1,0:T(2,128)S(1)} %get-tuple-element.33.columns_ref, ...), custom_call_target="tpu_custom_call" | custom-call | flops 838860800 | bytes 6291456 | tf_op jit(solution)/shard_map/far_own/pallas_call | solution.py:175
  15.4 0.0 collective-permute-done.came_ref
  15.4 1.1 %halves_sum.1 = bf16[4,4,4,16,512]{4,3,2,1,0:T(8,128)(2,1)} custom-call(bf16[4,4,4,16,512]{4,3,2,1,0:T(8,128)(2,1)S(1)} %far_own.1.mine_ref, bf16[4,4,4,16,512]{4,3,2,1,0:T(8,128)(2,1)S(1)} %collective-permute-done.came_ref), custom_call_target="tpu_custom_call" | custom-call | flops 524288 | bytes 3145728 | tf_op jit(solution)/shard_map/halves_sum/pallas_call | solution.py:208
  16.5 7.0 %all-to-all-start = ((bf16[16,64,512]{2,1,0:T(8,128)(2,1)}), bf16[16,64,512]{2,1,0:T(8,128)(2,1)S(1)}, u32[]{:S(2)}, u32[]{:S(2)}) async-start(bf16[16,64,512]{2,1,0:T(8,128)(2,1)} %bitcast.7), calls=%async_computation | async-start | bytes 2097152 | tf_op jit(solution)/shard_map/all_to_all | solution.py:421
  23.5 1.5 %slice_bitcast_fusion.1 = (bf16[512,512]{1,0:T(8,128)(2,1)S(1)}, bf16[512,512]{1,0:T(8,128)(2,1)S(1)}) fusion(bf16[3,512,512]{2,1,0:T(8,128)(2,1)} %param.13, pred[]{:T(512)S(6)} %eq.28), kind=kLoop, calls=%fused_computation.2 | loop fusion | flops 262144 | bytes 2621441 | tf_op jit(solution)/shard_map/squeeze | solution.py:435
  25.0 0.0 slice-start
  25.0 2.2 %multiply_convert_fusion = (bf16[512,512]{1,0:T(8,128)(2,1)}, bf16[512,512]{1,0:T(8,128)(2,1)S(1)}) fusion(f32[512]{0:T(512)S(1)} %broadcast_divide_fusion, bf16[3,512,512]{2,1,0:T(8,128)(2,1)} %param.13, pred[]{:T(512)S(6)} %eq.28, pred[]{:T(512)S(6)} %or.7), kind=kLoop, calls=%fused_computation | loop fusion | flops 1310720 | bytes 2099202 | tf_op jit(solution)/shard_map/convert_element_type | solution.py:437
  27.2 0.8 dynamic-slice_multiply_fusion.given_ref
  28.0 0.0 collective-permute-done.3
  28.0 0.0 collective-permute-done.1.incoming_ref
  28.0 0.0 collective-permute-done.2
  28.0 11.0 %all-to-all-done.in_ref = bf16[16,64,512]{2,1,0:T(8,128)(2,1)S(1)} async-done(((bf16[16,64,512]{2,1,0:T(8,128)(2,1)}), bf16[16,64,512]{2,1,0:T(8,128)(2,1)S(1)}, u32[]{:S(2)}, u32[]{:S(2)}) %all-to-all-start) | async-done | bytes 1048608 | tf_op jit(solution)/shard_map/all_to_all | solution.py:421
  39.0 0.2 collective-permute-start.7
  39.3 0.8 plane_sum.1
  40.1 5.2 %all-to-all-start.1 = ((bf16[8,16,512]{2,1,0:T(8,128)(2,1)}), bf16[8,16,512]{2,1,0:T(8,128)(2,1)S(1)}, u32[]{:S(2)}, u32[]{:S(2)}) async-start(bf16[8,16,512]{2,1,0:T(8,128)(2,1)} %bitcast.12), calls=%async_computation.1 | async-start | bytes 262144 | tf_op jit(solution)/shard_map/all_to_all | solution.py:461
  45.3 0.7 pad_maximum_fusion.shifted_ref
  46.1 1.5 %slice_bitcast_fusion = (bf16[512,512]{1,0:T(8,128)(2,1)S(1)}, bf16[512,512]{1,0:T(8,128)(2,1)S(1)}, bf16[512,512]{1,0:T(8,128)(2,1)S(1)}) fusion(bf16[3,512,512]{2,1,0:T(8,128)(2,1)} %collective-permute-done.2, pred[]{:T(512)S(6)} %eq.31, pred[]{:T(512)S(6)} %or.8), kind=kLoop, calls=%fused_computation.1 | loop fusion | flops 786432 | bytes 3145730 | tf_op jit(solution)/shard_map/squeeze | solution.py:447
  47.5 5.5 %all-to-all-done.1.arrived_ref = bf16[8,16,512]{2,1,0:T(8,128)(2,1)S(1)} async-done(((bf16[8,16,512]{2,1,0:T(8,128)(2,1)}), bf16[8,16,512]{2,1,0:T(8,128)(2,1)S(1)}, u32[]{:S(2)}, u32[]{:S(2)}) %all-to-all-start.1) | async-done | bytes 131104 | tf_op jit(solution)/shard_map/all_to_all | solution.py:461
  53.0 0.1 collective-permute-start.4
  53.1 1.8 %collective-permute-start.5 = (bf16[16,512]{1,0:T(8,128)(2,1)S(1)}, bf16[16,512]{1,0:T(8,128)(2,1)S(1)}, u32[]{:S(2)}, u32[]{:S(2)}) collective-permute-start(bf16[16,512]{1,0:T(8,128)(2,1)S(1)} %get-tuple-element.40.value_ref), channel_id=1, source_target_pairs={{0,1},{1,0},{2,3},{3,2},{248,249},{249,248},{250,251},{251,250},{8... | collective-permute-start | bytes 49160 | tf_op jit(solution)/shard_map/ppermute | solution.py:458
  54.9 0.4 shard_map.96.part_ref
  55.3 3.1 %collective-permute-done.5.got_ref = bf16[16,512]{1,0:T(8,128)(2,1)S(1)} collective-permute-done((bf16[16,512]{1,0:T(8,128)(2,1)S(1)}, bf16[16,512]{1,0:T(8,128)(2,1)S(1)}, u32[]{:S(2)}, u32[]{:S(2)}) %collective-permute-start.5) | collective-permute-done | bytes 16416 | tf_op jit(solution)/shard_map/ppermute | solution.py:458
  58.5 0.2 shard_map.97.value_ref
  58.7 0.2 shard_map.98.part_ref
  59.0 0.9 %collective-permute-done.6.beside_ref = bf16[16,512]{1,0:T(8,128)(2,1)S(1)} collective-permute-done((bf16[16,512]{1,0:T(8,128)(2,1)S(1)}, bf16[16,512]{1,0:T(8,128)(2,1)S(1)}, u32[]{:S(2)}, u32[]{:S(2)}) %collective-permute-start.6) | collective-permute-done | bytes 16416 | tf_op jit(solution)/shard_map/ppermute | solution.py:475
  59.9 0.2 shard_map.99
  60.1 1.8 %collective-permute-start.8 = (bf16[2,16,512]{2,1,0:T(8,128)(2,1)S(1)}, bf16[2,16,512]{2,1,0:T(8,128)(2,1)S(1)}, u32[]{:S(2)}, u32[]{:S(2)}) collective-permute-start(bf16[2,16,512]{2,1,0:T(8,128)(2,1)S(1)} %get-tuple-element.44.pack_ref), channel_id=1, source_target_pairs={{0,1},{1,0},{2,3},{3,2},{248,249},{249,248},{250,251},{251,250},{8... | collective-permute-start | bytes 98312 | tf_op jit(solution)/shard_map/ppermute | solution.py:458
  61.9 0.0 collective-permute-done.7
  61.9 1.1 %broadcast_select_fusion.back_ref = bf16[512,512]{1,0:T(8,128)(2,1)S(1)} fusion(bf16[512,512]{1,0:T(8,128)(2,1)} %collective-permute-done.7, pred[]{:T(512)S(6)} %or.7), kind=kLoop, calls=%fused_computation.7 | loop fusion | flops 262144 | bytes 1048577 | tf_op jit(solution)/shard_map/jit(_where)/select_n | solution.py:472
  63.0 0.2 shard_map.100.known_ref
  63.2 2.4 %collective-permute-done.8.got_ref = bf16[2,16,512]{2,1,0:T(8,128)(2,1)S(1)} collective-permute-done((bf16[2,16,512]{2,1,0:T(8,128)(2,1)S(1)}, bf16[2,16,512]{2,1,0:T(8,128)(2,1)S(1)}, u32[]{:S(2)}, u32[]{:S(2)}) %collective-permute-start.8) | collective-permute-done | bytes 32800 | tf_op jit(solution)/shard_map/ppermute | solution.py:458
  65.6 0.2 shard_map.101.next_ref
  65.9 0.5 shard_map.102
  66.4 0.7 collective-permute-done.9.got_ref
  67.1 0.8 shard_map.103
  67.9 1.8 %collective-permute-start.10 = (bf16[2,16,512]{2,1,0:T(8,128)(2,1)S(1)}, bf16[2,16,512]{2,1,0:T(8,128)(2,1)S(1)}, u32[]{:S(2)}, u32[]{:S(2)}) collective-permute-start(bf16[2,16,512]{2,1,0:T(8,128)(2,1)S(1)} %get-tuple-element.52.pack_ref), channel_id=1, source_target_pairs={{0,1},{1,0},{2,3},{3,2},{248,249},{249,248},{250,251},{251,250},{8... | collective-permute-start | bytes 98312 | tf_op jit(solution)/shard_map/ppermute | solution.py:458
  69.7 0.2 shard_map.104.known_ref
  69.9 3.5 %collective-permute-done.10.got_ref = bf16[2,16,512]{2,1,0:T(8,128)(2,1)S(1)} collective-permute-done((bf16[2,16,512]{2,1,0:T(8,128)(2,1)S(1)}, bf16[2,16,512]{2,1,0:T(8,128)(2,1)S(1)}, u32[]{:S(2)}, u32[]{:S(2)}) %collective-permute-start.10) | collective-permute-done | bytes 32800 | tf_op jit(solution)/shard_map/ppermute | solution.py:458
  73.4 0.2 shard_map.105.next_ref
  73.6 0.2 collective-permute-start.11
  73.8 0.5 shard_map.106
  74.3 0.7 collective-permute-done.11.got_ref
  75.0 0.8 shard_map.107
  75.8 1.8 %collective-permute-start.12 = (bf16[2,16,512]{2,1,0:T(8,128)(2,1)S(1)}, bf16[2,16,512]{2,1,0:T(8,128)(2,1)S(1)}, u32[]{:S(2)}, u32[]{:S(2)}) collective-permute-start(bf16[2,16,512]{2,1,0:T(8,128)(2,1)S(1)} %get-tuple-element.56.pack_ref), channel_id=1, source_target_pairs={{0,1},{1,0},{2,3},{3,2},{248,249},{249,248},{250,251},{251,250},{8... | collective-permute-start | bytes 98312 | tf_op jit(solution)/shard_map/ppermute | solution.py:458
  77.6 0.2 shard_map.108.known_ref
  77.8 3.5 %collective-permute-done.12.got_ref = bf16[2,16,512]{2,1,0:T(8,128)(2,1)S(1)} collective-permute-done((bf16[2,16,512]{2,1,0:T(8,128)(2,1)S(1)}, bf16[2,16,512]{2,1,0:T(8,128)(2,1)S(1)}, u32[]{:S(2)}, u32[]{:S(2)}) %collective-permute-start.12) | collective-permute-done | bytes 32800 | tf_op jit(solution)/shard_map/ppermute | solution.py:458
  81.3 0.2 shard_map.109.next_ref
  81.5 0.0 collective-permute-start.13
  81.5 0.4 shard_map.110.part_ref
  81.9 0.8 collective-permute-done.13.got_ref
  82.7 0.2 shard_map.111.own_ref
  83.0 3.3 %collective-permute-start.14 = (f32[16,512]{1,0:T(8,128)S(1)}, f32[16,512]{1,0:T(8,128)S(1)}, u32[]{:S(2)}, u32[]{:S(2)}) collective-permute-start(f32[16,512]{1,0:T(8,128)S(1)} %shard_map.111.own_ref), channel_id=1, source_target_pairs={{0,2},{1,3},{2,0},{3,1},{4,6},{5,7},{6,4},{7,5},{8,10},{9,11},{10,... | collective-permute-start | bytes 98312 | tf_op jit(solution)/shard_map/ppermute | solution.py:504
  86.3 0.4 collective-permute-start.15
  86.7 1.6 %collective-permute-start.16 = (f32[16,512]{1,0:T(8,128)S(1)}, f32[16,512]{1,0:T(8,128)S(1)}, u32[]{:S(2)}, u32[]{:S(2)}) collective-permute-start(f32[16,512]{1,0:T(8,128)S(1)} %shard_map.111.own_ref), channel_id=1, source_target_pairs={{0,3},{1,0},{2,1},{3,2},{4,7},{5,4},{6,5},{7,6},{8,11},{9,8},{10,9... | collective-permute-start | bytes 98312 | tf_op jit(solution)/shard_map/ppermute | solution.py:504
  88.4 0.1 pad_add_fusion.where_ref
  88.4 1.8 %collective-permute-done.15.first_ref = f32[16,512]{1,0:T(8,128)S(1)} collective-permute-done((f32[16,512]{1,0:T(8,128)S(1)}, f32[16,512]{1,0:T(8,128)S(1)}, u32[]{:S(2)}, u32[]{:S(2)}) %collective-permute-start.15) | collective-permute-done | bytes 32800 | tf_op jit(solution)/shard_map/ppermute | solution.py:504
  90.2 1.6 %collective-permute-done.16.third_ref = f32[16,512]{1,0:T(8,128)S(1)} collective-permute-done((f32[16,512]{1,0:T(8,128)S(1)}, f32[16,512]{1,0:T(8,128)S(1)}, u32[]{:S(2)}, u32[]{:S(2)}) %collective-permute-start.16) | collective-permute-done | bytes 32800 | tf_op jit(solution)/shard_map/ppermute | solution.py:504
  91.9 1.3 %finish.1 = (f32[64,512]{1,0:T(8,128)}, bf16[4,64,512]{2,1,0:T(8,128)(2,1)}) custom-call(s32[2]{0:T(128)S(1)} %pad_add_fusion.where_ref, f32[16,512]{1,0:T(8,128)S(1)} %shard_map.111.own_ref, f32[16,512]{1,0:T(8,128)S(1)} %collective-permute-done.14.second_ref, f32[16,512]{1,0:T(8,128)S(1)} %collective-permute-done.15.first_ref, ...), custom_call_target="tpu_custom_call", output_to_operand_aliasing={{1}: (6, {})} | custom-call | tf_op jit(solution)/shard_map/finish/pallas_call | solution.py:286
  (12 shorter events, 0.1 us)
Async XLA Ops:
  0.6 5.5 %copy-start = (bf16[4,64,512]{2,1,0:T(8,128)(2,1)S(1)}, bf16[4,64,512]{2,1,0:T(8,128)(2,1)}, u32[]{:S(2)}) copy-start(bf16[4,64,512]{2,1,0:T(8,128)(2,1)} %hist_ref.1) | copy-start | bytes 786436
  0.6 11.6 %copy-start.1 = (f32[512]{0:T(512)S(1)}, f32[512]{0:T(512)}, u32[]{:S(2)}) copy-start(f32[512]{0:T(512)} %param.14) | copy-start | bytes 6148
  5.6 9.8 %collective-permute-start = (bf16[4,4,4,16,512]{4,3,2,1,0:T(8,128)(2,1)S(1)}, bf16[4,4,4,16,512]{4,3,2,1,0:T(8,128)(2,1)S(1)}, u32[]{:S(2)}, u32[]{:S(2)}) collective-permute-start(bf16[4,4,4,16,512]{4,3,2,1,0:T(8,128)(2,1)S(1)} %get-tuple-element.34), channel_id=1, source_target_pairs={{0,8},{8,0},{1,9},{9,1},{2,10},{10,2},{3,11},{11,3},{4,12},{12,4},... | collective-permute-start | bytes 3145736 | tf_op jit(solution)/shard_map/ppermute | solution.py:418
  5.7 22.3 %collective-permute-start.2 = (bf16[3,512,512]{2,1,0:T(8,128)(2,1)}, bf16[3,512,512]{2,1,0:T(8,128)(2,1)}, u32[]{:S(2)}, u32[]{:S(2)}) collective-permute-start(bf16[3,512,512]{2,1,0:T(8,128)(2,1)} %param.13), channel_id=1, source_target_pairs={{0,8},{8,0},{1,9},{9,1},{2,10},{10,2},{3,11},{11,3},{4,12},{12,4},... | collective-permute-start | bytes 4718600 | tf_op jit(solution)/shard_map/ppermute | solution.py:423
  6.2 21.8 %collective-permute-start.1 = (bf16[64,512]{1,0:T(8,128)(2,1)S(1)}, bf16[64,512]{1,0:T(8,128)(2,1)S(1)}, u32[]{:S(2)}, u32[]{:S(2)}) collective-permute-start(bf16[64,512]{1,0:T(8,128)(2,1)S(1)} %slice_bitcast_fusion.2), channel_id=1, source_target_pairs={{0,1},{1,2},{2,3},{3,4},{4,5},{5,6},{6,7},{7,0},{8,9},{9,10},{10,1... | collective-permute-start | bytes 196616 | tf_op jit(solution)/shard_map/ppermute | solution.py:422
  12.2 15.8 %collective-permute-start.3 = (f32[1,512]{1,0:T(1,128)S(1)}, f32[1,512]{1,0:T(1,128)S(1)}, u32[]{:S(2)}, u32[]{:S(2)}) collective-permute-start(f32[1,512]{1,0:T(1,128)S(1)} %bitcast.46), channel_id=1, source_target_pairs={{0,8},{8,0},{1,9},{9,1},{2,10},{10,2},{3,11},{11,3},{4,12},{12,4},... | collective-permute-start | bytes 6152 | tf_op jit(solution)/shard_map/ppermute | solution.py:424
  16.5 22.5 %all-to-all-start = ((bf16[16,64,512]{2,1,0:T(8,128)(2,1)}), bf16[16,64,512]{2,1,0:T(8,128)(2,1)S(1)}, u32[]{:S(2)}, u32[]{:S(2)}) async-start(bf16[16,64,512]{2,1,0:T(8,128)(2,1)} %bitcast.7), calls=%async_computation | async-start | bytes 2097152 | tf_op jit(solution)/shard_map/all_to_all | solution.py:421
  25.0 20.4 %slice-start = ((bf16[4,64,512]{2,1,0:T(8,128)(2,1)}), bf16[3,64,512]{2,1,0:T(8,128)(2,1)S(1)}, s32[]{:S(2)}) async-start(bf16[4,64,512]{2,1,0:T(8,128)(2,1)} %hist_ref.1), calls=%async_computation.2 | async-start | bytes 393216 | tf_op jit(solution)/shard_map/slice | solution.py:448
  39.0 22.9 %collective-permute-start.7 = (bf16[512,512]{1,0:T(8,128)(2,1)}, bf16[512,512]{1,0:T(8,128)(2,1)}, u32[]{:S(2)}, u32[]{:S(2)}) collective-permute-start(bf16[512,512]{1,0:T(8,128)(2,1)} %get-tuple-element.45), channel_id=1, source_target_pairs={{0,1},{1,0},{2,3},{3,2},{248,249},{249,248},{250,251},{251,250},{8... | collective-permute-start | bytes 1572872 | tf_op jit(solution)/shard_map/ppermute | solution.py:458
  40.1 12.9 %all-to-all-start.1 = ((bf16[8,16,512]{2,1,0:T(8,128)(2,1)}), bf16[8,16,512]{2,1,0:T(8,128)(2,1)S(1)}, u32[]{:S(2)}, u32[]{:S(2)}) async-start(bf16[8,16,512]{2,1,0:T(8,128)(2,1)} %bitcast.12), calls=%async_computation.1 | async-start | bytes 262144 | tf_op jit(solution)/shard_map/all_to_all | solution.py:461
  53.0 1.9 %collective-permute-start.4 = (f32[16,512]{1,0:T(8,128)S(1)}, f32[16,512]{1,0:T(8,128)S(1)}, u32[]{:S(2)}, u32[]{:S(2)}) collective-permute-start(f32[16,512]{1,0:T(8,128)S(1)} %get-tuple-element.41.c_ref), channel_id=1, source_target_pairs={{0,8},{8,0},{1,9},{9,1},{2,10},{10,2},{3,11},{11,3},{4,12},{12,4},... | collective-permute-start | bytes 98312 | tf_op jit(solution)/shard_map/ppermute | solution.py:470
  53.1 5.4 %collective-permute-start.5 = (bf16[16,512]{1,0:T(8,128)(2,1)S(1)}, bf16[16,512]{1,0:T(8,128)(2,1)S(1)}, u32[]{:S(2)}, u32[]{:S(2)}) collective-permute-start(bf16[16,512]{1,0:T(8,128)(2,1)S(1)} %get-tuple-element.40.value_ref), channel_id=1, source_target_pairs={{0,1},{1,0},{2,3},{3,2},{248,249},{249,248},{250,251},{251,250},{8... | collective-permute-start | bytes 49160 | tf_op jit(solution)/shard_map/ppermute | solution.py:458
  58.7 1.2 %collective-permute-start.6 = (bf16[16,512]{1,0:T(8,128)(2,1)S(1)}, bf16[16,512]{1,0:T(8,128)(2,1)S(1)}, u32[]{:S(2)}, u32[]{:S(2)}) collective-permute-start(bf16[16,512]{1,0:T(8,128)(2,1)S(1)} %shard_map.97.value_ref), channel_id=1, source_target_pairs={{0,8},{8,0},{1,9},{9,1},{2,10},{10,2},{3,11},{11,3},{4,12},{12,4},... | collective-permute-start | bytes 49160 | tf_op jit(solution)/shard_map/ppermute | solution.py:475
  60.1 5.5 %collective-permute-start.8 = (bf16[2,16,512]{2,1,0:T(8,128)(2,1)S(1)}, bf16[2,16,512]{2,1,0:T(8,128)(2,1)S(1)}, u32[]{:S(2)}, u32[]{:S(2)}) collective-permute-start(bf16[2,16,512]{2,1,0:T(8,128)(2,1)S(1)} %get-tuple-element.44.pack_ref), channel_id=1, source_target_pairs={{0,1},{1,0},{2,3},{3,2},{248,249},{249,248},{250,251},{251,250},{8... | collective-permute-start | bytes 98312 | tf_op jit(solution)/shard_map/ppermute | solution.py:458
  65.8 1.2 %collective-permute-start.9 = (bf16[2,16,512]{2,1,0:T(8,128)(2,1)S(1)}, bf16[2,16,512]{2,1,0:T(8,128)(2,1)S(1)}, u32[]{:S(2)}, u32[]{:S(2)}) collective-permute-start(bf16[2,16,512]{2,1,0:T(8,128)(2,1)S(1)} %shard_map.101.next_ref), channel_id=1, source_target_pairs={{0,8},{8,0},{1,9},{9,1},{2,10},{10,2},{3,11},{11,3},{4,12},{12,4},... | collective-permute-start | bytes 98312 | tf_op jit(solution)/shard_map/ppermute | solution.py:484
  67.9 5.5 %collective-permute-start.10 = (bf16[2,16,512]{2,1,0:T(8,128)(2,1)S(1)}, bf16[2,16,512]{2,1,0:T(8,128)(2,1)S(1)}, u32[]{:S(2)}, u32[]{:S(2)}) collective-permute-start(bf16[2,16,512]{2,1,0:T(8,128)(2,1)S(1)} %get-tuple-element.52.pack_ref), channel_id=1, source_target_pairs={{0,1},{1,0},{2,3},{3,2},{248,249},{249,248},{250,251},{251,250},{8... | collective-permute-start | bytes 98312 | tf_op jit(solution)/shard_map/ppermute | solution.py:458
  73.6 1.4 %collective-permute-start.11 = (bf16[2,16,512]{2,1,0:T(8,128)(2,1)S(1)}, bf16[2,16,512]{2,1,0:T(8,128)(2,1)S(1)}, u32[]{:S(2)}, u32[]{:S(2)}) collective-permute-start(bf16[2,16,512]{2,1,0:T(8,128)(2,1)S(1)} %shard_map.105.next_ref), channel_id=1, source_target_pairs={{0,8},{8,0},{1,9},{9,1},{2,10},{10,2},{3,11},{11,3},{4,12},{12,4},... | collective-permute-start | bytes 98312 | tf_op jit(solution)/shard_map/ppermute | solution.py:484
  75.8 5.5 %collective-permute-start.12 = (bf16[2,16,512]{2,1,0:T(8,128)(2,1)S(1)}, bf16[2,16,512]{2,1,0:T(8,128)(2,1)S(1)}, u32[]{:S(2)}, u32[]{:S(2)}) collective-permute-start(bf16[2,16,512]{2,1,0:T(8,128)(2,1)S(1)} %get-tuple-element.56.pack_ref), channel_id=1, source_target_pairs={{0,1},{1,0},{2,3},{3,2},{248,249},{249,248},{250,251},{251,250},{8... | collective-permute-start | bytes 98312 | tf_op jit(solution)/shard_map/ppermute | solution.py:458
  81.5 1.2 %collective-permute-start.13 = (bf16[2,16,512]{2,1,0:T(8,128)(2,1)S(1)}, bf16[2,16,512]{2,1,0:T(8,128)(2,1)S(1)}, u32[]{:S(2)}, u32[]{:S(2)}) collective-permute-start(bf16[2,16,512]{2,1,0:T(8,128)(2,1)S(1)} %shard_map.109.next_ref), channel_id=1, source_target_pairs={{0,8},{8,0},{1,9},{9,1},{2,10},{10,2},{3,11},{11,3},{4,12},{12,4},... | collective-permute-start | bytes 98312 | tf_op jit(solution)/shard_map/ppermute | solution.py:484
  83.0 5.5 %collective-permute-start.14 = (f32[16,512]{1,0:T(8,128)S(1)}, f32[16,512]{1,0:T(8,128)S(1)}, u32[]{:S(2)}, u32[]{:S(2)}) collective-permute-start(f32[16,512]{1,0:T(8,128)S(1)} %shard_map.111.own_ref), channel_id=1, source_target_pairs={{0,2},{1,3},{2,0},{3,1},{4,6},{5,7},{6,4},{7,5},{8,10},{9,11},{10,... | collective-permute-start | bytes 98312 | tf_op jit(solution)/shard_map/ppermute | solution.py:504
  86.3 3.9 %collective-permute-start.15 = (f32[16,512]{1,0:T(8,128)S(1)}, f32[16,512]{1,0:T(8,128)S(1)}, u32[]{:S(2)}, u32[]{:S(2)}) collective-permute-start(f32[16,512]{1,0:T(8,128)S(1)} %shard_map.111.own_ref), channel_id=1, source_target_pairs={{0,1},{1,2},{2,3},{3,0},{4,5},{5,6},{6,7},{7,4},{8,9},{9,10},{10,1... | collective-permute-start | bytes 98312 | tf_op jit(solution)/shard_map/ppermute | solution.py:504
  86.7 5.1 %collective-permute-start.16 = (f32[16,512]{1,0:T(8,128)S(1)}, f32[16,512]{1,0:T(8,128)S(1)}, u32[]{:S(2)}, u32[]{:S(2)}) collective-permute-start(f32[16,512]{1,0:T(8,128)S(1)} %shard_map.111.own_ref), channel_id=1, source_target_pairs={{0,3},{1,0},{2,1},{3,2},{4,7},{5,4},{6,5},{7,6},{8,11},{9,8},{10,9... | collective-permute-start | bytes 98312 | tf_op jit(solution)/shard_map/ppermute | solution.py:504
